TPU v7x, 32 devices: a whole 2x2x4 slice. The times are simulated.
32 devices in a mesh: dp: 4 (over y, core), ctx: 4 (over z), tp: 2 (over x).
Axes of the slice: x: 2, y: 2, z: 4, core: 2. Of those that a mesh axis runs over, the one named last changes fastest.
Arguments:
- prompt_in: bfloat16 [8, 1024, 768], P('dp', ('ctx', 'tp')), may hold values from -6 to 6
- cont_in: bfloat16 [8, 8, 128, 768], P('dp', 'ctx', 'tp'), may hold values from -6 to 6
- prompt_embed: bfloat16 [8, 1024, 768], P('dp', ('ctx', 'tp')), may hold values from -6 to 6
- cont_embed: bfloat16 [8, 8, 128, 768], P('dp', 'ctx', 'tp'), may hold values from -6 to 6
- prompt_earlier: bfloat16 [3, 8, 1024, 768], P(None, 'dp', ('ctx', 'tp')), may hold values from -6 to 6
- cont_earlier: bfloat16 [3, 8, 8, 128, 768], P(None, 'dp', 'ctx', 'tp'), may hold values from -6 to 6
- ln1_gain: bfloat16 [768], P('dp'), may hold values from 0.5 to 1.5
- ln1_bias: bfloat16 [768], P('dp'), may hold values from -1.75 to 1.75
- ln2_gain: bfloat16 [768], P('dp'), may hold values from 0.5 to 1.5
- ln2_bias: bfloat16 [768], P('dp'), may hold values from -1.75 to 1.75
- w_qkv: bfloat16 [768, 3, 768], P('dp', None, 'tp'), may hold values from -0.21875 to 0.21875
- w_out: bfloat16 [768, 768], P('tp', 'dp'), may hold values from -3 to 3
- w_up: bfloat16 [768, 3072], P('dp', 'tp'), may hold values from -0.21875 to 0.21875
- w_down: bfloat16 [3072, 768], P('tp', 'dp'), may hold values from -0.109375 to 0.109375
- mix_weights: float32 [5], replicated, may hold values from 0.3 to 1
- prompt_cot: bfloat16 [8, 1024, 768], P('dp', ('ctx', 'tp')), may hold values from -6 to 6
- cont_cot: bfloat16 [8, 8, 128, 768], P('dp', 'ctx', 'tp'), may hold values from -6 to 6
Outputs:
- prompt_out: bfloat16 [8, 1024, 768], P('dp', ('ctx', 'tp'))
- cont_out: bfloat16 [8, 8, 128, 768], P('dp', 'ctx', 'tp')
- prompt_in_grad: bfloat16 [8, 1024, 768], P('dp', ('ctx', 'tp'))
- cont_in_grad: bfloat16 [8, 8, 128, 768], P('dp', 'ctx', 'tp')
- ln1_gain_grad: float32 [768], P('dp')
- ln1_bias_grad: float32 [768], P('dp')
- ln2_gain_grad: float32 [768], P('dp')
- ln2_bias_grad: float32 [768], P('dp')
- w_qkv_grad: float32 [768, 3, 768], P('dp', None, 'tp')
- w_out_grad: float32 [768, 768], P('tp', 'dp')
- w_up_grad: float32 [768, 3072], P('dp', 'tp')
- w_down_grad: float32 [3072, 768], P('tp', 'dp')
- mix_grad: float32 [5], replicated
All inputs are finite; a program needn't handle non-finite values.
Results may differ from a plain program's by a relative error of at most 0.02.
Values may be sent and summed in bfloat16 or wider, within the bound.
A program may use at most 256 MiB of HBM per device.

v0:
```python
from functools import partial

import jax
import jax.numpy as jnp
from jax import lax
from jax.sharding import PartitionSpec as P

D = 768
HD = 64
PROMPT = 1024
CL = 128


eps_norm = 1e-05
neg_fill = -1e30
theta_base = 10000.0


def norm_rows(features, norm_gain, norm_bias):
    average = jnp.mean(features, axis=-1, keepdims=True)
    centered = features - average
    variance = jnp.mean(centered * centered, axis=-1, keepdims=True)
    return centered * lax.rsqrt(variance + eps_norm) * norm_gain + norm_bias


def norm_pair(row_pair, norm_gain, norm_bias):
    return (
        norm_rows(row_pair[0], norm_gain, norm_bias),
        norm_rows(row_pair[1], norm_gain, norm_bias),
    )


def angle_tables(positions, half_dim):
    frequency = theta_base ** (
        -(jnp.arange(half_dim, dtype=jnp.int32).astype(jnp.float32) / half_dim)
    )
    angles = positions.astype(jnp.float32)[:, None] * frequency[None, :]
    return (jnp.cos(angles), jnp.sin(angles))


def rotate_rows(features, cosine, sine_table):
    half_dim = features.shape[-1] // 2
    leading = features[..., :half_dim]
    trailing = features[..., half_dim:]
    cos_rows = cosine[None, :, None, :]
    sin_rows = sine_table[None, :, None, :]
    return jnp.concatenate(
        [leading * cos_rows - trailing * sin_rows, trailing * cos_rows + leading * sin_rows],
        axis=-1,
    )


def rotate_pair(query_raw, key_raw, cosine, sine_table):
    return (rotate_rows(query_raw, cosine, sine_table), rotate_rows(key_raw, cosine, sine_table))


def gelu_tanh(inputs):
    return jax.nn.gelu(inputs, approximate=True)


def spread(prompt_part, cont_part):
    prompt_full, cont_full = (
        lax.all_gather(prompt_part, "tp", axis=1, tiled=True),
        lax.all_gather(cont_part, "tp", axis=2, tiled=True),
    )
    return jnp.concatenate(
        [prompt_full, cont_full.reshape(cont_full.shape[0], -1, cont_full.shape[3])], axis=1
    )


def collect(joined, block_len, cont_count):
    prompt_part = joined[:, :block_len]
    cont_part = joined[:, block_len:].reshape(joined.shape[0], cont_count, -1, joined.shape[2])
    return (
        lax.psum_scatter(
            prompt_part.astype(jnp.bfloat16), "tp", scatter_dimension=1, tiled=True
        ).astype(jnp.float32),
        lax.psum_scatter(
            cont_part.astype(jnp.bfloat16), "tp", scatter_dimension=2, tiled=True
        ).astype(jnp.float32),
    )


def per_device(
    prompt_in,
    cont_in,
    prompt_embed,
    cont_embed,
    prompt_earlier,
    cont_earlier,
    ln1_gain,
    ln1_bias,
    ln2_gain,
    ln2_bias,
    w_qkv,
    w_out,
    w_up,
    w_down,
    mix_weights,
    prompt_cot,
    cont_cot,
):
    gathered = (
        lax.all_gather(ln1_gain, "dp", axis=0, tiled=True),
        lax.all_gather(ln1_bias, "dp", axis=0, tiled=True),
        lax.all_gather(ln2_gain, "dp", axis=0, tiled=True),
        lax.all_gather(ln2_bias, "dp", axis=0, tiled=True),
        lax.all_gather(w_qkv, "dp", axis=0, tiled=True),
        lax.all_gather(w_out, "dp", axis=1, tiled=True),
        lax.all_gather(w_up, "dp", axis=0, tiled=True),
        lax.all_gather(w_down, "dp", axis=1, tiled=True),
    )
    gain_one = gathered[0].astype(jnp.float32)
    bias_one = gathered[1].astype(jnp.float32)
    gain_two = gathered[2].astype(jnp.float32)
    bias_two = gathered[3].astype(jnp.float32)
    full_qkv, full_out, full_up, full_down = (gathered[4], gathered[5], gathered[6], gathered[7])
    groups = prompt_in.shape[0]
    block_len = prompt_in.shape[1] * lax.axis_size("tp")
    cont_count = cont_in.shape[1]
    head_cols = full_qkv.shape[2]
    local_heads = head_cols // HD
    query_rows = block_len + cont_count * CL
    start_pos = lax.axis_index("ctx") * block_len
    flat_qkv = full_qkv.reshape(D, 3 * head_cols)
    local_index = jnp.arange(cont_count * CL, dtype=jnp.int32)
    prompt_index = start_pos + jnp.arange(block_len, dtype=jnp.int32)
    query_index = jnp.concatenate([prompt_index, PROMPT + local_index])
    query_segment = jnp.concatenate([jnp.zeros((block_len,), jnp.int32), 1 + local_index // CL])
    key_index = jnp.concatenate([jnp.arange(PROMPT, dtype=jnp.int32), PROMPT + local_index])
    key_segment = jnp.concatenate([jnp.zeros((PROMPT,), jnp.int32), 1 + local_index // CL])
    allowed = (key_index[None, :] <= query_index[:, None]) & (
        (key_segment[None, :] == 0) | (key_segment[None, :] == query_segment[:, None])
    )
    positions = jnp.concatenate([prompt_index, PROMPT + local_index % CL])
    cosine, sine_table = angle_tables(positions, HD // 2)
    block_count = groups // 2

    def to_blocks(array):
        return array.reshape((block_count, 2) + array.shape[1:])

    def from_blocks(array):
        return array.reshape((groups,) + array.shape[2:])

    def score_block(query_block, key_block):
        raw_scores = (
            jnp.einsum(
                "bqhd,bkhd->bhqk", query_block, key_block, preferred_element_type=jnp.float32
            )
            * 0.125
        )
        return jnp.where(allowed[None, None], raw_scores, neg_fill)

    def attend_block(member):
        query_block, key_block, value_block = member
        scores = score_block(query_block, key_block)
        row_max = jnp.max(scores, axis=-1, keepdims=True)
        exponent = jnp.exp(scores - row_max)
        row_total = jnp.sum(exponent, axis=-1, keepdims=True)
        weights_low = (exponent / row_total).astype(jnp.bfloat16)
        attended_block = jnp.einsum(
            "bhqk,bkhd->bqhd", weights_low, value_block, preferred_element_type=jnp.float32
        )
        return (attended_block.astype(jnp.bfloat16), (row_max + jnp.log(row_total))[..., 0])

    def attend_back(member):
        query_block, key_block, value_block, grad_block, logsum_block = member
        scores = score_block(query_block, key_block)
        probabilities = jnp.exp(scores - logsum_block[..., None])
        grad_probs = jnp.einsum(
            "bqhd,bkhd->bhqk", grad_block, value_block, preferred_element_type=jnp.float32
        )
        grad_vals = jnp.einsum(
            "bhqk,bqhd->bkhd",
            probabilities.astype(jnp.bfloat16),
            grad_block,
            preferred_element_type=jnp.float32,
        )
        inner_sum = jnp.sum(probabilities * grad_probs, axis=-1, keepdims=True)
        grad_scores = (probabilities * (grad_probs - inner_sum)).astype(jnp.bfloat16)
        grad_query = (
            jnp.einsum(
                "bhqk,bkhd->bqhd", grad_scores, key_block, preferred_element_type=jnp.float32
            )
            * 0.125
        )
        grad_key = (
            jnp.einsum(
                "bhqk,bqhd->bkhd", grad_scores, query_block, preferred_element_type=jnp.float32
            )
            * 0.125
        )
        return (grad_query, grad_key, grad_vals)

    input_pair = (prompt_in.astype(jnp.float32), cont_in.astype(jnp.float32))
    normed_one, first_back = jax.vjp(norm_pair, input_pair, gain_one, bias_one)
    normed_rows = spread(normed_one[0].astype(jnp.bfloat16), normed_one[1].astype(jnp.bfloat16))
    flat_rows = normed_rows.reshape(groups * query_rows, D)
    mixed_qkv = jnp.dot(flat_rows, flat_qkv, preferred_element_type=jnp.float32).reshape(
        groups, query_rows, 3, local_heads, HD
    )
    rotated, rotate_back = jax.vjp(
        partial(rotate_pair, cosine=cosine, sine_table=sine_table),
        mixed_qkv[:, :, 0],
        mixed_qkv[:, :, 1],
    )
    queries = rotated[0].astype(jnp.bfloat16)
    keys_own = rotated[1].astype(jnp.bfloat16)
    values_own = mixed_qkv[:, :, 2].astype(jnp.bfloat16)
    prompt_kv = jnp.stack(
        [
            keys_own[:, :block_len].reshape(groups, block_len, head_cols),
            values_own[:, :block_len].reshape(groups, block_len, head_cols),
        ],
        axis=2,
    )
    all_kv = lax.all_gather(prompt_kv, "ctx", axis=1, tiled=True)
    keys_all = jnp.concatenate(
        [all_kv[:, :, 0].reshape(groups, PROMPT, local_heads, HD), keys_own[:, block_len:]], axis=1
    )
    values_all = jnp.concatenate(
        [all_kv[:, :, 1].reshape(groups, PROMPT, local_heads, HD), values_own[:, block_len:]],
        axis=1,
    )
    attended, logsum = lax.map(
        attend_block, (to_blocks(queries), to_blocks(keys_all), to_blocks(values_all))
    )
    flat_attended = from_blocks(attended).reshape(groups * query_rows, head_cols)
    branch = jnp.dot(flat_attended, full_out, preferred_element_type=jnp.float32).reshape(
        groups, query_rows, D
    )
    branch_pair = collect(branch, block_len, cont_count)
    resid_pair = (input_pair[0] + branch_pair[0], input_pair[1] + branch_pair[1])
    normed_second, second_back = jax.vjp(norm_pair, resid_pair, gain_two, bias_two)
    normed_two = spread(
        normed_second[0].astype(jnp.bfloat16), normed_second[1].astype(jnp.bfloat16)
    )
    flat_two = normed_two.reshape(groups * query_rows, D)
    up_proj = jnp.dot(flat_two, full_up, preferred_element_type=jnp.float32)
    activated, gelu_back = jax.vjp(gelu_tanh, up_proj)
    activated_low = activated.astype(jnp.bfloat16)
    down_proj = jnp.dot(activated_low, full_down, preferred_element_type=jnp.float32).reshape(
        groups, query_rows, D
    )
    down_pair = collect(down_proj, block_len, cont_count)
    block_pair = (resid_pair[0] + down_pair[0], resid_pair[1] + down_pair[1])
    embed_pair = (prompt_embed.astype(jnp.float32), cont_embed.astype(jnp.float32))
    early_pair = (prompt_earlier.astype(jnp.float32), cont_earlier.astype(jnp.float32))
    cot_pair = (prompt_cot.astype(jnp.float32), cont_cot.astype(jnp.float32))
    out_pair = tuple(
        (
            mix_weights[0] * embed_pair[which]
            + mix_weights[1] * early_pair[which][0]
            + mix_weights[2] * early_pair[which][1]
            + mix_weights[3] * early_pair[which][2]
            + mix_weights[4] * block_pair[which]
            for which in (0, 1)
        )
    )
    mix_local = jnp.stack(
        [
            jnp.sum(cot_pair[0] * embed_pair[0]) + jnp.sum(cot_pair[1] * embed_pair[1]),
            jnp.sum(cot_pair[0] * early_pair[0][0]) + jnp.sum(cot_pair[1] * early_pair[1][0]),
            jnp.sum(cot_pair[0] * early_pair[0][1]) + jnp.sum(cot_pair[1] * early_pair[1][1]),
            jnp.sum(cot_pair[0] * early_pair[0][2]) + jnp.sum(cot_pair[1] * early_pair[1][2]),
            jnp.sum(cot_pair[0] * block_pair[0]) + jnp.sum(cot_pair[1] * block_pair[1]),
        ]
    )
    grad_block = (mix_weights[4] * cot_pair[0], mix_weights[4] * cot_pair[1])
    grad_down = spread(
        grad_block[0].astype(jnp.bfloat16), grad_block[1].astype(jnp.bfloat16)
    ).reshape(groups * query_rows, D)
    grad_wdown = jnp.dot(activated_low.T, grad_down, preferred_element_type=jnp.float32)
    grad_activated = jnp.dot(grad_down, full_down.T, preferred_element_type=jnp.float32)
    grad_upper = gelu_back(grad_activated)[0].astype(jnp.bfloat16)
    grad_wup = jnp.dot(flat_two.T, grad_upper, preferred_element_type=jnp.float32)
    grad_normed_two = collect(
        jnp.dot(grad_upper, full_up.T, preferred_element_type=jnp.float32).reshape(
            groups, query_rows, D
        ),
        block_len,
        cont_count,
    )
    grad_resid_norm, grad_gain_two, grad_bias_two = second_back(
        (grad_normed_two[0], grad_normed_two[1])
    )
    grad_resid = (grad_block[0] + grad_resid_norm[0], grad_block[1] + grad_resid_norm[1])
    grad_branch = spread(
        grad_resid[0].astype(jnp.bfloat16), grad_resid[1].astype(jnp.bfloat16)
    ).reshape(groups * query_rows, D)
    grad_wout = jnp.dot(flat_attended.T, grad_branch, preferred_element_type=jnp.float32)
    grad_attended = (
        jnp.dot(grad_branch, full_out.T, preferred_element_type=jnp.float32)
        .astype(jnp.bfloat16)
        .reshape(groups, query_rows, local_heads, HD)
    )
    grad_query, grad_key, grad_vals = lax.map(
        attend_back,
        (
            to_blocks(queries),
            to_blocks(keys_all),
            to_blocks(values_all),
            to_blocks(grad_attended),
            logsum,
        ),
    )
    grad_query = from_blocks(grad_query)
    grad_key = from_blocks(grad_key)
    grad_vals = from_blocks(grad_vals)
    prompt_grads = jnp.stack(
        [
            grad_key[:, :PROMPT].reshape(groups, PROMPT, head_cols),
            grad_vals[:, :PROMPT].reshape(groups, PROMPT, head_cols),
        ],
        axis=2,
    )
    own_grads = lax.psum_scatter(
        prompt_grads.astype(jnp.bfloat16), "ctx", scatter_dimension=1, tiled=True
    ).astype(jnp.float32)
    grad_keys_own = jnp.concatenate(
        [own_grads[:, :, 0].reshape(groups, block_len, local_heads, HD), grad_key[:, PROMPT:]],
        axis=1,
    )
    grad_values_own = jnp.concatenate(
        [own_grads[:, :, 1].reshape(groups, block_len, local_heads, HD), grad_vals[:, PROMPT:]],
        axis=1,
    )
    grad_query_raw, grad_key_raw = rotate_back((grad_query, grad_keys_own))
    grad_mixed = (
        jnp.stack([grad_query_raw, grad_key_raw, grad_values_own], axis=2)
        .astype(jnp.bfloat16)
        .reshape(groups * query_rows, 3 * head_cols)
    )
    grad_wqkv = jnp.dot(flat_rows.T, grad_mixed, preferred_element_type=jnp.float32).reshape(
        D, 3, head_cols
    )
    grad_normed_one = collect(
        jnp.dot(grad_mixed, flat_qkv.T, preferred_element_type=jnp.float32).reshape(
            groups, query_rows, D
        ),
        block_len,
        cont_count,
    )
    grad_input_norm, grad_gain_one, grad_bias_one = first_back(
        (grad_normed_one[0], grad_normed_one[1])
    )
    grad_input = (grad_resid[0] + grad_input_norm[0], grad_resid[1] + grad_input_norm[1])
    summed = (
        lax.psum(grad_wqkv.astype(jnp.bfloat16), "ctx").astype(jnp.float32),
        lax.psum(grad_wout.astype(jnp.bfloat16), "ctx").astype(jnp.float32),
        lax.psum(grad_wup.astype(jnp.bfloat16), "ctx").astype(jnp.float32),
        lax.psum(grad_wdown.astype(jnp.bfloat16), "ctx").astype(jnp.float32),
    )
    reduced = (
        lax.psum_scatter(
            summed[0].astype(jnp.bfloat16), "dp", scatter_dimension=0, tiled=True
        ).astype(jnp.float32),
        lax.psum_scatter(
            summed[1].astype(jnp.bfloat16), "dp", scatter_dimension=1, tiled=True
        ).astype(jnp.float32),
        lax.psum_scatter(
            summed[2].astype(jnp.bfloat16), "dp", scatter_dimension=0, tiled=True
        ).astype(jnp.float32),
        lax.psum_scatter(
            summed[3].astype(jnp.bfloat16), "dp", scatter_dimension=1, tiled=True
        ).astype(jnp.float32),
    )
    small_sums = lax.psum(
        (grad_gain_one, grad_bias_one, grad_gain_two, grad_bias_two, mix_local), ("dp", "ctx", "tp")
    )
    shard_len = D // lax.axis_size("dp")
    shard_start = lax.axis_index("dp") * shard_len

    def own_slice(vector):
        return lax.dynamic_slice_in_dim(vector, shard_start, shard_len)

    return (
        out_pair[0].astype(jnp.bfloat16),
        out_pair[1].astype(jnp.bfloat16),
        grad_input[0].astype(jnp.bfloat16),
        grad_input[1].astype(jnp.bfloat16),
        own_slice(small_sums[0]),
        own_slice(small_sums[1]),
        own_slice(small_sums[2]),
        own_slice(small_sums[3]),
        reduced[0],
        reduced[1],
        reduced[2],
        reduced[3],
        small_sums[4],
    )


def solution(mesh):
    in_specs = (
        P("dp", ("ctx", "tp"), None),
        P("dp", "ctx", "tp", None),
        P("dp", ("ctx", "tp"), None),
        P("dp", "ctx", "tp", None),
        P(None, "dp", ("ctx", "tp"), None),
        P(None, "dp", "ctx", "tp", None),
        P("dp"),
        P("dp"),
        P("dp"),
        P("dp"),
        P("dp", None, "tp"),
        P("tp", "dp"),
        P("dp", "tp"),
        P("tp", "dp"),
        P(),
        P("dp", ("ctx", "tp"), None),
        P("dp", "ctx", "tp", None),
    )
    out_specs = (
        P("dp", ("ctx", "tp"), None),
        P("dp", "ctx", "tp", None),
        P("dp", ("ctx", "tp"), None),
        P("dp", "ctx", "tp", None),
        P("dp"),
        P("dp"),
        P("dp"),
        P("dp"),
        P("dp", None, "tp"),
        P("tp", "dp"),
        P("dp", "tp"),
        P("tp", "dp"),
        P(),
    )
    return jax.shard_map(
        per_device, mesh=mesh, in_specs=in_specs, out_specs=out_specs, check_vma=False
    )
```

profile of v0, /device:TPU:0, one launch (start us, length us, event | category | flops | bytes accessed | tf_op | source)
XLA Modules:
  0.0 783.1 jit_solution(10265192341165547993)
XLA Ops:
  13.3 8.5 %all-reduce.12 = (bf16[768]{0:T(1024)(128)(2,1)S(1)}, bf16[768]{0:T(1024)(128)(2,1)S(1)}, bf16[768]{0:T(1024)(128)(2,1)S(1)}, bf16[768]{0:T(1024)(128)(2,1)S(1)}) all-reduce(bf16[768]{0:T(1024)(128)(2,1)S(1)} %dynamic-update-slice.1, bf16[768]{0:T(1024)(128)(2,1)S(1)} %dynamic-update-slice, ...), channel_id=1, replica_groups=mesh['dp'=4,'ctx'=4,'tp'=2] {'dp'}, use_global_device_ids=true, to_apply=%add.7 | all-reduce | flops 3072 | bytes 12288
  27.9 10.1 %all_gather.53 = bf16[2,256,768]{2,1,0:T(8,128)(2,1)S(1)} all-gather(bf16[2,128,768]{2,1,0:T(8,128)(2,1)S(1)} %fusion.48), channel_id=1, replica_groups=mesh['dp'=4,'ctx'=4,'tp'=2] {'tp'}, dimensions={1}, use_global_device_ids=true | all-gather | bytes 1179648 | tf_op jit(solution)/shard_map/all_gather | solution.py:63
  38.4 9.2 %all_gather.54 = bf16[2,2,128,768]{3,2,1,0:T(8,128)(2,1)S(1)} all-gather(bf16[2,2,64,768]{3,2,1,0:T(8,128)(2,1)S(1)} %fusion.46), channel_id=1, replica_groups=mesh['dp'=4,'ctx'=4,'tp'=2] {'tp'}, dimensions={2}, use_global_device_ids=true | all-gather | bytes 1179648 | tf_op jit(solution)/shard_map/all_gather | solution.py:64
  48.6 3.8 copy.49
  52.4 3.5 fusion.21
  60.2 9.8 %all_gather.57 = bf16[384,768]{0,1:T(8,128)(2,1)} all-gather(bf16[384,192]{0,1:T(8,128)(2,1)S(1)} %copy-done.49), channel_id=1, replica_groups=mesh['dp'=4,'ctx'=4,'tp'=2] {'dp'}, dimensions={1}, use_global_device_ids=true | all-gather | bytes 737280 | tf_op jit(solution)/shard_map/all_gather | solution.py:109
  71.6 54.0 %all-gather.7.cloned.1.call-done = bf16[2,1024,2,384]{1,3,0,2:T(8,128)(2,1)} async-done(((bf16[2,256,2,384]{1,3,0,2:T(8,128)(2,1)}), bf16[2,1024,2,384]{1,3,0,2:T(8,128)(2,1)}) %all-gather.7.cloned.1.call-update) | async-done | bytes 3145744 | tf_op jit(solution)/shard_map/all_gather | solution.py:217
  125.6 2.3 fusion.109
  127.9 13.7 %fusion.116 = (f32[2,6,512]{2,1,0:T(8,128)S(1)}, f32[2,6,512,1280]{3,2,1,0:T(8,128)}) fusion(bf16[2,512,6,32]{1,3,2,0:T(8,128)(2,1)S(1)} %get-tuple-element.120, bf16[2,512,6,32]{1,3,2,0:T(8,128)(2,1)S(1)} %get-tuple-element.119, bf16[2,1024,6,64]{1,3,2,0:T(8,128)(2,1)S(1)} %bitcast.180, bf16[2,512,6,32]{1,3,2,0:T(8,128)(2,1)S(1)} %get-tuple-element.135, ...), kind=kOutput, calls=%fused_computation.244 | convolution fusion | flops 1040640000 | bytes 35282944 | tf_op jit(solution)/shard_map/while/body/eval_jaxpr/bqhd,bkhd->bhqk/dot_general | solution.py:147
  141.6 13.3 %fusion = f32[2,6,512]{2,1,0:T(8,128)S(1)} fusion(f32[2,6,512,1280]{3,2,1,0:T(8,128)} %get-tuple-element.147, f32[2,6,512]{2,1,0:T(8,128)S(1)} %get-tuple-element.146), kind=kLoop, calls=%fused_computation.6 | loop fusion | flops 15722496 | bytes 31506432 | tf_op jit(solution)/shard_map/while/body/eval_jaxpr/reduce_sum | solution.py:159
  154.9 12.3 %fusion.23 = bf16[2,6,64,512]{3,2,1,0:T(8,128)(2,1)S(1)} fusion(f32[2,6,512,1280]{3,2,1,0:T(8,128)} %get-tuple-element.147, f32[2,6,512]{2,1,0:T(8,128)S(1)} %fusion, f32[2,6,512]{2,1,0:T(8,128)} %copy-done.50, bf16[2,256,6,64]{1,3,2,0:T(8,128)(2,1)S(1)} %get-tuple-element.131, bf16[2,1024,6,64]{1,3,2,0:T(8,128)(2,1)S(1)} %bitcast.153), kind=kOutput, calls=%fused_computation.70 | convolution fusion | flops 1034551296 | bytes 34258944 | tf_op jit(solution)/shard_map/while/body/eval_jaxpr/bhqk,bkhd->bqhd/dot_general | solution.py:161
  167.2 2.4 convolution_convert_fusion.3
  174.1 20.1 %all_gather.64 = bf16[2,256,768]{2,1,0:T(8,128)(2,1)S(1)} all-gather(bf16[2,128,768]{2,1,0:T(8,128)(2,1)S(1)} %fusion.40), channel_id=1, replica_groups=mesh['dp'=4,'ctx'=4,'tp'=2] {'tp'}, dimensions={1}, use_global_device_ids=true | all-gather | bytes 1179648 | tf_op jit(solution)/shard_map/all_gather | solution.py:63
  194.2 14.2 %all_gather.65 = bf16[2,2,128,768]{3,2,1,0:T(8,128)(2,1)S(1)} all-gather(bf16[2,2,64,768]{3,2,1,0:T(8,128)(2,1)S(1)} %fusion.42), channel_id=1, replica_groups=mesh['dp'=4,'ctx'=4,'tp'=2] {'tp'}, dimensions={2}, use_global_device_ids=true | all-gather | bytes 1179648 | tf_op jit(solution)/shard_map/all_gather | solution.py:64
  208.6 6.7 fusion.117
  221.2 10.6 %all_gather.60 = bf16[2,256,768]{2,1,0:T(8,128)(2,1)S(1)} all-gather(bf16[2,128,768]{2,1,0:T(8,128)(2,1)S(1)} %add_convert_fusion.3), channel_id=1, replica_groups=mesh['dp'=4,'ctx'=4,'tp'=2] {'tp'}, dimensions={1}, use_global_device_ids=true | all-gather | bytes 1179648 | tf_op jit(solution)/shard_map/all_gather | solution.py:63
  232.8 10.2 %all_gather.61 = bf16[2,2,128,768]{3,2,1,0:T(8,128)(2,1)S(1)} all-gather(bf16[2,2,64,768]{3,2,1,0:T(8,128)(2,1)S(1)} %add_convert_fusion.2), channel_id=1, replica_groups=mesh['dp'=4,'ctx'=4,'tp'=2] {'tp'}, dimensions={2}, use_global_device_ids=true | all-gather | bytes 1179648 | tf_op jit(solution)/shard_map/all_gather | solution.py:64
  244.3 10.3 %fusion.12 = (bf16[1024,1536]{1,0:T(8,128)(2,1)S(1)}, f32[1024,1536]{1,0:T(8,128)}) fusion(f32[1024,1536]{1,0:T(8,128)} %fusion.117, bf16[1024,768]{1,0:T(8,128)(2,1)} %bitcast.173, bf16[768,1536]{1,0:T(8,128)(2,1)} %all-gather.9.cloned.1.call-done), kind=kOutput, calls=%fused_computation.19 | convolution fusion | flops 2447376384 | bytes 19660800 | tf_op jit(solution)/shard_map/dot_general | solution.py:239
  254.6 2.6 convolution_convert_fusion.5
  258.7 7.3 convolution_convert_fusion.6
  272.5 2.7 reduce-scatter.24.cloned.1.call-done
  275.2 20.4 %reduce-scatter.20.cloned.1.call-done = bf16[2,2,64,768]{3,2,1,0:T(8,128)(2,1)} async-done(((bf16[2,2,128,768]{3,2,1,0:T(8,128)(2,1)}), bf16[2,2,64,768]{3,2,1,0:T(8,128)(2,1)}) %reduce-scatter.20.cloned.1.call-update) | async-done | bytes 393232 | tf_op jit(solution)/shard_map/reduce_scatter | solution.py:78
  295.6 7.5 fusion.80
  303.8 12.2 %reduce-scatter.22.cloned.1.call-done = bf16[2,128,768]{2,1,0:T(8,128)(2,1)} async-done(((bf16[2,256,768]{2,1,0:T(8,128)(2,1)}), bf16[2,128,768]{2,1,0:T(8,128)(2,1)}) %reduce-scatter.22.cloned.1.call-update) | async-done | bytes 393232 | tf_op jit(solution)/shard_map/reduce_scatter | solution.py:75
  315.9 20.2 %reduce-scatter.18.cloned.1.call-done = bf16[2,128,768]{2,1,0:T(8,128)(2,1)} async-done(((bf16[2,256,768]{2,1,0:T(8,128)(2,1)}), bf16[2,128,768]{2,1,0:T(8,128)(2,1)}) %reduce-scatter.18.cloned.1.call-update) | async-done | bytes 393232 | tf_op jit(solution)/shard_map/reduce_scatter | solution.py:75
  336.2 7.5 fusion.75
  348.3 11.5 %all_gather.67 = bf16[2,2,128,768]{3,2,1,0:T(8,128)(2,1)S(1)} all-gather(bf16[2,2,64,768]{3,2,1,0:T(8,128)(2,1)S(1)} %fusion.90), channel_id=1, replica_groups=mesh['dp'=4,'ctx'=4,'tp'=2] {'tp'}, dimensions={2}, use_global_device_ids=true | all-gather | bytes 1179648 | tf_op jit(solution)/shard_map/all_gather | solution.py:64
  360.8 11.0 %all_gather.66 = bf16[2,256,768]{2,1,0:T(8,128)(2,1)S(1)} all-gather(bf16[2,128,768]{2,1,0:T(8,128)(2,1)S(1)} %fusion.91), channel_id=1, replica_groups=mesh['dp'=4,'ctx'=4,'tp'=2] {'tp'}, dimensions={1}, use_global_device_ids=true | all-gather | bytes 1179648 | tf_op jit(solution)/shard_map/all_gather | solution.py:63
  375.0 12.9 %fusion.15 = bf16[2,1280,6,64]{1,3,2,0:T(8,128)(2,1)S(1)} fusion(f32[2,6,512,1280]{3,2,1,0:T(8,128)} %get-tuple-element.147, f32[2,6,512]{2,1,0:T(8,128)} %log_add_fusion, bf16[2,512,6,64]{1,0,3,2:T(2,128)(2,1)S(1)} %squeeze.89), kind=kOutput, calls=%fused_computation.26 | convolution fusion | flops 1022361600 | bytes 34234368 | tf_op jit(solution)/shard_map/while/body/eval_jaxpr/bhqk,bqhd->bkhd/dot_general | solution.py:173
  387.9 24.6 %multiply_reduce_fusion = (f32[2,6,512]{2,1,0:T(8,128)S(1)}, f32[2,6,512,1280]{3,2,1,0:T(8,128)}) fusion(f32[2,6,512,1280]{3,2,1,0:T(8,128)} %get-tuple-element.147, f32[2,6,512]{2,1,0:T(8,128)S(1)} %copy-done.21, bf16[2,256,6,64]{1,3,2,0:T(8,128)(2,1)S(1)} %copy-done.23, bf16[2,1024,6,64]{1,3,2,0:T(8,128)(2,1)S(1)} %bitcast.154, ...), kind=kOutput, calls=%fused_computation.1 | convolution fusion | flops 1034151936 | bytes 65716224 | tf_op jit(solution)/shard_map/while/body/eval_jaxpr/bqhd,bkhd->bhqk/dot_general | solution.py:170
  412.5 26.3 %multiply_convert_fusion = bf16[2,6,512,1280]{3,2,1,0:T(8,128)(2,1)} fusion(f32[2,6,512,1280]{3,2,1,0:T(8,128)} %get-tuple-element.151, f32[2,6,512,1280]{3,2,1,0:T(8,128)} %get-tuple-element.147, f32[2,6,512]{2,1,0:T(8,128)S(1)} %get-tuple-element.150, f32[2,6,512]{2,1,0:T(8,128)S(1)} %copy-done.21), kind=kLoop, calls=%fused_computation | loop fusion | flops 31457280 | bytes 78692352 | tf_op jit(solution)/shard_map/while/body/eval_jaxpr/convert_element_type | solution.py:180
  438.9 8.2 %fusion.18 = f32[2,1280,6,64]{1,3,2,0:T(8,128)S(1)} fusion(bf16[2,6,512,1280]{3,2,1,0:T(8,128)(2,1)} %multiply_convert_fusion, bf16[2,512,6,32]{1,3,2,0:T(8,128)(2,1)S(1)} %copy-done.34, bf16[2,512,6,32]{1,3,2,0:T(8,128)(2,1)S(1)} %copy-done.36), kind=kOutput, calls=%fused_computation.27 | convolution fusion | flops 1009188864 | bytes 20447232 | tf_op jit(solution)/shard_map/while/body/eval_jaxpr/bhqk,bqhd->bkhd/dot_general | solution.py:188
  453.4 12.7 %multiply_bitcast_fusion = f32[2,512,6,64]{1,3,2,0:T(8,128)} fusion(bf16[2,6,512,1280]{3,2,1,0:T(8,128)(2,1)} %multiply_convert_fusion, bf16[2,512,6,32]{1,3,2,0:T(8,128)(2,1)S(1)} %copy-done.30, bf16[2,512,6,32]{1,3,2,0:T(8,128)(2,1)S(1)} %copy-done.28, bf16[2,1024,6,64]{1,3,2,0:T(8,128)(2,1)} %bitcast.181), kind=kOutput, calls=%fused_computation.68 | convolution fusion | flops 1015873536 | bytes 19660800 | tf_op jit(solution)/shard_map/while/body/eval_jaxpr/bhqk,bkhd->bqhd/dot_general | solution.py:182
  466.1 46.7 %reduce-scatter.26.cloned.1.call-done = bf16[2,256,2,384]{1,3,0,2:T(8,128)(2,1)} async-done(((bf16[2,1024,2,384]{1,3,0,2:T(8,128)(2,1)}), bf16[2,256,2,384]{1,3,0,2:T(8,128)(2,1)}) %reduce-scatter.26.cloned.1.call-update) | async-done | bytes 786448 | tf_op jit(solution)/shard_map/reduce_scatter | solution.py:317
  518.7 2.3 convolution_convert_fusion.4
  527.3 6.7 convolution_convert_fusion.1
  534.3 7.6 convolution_convert_fusion
  543.5 2.4 copy.58
  546.6 3.5 convolution_convert_fusion.2
  562.9 22.5 %reduce-scatter.34.cloned.1.call-done = bf16[384,192]{0,1:T(8,128)(2,1)} async-done(((bf16[384,768]{0,1:T(8,128)(2,1)}), bf16[384,192]{0,1:T(8,128)(2,1)}) %reduce-scatter.34.cloned.1.call-update) | async-done | bytes 147472 | tf_op jit(solution)/shard_map/reduce_scatter | solution.py:358
  585.4 35.5 %reduce-scatter.36.cloned.1.call-done = bf16[192,1536]{1,0:T(8,128)(2,1)} async-done(((bf16[768,1536]{1,0:T(8,128)(2,1)}), bf16[192,1536]{1,0:T(8,128)(2,1)}) %reduce-scatter.36.cloned.1.call-update) | async-done | bytes 589840 | tf_op jit(solution)/shard_map/reduce_scatter | solution.py:361
  620.8 35.6 %reduce-scatter.38.cloned.1.call-done = bf16[1536,192]{0,1:T(8,128)(2,1)} async-done(((bf16[1536,768]{0,1:T(8,128)(2,1)}), bf16[1536,192]{0,1:T(8,128)(2,1)}) %reduce-scatter.38.cloned.1.call-update) | async-done | bytes 589840 | tf_op jit(solution)/shard_map/reduce_scatter | solution.py:364
  656.5 31.8 %reduce-scatter.32.cloned.1.call-done = bf16[192,3,384]{2,0,1:T(8,128)(2,1)} async-done(((bf16[768,3,384]{2,0,1:T(8,128)(2,1)}), bf16[192,3,384]{2,0,1:T(8,128)(2,1)}) %reduce-scatter.32.cloned.1.call-update) | async-done | bytes 442384 | tf_op jit(solution)/shard_map/reduce_scatter | solution.py:355
  694.8 43.3 %all-reduce.10 = (f32[768]{0:T(1024)}, f32[768]{0:T(1024)}, f32[768]{0:T(1024)}, f32[768]{0:T(1024)}, f32[5]{0:T(128)}) all-reduce(f32[768]{0:T(1024)} %add_any.92, f32[768]{0:T(1024)} %add_any.93, f32[768]{0:T(1024)} %add_any.94, f32[768]{0:T(1024)} %add_any.95, f32[5]{0:T(128)} %stack.48), channel_id=1, replica_groups=mesh['dp'=4,'ctx'=4,'tp'=2] {'dp','ctx','tp'}, use_global_device_ids=true, to_apply=%region_30.31 | all-reduce | flops 3077 | bytes 24616 | tf_op jit(solution)/shard_map/psum | solution.py:368
  744.7 3.0 add_convert_fusion.1
  747.7 2.7 add_convert_fusion
  750.4 18.3 %all-reduce.15.cloned.1.call-done = (bf16[192,3,384]{2,0,1:T(8,128)(2,1)}, bf16[384,192]{0,1:T(8,128)(2,1)}, bf16[192,1536]{1,0:T(8,128)(2,1)}, bf16[1536,192]{0,1:T(8,128)(2,1)}) async-done(((bf16[192,3,384]{2,0,1:T(8,128)(2,1)}, bf16[384,192]{0,1:T(8,128)(2,1)}, bf16[192,1536]{1,0:T(8,128)(2,1)}, bf16[1536,192]{0,1:T(8,128)(2,1)}), (bf16[192,3,384]{2,0,1:T(8,128)(2,1)}, bf16[384,192]{0,1:T(8,128)(2,1)}, ...) | async-done | bytes 1769488 | tf_op jit(solution)/shard_map/psum | solution.py:349
  772.4 2.2 convert_element_type.273
  (326 shorter events, 93.4 us)
Async XLA Ops:
  7.2 30.9 %copy-start.1 = (bf16[2,2,64,768]{3,2,1,0:T(8,128)(2,1)S(1)}, bf16[2,2,64,768]{3,2,1,0:T(8,128)(2,1)}, u32[]{:S(2)}) copy-start(bf16[2,2,64,768]{3,2,1,0:T(8,128)(2,1)} %param.18) | copy-start | bytes 1179652
  7.2 41.4 %all-gather.5.cloned.1.call-start = ((), (), s32[]{:S(2)}) async-start(), calls=%async_computation.13 | async-start | bytes 2211840 | tf_op jit(solution)/shard_map/all_gather | solution.py:108
  7.9 117.6 %all-gather.7.cloned.1.call-start = ((), (), s32[]{:S(2)}) async-start(), calls=%async_computation.14 | async-start | bytes 3932160 | tf_op jit(solution)/shard_map/all_gather | solution.py:217
  21.8 25.8 %copy-start.47 = (f32[768]{0:T(1024)}, f32[768]{0:T(1024)S(1)}, u32[]{:S(2)}) copy-start(f32[768]{0:T(1024)S(1)} %convert_element_type.220) | copy-start | bytes 9220
  24.1 23.5 %copy-start.58 = (f32[2,128]{1,0:T(2,128)}, f32[2,128]{1,0:T(2,128)S(1)}, u32[]{:S(2)}) copy-start(f32[2,128]{1,0:T(2,128)S(1)} %broadcast_multiply_fusion.3) | copy-start | bytes 3076
  25.4 22.2 %copy-start.54 = (f32[2,2,64]{2,1,0:T(2,128)}, f32[2,2,64]{2,1,0:T(2,128)S(1)}, u32[]{:S(2)}) copy-start(f32[2,2,64]{2,1,0:T(2,128)S(1)} %broadcast_multiply_fusion.1) | copy-start | bytes 3076
  26.6 21.0 %copy-start.65 = (f32[2,2,64]{2,1,0:T(2,128)}, f32[2,2,64]{2,1,0:T(2,128)S(1)}, u32[]{:S(2)}) copy-start(f32[2,2,64]{2,1,0:T(2,128)S(1)} %fusion.63) | copy-start | bytes 3076
  56.6 98.2 %copy-start.22 = (bf16[2,256,6,64]{1,3,2,0:T(8,128)(2,1)}, bf16[2,256,6,64]{1,3,2,0:T(8,128)(2,1)S(1)}, u32[]{:S(2)}) copy-start(bf16[2,256,6,64]{1,3,2,0:T(8,128)(2,1)S(1)} %get-tuple-element.131) | copy-start | bytes 1179652
  58.3 69.6 %copy-start.27 = (bf16[2,512,6,32]{1,3,2,0:T(8,128)(2,1)}, bf16[2,512,6,32]{1,3,2,0:T(8,128)(2,1)S(1)}, u32[]{:S(2)}) copy-start(bf16[2,512,6,32]{1,3,2,0:T(8,128)(2,1)S(1)} %get-tuple-element.119) | copy-start | bytes 1179652
  58.3 69.6 %copy-start.29 = (bf16[2,512,6,32]{1,3,2,0:T(8,128)(2,1)}, bf16[2,512,6,32]{1,3,2,0:T(8,128)(2,1)S(1)}, u32[]{:S(2)}) copy-start(bf16[2,512,6,32]{1,3,2,0:T(8,128)(2,1)S(1)} %get-tuple-element.120) | copy-start | bytes 1179652
  58.3 69.6 %copy-start.33 = (bf16[2,512,6,32]{1,3,2,0:T(8,128)(2,1)}, bf16[2,512,6,32]{1,3,2,0:T(8,128)(2,1)S(1)}, u32[]{:S(2)}) copy-start(bf16[2,512,6,32]{1,3,2,0:T(8,128)(2,1)S(1)} %get-tuple-element.135) | copy-start | bytes 1179652
  59.3 149.3 %all-gather.11.cloned.1.call-start = ((), (), s32[]{:S(2)}) async-start(), calls=%async_computation.18 | async-start | bytes 2949120 | tf_op jit(solution)/shard_map/all_gather | solution.py:111
  60.0 155.2 %reduce-scatter.14.cloned.1.call-start = ((), (), s32[]{:S(2)}) async-start(), calls=%async_computation.15 | async-start | bytes 1179648 | tf_op jit(solution)/shard_map/reduce_scatter | solution.py:75
  127.8 27.0 %copy-start.15 = (bf16[2,1024,1,384]{1,3,0,2:T(8,128)(2,1)}, bf16[2,1024,1,384]{1,3,0,2:T(8,128)(2,1)S(1)}, u32[]{:S(2)}) copy-start(bf16[2,1024,1,384]{1,3,0,2:T(8,128)(2,1)S(1)} %get-tuple-element.113) | copy-start | bytes 4718596
  170.9 45.6 %reduce-scatter.16.cloned.1.call-start = ((), (), s32[]{:S(2)}) async-start(), calls=%async_computation.16 | async-start | bytes 1179648 | tf_op jit(solution)/shard_map/reduce_scatter | solution.py:78
  171.5 72.8 %all-gather.9.cloned.1.call-start = ((), (), s32[]{:S(2)}) async-start(), calls=%async_computation.17 | async-start | bytes 2949120 | tf_op jit(solution)/shard_map/all_gather | solution.py:110
  172.1 103.2 %reduce-scatter.24.cloned.1.call-start = ((), (), s32[]{:S(2)}) async-start(), calls=%async_computation.22 | async-start | bytes 1179648 | tf_op jit(solution)/shard_map/reduce_scatter | solution.py:78
  194.2 26.1 %copy-start.60 = (f32[768]{0:T(1024)}, f32[768]{0:T(1024)S(1)}, u32[]{:S(2)}) copy-start(f32[768]{0:T(1024)S(1)} %convert_element_type.233) | copy-start | bytes 9220
  217.8 142.0 %copy-start.57 = (f32[2,128]{1,0:T(2,128)}, f32[2,128]{1,0:T(2,128)S(1)}, u32[]{:S(2)}) copy-start(f32[2,128]{1,0:T(2,128)S(1)} %broadcast_multiply_fusion.2) | copy-start | bytes 3076
  220.3 22.7 %copy-start.66 = (f32[2,2,64]{2,1,0:T(2,128)}, f32[2,2,64]{2,1,0:T(2,128)S(1)}, u32[]{:S(2)}) copy-start(f32[2,2,64]{2,1,0:T(2,128)S(1)} %multiply_reduce_fusion.1) | copy-start | bytes 3076
  231.8 115.4 %copy-start.56 = (f32[2,2,64]{2,1,0:T(2,128)}, f32[2,2,64]{2,1,0:T(2,128)S(1)}, u32[]{:S(2)}) copy-start(f32[2,2,64]{2,1,0:T(2,128)S(1)} %fusion.95) | copy-start | bytes 3076
  258.6 37.0 %reduce-scatter.20.cloned.1.call-start = ((), (), s32[]{:S(2)}) async-start(), calls=%async_computation.20 | async-start | bytes 1179648 | tf_op jit(solution)/shard_map/reduce_scatter | solution.py:78
  267.2 48.7 %reduce-scatter.22.cloned.1.call-start = ((), (), s32[]{:S(2)}) async-start(), calls=%async_computation.21 | async-start | bytes 1179648 | tf_op jit(solution)/shard_map/reduce_scatter | solution.py:75
  268.0 68.2 %reduce-scatter.18.cloned.1.call-start = ((), (), s32[]{:S(2)}) async-start(), calls=%async_computation.19 | async-start | bytes 1179648 | tf_op jit(solution)/shard_map/reduce_scatter | solution.py:75
  268.6 244.2 %reduce-scatter.26.cloned.1.call-start = ((), (), s32[]{:S(2)}) async-start(), calls=%async_computation.23 | async-start | bytes 3932160 | tf_op jit(solution)/shard_map/reduce_scatter | solution.py:317
  270.2 25.4 %copy-start.45 = (bf16[2,2,64,768]{3,2,1,0:T(8,128)(2,1)S(1)}, bf16[2,2,64,768]{3,2,1,0:T(8,128)(2,1)}, u32[]{:S(2)}) copy-start(bf16[2,2,64,768]{3,2,1,0:T(8,128)(2,1)} %param.20) | copy-start | bytes 1179652
  271.9 31.3 %copy-start.67 = (f32[2,2,64]{2,1,0:T(2,128)S(1)}, f32[2,2,64]{2,1,0:T(2,128)}, u32[]{:S(2)}) copy-start(f32[2,2,64]{2,1,0:T(2,128)} %copy-done.66) | copy-start | bytes 3076
  271.9 64.3 %copy-start.46 = (bf16[2,128,768]{2,1,0:T(8,128)(2,1)S(1)}, bf16[2,128,768]{2,1,0:T(8,128)(2,1)}, u32[]{:S(2)}) copy-start(bf16[2,128,768]{2,1,0:T(8,128)(2,1)} %param.19) | copy-start | bytes 1179652
  303.8 42.4 %copy-start.11 = (bf16[2,2,64,768]{3,2,1,0:T(8,128)(2,1)S(1)}, bf16[2,2,64,768]{3,2,1,0:T(8,128)(2,1)}, u32[]{:S(2)}) copy-start(bf16[2,2,64,768]{3,2,1,0:T(8,128)(2,1)} %reduce-scatter.24.cloned.1.call-done) | copy-start | bytes 1179652
  315.9 28.4 %copy-start.13 = (bf16[2,128,768]{2,1,0:T(8,128)(2,1)S(1)}, bf16[2,128,768]{2,1,0:T(8,128)(2,1)}, u32[]{:S(2)}) copy-start(bf16[2,128,768]{2,1,0:T(8,128)(2,1)} %reduce-scatter.22.cloned.1.call-done) | copy-start | bytes 1179652
  344.3 15.5 %copy-start.70 = (f32[2,128]{1,0:T(2,128)}, f32[2,128]{1,0:T(2,128)S(1)}, u32[]{:S(2)}) copy-start(f32[2,128]{1,0:T(2,128)S(1)} %multiply_multiply_fusion.5) | copy-start | bytes 3076
  387.9 24.6 %copy-start.6 = (bf16[2,1280,6,64]{1,3,2,0:T(8,128)(2,1)}, bf16[2,1280,6,64]{1,3,2,0:T(8,128)(2,1)S(1)}, u32[]{:S(2)}) copy-start(bf16[2,1280,6,64]{1,3,2,0:T(8,128)(2,1)S(1)} %fusion.15) | copy-start | bytes 5898244
  412.5 26.3 %copy-start.34 = (bf16[2,512,6,32]{1,3,2,0:T(8,128)(2,1)S(1)}, bf16[2,512,6,32]{1,3,2,0:T(8,128)(2,1)}, u32[]{:S(2)}) copy-start(bf16[2,512,6,32]{1,3,2,0:T(8,128)(2,1)} %copy-done.33) | copy-start | bytes 1179652
  412.5 26.3 %copy-start.36 = (bf16[2,512,6,32]{1,3,2,0:T(8,128)(2,1)S(1)}, bf16[2,512,6,32]{1,3,2,0:T(8,128)(2,1)}, u32[]{:S(2)}) copy-start(bf16[2,512,6,32]{1,3,2,0:T(8,128)(2,1)} %get-tuple-element.136) | copy-start | bytes 1179652
  452.3 105.9 %reduce-scatter.28.cloned.1.call-start = ((), (), s32[]{:S(2)}) async-start(), calls=%async_computation.24 | async-start | bytes 1179648 | tf_op jit(solution)/shard_map/reduce_scatter | solution.py:75
  453.4 60.5 %slice-start = ((f32[2,1280,6,64]{1,3,2,0:T(8,128)}), f32[2,256,6,64]{1,3,2,0:T(8,128)S(1)}, s32[]{:S(2)}) async-start(f32[2,1280,6,64]{1,3,2,0:T(8,128)} %copy-done.5), calls=%async_computation.31 | async-start | bytes 1572864 | tf_op jit(solution)/shard_map/slice | solution.py:321
  522.3 38.0 %reduce-scatter.30.cloned.1.call-start = ((), (), s32[]{:S(2)}) async-start(), calls=%async_computation.25 | async-start | bytes 1179648 | tf_op jit(solution)/shard_map/reduce_scatter | solution.py:78
  523.1 62.3 %reduce-scatter.34.cloned.1.call-start = ((), (), s32[]{:S(2)}) async-start(), calls=%async_computation.27 | async-start | bytes 737280 | tf_op jit(solution)/shard_map/reduce_scatter | solution.py:358
  527.2 93.6 %reduce-scatter.36.cloned.1.call-start = ((), (), s32[]{:S(2)}) async-start(), calls=%async_computation.28 | async-start | bytes 2949120 | tf_op jit(solution)/shard_map/reduce_scatter | solution.py:361
  534.0 122.4 %reduce-scatter.38.cloned.1.call-start = ((), (), s32[]{:S(2)}) async-start(), calls=%async_computation.29 | async-start | bytes 2949120 | tf_op jit(solution)/shard_map/reduce_scatter | solution.py:364
  541.9 146.4 %reduce-scatter.32.cloned.1.call-start = ((), (), s32[]{:S(2)}) async-start(), calls=%async_computation.26 | async-start | bytes 2211840 | tf_op jit(solution)/shard_map/reduce_scatter | solution.py:355
  550.1 194.6 %copy-start.4 = (bf16[2,128,768]{2,1,0:T(8,128)(2,1)S(1)}, bf16[2,128,768]{2,1,0:T(8,128)(2,1)}, u32[]{:S(2)}) copy-start(bf16[2,128,768]{2,1,0:T(8,128)(2,1)} %reduce-scatter.14.cloned.1.call-done) | copy-start | bytes 1179652
  550.1 194.6 %copy-start.8 = (bf16[2,128,768]{2,1,0:T(8,128)(2,1)S(1)}, bf16[2,128,768]{2,1,0:T(8,128)(2,1)}, u32[]{:S(2)}) copy-start(bf16[2,128,768]{2,1,0:T(8,128)(2,1)} %param.32) | copy-start | bytes 1179652
  550.1 194.6 %copy-start.14 = (bf16[2,128,768]{2,1,0:T(8,128)(2,1)S(1)}, bf16[2,128,768]{2,1,0:T(8,128)(2,1)}, u32[]{:S(2)}) copy-start(bf16[2,128,768]{2,1,0:T(8,128)(2,1)} %reduce-scatter.22.cloned.1.call-done) | copy-start | bytes 1179652
  550.1 218.6 %all-reduce.15.cloned.1.call-start = ((), (), s32[]{:S(2)}) async-start(), calls=%async_computation.30 | async-start | bytes 3538944 | tf_op jit(solution)/shard_map/psum | solution.py:349
  560.3 132.2 %copy-start.17 = (bf16[2,2,64,768]{3,2,1,0:T(8,128)(2,1)S(1)}, bf16[2,2,64,768]{3,2,1,0:T(8,128)(2,1)}, u32[]{:S(2)}) copy-start(bf16[2,2,64,768]{3,2,1,0:T(8,128)(2,1)} %reduce-scatter.30.cloned.1.call-done) | copy-start | bytes 1179652
  688.3 59.4 %copy-start.10 = (bf16[2,2,64,768]{3,2,1,0:T(8,128)(2,1)S(1)}, bf16[2,2,64,768]{3,2,1,0:T(8,128)(2,1)}, u32[]{:S(2)}) copy-start(bf16[2,2,64,768]{3,2,1,0:T(8,128)(2,1)} %param.33) | copy-start | bytes 1179652
  688.3 59.4 %copy-start.12 = (bf16[2,2,64,768]{3,2,1,0:T(8,128)(2,1)S(1)}, bf16[2,2,64,768]{3,2,1,0:T(8,128)(2,1)}, u32[]{:S(2)}) copy-start(bf16[2,2,64,768]{3,2,1,0:T(8,128)(2,1)} %reduce-scatter.24.cloned.1.call-done) | copy-start | bytes 1179652
  (57 other events, 341.4 us)
Sparse Core Ops, SparseCore 0:
  9.6 23.4 all-gather.4
  59.4 66.0 all-gather.6
  127.1 22.2 all-gather.10
  171.0 24.0 reduce-scatter.13
  197.9 17.5 reduce-scatter.15
  216.9 22.3 all-gather.8
  258.7 16.4 reduce-scatter.23
  278.1 17.4 reduce-scatter.19
  298.4 17.4 reduce-scatter.21
  318.7 17.4 reduce-scatter.17
  452.4 60.2 reduce-scatter.25
  522.5 17.4 reduce-scatter.27
  542.9 17.4 reduce-scatter.29
  563.2 22.0 reduce-scatter.33
  587.7 33.0 reduce-scatter.35
  623.4 33.0 reduce-scatter.37
  658.9 29.3 reduce-scatter.31
  691.0 77.6 all-reduce.14
where the time goes:
time: 790 us; the launch traced here: 783 us
  waiting for transfers between devices  305 us (39%)
  blocking collectives  159 us (20%)
  matrix products  140 us (18%)
  other arithmetic  116 us (15%)
  local copies, waits for them, and re-layouts  40 us (5%)
  between operations  22.9 us (3%)
    all_gather x1, waiting for transfers between devices, per_device(): all_kv = lax.all_gather(prompt_kv, 'ctx', axis=1, tiled=True)  54 us
    all_gather x4, blocking collectives, spread(): lax.all_gather(prompt_part, 'tp', axis=1, tiled=True)  51.9 us
    reduce_scatter x1, waiting for transfers between devices, per_device(): lax.psum_scatter(prompt_grads.astype(jnp.bfloat16), 'ctx', scatter_dimens...  46.7 us
    all_gather x4, blocking collectives, spread(): lax.all_gather(cont_part, 'tp', axis=2, tiled=True)  45.2 us
    psum x1, blocking collectives, per_device(): lax.psum((grad_gain_one, grad_bias_one, grad_gain_two, grad_bias_two, mix...  43.3 us
    reduce_scatter x1, waiting for transfers between devices, per_device(): lax.psum_scatter(summed[3].astype(jnp.bfloat16), 'dp', scatter_dimension=...  35.6 us
    reduce_scatter x1, waiting for transfers between devices, per_device(): lax.psum_scatter(summed[2].astype(jnp.bfloat16), 'dp', scatter_dimension=...  35.5 us
    reduce_scatter x4, waiting for transfers between devices, collect(): lax.psum_scatter(prompt_part.astype(jnp.bfloat16), 'tp', scatter_dimensio...  32.4 us
  transfers between devices with their start and end apart: 18, of which 12 were waited for; matrix products, arithmetic and copies ran while one was open for 20% of the time, Pallas kernels for 0%

commit v1 on v0

v1 whole, which is shorter than its diff:
```python
from functools import partial

import jax
import jax.numpy as jnp
import numpy as np
from jax import lax
from jax.experimental import pallas as pl
from jax.experimental.pallas import tpu as pltpu
from jax.sharding import PartitionSpec as P

HD = 64
CL = 128
EPS = 1e-05
NEG = -1e30
F32 = jnp.float32
BF16 = jnp.bfloat16
VMEM_LIMIT = 62 * 1024 * 1024


def dot(a, b):
    return lax.dot_general(a, b, (((1,), (0,)), ((), ())), preferred_element_type=F32)


def dot_nt(a, b):
    return lax.dot_general(a, b, (((1,), (1,)), ((), ())), preferred_element_type=F32)


def norm_stats(x):
    mean = jnp.mean(x, axis=-1, keepdims=True)
    centered = x - mean
    var = jnp.mean(centered * centered, axis=-1, keepdims=True)
    scale = lax.rsqrt(var + EPS)
    return centered * scale, scale


def norm_back(grad, gain, hat, scale):
    gh = grad * gain
    return scale * (
        gh
        - jnp.mean(gh, axis=-1, keepdims=True)
        - hat * jnp.mean(gh * hat, axis=-1, keepdims=True)
    )


def rotate(x, cos, sin_hi, sin_lo):
    return x * cos + pltpu.roll(x, 32, 1) * sin_hi + pltpu.roll(x, 96, 1) * sin_lo


def rotate_back(x, cos, sin_hi, sin_lo):
    return x * cos - pltpu.roll(x, 32, 1) * sin_hi - pltpu.roll(x, 96, 1) * sin_lo


def lane_pick(shape, low):
    lanes = lax.broadcasted_iota(jnp.int32, shape, 1)
    return lanes < HD if low else lanes >= HD


def sublane_pick(shape, low):
    rows = lax.broadcasted_iota(jnp.int32, shape, 0)
    return rows < HD if low else rows >= HD


def transpose(x):
    return x.astype(F32).T.astype(x.dtype)


class Dims:
    def __init__(self, groups, prompt, pb, nc, ch, d, heads):
        self.G, self.P, self.PB, self.NC, self.CH, self.D = groups, prompt, pb, nc, ch, d
        self.NCH = nc * ch
        self.R = prompt + nc * CL
        self.NX = nc * CL
        self.NR = pb + self.NCH
        self.NP = groups * pb
        self.NT = groups * self.NR
        self.PAIRS = heads // 2
        self.COLS = 2 * self.NR


def fill_masks(dm, maskp, maskx):
    block = lax.axis_index("ctx") * lax.axis_size("tp") + lax.axis_index("tp")
    keys = lax.broadcasted_iota(jnp.int32, maskp.shape, 0)
    cols = lax.broadcasted_iota(jnp.int32, maskp.shape, 1) % dm.PB
    maskp[...] = jnp.where(keys <= cols + block * dm.PB, 0.0, NEG)
    keys = lax.broadcasted_iota(jnp.int32, maskx.shape, 0)
    cols = lax.broadcasted_iota(jnp.int32, maskx.shape, 1) % dm.NCH
    seen = (keys // CL == cols // dm.CH) & (
        keys % CL <= cols % dm.CH + lax.axis_index("tp") * dm.CH
    )
    maskx[...] = jnp.where(seen, 0.0, NEG)


def heads_columns(a, b):
    lo_a, lo_b = sublane_pick(a.shape, True), sublane_pick(b.shape, True)
    zero_a, zero_b = jnp.zeros_like(a), jnp.zeros_like(b)
    return jnp.concatenate(
        [
            jnp.where(lo_a, a, zero_a),
            jnp.where(lo_a, zero_a, a),
            jnp.where(lo_b, b, zero_b),
            jnp.where(lo_b, zero_b, b),
        ],
        axis=1,
    )


def heads_rows(a, b):
    lo_a, lo_b = lane_pick(a.shape, True), lane_pick(b.shape, True)
    zero_a, zero_b = jnp.zeros_like(a), jnp.zeros_like(b)
    return jnp.concatenate(
        [
            jnp.where(lo_a, a, zero_a),
            jnp.where(lo_a, zero_a, a),
            jnp.where(lo_b, b, zero_b),
            jnp.where(lo_b, zero_b, b),
        ],
        axis=0,
    )


def forward_kernel(
    dm,
    xp,
    xc,
    op,
    oc,
    ln,
    cos,
    shi,
    slo,
    w,
    n_out,
    k_out,
    v_out,
    q_out,
    att_out,
    lse_out,
    maskp,
    maskx,
    sbuf,
):
    G, R, PB, NCH, D = dm.G, dm.R, dm.PB, dm.NCH, dm.D
    HC = w.shape[2] // 3
    TP = w.shape[0]
    gain, bias = ln[0:1, :].astype(F32), ln[1:2, :].astype(F32)
    fill_masks(dm, maskp, maskx)

    def normed(x):
        hat, _ = norm_stats(x.astype(F32))
        return (hat * gain + bias).astype(BF16)

    def keys_values(g, x, row, table):
        rows = x.shape[0]
        n = normed(x)
        n_out[g, pl.ds(row, rows), :] = n
        c = cos[pl.ds(table, rows), :]
        hi = shi[pl.ds(table, rows), :]
        lo = slo[pl.ds(table, rows), :]
        for t in range(TP):
            kk = dot(n, w[t, :, HC : 2 * HC])
            for j in range(HC // 128):
                tile = rotate(kk[:, j * 128 : (j + 1) * 128], c, hi, lo)
                k_out[g, pl.ds(row, rows), t * HC + j * 128 : t * HC + (j + 1) * 128] = tile.astype(BF16)
            v_out[g, pl.ds(row, rows), t * HC : (t + 1) * HC] = dot(n, w[t, :, 2 * HC :]).astype(BF16)

    CHUNK = 256
    steps = dm.P // CHUNK

    def prompt_chunk(i, carry):
        g, row = i // steps, pl.multiple_of((i % steps) * CHUNK, CHUNK)
        keys_values(g, xp[g, pl.ds(row, CHUNK), :], row, row)
        return carry

    lax.fori_loop(0, G * steps, prompt_chunk, 0)

    def cont_chunk(i, carry):
        g, c = i // dm.NC, i % dm.NC
        row = pl.multiple_of(dm.P + c * CL, CL)
        keys_values(g, xc[g, c], row, dm.P)
        return carry

    lax.fori_loop(0, G * dm.NC, cont_chunk, 0)

    block = lax.axis_index("ctx") * lax.axis_size("tp") + lax.axis_index("tp")

    def queries(x, row, table):
        rows = x.shape[0]
        n = normed(x)
        c = cos[pl.ds(table, rows), :]
        hi = shi[pl.ds(table, rows), :]
        lo = slo[pl.ds(table, rows), :]
        for t in range(TP):
            qq = dot(n, w[t, :, :HC])
            for j in range(HC // 128):
                tile = rotate(qq[:, j * 128 : (j + 1) * 128], c, hi, lo).astype(BF16)
                q_out[pl.ds(row, rows), t * HC + j * 128 : t * HC + (j + 1) * 128] = (
                    tile.astype(F32) * 0.125
                ).astype(BF16)

    def own_prompt(g, carry):
        queries(op[g], pl.multiple_of(g * PB, PB), pl.multiple_of(block * PB, PB))
        return carry

    lax.fori_loop(0, G, own_prompt, 0)

    def own_cont(i, carry):
        g, c = i // dm.NC, i % dm.NC
        queries(
            oc[g, c],
            pl.multiple_of(dm.NP + i * dm.CH, dm.CH),
            pl.multiple_of(dm.P + lax.axis_index("tp") * dm.CH, dm.CH),
        )
        return carry

    lax.fori_loop(0, G * dm.NC, own_cont, 0)

    TILE = 256
    tiles = dm.P // TILE

    def attend(i, carry):
        g, pair = i // dm.PAIRS, i % dm.PAIRS
        lanes = pl.ds(pl.multiple_of(pair * 128, 128), 128)
        qp = q_out[pl.ds(pl.multiple_of(g * PB, PB), PB), lanes]
        qc = q_out[pl.ds(pl.multiple_of(dm.NP + g * NCH, NCH), NCH), lanes]
        qt = heads_columns(transpose(qp), transpose(qc))
        top = None
        for j in range(tiles):
            s = dot(k_out[g, j * TILE : (j + 1) * TILE, lanes], qt)
            sbuf[j * TILE : (j + 1) * TILE, : 2 * PB] = (
                s[:, : 2 * PB] + maskp[j * TILE : (j + 1) * TILE, :]
            )
            sbuf[j * TILE : (j + 1) * TILE, 2 * PB :] = s[:, 2 * PB :]
            here = jnp.max(sbuf[j * TILE : (j + 1) * TILE, :], axis=0, keepdims=True)
            top = here if top is None else jnp.maximum(top, here)
        sx = dot(k_out[g, dm.P :, lanes], qt[:, 2 * PB :]) + maskx[...]
        topx = jnp.max(sx, axis=0, keepdims=True)
        top = jnp.concatenate([top[:, : 2 * PB], jnp.maximum(top[:, 2 * PB :], topx)], axis=1)
        total, acc = None, None
        for j in range(tiles):
            e = jnp.exp(sbuf[j * TILE : (j + 1) * TILE, :] - top)
            here = jnp.sum(e, axis=0, keepdims=True)
            vt = transpose(v_out[g, j * TILE : (j + 1) * TILE, lanes])
            part = dot(vt, e.astype(BF16))
            total = here if total is None else total + here
            acc = part if acc is None else acc + part
        ex = jnp.exp(sx - top[:, 2 * PB :])
        partx = dot(transpose(v_out[g, dm.P :, lanes]), ex.astype(BF16))
        totalx = jnp.sum(ex, axis=0, keepdims=True)
        total = jnp.concatenate([total[:, : 2 * PB], total[:, 2 * PB :] + totalx], axis=1)
        acc_p = acc[:, : 2 * PB] / total[:, : 2 * PB]
        acc_c = (acc[:, 2 * PB :] + partx) / total[:, 2 * PB :]
        lse_out[i] = top + jnp.log(total)
        outp = jnp.where(sublane_pick((128, PB), True), acc_p[:, :PB], acc_p[:, PB:])
        outc = jnp.where(sublane_pick((128, NCH), True), acc_c[:, :NCH], acc_c[:, NCH:])
        att_out[pl.ds(pl.multiple_of(g * PB, PB), PB), lanes] = outp.T.astype(BF16)
        att_out[pl.ds(pl.multiple_of(dm.NP + g * NCH, NCH), NCH), lanes] = outc.T.astype(BF16)
        return carry

    lax.fori_loop(0, G * dm.PAIRS, attend, 0)


def mlp_kernel(
    dm,
    steps,
    mix,
    att,
    op,
    oc,
    ep,
    ec,
    yp,
    yc,
    tp_,
    tc,
    ln,
    wo,
    wu,
    wd,
    outp,
    outc,
    resg,
    gatt,
    gwo,
    gwu,
    gwd,
    small,
    resid,
    hat,
    scale,
    hn,
    hnt,
    gd,
    gdt,
    blk,
    gh,
):
    D, NP, NT, G, PB = dm.D, dm.NP, dm.NT, dm.G, dm.PB
    TP, HC = wo.shape[0], wo.shape[2]
    t, j = pl.program_id(0), pl.program_id(1)
    gain, bias = ln[2:3, :].astype(F32), ln[3:4, :].astype(F32)

    def own(prompt, cont):
        return jnp.concatenate([prompt.reshape(NP, D), cont.reshape(NT - NP, D)], axis=0)

    @pl.when((t == 0) & (j == 0))
    def _():
        branch = dot_nt(att[:, :HC], wo[0])
        for s in range(1, TP):
            branch += dot_nt(att[:, s * HC : (s + 1) * HC], wo[s])
        r = own(op[...], oc[...]).astype(F32) + branch
        resid[...] = r
        h, sc = norm_stats(r)
        hat[...] = h
        scale[...] = jnp.broadcast_to(sc, scale.shape)
        n = (h * gain + bias).astype(BF16)
        hn[...] = n
        hnt[...] = transpose(n)
        g = (mix[4] * own(tp_[...], tc[...]).astype(F32)).astype(BF16)
        gd[...] = g
        gdt[...] = transpose(g)
        blk[...] = r
        gh[...] = jnp.zeros_like(gh)

    up, dn = wu[0], wd[0]
    u = dot(hn[...], up)
    c0 = 0.7978845608028654
    u2 = u * u
    th = jnp.tanh(c0 * u * (1.0 + 0.044715 * u2))
    half = 0.5 * (1.0 + th)
    act = (u * half).astype(BF16)
    slope = half + 0.5 * u * (1.0 - th * th) * (c0 * (1.0 + 3 * 0.044715 * u2))
    blk[...] += dot_nt(act, dn)
    gwd[0] = dot(gdt[...], act).astype(BF16)
    gu = (dot(gd[...], dn) * slope).astype(BF16)
    gwu[0] = dot(hnt[...], gu).astype(BF16)
    gh[...] += dot_nt(gu, up)

    @pl.when((t == TP - 1) & (j == steps - 1))
    def _():
        cot = own(tp_[...], tc[...]).astype(F32)
        block = blk[...]
        arrays = [own(ep[...], ec[...])] + [own(yp[i], yc[i]) for i in range(3)]
        res = mix[4] * block
        for i in range(4):
            a = arrays[i].astype(F32)
            res += mix[i] * a
            small[2 + i : 3 + i, :] = jnp.sum(cot * a, axis=0, keepdims=True)
        small[6:7, :] = jnp.sum(cot * block, axis=0, keepdims=True)
        small[7:8, :] = jnp.zeros((1, D), F32)
        res = res.astype(BF16)
        outp[...] = res[:NP].reshape(outp.shape)
        outc[...] = res[NP:].reshape(outc.shape)
        g = gh[...]
        h = hat[...]
        small[0:1, :] = jnp.sum(g * h, axis=0, keepdims=True)
        small[1:2, :] = jnp.sum(g, axis=0, keepdims=True)
        gr = mix[4] * cot + norm_back(g, gain, h, scale[:, 0:1])
        resg[...] = gr
        gb = gr.astype(BF16)
        gbt = transpose(gb)
        for s in range(TP):
            gatt[:, s * HC : (s + 1) * HC] = dot(gb, wo[s]).astype(BF16)
            gwo[s] = dot(gbt, att[:, s * HC : (s + 1) * HC]).astype(BF16)


def backward_kernel(
    dm,
    q,
    k,
    v,
    att,
    gatt,
    lse,
    n_all,
    cos,
    shi,
    slo,
    w,
    dx,
    dxq,
    gw,
    maskp,
    maskx,
    dk,
    dv,
    dq,
    nt,
):
    G, R, PB, NCH, D, NX = dm.G, dm.R, dm.PB, dm.NCH, dm.D, dm.NX
    TP, HC = w.shape[0], w.shape[2] // 3
    fill_masks(dm, maskp, maskx)
    block = lax.axis_index("ctx") * lax.axis_size("tp") + lax.axis_index("tp")
    TILE = 256
    tiles = dm.P // TILE

    def attend(i, carry):
        g, pair = i // dm.PAIRS, i % dm.PAIRS
        lanes = pl.ds(pl.multiple_of(pair * 128, 128), 128)
        rp = pl.ds(pl.multiple_of(g * PB, PB), PB)
        rc = pl.ds(pl.multiple_of(dm.NP + g * NCH, NCH), NCH)
        qp, qc = q[rp, lanes], q[rc, lanes]
        gp, gc = gatt[rp, lanes], gatt[rc, lanes]
        ap, ac = att[rp, lanes].astype(F32), att[rc, lanes].astype(F32)
        qt = heads_columns(transpose(qp), transpose(qc))
        gpt, gct = gp.astype(F32).T, gc.astype(F32).T
        gt = heads_columns(gpt.astype(BF16), gct.astype(BF16))
        qs, gs = heads_rows(qp, qc), heads_rows(gp, gc)
        prodp, prodc = gpt * ap.T, gct * ac.T
        delta = jnp.concatenate(
            [
                jnp.sum(prodp[:HD], axis=0, keepdims=True),
                jnp.sum(prodp[HD:], axis=0, keepdims=True),
                jnp.sum(prodc[:HD], axis=0, keepdims=True),
                jnp.sum(prodc[HD:], axis=0, keepdims=True),
            ],
            axis=1,
        )
        stat = lse[i]

        def grads(s, kt, vt, cols):
            p = jnp.exp(s - stat[:, cols:])
            dp = dot(vt, gt[:, cols:])
            ds = (p * (dp - delta[:, cols:])).astype(BF16)
            gv = dot(p.astype(BF16), gs[cols:])
            gk = dot(ds, qs[cols:])
            gq = dot(transpose(kt), ds)
            return gk, gv, gq

        acc = None
        for j in range(tiles):
            rows = slice(j * TILE, (j + 1) * TILE)
            kt = k[g, rows, lanes]
            s = dot(kt, qt)
            s = jnp.concatenate([s[:, : 2 * PB] + maskp[rows, :], s[:, 2 * PB :]], axis=1)
            gk, gv, gq = grads(s, kt, v[g, rows, lanes], 0)
            gk = rotate_back(gk, cos[rows, :], shi[rows, :], slo[rows, :])
            out = pl.ds(pl.multiple_of(g * R + j * TILE, 128), TILE)
            dk[out, lanes] = gk.astype(BF16)
            dv[out, lanes] = gv.astype(BF16)
            acc = gq if acc is None else acc + gq
        kt = k[g, dm.P :, lanes]
        s = dot(kt, qt[:, 2 * PB :]) + maskx[...]
        gk, gv, gq = grads(s, kt, v[g, dm.P :, lanes], 2 * PB)
        for c in range(dm.NC):
            rows = slice(dm.P, dm.P + CL)
            out = pl.ds(pl.multiple_of(g * R + dm.P + c * CL, 128), CL)
            part = rotate_back(gk[c * CL : (c + 1) * CL], cos[rows, :], shi[rows, :], slo[rows, :])
            dk[out, lanes] = part.astype(BF16)
            dv[out, lanes] = gv[c * CL : (c + 1) * CL].astype(BF16)
        accp = acc[:, : 2 * PB] * 0.125
        accc = (acc[:, 2 * PB :] + gq) * 0.125
        outp = jnp.where(sublane_pick((128, PB), True), accp[:, :PB], accp[:, PB:]).T
        outc = jnp.where(sublane_pick((128, NCH), True), accc[:, :NCH], accc[:, NCH:]).T
        tab = pl.ds(pl.multiple_of(block * PB, PB), PB)
        dq[rp, lanes] = rotate_back(outp, cos[tab, :], shi[tab, :], slo[tab, :]).astype(BF16)
        tab = pl.ds(pl.multiple_of(dm.P + lax.axis_index("tp") * dm.CH, dm.CH), dm.CH)
        for c in range(dm.NC):
            part = rotate_back(outc[c * dm.CH : (c + 1) * dm.CH], cos[tab, :], shi[tab, :], slo[tab, :])
            rows = pl.ds(pl.multiple_of(dm.NP + g * NCH + c * dm.CH, dm.CH), dm.CH)
            dq[rows, lanes] = part.astype(BF16)
        return carry

    lax.fori_loop(0, G * dm.PAIRS, attend, 0)

    CHUNK = 256 if R % 256 == 0 else 128

    def project(i, carry):
        rows = pl.ds(pl.multiple_of(i * CHUNK, CHUNK), CHUNK)
        total = None
        for t in range(TP):
            part = dot_nt(dk[rows, t * HC : (t + 1) * HC], w[t, :, HC : 2 * HC])
            total = part if total is None else total + part
            total += dot_nt(dv[rows, t * HC : (t + 1) * HC], w[t, :, 2 * HC :])
        dx[rows, :] = total.astype(BF16)
        nt[:, rows] = transpose(n_all[rows, :])
        return carry

    lax.fori_loop(0, G * R // CHUNK, project, 0)
    total = dot_nt(dq[:, :HC], w[0, :, :HC])
    for t in range(1, TP):
        total += dot_nt(dq[:, t * HC : (t + 1) * HC], w[t, :, :HC])
    dxq[...] = total
    for t in range(TP):
        gw[t, :, HC : 2 * HC] = dot(nt[...], dk[:, t * HC : (t + 1) * HC]).astype(BF16)
        gw[t, :, 2 * HC :] = dot(nt[...], dv[:, t * HC : (t + 1) * HC]).astype(BF16)
        acc = None
        for g in range(G):
            rows = pl.ds(pl.multiple_of(g * R + block * PB, PB), PB)
            part = dot(transpose(n_all[rows, :]), dq[g * PB : (g + 1) * PB, t * HC : (t + 1) * HC])
            acc = part if acc is None else acc + part
            for c in range(dm.NC):
                first = g * R + dm.P + c * CL + lax.axis_index("tp") * dm.CH
                rows = pl.ds(pl.multiple_of(first, dm.CH), dm.CH)
                mine = dm.NP + g * NCH + c * dm.CH
                acc += dot(
                    transpose(n_all[rows, :]),
                    dq[mine : mine + dm.CH, t * HC : (t + 1) * HC],
                )
        gw[t, :, :HC] = acc.astype(BF16)


def whole(shape):
    zeros = (0,) * len(shape)
    return pl.BlockSpec(shape, lambda *_: zeros)


def params(**more):
    return pltpu.CompilerParams(vmem_limit_bytes=VMEM_LIMIT, **more)


def per_device(
    prompt_in,
    cont_in,
    prompt_embed,
    cont_embed,
    prompt_earlier,
    cont_earlier,
    ln1_gain,
    ln1_bias,
    ln2_gain,
    ln2_bias,
    w_qkv,
    w_out,
    w_up,
    w_down,
    mix_weights,
    prompt_cot,
    cont_cot,
):
    G, PB, D = prompt_in.shape
    NC, CH = cont_in.shape[1], cont_in.shape[2]
    TP = lax.axis_size("tp")
    PROMPT = PB * TP * lax.axis_size("ctx")
    HC, FC = w_qkv.shape[2], w_up.shape[1]
    S = w_qkv.shape[0]
    dm = Dims(G, PROMPT, PB, NC, CH, D, HC * TP // HD)
    R, NT, NP = dm.R, dm.NT, dm.NP

    sds = jax.ShapeDtypeStruct
    ln = lax.all_gather(jnp.stack([ln1_gain, ln1_bias, ln2_gain, ln2_bias]), "dp", axis=1, tiled=True)
    xp = lax.all_gather(prompt_in, ("ctx", "tp"), axis=1, tiled=True)
    xc = lax.all_gather(cont_in, "tp", axis=2, tiled=True)
    wq = lax.all_gather(w_qkv.reshape(S, 3 * HC), ("tp", "dp"), axis=0, tiled=True)
    wq = wq.reshape(TP, D, 3 * HC)
    shard = jnp.concatenate([w_out.T, w_up, w_down.T], axis=1)
    wm = lax.all_gather(shard, ("tp", "dp"), axis=0, tiled=True).reshape(TP, D, HC + 2 * FC)
    wo, wu, wd = wm[:, :, :HC], wm[:, :, HC : HC + FC], wm[:, :, HC + FC :]

    positions = jnp.arange(PROMPT + CL, dtype=jnp.int32).astype(F32)
    lane = jnp.arange(128, dtype=jnp.int32)
    freq = 10000.0 ** (-((lane % 32).astype(F32) / 32))
    angles = positions[:, None] * freq[None, :]
    cos, sin = jnp.cos(angles), jnp.sin(angles)
    second = (lane % 64) >= 32
    shi = jnp.where(second[None, :], sin, 0.0)
    slo = jnp.where(second[None, :], 0.0, -sin)

    n_all, k, v, q, att, lse = pl.pallas_call(
        partial(forward_kernel, dm),
        out_shape=(
            sds((G, R, D), BF16),
            sds((G, R, D), BF16),
            sds((G, R, D), BF16),
            sds((NT, D), BF16),
            sds((NT, D), BF16),
            sds((G * dm.PAIRS, 1, dm.COLS), F32),
        ),
        scratch_shapes=[
            pltpu.VMEM((PROMPT, 2 * PB), F32),
            pltpu.VMEM((dm.NX, 2 * dm.NCH), F32),
            pltpu.VMEM((PROMPT, dm.COLS), F32),
        ],
        compiler_params=params(),
        name="forward",
    )(xp, xc, prompt_in, cont_in, ln, cos, shi, slo, wq)

    T = 512 if FC % 512 == 0 else 256
    steps = FC // T
    row_specs = [whole(a.shape) for a in (att, prompt_in, cont_in, prompt_embed, cont_embed, prompt_earlier, cont_earlier, prompt_cot, cont_cot, ln, wo)]
    tile = pl.BlockSpec((1, D, T), lambda t, j: (t, 0, j))
    outp, outc, resg, gatt, gwo, gwu, gwd, small = pl.pallas_call(
        partial(mlp_kernel, dm, steps),
        grid=(TP, steps),
        out_shape=(
            sds(prompt_in.shape, BF16),
            sds(cont_in.shape, BF16),
            sds((NT, D), F32),
            sds((NT, D), BF16),
            sds((TP, D, HC), BF16),
            sds((TP, D, FC), BF16),
            sds((TP, D, FC), BF16),
            sds((8, D), F32),
        ),
        in_specs=[pl.BlockSpec(memory_space=pltpu.SMEM)] + row_specs + [tile, tile],
        out_specs=(
            whole(prompt_in.shape),
            whole(cont_in.shape),
            whole((NT, D)),
            whole((NT, D)),
            whole((TP, D, HC)),
            tile,
            tile,
            whole((8, D)),
        ),
        scratch_shapes=[
            pltpu.VMEM((NT, D), F32),
            pltpu.VMEM((NT, D), F32),
            pltpu.VMEM((NT, 128), F32),
            pltpu.VMEM((NT, D), BF16),
            pltpu.VMEM((D, NT), BF16),
            pltpu.VMEM((NT, D), BF16),
            pltpu.VMEM((D, NT), BF16),
            pltpu.VMEM((NT, D), F32),
            pltpu.VMEM((NT, D), F32),
        ],
        compiler_params=params(),
        name="feed",
    )(
        mix_weights,
        att,
        prompt_in,
        cont_in,
        prompt_embed,
        cont_embed,
        prompt_earlier,
        cont_earlier,
        prompt_cot,
        cont_cot,
        ln,
        wo,
        wu,
        wd,
    )

    dx, dxq, gwq = pl.pallas_call(
        partial(backward_kernel, dm),
        out_shape=(sds((G * R, D), BF16), sds((NT, D), F32), sds((TP, D, 3 * HC), BF16)),
        scratch_shapes=[
            pltpu.VMEM((PROMPT, 2 * PB), F32),
            pltpu.VMEM((dm.NX, 2 * dm.NCH), F32),
            pltpu.VMEM((G * R, D), BF16),
            pltpu.VMEM((G * R, D), BF16),
            pltpu.VMEM((NT, D), BF16),
            pltpu.VMEM((D, G * R), BF16),
        ],
        compiler_params=params(),
        name="backward",
    )(q, k, v, att, gatt, lse, n_all.reshape(G * R, D), cos, shi, slo, wq)

    dx = dx.reshape(G, R, D)
    gp = lax.psum_scatter(dx[:, :PROMPT], ("ctx", "tp"), scatter_dimension=1, tiled=True)
    gc = lax.psum_scatter(dx[:, PROMPT:].reshape(G, NC, CL, D), "tp", scatter_dimension=2, tiled=True)
    gn = jnp.concatenate([gp.reshape(NP, D), gc.reshape(NT - NP, D)], axis=0).astype(F32) + dxq
    x = jnp.concatenate([prompt_in.reshape(NP, D), cont_in.reshape(NT - NP, D)], axis=0).astype(F32)
    hat, scale = norm_stats(x)
    gin = (resg + norm_back(gn, ln[0:1].astype(F32), hat, scale)).astype(BF16)
    small = jnp.concatenate(
        [small[:7], jnp.sum(gn * hat, axis=0)[None], jnp.sum(gn, axis=0)[None]], axis=0
    )
    small = lax.psum(small, ("dp", "ctx", "tp"))

    def reduce(g):
        g = lax.psum_scatter(g.reshape(TP * D, -1), ("tp", "dp"), scatter_dimension=0, tiled=True)
        return lax.psum(g, "ctx").astype(F32)

    gm = reduce(jnp.concatenate([gwo, gwu, gwd], axis=2))
    gq = reduce(gwq)
    start = lax.axis_index("dp") * S
    mine = lax.dynamic_slice_in_dim(small, start, S, axis=1)
    return (
        outp,
        outc,
        gin[:NP].reshape(prompt_in.shape),
        gin[NP:].reshape(cont_in.shape),
        mine[7],
        mine[8],
        mine[0],
        mine[1],
        gq.reshape(S, 3, HC),
        gm[:, :HC].T,
        gm[:, HC : HC + FC],
        gm[:, HC + FC :].T,
        jnp.sum(small[2:7], axis=1),
    )


def solution(mesh):
    tokens = P("dp", ("ctx", "tp"), None)
    conts = P("dp", "ctx", "tp", None)
    weights = (P("dp", None, "tp"), P("tp", "dp"), P("dp", "tp"), P("tp", "dp"))
    in_specs = (
        tokens,
        conts,
        tokens,
        conts,
        P(None, "dp", ("ctx", "tp"), None),
        P(None, "dp", "ctx", "tp", None),
        P("dp"),
        P("dp"),
        P("dp"),
        P("dp"),
        *weights,
        P(),
        tokens,
        conts,
    )
    out_specs = (
        tokens,
        conts,
        tokens,
        conts,
        P("dp"),
        P("dp"),
        P("dp"),
        P("dp"),
        *weights,
        P(),
    )
    return jax.shard_map(
        per_device, mesh=mesh, in_specs=in_specs, out_specs=out_specs, check_vma=False
    )
```

time: 790 us -> 600 us (0.76)
  matrix products: 140 us -> 0 us
  Pallas kernels: 0 us -> 126 us
  other arithmetic: 116 us -> 20.4 us
  blocking collectives: 159 us -> 66 us
  waiting for transfers between devices: 305 us -> 344 us
  local copies, waits for them, and re-layouts: 40 us -> 28.9 us
  between operations: 22.9 us -> 14.4 us
    dot_general x18 -> x0, matrix products: 140 us -> none  [the longest x1 24.6 us: attend_back(): jnp.einsum('bqhd,bkhd->bhqk', grad_block, value_block, preferred_element_...]
    pallas_call x0 -> x3, Pallas kernels: none -> 126 us  [the longest x1 53.4 us: per_device(): pl.pallas_call(partial(backward_kernel, dm), out_shape=(sds((G * R, D), B...]
    all_gather x9 -> x2, blocking collectives: 107 us -> 22.7 us  [the longest x1 16.5 us: per_device(): xc = lax.all_gather(cont_in, 'tp', axis=2, tiled=True)]
    reduce_sum x17 -> x4, other arithmetic: 48.5 us -> 3.21 us  [the longest x1 2.04 us: per_device(): jnp.sum(gn * hat, axis=0)[None]]
    convert_element_type x23 -> x3, other arithmetic: 48.4 us -> 3.54 us  [the longest x1 2.05 us: per_device(): gin = (resg + norm_back(gn, ln[0:1].astype(F32), hat, scale)).astype(BF16)]
    all_gather x4 -> x3, waiting for transfers between devices: 54 us -> 96.1 us  [the longest x1 38 us: per_device(): xp = lax.all_gather(prompt_in, ('ctx', 'tp'), axis=1, tiled=True)]
    psum x1, waiting for transfers between devices: 18.3 us -> 34.6 us  [reduce(): return lax.psum(g, 'ctx').astype(F32)]
    reduce_scatter x13 -> x4, waiting for transfers between devices: 228 us -> 212 us  [the longest x2 114 us: reduce(): lax.psum_scatter(g.reshape(TP * D, -1), ('tp', 'dp'), scatter_dimension=0...]
  transfers between devices with their start and end apart: 18 -> 8, of which waited for: 12 -> 8; matrix products, arithmetic and copies ran while one was open for 20% -> 5% of each run, Pallas kernels for 0% -> 7%
where the time goes in v1:
time: 600 us
  waiting for transfers between devices  344 us (57%)
  Pallas kernels  126 us (21%)
  blocking collectives  66 us (11%)
  local copies, waits for them, and re-layouts  28.9 us (5%)
  other arithmetic  20.4 us (3%)
  between operations  14.4 us (2%)
    reduce_scatter x2, waiting for transfers between devices, reduce(): lax.psum_scatter(g.reshape(TP * D, -1), ('tp', 'dp'), scatter_dimension=0...  114 us
    reduce_scatter x1, waiting for transfers between devices, per_device(): lax.psum_scatter(dx[:, :PROMPT], ('ctx', 'tp'), scatter_dimension=1, tile...  78.5 us
    pallas_call x1, Pallas kernels, per_device(): pl.pallas_call(partial(backward_kernel, dm), out_shape=(sds((G * R, D), B...  53.4 us
    psum x1, blocking collectives, per_device(): small = lax.psum(small, ('dp', 'ctx', 'tp'))  43.3 us
    pallas_call x1, Pallas kernels, per_device(): pl.pallas_call(partial(forward_kernel, dm), out_shape=(sds((G, R, D), BF1...  42.7 us
    all_gather x1, waiting for transfers between devices, per_device(): xp = lax.all_gather(prompt_in, ('ctx', 'tp'), axis=1, tiled=True)  38 us
    all_gather x1, waiting for transfers between devices, per_device(): lax.all_gather(w_qkv.reshape(S, 3 * HC), ('tp', 'dp'), axis=0, tiled=True)  35.1 us
    psum x1, waiting for transfers between devices, reduce(): return lax.psum(g, 'ctx').astype(F32)  34.6 us
  transfers between devices with their start and end apart: 8, of which 8 were waited for; matrix products, arithmetic and copies ran while one was open for 5% of the time, Pallas kernels for 7%

profile of v1, /device:TPU:0, one launch (start us, length us, event | category | flops | bytes accessed | tf_op | source)
XLA Modules:
  0.0 599.6 jit_solution(9707546236975300787)
XLA Ops:
  7.2 0.0 all-gather.5.cloned.1.call-start
  7.3 0.7 all-gather.5.cloned.1.call-update
  7.9 0.0 all-gather.7.cloned.1.call-start
  8.0 1.8 copy.36
  9.8 0.0 all-gather.9.cloned.1.call-start
  10.0 1.2 pad_maximum_fusion.1
  11.2 0.0 reduce-scatter.9.cloned.1.call-start
  11.3 6.1 %all-gather = bf16[4,192,4]{1,2,0:T(4,128)(2,1)S(1)} all-gather(bf16[1,192,4]{1,2,0:T(4,128)(2,1)S(1)} %maximum_bitcast_fusion), channel_id=1, replica_groups=mesh['dp'=4,'ctx'=4,'tp'=2] {'dp'}, dimensions={0}, use_global_device_ids=true | all-gather | bytes 7680 | tf_op jit(solution)/shard_map/all_gather | solution.py:540
  17.5 0.7 reshape.139
  18.2 16.5 %all_gather.16.xc = bf16[2,2,128,768]{3,2,1,0:T(8,128)(2,1)} all-gather(bf16[2,2,64,768]{3,2,1,0:T(8,128)(2,1)S(1)} %copy-done.1), channel_id=1, replica_groups=mesh['dp'=4,'ctx'=4,'tp'=2] {'tp'}, dimensions={2}, use_global_device_ids=true | all-gather | bytes 1179648 | tf_op jit(solution)/shard_map/all_gather | solution.py:542
  34.7 3.4 fusion.14
  38.2 38.0 %all-gather.5.cloned.1.call-done.xp = bf16[2,1024,768]{2,1,0:T(8,128)(2,1)} async-done(((bf16[2,128,768]{2,1,0:T(8,128)(2,1)}), bf16[2,1024,768]{2,1,0:T(8,128)(2,1)}) %all-gather.5.cloned.1.call-update) | async-done | bytes 3145744 | tf_op jit(solution)/shard_map/all_gather | solution.py:541
  76.2 35.1 %all-gather.7.cloned.1.call-done = bf16[1536,1152]{1,0:T(8,128)(2,1)} async-done(((bf16[192,1152]{1,0:T(8,128)(2,1)}), bf16[1536,1152]{1,0:T(8,128)(2,1)}) %all-gather.7.cloned.1.call-update) | async-done | bytes 3538960 | tf_op jit(solution)/shard_map/all_gather | solution.py:543
  111.2 42.7 %forward.1 = (bf16[2,1280,768]{2,1,0:T(8,128)(2,1)}, bf16[2,1280,768]{2,1,0:T(8,128)(2,1)}, bf16[2,1280,768]{2,1,0:T(8,128)(2,1)}, bf16[512,768]{1,0:T(8,128)(2,...) custom-call(bf16[2,1024,768]{2,1,0:T(8,128)(2,1)} %all-gather.5.cloned.1.call-done.xp, ...), custom_call_target="tpu_custom_call" | custom-call | tf_op jit(solution)/shard_map/forward/pallas_call | solution.py:558
  153.9 23.0 %all-gather.9.cloned.1.call-done = bf16[1536,3456]{1,0:T(8,128)(2,1)} async-done(((bf16[192,3456]{1,0:T(8,128)(2,1)}), bf16[1536,3456]{1,0:T(8,128)(2,1)}) %all-gather.9.cloned.1.call-update) | async-done | bytes 10616848 | tf_op jit(solution)/shard_map/all_gather | solution.py:546
  177.0 8.0 %fusion.22 = (bf16[2,768,1536]{2,1,0:T(8,128)(2,1)}, bf16[2,768,1536]{2,1,0:T(8,128)(2,1)}) fusion(bf16[2,768,3456]{2,1,0:T(8,128)(2,1)} %bitcast.44), kind=kLoop, calls=%fused_computation.45 | loop fusion | bytes 18874368 | tf_op jit(solution)/shard_map/slice | solution.py:547
  185.0 2.4 slice.68.wo
  187.4 29.5 %feed.1 = (bf16[2,128,768]{2,1,0:T(8,128)(2,1)}, bf16[2,2,64,768]{3,2,1,0:T(8,128)(2,1)}, f32[512,768]{1,0:T(8,128)}, bf16[512,768]{1,0:T(8,128)(2,1)}, bf16[2,7...) custom-call(f32[5]{0:T(128)} %mix.1, ...), custom_call_target="tpu_custom_call" | custom-call | tf_op jit(solution)/shard_map/feed/pallas_call | solution.py:581
  216.9 53.4 %backward.1 = (bf16[2560,768]{1,0:T(8,128)(2,1)}, f32[512,768]{1,0:T(8,128)}, bf16[2,768,1152]{2,1,0:T(8,128)(2,1)}) custom-call(bf16[512,768]{1,0:T(8,128)(2,1)} %get-tuple-element.34.q, bf16[2,1280,768]{2,1,0:T(8,128)(2,1)} %get-tuple-element.35.k, bf16[2,1280,768]{2,1,0:T(8,128)(2,1)} %get-tuple-element.36.v, bf16[512,768]{1,0:T(8,128)(2,1)} %get-tuple-element.30.att, ...), custom_call_target="tpu_custom_call" | custom-call | tf_op jit(solution)/shard_map/backward/pallas_call | solution.py:635
  270.3 0.0 reduce-scatter.11.cloned.1.call-start
  270.4 1.2 copy-done.7
  271.6 9.0 %pad_maximum_fusion = bf16[2,768,3456]{2,1,0:T(8,128)(2,1)} fusion(bf16[2,768,1536]{2,1,0:T(8,128)(2,1)} %get-tuple-element.46, bf16[2,768,1536]{2,1,0:T(8,128)(2,1)} %get-tuple-element.45, bf16[2,768,384]{2,1,0:T(8,128)(2,1)S(1)} %copy-done.7), kind=kLoop, calls=%fused_computation | loop fusion | flops 31850496 | bytes 21233664 | tf_op jit(solution)/shard_map/concatenate | solution.py:666
  280.6 0.0 reduce-scatter.7.cloned.1.call-start
  280.7 2.1 slice.72
  282.8 0.0 reduce-scatter.5.cloned.1.call-start
  282.8 3.8 slice.71
  286.7 0.0 all-reduce.3.cloned.1.call-start
  286.8 0.9 copy-done
  287.7 0.1 copy-done.2
  287.8 0.2 convert_reduce_fusion
  288.0 0.4 fusion.11
  288.4 30.3 %reduce-scatter.9.cloned.1.call-done = bf16[192,1152]{1,0:T(8,128)(2,1)} async-done(((bf16[1536,1152]{1,0:T(8,128)(2,1)}), bf16[192,1152]{1,0:T(8,128)(2,1)}) %reduce-scatter.9.cloned.1.call-update) | async-done | bytes 442384 | tf_op jit(solution)/shard_map/reduce_scatter | solution.py:663
  318.7 2.1 reshape.134
  320.8 83.5 %reduce-scatter.11.cloned.1.call-done = bf16[192,3456]{1,0:T(8,128)(2,1)} async-done(((bf16[1536,3456]{1,0:T(8,128)(2,1)}), bf16[192,3456]{1,0:T(8,128)(2,1)}) %reduce-scatter.11.cloned.1.call-update) | async-done | bytes 1327120 | tf_op jit(solution)/shard_map/reduce_scatter | solution.py:663
  404.3 20.1 %reduce-scatter.7.cloned.1.call-done = bf16[2,2,64,768]{3,2,1,0:T(8,128)(2,1)} async-done(((bf16[2,2,128,768]{3,2,1,0:T(8,128)(2,1)}), bf16[2,2,64,768]{3,2,1,0:T(8,128)(2,1)}) %reduce-scatter.7.cloned.1.call-update) | async-done | bytes 393232 | tf_op jit(solution)/shard_map/reduce_scatter | solution.py:652
  424.4 78.5 %reduce-scatter.5.cloned.1.call-done = bf16[2,128,768]{2,1,0:T(8,128)(2,1)} async-done(((bf16[2,1024,768]{2,1,0:T(8,128)(2,1)}), bf16[2,128,768]{2,1,0:T(8,128)(2,1)}) %reduce-scatter.5.cloned.1.call-update) | async-done | bytes 393232 | tf_op jit(solution)/shard_map/reduce_scatter | solution.py:651
  502.9 2.0 fusion.10
  505.0 43.3 %psum.21 = f32[9,768]{1,0:T(8,128)S(1)} all-reduce(f32[9,768]{1,0:T(8,128)S(1)} %pad_maximum_fusion.3), channel_id=1, replica_groups=mesh['dp'=4,'ctx'=4,'tp'=2] {'dp','ctx','tp'}, use_global_device_ids=true, to_apply=%region_8.9 | all-reduce | flops 6912 | bytes 55296 | tf_op jit(solution)/shard_map/psum | solution.py:660
  548.3 0.7 fusion.24
  549.0 0.6 slice_reduce_fusion
  549.6 2.0 fusion.9
  551.7 0.9 fusion.23
  552.6 34.6 %all-reduce.3.cloned.1.call-done = (bf16[192,3,384]{2,1,0:T(4,128)(2,1)}, bf16[192,3456]{1,0:T(8,128)(2,1)}) async-done(((bf16[192,3,384]{2,1,0:T(4,128)(2,1)}, bf16[192,3456]{1,0:T(8,128)(2,1)}), (bf16[192,3,384]{2,1,0:T(4,128)(2,1)}, bf16[192,3456]{1,0:T(8,128)(2,1)})) %all-reduce.3.cloned.1.call-update) | async-done | bytes 1769488 | tf_op jit(solution)/shard_map/psum | solution.py:664
  587.2 1.5 convert_element_type.53
  588.7 1.1 slice_bitcast_fusion
  589.9 0.7 slice_bitcast_fusion.1
  590.6 1.1 slice.77
  591.8 1.0 copy.35
  (56 shorter events, 0.3 us)
Async XLA Ops:
  7.2 2.7 copy-start.11
  7.2 2.7 copy-start.8
  7.2 2.7 copy-start.9
  7.2 68.9 %all-gather.5.cloned.1.call-start = ((), (), s32[]{:S(2)}) async-start(), calls=%async_computation.4 | async-start | bytes 3538944 | tf_op jit(solution)/shard_map/all_gather | solution.py:541
  7.9 103.3 %all-gather.7.cloned.1.call-start = ((), (), s32[]{:S(2)}) async-start(), calls=%async_computation.5 | async-start | bytes 3981312 | tf_op jit(solution)/shard_map/all_gather | solution.py:543
  9.8 167.1 %all-gather.9.cloned.1.call-start = ((), (), s32[]{:S(2)}) async-start(), calls=%async_computation.6 | async-start | bytes 11943936 | tf_op jit(solution)/shard_map/all_gather | solution.py:546
  9.9 1.3 copy-start.14
  9.9 1.3 copy-start.15
  9.9 1.3 copy-start.16
  10.0 1.4 copy-start.17
  10.0 8.2 %copy-start.1 = (bf16[2,2,64,768]{3,2,1,0:T(8,128)(2,1)S(1)}, bf16[2,2,64,768]{3,2,1,0:T(8,128)(2,1)}, u32[]{:S(2)}) copy-start(bf16[2,2,64,768]{3,2,1,0:T(8,128)(2,1)} %oc.3) | copy-start | bytes 1179652
  11.2 307.5 %reduce-scatter.9.cloned.1.call-start = ((), (), s32[]{:S(2)}) async-start(), calls=%async_computation.9 | async-start | bytes 3981312 | tf_op jit(solution)/shard_map/reduce_scatter | solution.py:663
  270.3 1.3 copy-start.7
  270.3 133.9 %reduce-scatter.11.cloned.1.call-start = ((), (), s32[]{:S(2)}) async-start(), calls=%async_computation.10 | async-start | bytes 11943936 | tf_op jit(solution)/shard_map/reduce_scatter | solution.py:663
  280.6 143.8 %reduce-scatter.7.cloned.1.call-start = ((), (), s32[]{:S(2)}) async-start(), calls=%async_computation.8 | async-start | bytes 1179648 | tf_op jit(solution)/shard_map/reduce_scatter | solution.py:652
  282.8 220.1 %reduce-scatter.5.cloned.1.call-start = ((), (), s32[]{:S(2)}) async-start(), calls=%async_computation.7 | async-start | bytes 3538944 | tf_op jit(solution)/shard_map/reduce_scatter | solution.py:651
  286.7 1.0 copy-start
  286.7 1.1 copy-start.2
  286.7 300.5 %all-reduce.3.cloned.1.call-start = ((), (), s32[]{:S(2)}) async-start(), calls=%async_computation.11 | async-start | bytes 3833856 | tf_op jit(solution)/shard_map/psum | solution.py:664
  288.3 115.9 %copy-start.12 = (bf16[768,4]{0,1:T(4,128)(2,1)S(1)}, bf16[768,4]{0,1:T(4,128)(2,1)}, u32[]{:S(2)}) copy-start(bf16[768,4]{0,1:T(4,128)(2,1)} %reshape.139) | copy-start | bytes 18436
  288.3 214.5 %copy-start.3 = (f32[512,768]{1,0:T(8,128)S(1)}, f32[512,768]{1,0:T(8,128)}, u32[]{:S(2)}) copy-start(f32[512,768]{1,0:T(8,128)} %get-tuple-element.41) | copy-start | bytes 4718596
  502.9 2.1 copy-start.13
  502.9 46.7 %copy-start.5 = (bf16[2,2,64,768]{3,2,1,0:T(8,128)(2,1)S(1)}, bf16[2,2,64,768]{3,2,1,0:T(8,128)(2,1)}, u32[]{:S(2)}) copy-start(bf16[2,2,64,768]{3,2,1,0:T(8,128)(2,1)} %reduce-scatter.7.cloned.1.call-done) | copy-start | bytes 1179652
  502.9 46.7 %copy-start.6 = (bf16[2,128,768]{2,1,0:T(8,128)(2,1)S(1)}, bf16[2,128,768]{2,1,0:T(8,128)(2,1)}, u32[]{:S(2)}) copy-start(bf16[2,128,768]{2,1,0:T(8,128)(2,1)} %reduce-scatter.5.cloned.1.call-done) | copy-start | bytes 1179652
  588.7 1.9 copy-start.4
  589.9 1.9 copy-start.10
Sparse Core Ops, SparseCore 0:
  10.2 65.8 all-gather.4
  78.6 32.5 all-gather.6
  113.1 63.8 all-gather.8
  270.5 48.1 reduce-scatter.8
  322.0 82.1 reduce-scatter.10
  406.9 17.4 reduce-scatter.6
  428.4 74.4 reduce-scatter.4
  506.1 81.0 all-reduce.2

commit v2 on v1

--- a/solution.py
+++ b/solution.py
@@ -77,15 +77,162 @@
         self.COLS = 2 * self.NR
 
 
+MESH = pl.DeviceIdType.MESH
+
+
+def half_index():
+    return lax.axis_index("dp") % 2
+
+
+def block_index():
+    return lax.axis_index("ctx") * 2 + half_index()
+
+
+class Peers:
+    def __init__(self):
+        self.ctxs = lax.axis_size("ctx")
+        self.chips = lax.axis_size("dp") // 2
+        self.tps = lax.axis_size("tp")
+        self.dp = lax.axis_index("dp")
+        self.ctx = lax.axis_index("ctx")
+        self.tp = lax.axis_index("tp")
+        self.core = self.dp % 2
+        self.chip = self.dp // 2
+
+    def at(self, dp=None, ctx=None, tp=None):
+        return {
+            "dp": self.dp if dp is None else dp,
+            "ctx": self.ctx if ctx is None else ctx,
+            "tp": self.tp if tp is None else tp,
+        }
+
+    def across(self):
+        return self.at(tp=1 - self.tp)
+
+    def mate(self):
+        return self.at(dp=self.chip * 2 + 1 - self.core)
+
+    def chip_after(self, k):
+        return lax.rem(self.chip + k, self.chips)
+
+    def chip_before(self, k):
+        return lax.rem(self.chip + self.chips - k, self.chips)
+
+    def row(self, k):
+        return self.at(dp=self.chip_after(k) * 2 + self.core)
+
+    def ctx_after(self, k):
+        return lax.rem(self.ctx + k, self.ctxs)
+
+    def ctx_before(self, k):
+        return lax.rem(self.ctx + self.ctxs - k, self.ctxs)
+
+    def plane(self, k):
+        return self.at(ctx=self.ctx_after(k))
+
+    def greet(self):
+        barrier = pltpu.get_barrier_semaphore()
+        peers = [self.across(), self.mate()]
+        peers += [self.row(k) for k in range(1, self.chips)]
+        peers += [self.plane(k) for k in range(1, self.ctxs)]
+        for peer in peers:
+            pl.semaphore_signal(barrier, inc=1, device_id=peer, device_id_type=MESH)
+        pl.semaphore_wait(barrier, len(peers))
+
+
+def send(src, dst, send_sem, recv_sem, device):
+    copy = pltpu.make_async_remote_copy(
+        src_ref=src,
+        dst_ref=dst,
+        send_sem=send_sem,
+        recv_sem=recv_sem,
+        device_id=device,
+        device_id_type=MESH,
+    )
+    copy.start()
+    return copy
+
+
+def arrived(ref, sem, peers):
+    pltpu.make_async_remote_copy(
+        src_ref=ref,
+        dst_ref=ref,
+        send_sem=sem,
+        recv_sem=sem,
+        device_id=peers.mate(),
+        device_id_type=MESH,
+    ).wait_recv()
+
+
+class WeightGather:
+    def __init__(self, peers, shard, full, sends, across, rows, mate):
+        self.p, self.shard, self.full = peers, shard, full
+        self.sends, self.across, self.rows, self.from_mate = sends, across, rows, mate
+        self.copies = []
+        self.count = 0
+        self.size = shard.shape[0]
+
+    @staticmethod
+    def semaphores(chips):
+        return [
+            pltpu.SemaphoreType.DMA((1 + 2 * (chips - 1) + 2 * chips,)),
+            pltpu.SemaphoreType.DMA((1,)),
+            pltpu.SemaphoreType.DMA((2, max(chips - 1, 1))),
+            pltpu.SemaphoreType.DMA((2, chips)),
+        ]
+
+    def piece(self, tp, dp):
+        return self.full.at[tp, pl.ds(pl.multiple_of(dp * self.size, 16), self.size), :]
+
+    def go(self, src, dst, recv_sem, device):
+        self.copies.append(send(src, dst, self.sends.at[self.count], recv_sem, device))
+        self.count += 1
+
+    def start(self):
+        p = self.p
+        self.go(self.shard, self.piece(p.tp, p.dp), self.across.at[0], p.across())
+        for k in range(1, p.chips):
+            self.go(self.shard, self.piece(p.tp, p.dp), self.rows.at[0, k - 1], p.row(k))
+        self.go(self.shard, self.piece(p.tp, p.dp), self.from_mate.at[0, 0], p.mate())
+
+    def relay_across(self):
+        p = self.p
+        got = self.piece(1 - p.tp, p.dp)
+        arrived(got, self.across.at[0], p)
+        for k in range(1, p.chips):
+            self.go(got, got, self.rows.at[1, k - 1], p.row(k))
+        self.go(got, got, self.from_mate.at[1, 0], p.mate())
+
+    def relay_rows(self, part):
+        p = self.p
+        tp = p.tp if part == 0 else 1 - p.tp
+        for k in range(1, p.chips):
+            got = self.piece(tp, p.chip_before(k) * 2 + p.core)
+            arrived(got, self.rows.at[part, k - 1], p)
+            self.go(got, got, self.from_mate.at[part, k], p.mate())
+
+    def finish(self):
+        p = self.p
+        for part in range(2):
+            tp = p.tp if part == 0 else 1 - p.tp
+            for k in range(p.chips):
+                dp = p.chip_before(k) * 2 + 1 - p.core
+                arrived(self.piece(tp, dp), self.from_mate.at[part, k], p)
+
+    def drain(self):
+        for copy in self.copies:
+            copy.wait_send()
+
+
 def fill_masks(dm, maskp, maskx):
-    block = lax.axis_index("ctx") * lax.axis_size("tp") + lax.axis_index("tp")
+    block = block_index()
     keys = lax.broadcasted_iota(jnp.int32, maskp.shape, 0)
     cols = lax.broadcasted_iota(jnp.int32, maskp.shape, 1) % dm.PB
     maskp[...] = jnp.where(keys <= cols + block * dm.PB, 0.0, NEG)
     keys = lax.broadcasted_iota(jnp.int32, maskx.shape, 0)
     cols = lax.broadcasted_iota(jnp.int32, maskx.shape, 1) % dm.NCH
     seen = (keys // CL == cols // dm.CH) & (
-        keys % CL <= cols % dm.CH + lax.axis_index("tp") * dm.CH
+        keys % CL <= cols % dm.CH + half_index() * dm.CH
     )
     maskx[...] = jnp.where(seen, 0.0, NEG)
 
@@ -120,68 +267,78 @@
 
 def forward_kernel(
     dm,
-    xp,
-    xc,
     op,
     oc,
-    ln,
     cos,
     shi,
     slo,
-    w,
+    wq,
+    wm,
     n_out,
     k_out,
     v_out,
     q_out,
     att_out,
     lse_out,
+    w_out,
+    ln_out,
+    wm_out,
     maskp,
     maskx,
     sbuf,
+    xp,
+    xc,
+    w,
+    put_sem,
+    x_send,
+    x_plane,
+    x_mate,
+    c_send,
+    c_mate,
+    own_sem,
+    *sems,
 ):
     G, R, PB, NCH, D = dm.G, dm.R, dm.PB, dm.NCH, dm.D
-    HC = w.shape[2] // 3
+    HC = (w.shape[2] - 128) // 3
     TP = w.shape[0]
-    gain, bias = ln[0:1, :].astype(F32), ln[1:2, :].astype(F32)
+    p = Peers()
+    block = block_index()
+    gq = WeightGather(p, wq, w, *sems[:4])
+    gm = WeightGather(p, wm, wm_out, *sems[4:])
+    size = wq.shape[0]
+    mine = pl.ds(pl.multiple_of(p.dp * size, 16), size)
+    local = [
+        pltpu.make_async_copy(wq, w.at[p.tp, mine, :], own_sem.at[0]),
+        pltpu.make_async_copy(wm, wm_out.at[p.tp, mine, :], own_sem.at[1]),
+        pltpu.make_async_copy(op, xp.at[block], own_sem.at[2]),
+        pltpu.make_async_copy(oc, xc.at[p.core], own_sem.at[3]),
+    ]
+    for copy in local:
+        copy.start()
+    p.greet()
+    gq.start()
+    sent = []
+    for k in range(1, p.ctxs):
+        sent.append(send(op, xp.at[block], x_send.at[k - 1], x_plane.at[k - 1], p.plane(k)))
+    sent.append(send(op, xp.at[block], x_send.at[p.ctxs - 1], x_mate.at[0], p.mate()))
+    sent.append(send(oc, xc.at[p.core], c_send, c_mate, p.mate()))
     fill_masks(dm, maskp, maskx)
+    gq.relay_across()
+    gq.relay_rows(0)
+    gq.relay_rows(1)
+    gm.start()
+    gq.finish()
+    for copy in local:
+        copy.wait()
+    put = pltpu.make_async_copy(w, w_out, put_sem)
+    put.start()
+    ln = w[0, :, 3 * HC :].astype(F32).T[:8, :]
+    ln_out[...] = ln
+    gain, bias = ln[0:1, :], ln[1:2, :]
 
     def normed(x):
         hat, _ = norm_stats(x.astype(F32))
         return (hat * gain + bias).astype(BF16)
-
-    def keys_values(g, x, row, table):
-        rows = x.shape[0]
-        n = normed(x)
-        n_out[g, pl.ds(row, rows), :] = n
-        c = cos[pl.ds(table, rows), :]
-        hi = shi[pl.ds(table, rows), :]
-        lo = slo[pl.ds(table, rows), :]
-        for t in range(TP):
-            kk = dot(n, w[t, :, HC : 2 * HC])
-            for j in range(HC // 128):
-                tile = rotate(kk[:, j * 128 : (j + 1) * 128], c, hi, lo)
-                k_out[g, pl.ds(row, rows), t * HC + j * 128 : t * HC + (j + 1) * 128] = tile.astype(BF16)
-            v_out[g, pl.ds(row, rows), t * HC : (t + 1) * HC] = dot(n, w[t, :, 2 * HC :]).astype(BF16)
-
-    CHUNK = 256
-    steps = dm.P // CHUNK
-
-    def prompt_chunk(i, carry):
-        g, row = i // steps, pl.multiple_of((i % steps) * CHUNK, CHUNK)
-        keys_values(g, xp[g, pl.ds(row, CHUNK), :], row, row)
-        return carry
-
-    lax.fori_loop(0, G * steps, prompt_chunk, 0)
-
-    def cont_chunk(i, carry):
-        g, c = i // dm.NC, i % dm.NC
-        row = pl.multiple_of(dm.P + c * CL, CL)
-        keys_values(g, xc[g, c], row, dm.P)
-        return carry
-
-    lax.fori_loop(0, G * dm.NC, cont_chunk, 0)
-
-    block = lax.axis_index("ctx") * lax.axis_size("tp") + lax.axis_index("tp")
 
     def queries(x, row, table):
         rows = x.shape[0]
@@ -208,11 +365,57 @@
         queries(
             oc[g, c],
             pl.multiple_of(dm.NP + i * dm.CH, dm.CH),
-            pl.multiple_of(dm.P + lax.axis_index("tp") * dm.CH, dm.CH),
+            pl.multiple_of(dm.P + p.core * dm.CH, dm.CH),
         )
         return carry
 
     lax.fori_loop(0, G * dm.NC, own_cont, 0)
+
+    def keys_values(g, x, row, table):
+        rows = x.shape[0]
+        n = normed(x)
+        n_out[g, pl.ds(row, rows), :] = n
+        c = cos[pl.ds(table, rows), :]
+        hi = shi[pl.ds(table, rows), :]
+        lo = slo[pl.ds(table, rows), :]
+        for t in range(TP):
+            kk = dot(n, w[t, :, HC : 2 * HC])
+            for j in range(HC // 128):
+                tile = rotate(kk[:, j * 128 : (j + 1) * 128], c, hi, lo)
+                k_out[g, pl.ds(row, rows), t * HC + j * 128 : t * HC + (j + 1) * 128] = tile.astype(BF16)
+            v_out[g, pl.ds(row, rows), t * HC : (t + 1) * HC] = dot(n, w[t, :, 2 * HC : 3 * HC]).astype(BF16)
+
+    def block_chunk(g, b):
+        row = pl.multiple_of(b * PB, PB)
+        keys_values(g, xp[b, g], row, row)
+
+    arrived(xc.at[1 - p.core], c_mate, p)
+
+    def cont_chunk(i, carry):
+        g, c = i // dm.NC, i % dm.NC
+        row = pl.multiple_of(dm.P + c * CL, CL)
+        x = jnp.concatenate([xc[0, g, c], xc[1, g, c]], axis=0)
+        keys_values(g, x, row, dm.P)
+        return carry
+
+    lax.fori_loop(0, G * dm.NC, cont_chunk, 0)
+
+    def relay(k):
+        b = p.ctx_before(k) * 2 + p.core
+        arrived(xp.at[b], x_plane.at[k - 1], p)
+        return send(xp.at[b], xp.at[b], x_send.at[p.ctxs + k - 1], x_mate.at[k], p.mate())
+
+    for k in range(1, p.ctxs):
+        sent.append(relay(k))
+    for k in range(p.ctxs):
+        arrived(xp.at[p.ctx_before(k) * 2 + 1 - p.core], x_mate.at[k], p)
+
+    def prompt_chunk(i, carry):
+        block_chunk(i // (2 * p.ctxs), i % (2 * p.ctxs))
+        return carry
+
+    lax.fori_loop(0, G * 2 * p.ctxs, prompt_chunk, 0)
+    gm.relay_across()
 
     TILE = 256
     tiles = dm.P // TILE
@@ -257,6 +460,14 @@
         return carry
 
     lax.fori_loop(0, G * dm.PAIRS, attend, 0)
+    gm.relay_rows(0)
+    gm.relay_rows(1)
+    gm.finish()
+    gq.drain()
+    gm.drain()
+    for copy in sent:
+        copy.wait_send()
+    put.wait()
 
 
 def mlp_kernel(
@@ -266,18 +477,13 @@
     att,
     op,
     oc,
-    ep,
-    ec,
-    yp,
-    yc,
     tp_,
     tc,
     ln,
     wo,
     wu,
     wd,
-    outp,
-    outc,
+    blk_out,
     resg,
     gatt,
     gwo,
@@ -297,7 +503,7 @@
     D, NP, NT, G, PB = dm.D, dm.NP, dm.NT, dm.G, dm.PB
     TP, HC = wo.shape[0], wo.shape[2]
     t, j = pl.program_id(0), pl.program_id(1)
-    gain, bias = ln[2:3, :].astype(F32), ln[3:4, :].astype(F32)
+    gain, bias = ln[2:3, :], ln[3:4, :]
 
     def own(prompt, cont):
         return jnp.concatenate([prompt.reshape(NP, D), cont.reshape(NT - NP, D)], axis=0)
@@ -339,17 +545,9 @@
     def _():
         cot = own(tp_[...], tc[...]).astype(F32)
         block = blk[...]
-        arrays = [own(ep[...], ec[...])] + [own(yp[i], yc[i]) for i in range(3)]
-        res = mix[4] * block
-        for i in range(4):
-            a = arrays[i].astype(F32)
-            res += mix[i] * a
-            small[2 + i : 3 + i, :] = jnp.sum(cot * a, axis=0, keepdims=True)
-        small[6:7, :] = jnp.sum(cot * block, axis=0, keepdims=True)
-        small[7:8, :] = jnp.zeros((1, D), F32)
-        res = res.astype(BF16)
-        outp[...] = res[:NP].reshape(outp.shape)
-        outc[...] = res[NP:].reshape(outc.shape)
+        blk_out[...] = block.astype(BF16)
+        small[2:3, :] = jnp.sum(cot * block, axis=0, keepdims=True)
+        small[3:, :] = jnp.zeros((5, D), F32)
         g = gh[...]
         h = hat[...]
         small[0:1, :] = jnp.sum(g * h, axis=0, keepdims=True)
@@ -387,9 +585,9 @@
     nt,
 ):
     G, R, PB, NCH, D, NX = dm.G, dm.R, dm.PB, dm.NCH, dm.D, dm.NX
-    TP, HC = w.shape[0], w.shape[2] // 3
+    TP, HC = w.shape[0], (w.shape[2] - 128) // 3
     fill_masks(dm, maskp, maskx)
-    block = lax.axis_index("ctx") * lax.axis_size("tp") + lax.axis_index("tp")
+    block = block_index()
     TILE = 256
     tiles = dm.P // TILE
 
@@ -453,7 +651,7 @@
         outc = jnp.where(sublane_pick((128, NCH), True), accc[:, :NCH], accc[:, NCH:]).T
         tab = pl.ds(pl.multiple_of(block * PB, PB), PB)
         dq[rp, lanes] = rotate_back(outp, cos[tab, :], shi[tab, :], slo[tab, :]).astype(BF16)
-        tab = pl.ds(pl.multiple_of(dm.P + lax.axis_index("tp") * dm.CH, dm.CH), dm.CH)
+        tab = pl.ds(pl.multiple_of(dm.P + half_index() * dm.CH, dm.CH), dm.CH)
         for c in range(dm.NC):
             part = rotate_back(outc[c * dm.CH : (c + 1) * dm.CH], cos[tab, :], shi[tab, :], slo[tab, :])
             rows = pl.ds(pl.multiple_of(dm.NP + g * NCH + c * dm.CH, dm.CH), dm.CH)
@@ -470,7 +668,7 @@
         for t in range(TP):
             part = dot_nt(dk[rows, t * HC : (t + 1) * HC], w[t, :, HC : 2 * HC])
             total = part if total is None else total + part
-            total += dot_nt(dv[rows, t * HC : (t + 1) * HC], w[t, :, 2 * HC :])
+            total += dot_nt(dv[rows, t * HC : (t + 1) * HC], w[t, :, 2 * HC : 3 * HC])
         dx[rows, :] = total.astype(BF16)
         nt[:, rows] = transpose(n_all[rows, :])
         return carry
@@ -489,7 +687,7 @@
             part = dot(transpose(n_all[rows, :]), dq[g * PB : (g + 1) * PB, t * HC : (t + 1) * HC])
             acc = part if acc is None else acc + part
             for c in range(dm.NC):
-                first = g * R + dm.P + c * CL + lax.axis_index("tp") * dm.CH
+                first = g * R + dm.P + c * CL + half_index() * dm.CH
                 rows = pl.ds(pl.multiple_of(first, dm.CH), dm.CH)
                 mine = dm.NP + g * NCH + c * dm.CH
                 acc += dot(
@@ -537,14 +735,18 @@
     R, NT, NP = dm.R, dm.NT, dm.NP
 
     sds = jax.ShapeDtypeStruct
-    ln = lax.all_gather(jnp.stack([ln1_gain, ln1_bias, ln2_gain, ln2_bias]), "dp", axis=1, tiled=True)
-    xp = lax.all_gather(prompt_in, ("ctx", "tp"), axis=1, tiled=True)
-    xc = lax.all_gather(cont_in, "tp", axis=2, tiled=True)
-    wq = lax.all_gather(w_qkv.reshape(S, 3 * HC), ("tp", "dp"), axis=0, tiled=True)
-    wq = wq.reshape(TP, D, 3 * HC)
-    shard = jnp.concatenate([w_out.T, w_up, w_down.T], axis=1)
-    wm = lax.all_gather(shard, ("tp", "dp"), axis=0, tiled=True).reshape(TP, D, HC + 2 * FC)
-    wo, wu, wd = wm[:, :, :HC], wm[:, :, HC : HC + FC], wm[:, :, HC + FC :]
+    chips, ctxs = lax.axis_size("dp") // 2, lax.axis_size("ctx")
+    swap = [(4 * y + 2 * c + t, 4 * y + 2 * t + c) for y in range(chips) for c in (0, 1) for t in (0, 1)]
+
+    def trade(x):
+        return lax.ppermute(x, ("dp", "tp"), swap)
+
+    own_p, own_c = trade(prompt_in), trade(cont_in)
+    cot_p, cot_c = trade(prompt_cot), trade(cont_cot)
+    norms = jnp.stack([ln1_gain, ln1_bias, ln2_gain, ln2_bias], axis=1)
+    norms = jnp.pad(norms, ((0, 0), (0, 124)))
+    wq_shard = jnp.concatenate([w_qkv.reshape(S, 3 * HC), norms], axis=1)
+    wm_shard = jnp.concatenate([w_out.T, w_up, w_down.T], axis=1)
 
     positions = jnp.arange(PROMPT + CL, dtype=jnp.int32).astype(F32)
     lane = jnp.arange(128, dtype=jnp.int32)
@@ -555,7 +757,10 @@
     shi = jnp.where(second[None, :], sin, 0.0)
     slo = jnp.where(second[None, :], 0.0, -sin)
 
-    n_all, k, v, q, att, lse = pl.pallas_call(
+    any_ = pl.BlockSpec(memory_space=pl.ANY)
+    vmem = pl.BlockSpec(memory_space=pltpu.VMEM)
+    dma = pltpu.SemaphoreType.DMA
+    n_all, k, v, q, att, lse, wq, ln, wm = pl.pallas_call(
         partial(forward_kernel, dm),
         out_shape=(
             sds((G, R, D), BF16),
@@ -564,26 +769,43 @@
             sds((NT, D), BF16),
             sds((NT, D), BF16),
             sds((G * dm.PAIRS, 1, dm.COLS), F32),
+            sds((TP, D, 3 * HC + 128), BF16),
+            sds((8, D), F32),
+            sds((TP, D, HC + 2 * FC), BF16),
         ),
+        in_specs=[vmem] * 6 + [any_],
+        out_specs=(vmem,) * 6 + (any_, vmem, any_),
         scratch_shapes=[
             pltpu.VMEM((PROMPT, 2 * PB), F32),
             pltpu.VMEM((dm.NX, 2 * dm.NCH), F32),
             pltpu.VMEM((PROMPT, dm.COLS), F32),
-        ],
-        compiler_params=params(),
+            pltpu.VMEM((2 * ctxs, G, PB, D), BF16),
+            pltpu.VMEM((2, G, NC, CH, D), BF16),
+            pltpu.VMEM((TP, D, 3 * HC + 128), BF16),
+            dma,
+            dma((2 * ctxs - 1,)),
+            dma((ctxs - 1,)),
+            dma((ctxs,)),
+            dma,
+            dma,
+            dma((4,)),
+        ]
+        + WeightGather.semaphores(chips)
+        + WeightGather.semaphores(chips),
+        compiler_params=params(collective_id=0, has_side_effects=True),
         name="forward",
-    )(xp, xc, prompt_in, cont_in, ln, cos, shi, slo, wq)
+    )(own_p, own_c, cos, shi, slo, wq_shard, wm_shard)
+    wo, wu, wd = wm[:, :, :HC], wm[:, :, HC : HC + FC], wm[:, :, HC + FC :]
 
     T = 512 if FC % 512 == 0 else 256
     steps = FC // T
-    row_specs = [whole(a.shape) for a in (att, prompt_in, cont_in, prompt_embed, cont_embed, prompt_earlier, cont_earlier, prompt_cot, cont_cot, ln, wo)]
+    row_specs = [whole(a.shape) for a in (att, own_p, own_c, cot_p, cot_c, ln, wo)]
     tile = pl.BlockSpec((1, D, T), lambda t, j: (t, 0, j))
-    outp, outc, resg, gatt, gwo, gwu, gwd, small = pl.pallas_call(
+    blk, resg, gatt, gwo, gwu, gwd, small = pl.pallas_call(
         partial(mlp_kernel, dm, steps),
         grid=(TP, steps),
         out_shape=(
-            sds(prompt_in.shape, BF16),
-            sds(cont_in.shape, BF16),
+            sds((NT, D), BF16),
             sds((NT, D), F32),
             sds((NT, D), BF16),
             sds((TP, D, HC), BF16),
@@ -593,8 +815,7 @@
         ),
         in_specs=[pl.BlockSpec(memory_space=pltpu.SMEM)] + row_specs + [tile, tile],
         out_specs=(
-            whole(prompt_in.shape),
-            whole(cont_in.shape),
+            whole((NT, D)),
             whole((NT, D)),
             whole((NT, D)),
             whole((TP, D, HC)),
@@ -618,14 +839,10 @@
     )(
         mix_weights,
         att,
-        prompt_in,
-        cont_in,
-        prompt_embed,
-        cont_embed,
-        prompt_earlier,
-        cont_earlier,
-        prompt_cot,
-        cont_cot,
+        own_p,
+        own_c,
+        cot_p,
+        cot_c,
         ln,
         wo,
         wu,
@@ -635,6 +852,8 @@
     dx, dxq, gwq = pl.pallas_call(
         partial(backward_kernel, dm),
         out_shape=(sds((G * R, D), BF16), sds((NT, D), F32), sds((TP, D, 3 * HC), BF16)),
+        in_specs=[vmem] * 11,
+        out_specs=(vmem,) * 3,
         scratch_shapes=[
             pltpu.VMEM((PROMPT, 2 * PB), F32),
             pltpu.VMEM((dm.NX, 2 * dm.NCH), F32),
@@ -648,14 +867,34 @@
     )(q, k, v, att, gatt, lse, n_all.reshape(G * R, D), cos, shi, slo, wq)
 
     dx = dx.reshape(G, R, D)
-    gp = lax.psum_scatter(dx[:, :PROMPT], ("ctx", "tp"), scatter_dimension=1, tiled=True)
-    gc = lax.psum_scatter(dx[:, PROMPT:].reshape(G, NC, CL, D), "tp", scatter_dimension=2, tiled=True)
+    ways = [[2 * i, 2 * i + 1] for i in range(chips)]
+
+    def halves(x, axis):
+        return lax.psum_scatter(x, "dp", scatter_dimension=axis, axis_index_groups=ways, tiled=True)
+
+    gp = halves(dx[:, :PROMPT].reshape(G, ctxs, 2, PB, D), 2)
+    gp = lax.psum_scatter(gp.reshape(G, ctxs * PB, D), "ctx", scatter_dimension=1, tiled=True)
+    gc = halves(dx[:, PROMPT:].reshape(G, NC, CL, D), 2)
     gn = jnp.concatenate([gp.reshape(NP, D), gc.reshape(NT - NP, D)], axis=0).astype(F32) + dxq
-    x = jnp.concatenate([prompt_in.reshape(NP, D), cont_in.reshape(NT - NP, D)], axis=0).astype(F32)
+    x = jnp.concatenate([own_p.reshape(NP, D), own_c.reshape(NT - NP, D)], axis=0).astype(F32)
     hat, scale = norm_stats(x)
-    gin = (resg + norm_back(gn, ln[0:1].astype(F32), hat, scale)).astype(BF16)
+    gin = (resg + norm_back(gn, ln[0:1], hat, scale)).astype(BF16)
+    gin = trade(gin)
+    blk = trade(blk).astype(F32)
+    outs, sums = [], 0.0
+    for b, e, y, c in (
+        (blk[:NP].reshape(prompt_in.shape), prompt_embed, prompt_earlier, prompt_cot),
+        (blk[NP:].reshape(cont_in.shape), cont_embed, cont_earlier, cont_cot),
+    ):
+        terms = [e.astype(F32)] + [y[i].astype(F32) for i in range(3)]
+        total = mix_weights[4] * b
+        for i in range(4):
+            total += mix_weights[i] * terms[i]
+        outs.append(total.astype(BF16))
+        c = c.astype(F32)
+        sums += jnp.stack([jnp.sum((c * a).reshape(-1, D), axis=0) for a in terms])
     small = jnp.concatenate(
-        [small[:7], jnp.sum(gn * hat, axis=0)[None], jnp.sum(gn, axis=0)[None]], axis=0
+        [small[:3], sums, jnp.sum(gn * hat, axis=0)[None], jnp.sum(gn, axis=0)[None]], axis=0
     )
     small = lax.psum(small, ("dp", "ctx", "tp"))
 
@@ -668,8 +907,8 @@
     start = lax.axis_index("dp") * S
     mine = lax.dynamic_slice_in_dim(small, start, S, axis=1)
     return (
-        outp,
-        outc,
+        outs[0],
+        outs[1],
         gin[:NP].reshape(prompt_in.shape),
         gin[NP:].reshape(cont_in.shape),
         mine[7],
@@ -680,7 +919,7 @@
         gm[:, :HC].T,
         gm[:, HC : HC + FC],
         gm[:, HC + FC :].T,
-        jnp.sum(small[2:7], axis=1),
+        jnp.sum(jnp.concatenate([small[3:7], small[2:3]]), axis=1),
     )
 
 

time: 600 us -> 527 us (0.88)
  waiting for transfers between devices: 344 us -> 207 us
  Pallas kernels: 126 us -> 188 us
  blocking collectives: 66 us -> 42.2 us
  starting transfers between devices: 0.33 us -> 12.1 us
  other arithmetic: 20.4 us -> 30.5 us
    all_gather x3 -> x0, waiting for transfers between devices: 96.1 us -> none  [the longest x1 38 us: per_device(): xp = lax.all_gather(prompt_in, ('ctx', 'tp'), axis=1, tiled=True)]
    pallas_call x1, Pallas kernels: 42.7 us -> 107 us  [per_device(): pl.pallas_call(partial(forward_kernel, dm), out_shape=(sds((G, R, D), BF1...]
    reduce_scatter x2 -> x3, waiting for transfers between devices: 98.6 us -> 49.7 us  [the longest x1 38.6 us: per_device(): lax.psum_scatter(gp.reshape(G, ctxs * PB, D), 'ctx', scatter_dimension=1,...]
    all_gather x2 -> x0, blocking collectives: 22.7 us -> none  [the longest x1 16.5 us: per_device(): xc = lax.all_gather(cont_in, 'tp', axis=2, tiled=True)]
    reduce_scatter x2, waiting for transfers between devices: 114 us -> 130 us  [reduce(): lax.psum_scatter(g.reshape(TP * D, -1), ('tp', 'dp'), scatter_dimension=0...]
    ppermute x0 -> x6, starting transfers between devices: none -> 11.9 us  [trade(): return lax.ppermute(x, ('dp', 'tp'), swap)]
    psum x1, waiting for transfers between devices: 34.6 us -> 25.5 us  [reduce(): return lax.psum(g, 'ctx').astype(F32)]
    reduce_sum x1 -> x3, other arithmetic: 0.63 us -> 8.56 us  [the longest x2 7.92 us: per_device(): sums += jnp.stack([jnp.sum((c * a).reshape(-1, D), axis=0) for a in terms])]
  transfers between devices with their start and end apart: 8 -> 12, of which waited for: 8 -> 5; matrix products, arithmetic and copies ran while one was open for 5% -> 10% of each run, Pallas kernels for 7% -> 20%
where the time goes in v2:
time: 527 us; the launch traced here: 526 us
  waiting for transfers between devices  207 us (39%)
  Pallas kernels  188 us (36%)
  blocking collectives  42.2 us (8%)
  local copies, waits for them, and re-layouts  32.2 us (6%)
  other arithmetic  30.5 us (6%)
  between operations  14.5 us (3%)
  starting transfers between devices  12.1 us (2%)
    reduce_scatter x2, waiting for transfers between devices, reduce(): lax.psum_scatter(g.reshape(TP * D, -1), ('tp', 'dp'), scatter_dimension=0...  130 us
    pallas_call x1, Pallas kernels, per_device(): pl.pallas_call(partial(forward_kernel, dm), out_shape=(sds((G, R, D), BF1...  107 us
    pallas_call x1, Pallas kernels, per_device(): pl.pallas_call(partial(backward_kernel, dm), out_shape=(sds((G * R, D), B...  53.5 us
    psum x1, blocking collectives, per_device(): small = lax.psum(small, ('dp', 'ctx', 'tp'))  42.2 us
    reduce_scatter x1, waiting for transfers between devices, per_device(): lax.psum_scatter(gp.reshape(G, ctxs * PB, D), 'ctx', scatter_dimension=1,...  38.6 us
    pallas_call x1, Pallas kernels, per_device(): pl.pallas_call(partial(mlp_kernel, dm, steps), grid=(TP, steps), out_shap...  27.3 us
    psum x1, waiting for transfers between devices, reduce(): return lax.psum(g, 'ctx').astype(F32)  25.5 us
    ppermute x6, starting transfers between devices, trade(): return lax.ppermute(x, ('dp', 'tp'), swap)  11.9 us
  transfers between devices with their start and end apart: 12, of which 5 were waited for; matrix products, arithmetic and copies ran while one was open for 10% of the time, Pallas kernels for 20%

profile of v2, /device:TPU:0, one launch (start us, length us, event | category | flops | bytes accessed | tf_op | source)
XLA Modules:
  0.0 525.7 jit_solution(16950058590571974871)
XLA Ops:
  7.2 1.7 collective-permute-start
  8.9 1.6 collective-permute-start.1
  10.5 1.6 collective-permute-start.2
  12.2 4.5 collective-permute-start.3
  16.7 1.1 copy.47
  17.8 0.8 stack.45
  18.5 0.7 stack.46
  19.2 0.7 stack.47
  19.8 0.7 stack.48
  20.7 0.8 fusion.34.wq
  21.5 3.4 fusion.33
  24.9 1.2 pad_maximum_fusion.1.wm
  26.1 0.7 copy-done
  26.9 106.7 %forward.1 = (bf16[2,1280,768]{2,1,0:T(8,128)(2,1)}, bf16[2,1280,768]{2,1,0:T(8,128)(2,1)}, bf16[2,1280,768]{2,1,0:T(8,128)(2,1)}, bf16[512,768]{1,0:T(8,128)(2,...) custom-call(bf16[2,128,768]{2,1,0:T(8,128)(2,1)} %copy-done, ...), custom_call_target="tpu_custom_call" | custom-call | tf_op jit(solution)/shard_map/forward/pallas_call | solution.py:763
  133.7 8.0 %fusion.41 = (bf16[2,768,1536]{2,1,0:T(8,128)(2,1)}, bf16[2,768,1536]{2,1,0:T(8,128)(2,1)}) fusion(bf16[2,768,3456]{2,1,0:T(8,128)(2,1)} %get-tuple-element.34), kind=kLoop, calls=%fused_computation.84 | loop fusion | bytes 18874368 | tf_op jit(solution)/shard_map/slice | solution.py:798
  141.6 2.4 slice.99.wo
  144.0 0.7 copy-done.16
  144.8 27.3 %feed.1 = (bf16[512,768]{1,0:T(8,128)(2,1)}, f32[512,768]{1,0:T(8,128)}, bf16[512,768]{1,0:T(8,128)(2,1)}, bf16[2,768,384]{2,1,0:T(8,128)(2,1)}, bf16[2,768,1536...) custom-call(f32[5]{0:T(128)} %mix.1, bf16[512,768]{1,0:T(8,128)(2,1)} %get-tuple-element.32.att, ...), custom_call_target="tpu_custom_call" | custom-call | tf_op jit(solution)/shard_map/feed/pallas_call | solution.py:804
  172.1 53.5 %backward.1 = (bf16[2560,768]{1,0:T(8,128)(2,1)}, f32[512,768]{1,0:T(8,128)}, bf16[2,768,1152]{2,1,0:T(8,128)(2,1)}) custom-call(bf16[512,768]{1,0:T(8,128)(2,1)} %get-tuple-element.37.q, bf16[2,1280,768]{2,1,0:T(8,128)(2,1)} %get-tuple-element.38.k, bf16[2,1280,768]{2,1,0:T(8,128)(2,1)} %get-tuple-element.39.v, bf16[512,768]{1,0:T(8,128)(2,1)} %get-tuple-element.32.att, ...), custom_call_target="tpu_custom_call" | custom-call | tf_op jit(solution)/shard_map/backward/pallas_call | solution.py:852
  225.6 2.1 slice.131
  227.7 1.9 copy.45
  229.7 0.7 reduce-scatter.12.cloned.1.call-update
  231.0 9.0 %pad_maximum_fusion = bf16[2,768,3456]{2,1,0:T(8,128)(2,1)} fusion(bf16[2,768,1536]{2,1,0:T(8,128)(2,1)} %get-tuple-element.50, bf16[2,768,1536]{2,1,0:T(8,128)(2,1)} %get-tuple-element.49, bf16[2,768,384]{2,1,0:T(8,128)(2,1)S(1)} %copy-done.12), kind=kLoop, calls=%fused_computation | loop fusion | flops 31850496 | bytes 21233664 | tf_op jit(solution)/shard_map/concatenate | solution.py:905
  240.1 2.1 slice.132
  243.3 0.7 collective-permute-start.4
  244.0 0.6 fusion.44
  244.8 0.8 slice_reduce_fusion
  246.1 1.6 slice_multiply_fusion
  247.7 46.2 %reduce-scatter.12.cloned.1.call-done = bf16[192,1152]{1,0:T(8,128)(2,1)} async-done(((bf16[1536,1152]{1,0:T(8,128)(2,1)}), bf16[192,1152]{1,0:T(8,128)(2,1)}) %reduce-scatter.12.cloned.1.call-update) | async-done | bytes 442384 | tf_op jit(solution)/shard_map/reduce_scatter | solution.py:902
  293.9 2.1 reshape.160
  296.0 84.0 %reduce-scatter.14.cloned.1.call-done = bf16[192,3456]{1,0:T(8,128)(2,1)} async-done(((bf16[1536,3456]{1,0:T(8,128)(2,1)}), bf16[192,3456]{1,0:T(8,128)(2,1)}) %reduce-scatter.14.cloned.1.call-update) | async-done | bytes 1327120 | tf_op jit(solution)/shard_map/reduce_scatter | solution.py:902
  380.0 11.0 %reduce-scatter.10.cloned.1.call-done = bf16[2,2,64,768]{3,2,1,0:T(8,128)(2,1)} async-done(((bf16[2,2,128,768]{3,2,1,0:T(8,128)(2,1)}), bf16[2,2,64,768]{3,2,1,0:T(8,128)(2,1)}) %reduce-scatter.10.cloned.1.call-update) | async-done | bytes 393232 | tf_op jit(solution)/shard_map/reduce_scatter | solution.py:873
  391.1 38.6 %reduce-scatter.8.cloned.1.call-done = bf16[2,128,768]{2,1,0:T(8,128)(2,1)} async-done(((bf16[2,512,768]{2,1,0:T(8,128)(2,1)}), bf16[2,128,768]{2,1,0:T(8,128)(2,1)}) %reduce-scatter.8.cloned.1.call-update) | async-done | bytes 393232 | tf_op jit(solution)/shard_map/reduce_scatter | solution.py:876
  429.7 2.1 fusion.10
  431.9 1.6 fusion.9
  433.5 1.8 collective-permute-start.5
  435.3 4.0 fusion.30
  439.4 3.9 fusion.26
  443.4 42.2 %psum.21 = f32[9,768]{1,0:T(8,128)S(1)} all-reduce(f32[9,768]{1,0:T(8,128)S(1)} %pad_maximum_fusion.3), channel_id=1, replica_groups=mesh['dp'=4,'ctx'=4,'tp'=2] {'dp','ctx','tp'}, use_global_device_ids=true, to_apply=%region_17.18 | all-reduce | flops 6912 | bytes 55296 | tf_op jit(solution)/shard_map/psum | solution.py:899
  485.6 0.6 maximum_reduce_fusion
  486.3 0.7 fusion.43
  486.9 0.9 fusion.42
  487.8 25.5 %all-reduce.4.cloned.1.call-done = (bf16[192,3,384]{2,1,0:T(4,128)(2,1)}, bf16[192,3456]{1,0:T(8,128)(2,1)}) async-done(((bf16[192,3,384]{2,1,0:T(4,128)(2,1)}, bf16[192,3456]{1,0:T(8,128)(2,1)}), (bf16[192,3,384]{2,1,0:T(4,128)(2,1)}, bf16[192,3456]{1,0:T(8,128)(2,1)})) %all-reduce.4.cloned.1.call-update) | async-done | bytes 1769488 | tf_op jit(solution)/shard_map/psum | solution.py:903
  513.3 1.5 convert_element_type.130
  514.8 1.1 slice_bitcast_fusion
  516.0 0.7 slice_bitcast_fusion.1
  516.7 1.1 slice.136
  517.9 1.0 copy.46
  (92 shorter events, 3.0 us)
Async XLA Ops:
  7.2 235.1 %reduce-scatter.6.cloned.1.call-start = ((), (), s32[]{:S(2)}) async-start(), calls=%async_computation.5 | async-start | bytes 4718592 | tf_op jit(solution)/shard_map/reduce_scatter | solution.py:873
  7.2 18.8 %collective-permute-start = (bf16[2,128,768]{2,1,0:T(8,128)(2,1)}, bf16[2,128,768]{2,1,0:T(8,128)(2,1)S(1)}, u32[]{:S(2)}, u32[]{:S(2)}) collective-permute-start(bf16[2,128,768]{2,1,0:T(8,128)(2,1)} %param.17), channel_id=1, source_target_pairs={{0,0},{1,8},{8,1},{9,9},{16,16},{17,24},{24,17},{25,25},{2,2},{3,1... | collective-permute-start | bytes 1179656 | tf_op jit(solution)/shard_map/ppermute | solution.py:742
  8.9 17.2 %collective-permute-start.1 = (bf16[2,2,64,768]{3,2,1,0:T(8,128)(2,1)}, bf16[2,2,64,768]{3,2,1,0:T(8,128)(2,1)S(1)}, u32[]{:S(2)}, u32[]{:S(2)}) collective-permute-start(bf16[2,2,64,768]{3,2,1,0:T(8,128)(2,1)} %param.18), channel_id=1, source_target_pairs={{0,0},{1,8},{8,1},{9,9},{16,16},{17,24},{24,17},{25,25},{2,2},{3,1... | collective-permute-start | bytes 1179656 | tf_op jit(solution)/shard_map/ppermute | solution.py:742
  10.5 133.5 %collective-permute-start.2 = (bf16[2,128,768]{2,1,0:T(8,128)(2,1)}, bf16[2,128,768]{2,1,0:T(8,128)(2,1)S(1)}, u32[]{:S(2)}, u32[]{:S(2)}) collective-permute-start(bf16[2,128,768]{2,1,0:T(8,128)(2,1)} %param.32), channel_id=1, source_target_pairs={{0,0},{1,8},{8,1},{9,9},{16,16},{17,24},{24,17},{25,25},{2,2},{3,1... | collective-permute-start | bytes 1179656 | tf_op jit(solution)/shard_map/ppermute | solution.py:742
  12.2 131.9 %collective-permute-start.3 = (bf16[2,2,64,768]{3,2,1,0:T(8,128)(2,1)}, bf16[2,2,64,768]{3,2,1,0:T(8,128)(2,1)}, u32[]{:S(2)}, u32[]{:S(2)}) collective-permute-start(bf16[2,2,64,768]{3,2,1,0:T(8,128)(2,1)} %param.33), channel_id=1, source_target_pairs={{0,0},{1,8},{8,1},{9,9},{16,16},{17,24},{24,17},{25,25},{2,2},{3,1... | collective-permute-start | bytes 1179656 | tf_op jit(solution)/shard_map/ppermute | solution.py:742
  17.7 7.1 %copy-start.13 = (bf16[1536,192]{0,1:T(8,128)(2,1)S(1)}, bf16[1536,192]{0,1:T(8,128)(2,1)}, u32[]{:S(2)}) copy-start(bf16[1536,192]{0,1:T(8,128)(2,1)} %param.30) | copy-start | bytes 1769476
  17.7 7.1 %copy-start.14 = (bf16[192,1536]{1,0:T(8,128)(2,1)S(1)}, bf16[192,1536]{1,0:T(8,128)(2,1)}, u32[]{:S(2)}) copy-start(bf16[192,1536]{1,0:T(8,128)(2,1)} %param.29) | copy-start | bytes 1769476
  17.7 7.1 %copy-start.21 = (bf16[384,192]{0,1:T(8,128)(2,1)S(1)}, bf16[384,192]{0,1:T(8,128)(2,1)}, u32[]{:S(2)}) copy-start(bf16[384,192]{0,1:T(8,128)(2,1)} %param.28) | copy-start | bytes 442372
  26.0 0.7 copy-start
  26.0 0.9 copy-start.2
  144.0 0.7 copy-start.16
  229.6 64.2 %reduce-scatter.12.cloned.1.call-start = ((), (), s32[]{:S(2)}) async-start(), calls=%async_computation.8 | async-start | bytes 3981312 | tf_op jit(solution)/shard_map/reduce_scatter | solution.py:902
  229.7 1.3 copy-start.12
  230.4 149.6 %reduce-scatter.14.cloned.1.call-start = ((), (), s32[]{:S(2)}) async-start(), calls=%async_computation.9 | async-start | bytes 11943936 | tf_op jit(solution)/shard_map/reduce_scatter | solution.py:902
  240.0 151.0 %reduce-scatter.10.cloned.1.call-start = ((), (), s32[]{:S(2)}) async-start(), calls=%async_computation.7 | async-start | bytes 1179648 | tf_op jit(solution)/shard_map/reduce_scatter | solution.py:873
  242.2 1.1 copy-start.24
  242.2 1.8 copy-start.22
  242.2 2.4 copy-start.23
  242.2 2.4 copy-start.1
  242.2 2.4 copy-start.3
  242.2 187.5 %reduce-scatter.8.cloned.1.call-start = ((), (), s32[]{:S(2)}) async-start(), calls=%async_computation.6 | async-start | bytes 1966080 | tf_op jit(solution)/shard_map/reduce_scatter | solution.py:876
  242.8 270.5 %all-reduce.4.cloned.1.call-start = ((), (), s32[]{:S(2)}) async-start(), calls=%async_computation.10 | async-start | bytes 3833856 | tf_op jit(solution)/shard_map/psum | solution.py:903
  243.3 2.7 collective-permute-start.4
  247.7 182.0 %copy-start.4 = (f32[512,768]{1,0:T(8,128)S(1)}, f32[512,768]{1,0:T(8,128)}, u32[]{:S(2)}) copy-start(f32[512,768]{1,0:T(8,128)} %get-tuple-element.45) | copy-start | bytes 4718596
  429.7 2.1 copy-start.7
  429.7 2.2 copy-start.8
  429.7 2.2 copy-start.9
  431.9 3.4 copy-start.6
  431.9 3.4 copy-start.10
  431.9 3.4 copy-start.17
  431.9 3.4 copy-start.18
  433.5 53.4 %collective-permute-start.5 = (bf16[512,768]{1,0:T(8,128)(2,1)}, bf16[512,768]{1,0:T(8,128)(2,1)S(1)}, u32[]{:S(2)}, u32[]{:S(2)}) collective-permute-start(bf16[512,768]{1,0:T(8,128)(2,1)} %fusion.9), channel_id=1, source_target_pairs={{0,0},{1,8},{8,1},{9,9},{16,16},{17,24},{24,17},{25,25},{2,2},{3,1... | collective-permute-start | bytes 2359304 | tf_op jit(solution)/shard_map/ppermute | solution.py:742
  435.3 4.1 copy-start.11
  435.3 4.1 copy-start.19
  435.3 4.1 copy-start.20
  514.8 1.9 copy-start.5
  516.0 1.9 copy-start.15
Sparse Core Ops, SparseCore 0:
  229.8 10.9 reduce-scatter.5
  244.6 49.2 reduce-scatter.11
  297.8 82.1 reduce-scatter.13
  382.8 8.2 reduce-scatter.9
  393.2 36.4 reduce-scatter.7
  432.6 80.6 all-reduce.3

commit v3 on v2

--- a/solution.py
+++ b/solution.py
@@ -274,7 +274,8 @@
     slo,
     wq,
     wm,
-    n_out,
+    nt_out,
+    own_out,
     k_out,
     v_out,
     q_out,
@@ -286,6 +287,8 @@
     maskp,
     maskx,
     sbuf,
+    all_rows,
+    own_rows,
     xp,
     xc,
     w,
@@ -343,6 +346,7 @@
     def queries(x, row, table):
         rows = x.shape[0]
         n = normed(x)
+        own_rows[pl.ds(row, rows), :] = n
         c = cos[pl.ds(table, rows), :]
         hi = shi[pl.ds(table, rows), :]
         lo = slo[pl.ds(table, rows), :]
@@ -370,11 +374,12 @@
         return carry
 
     lax.fori_loop(0, G * dm.NC, own_cont, 0)
-
-    def keys_values(g, x, row, table):
+    own_out[...] = transpose(own_rows[...])
+
+    def keys_values(g, x, row, table, place):
         rows = x.shape[0]
         n = normed(x)
-        n_out[g, pl.ds(row, rows), :] = n
+        all_rows[pl.ds(place, rows), :] = n
         c = cos[pl.ds(table, rows), :]
         hi = shi[pl.ds(table, rows), :]
         lo = slo[pl.ds(table, rows), :]
@@ -387,7 +392,7 @@
 
     def block_chunk(g, b):
         row = pl.multiple_of(b * PB, PB)
-        keys_values(g, xp[b, g], row, row)
+        keys_values(g, xp[b, g], row, row, pl.multiple_of((b * G + g) * PB, PB))
 
     arrived(xc.at[1 - p.core], c_mate, p)
 
@@ -395,7 +400,7 @@
         g, c = i // dm.NC, i % dm.NC
         row = pl.multiple_of(dm.P + c * CL, CL)
         x = jnp.concatenate([xc[0, g, c], xc[1, g, c]], axis=0)
-        keys_values(g, x, row, dm.P)
+        keys_values(g, x, row, dm.P, pl.multiple_of(G * dm.P + i * CL, CL))
         return carry
 
     lax.fori_loop(0, G * dm.NC, cont_chunk, 0)
@@ -416,6 +421,13 @@
 
     lax.fori_loop(0, G * 2 * p.ctxs, prompt_chunk, 0)
     gm.relay_across()
+
+    def turn(i, carry):
+        rows = pl.ds(pl.multiple_of(i * 256, 256), 256)
+        nt_out[:, rows] = transpose(all_rows[rows, :])
+        return carry
+
+    lax.fori_loop(0, G * R // 256, turn, 0)
 
     TILE = 256
     tiles = dm.P // TILE
@@ -561,38 +573,363 @@
             gwo[s] = dot(gbt, att[:, s * HC : (s + 1) * HC]).astype(BF16)
 
 
+class Reduce:
+    def __init__(self, p, n, refs):
+        self.p, self.n = p, n
+        self.mine, self.got, self.row, self.acr, self.zin = refs[:5]
+        self.sc, self.rc, self.sy, self.ry, self.sx, self.rx, self.sz, self.rz = refs[5:13]
+        self.mid = p.ctxs // 2
+        self.left = p.ctx < self.mid
+        self.centre = (p.ctx == self.mid - 1) | (p.ctx == self.mid)
+        self.outer = (p.ctx > 0) & (p.ctx < p.ctxs - 1)
+        step = jnp.where(self.left, 1, -1)
+        self.inner_at = p.ctx + step
+        self.outer_at = jnp.clip(p.ctx - step, 0, p.ctxs - 1)
+
+    REFS = 13
+
+    @staticmethod
+    def scratch(n, chips, size, width, slots=2):
+        dma = pltpu.SemaphoreType.DMA
+        far = max(chips - 1, 1)
+        return [
+            pltpu.VMEM((slots, chips, 2, size, width), BF16),
+            pltpu.VMEM((2 * n, chips, size, width), BF16),
+            pltpu.VMEM((2 * n, far, size, width), BF16),
+            pltpu.VMEM((n, size, width), BF16),
+            pltpu.VMEM((n, 2, size, width), BF16),
+            dma((2 * n,)),
+            dma((2 * n,)),
+            dma((2 * n, far)),
+            dma((2 * n, far)),
+            dma((n,)),
+            dma((n,)),
+            dma((n, 2)),
+            dma((n, 2)),
+        ]
+
+    def copy(self, src, dst, send_sem, recv_sem, device):
+        return pltpu.make_async_remote_copy(
+            src_ref=src,
+            dst_ref=dst,
+            send_sem=send_sem,
+            recv_sem=recv_sem,
+            device_id=device,
+            device_id_type=MESH,
+        )
+
+    def by_core(self, i, slot):
+        p = self.p
+        return self.copy(
+            self.mine.at[slot, :, 1 - p.core], self.got.at[i], self.sc.at[i], self.rc.at[i], p.mate()
+        )
+
+    def by_row(self, i, k):
+        p = self.p
+        return self.copy(
+            self.got.at[i, p.chip_after(k)],
+            self.row.at[i, k - 1],
+            self.sy.at[i, k - 1],
+            self.ry.at[i, k - 1],
+            p.row(k),
+        )
+
+    def by_tp(self, j):
+        p = self.p
+        return self.copy(
+            self.got.at[j, p.chip], self.acr.at[j], self.sx.at[j], self.rx.at[j], p.across()
+        )
+
+    def inward(self, j):
+        slot = jnp.where(self.centre, 1, 0)
+        return self.copy(
+            self.got.at[self.n + j, self.p.chip],
+            self.zin.at[j, slot],
+            self.sz.at[j, 0],
+            self.rz.at[j, slot],
+            self.p.at(ctx=self.inner_at),
+        )
+
+    def outward(self, j):
+        return self.copy(
+            self.got.at[self.n + j, self.p.chip],
+            self.zin.at[j, 1],
+            self.sz.at[j, 1],
+            self.rz.at[j, 1],
+            self.p.at(ctx=self.outer_at),
+        )
+
+    def add(self, i, y, other):
+        self.got[i, y] = (self.got[i, y].astype(F32) + other.astype(F32)).astype(BF16)
+
+    def cores_send(self, i, slot):
+        self.by_core(i, slot).start()
+
+    def cores_sent(self, i, slot):
+        self.by_core(i, slot).wait_send()
+
+    def cores_sum(self, i, slot):
+        p = self.p
+        self.by_core(i, slot).wait_recv()
+        for y in range(p.chips):
+            self.add(i, y, self.mine[slot, y, p.core])
+        for k in range(1, p.chips):
+            self.by_row(i, k).start()
+
+    def rows_sum(self, i):
+        p = self.p
+        for k in range(1, p.chips):
+            self.by_row(i, k).wait_recv()
+            self.add(i, p.chip, self.row[i, k - 1])
+        if i < self.n:
+            self.by_tp(i).start()
+
+    def tp_sum(self, j):
+        self.by_tp(j).wait_recv()
+        self.add(self.n + j, self.p.chip, self.acr[j])
+
+        @pl.when(jnp.logical_not(self.outer))
+        def _():
+            self.inward(j).start()
+
+    def ctx_in(self, j):
+        @pl.when(self.outer)
+        def _():
+            pltpu.make_async_copy(self.zin.at[j, 0], self.zin.at[j, 0], self.rz.at[j, 0]).wait()
+            self.add(self.n + j, self.p.chip, self.zin[j, 0])
+            self.inward(j).start()
+
+    def ctx_out(self, j):
+        p = self.p
+        pltpu.make_async_copy(self.zin.at[j, 1], self.zin.at[j, 1], self.rz.at[j, 1]).wait()
+        self.inward(j).wait_send()
+
+        @pl.when(self.centre)
+        def _():
+            self.add(self.n + j, p.chip, self.zin[j, 1])
+
+        @pl.when(jnp.logical_not(self.centre))
+        def _():
+            self.got[self.n + j, p.chip] = self.zin[j, 1]
+
+        @pl.when(self.outer)
+        def _():
+            self.outward(j).start()
+        return self.got[self.n + j, p.chip]
+
+    def drain(self):
+        p = self.p
+        for i in range(2 * self.n):
+            for k in range(1, p.chips):
+                self.by_row(i, k).wait_send()
+        for j in range(self.n):
+            self.by_tp(j).wait_send()
+
+            @pl.when(self.outer)
+            def _():
+                self.outward(j).wait_send()
+
+
+def small_sum(p, sm, near, rows, across, planes, ss, rc, ry, rx, rz):
+    copies = []
+
+    def go(src, dst, recv_sem, device):
+        copies.append(send(src, dst, ss.at[len(copies)], recv_sem, device))
+
+    go(sm, near, rc, p.mate())
+    copies[-1].wait_recv()
+    rows[p.chip] = sm[...] + near[...]
+    for k in range(1, p.chips):
+        go(rows.at[p.chip], rows.at[p.chip], ry.at[k - 1], p.row(k))
+    for k in range(1, p.chips):
+        arrived(rows.at[p.chip_before(k)], ry.at[k - 1], p)
+    total = rows[0]
+    for y in range(1, p.chips):
+        total += rows[y]
+    across[0] = total
+    go(across.at[0], across.at[1], rx, p.across())
+    copies[-1].wait_recv()
+    planes[p.ctx] = across[0] + across[1]
+    for k in range(1, p.ctxs):
+        go(planes.at[p.ctx], planes.at[p.ctx], rz.at[k - 1], p.plane(k))
+    for k in range(1, p.ctxs):
+        arrived(planes.at[p.ctx_before(k)], rz.at[k - 1], p)
+    total = planes[0]
+    for z in range(1, p.ctxs):
+        total += planes[z]
+    for copy in copies:
+        copy.wait_send()
+    return total
+
+
 def backward_kernel(
     dm,
+    T,
     q,
-    k,
-    v,
     att,
     gatt,
     lse,
-    n_all,
+    nt,
+    own_nt,
     cos,
     shi,
     slo,
     w,
-    dx,
-    dxq,
-    gw,
+    ln,
+    own_p,
+    own_c,
+    resg,
+    small,
+    k_hbm,
+    v_hbm,
+    gwo,
+    gwu,
+    gwd,
+    gin_p,
+    gin_c,
+    gq_out,
+    go_out,
+    gu_out,
+    gd_out,
+    small_out,
     maskp,
     maskx,
+    kbuf,
+    vbuf,
     dk,
     dv,
     dq,
-    nt,
+    dxq,
+    dxm,
+    dxz,
+    dxc,
+    dxcm,
+    kv_sem,
+    load_a,
+    load_b,
+    m_send,
+    m_recv,
+    z_send,
+    z_recv,
+    c_send,
+    c_recv,
+    sm,
+    sm_near,
+    sm_rows,
+    sm_across,
+    sm_planes,
+    sm_ss,
+    sm_rc,
+    sm_ry,
+    sm_rx,
+    sm_rz,
+    *refs,
 ):
     G, R, PB, NCH, D, NX = dm.G, dm.R, dm.PB, dm.NCH, dm.D, dm.NX
     TP, HC = w.shape[0], (w.shape[2] - 128) // 3
-    fill_masks(dm, maskp, maskx)
+    PT = dm.PAIRS // TP
+    p = Peers()
+    n_a = gwu.shape[-1] // T
+    ra = Reduce(p, n_a, refs[: Reduce.REFS])
+    rb = Reduce(p, 1 + PT, refs[Reduce.REFS :])
     block = block_index()
     TILE = 256
     tiles = dm.P // TILE
-
-    def attend(i, carry):
-        g, pair = i // dm.PAIRS, i % dm.PAIRS
+    chips = p.chips
+
+    def tp_of(i, n):
+        return 1 - p.tp if i < n else p.tp
+
+    def load_slab(i):
+        t, cols, slot = tp_of(i, n_a), slice((i % n_a) * T, (i % n_a + 1) * T), i % 2
+        return [
+            pltpu.make_async_copy(gwu.at[t, :, :, :, cols], ra.mine.at[slot, :, :, :, :T], load_a.at[0, slot]),
+            pltpu.make_async_copy(gwd.at[t, :, :, :, cols], ra.mine.at[slot, :, :, :, T:], load_a.at[1, slot]),
+        ]
+
+    def begin(copies):
+        for copy in copies:
+            copy.start()
+
+    def ready(copies):
+        for copy in copies:
+            copy.wait()
+
+    def load_kv(it, slot):
+        pair_rel, g = it // G, it % G
+        t = jnp.where(pair_rel < PT, 1 - p.tp, p.tp)
+        lanes = pl.ds(pl.multiple_of((t * PT + pair_rel % PT) * 128, 128), 128)
+        return [
+            pltpu.make_async_copy(k_hbm.at[g, :, lanes], kbuf.at[slot], kv_sem.at[0, slot]),
+            pltpu.make_async_copy(v_hbm.at[g, :, lanes], vbuf.at[slot], kv_sem.at[1, slot]),
+        ]
+
+    begin(load_kv(0, 0))
+    begin(load_slab(0))
+    begin(load_slab(1))
+    wo_load = [
+        pltpu.make_async_copy(gwo.at[tp_of(i, 1)], rb.mine.at[i], load_b.at[i]) for i in range(2)
+    ]
+    begin(wo_load)
+    p.greet()
+    fill_masks(dm, maskp, maskx)
+    for i in range(2):
+        ready(load_slab(i))
+        ra.cores_send(i, i)
+    ready(wo_load)
+    NB = 1 + PT
+    rb.cores_send(0, 0)
+    rb.cores_send(NB, 1)
+    ra.cores_sum(0, 0)
+
+    def next_slab(i):
+        def run():
+            ra.cores_sent(i - 2, i % 2)
+            begin(load_slab(i))
+
+        return run
+
+    def send_slab(i):
+        def run():
+            ready(load_slab(i))
+            ra.cores_send(i, i % 2)
+
+        return run
+
+    events = {}
+
+    def on(it, step):
+        events.setdefault(it, []).append(step)
+
+    for i in range(1, 2 * n_a):
+        on(i, partial(ra.cores_sum, i, i % 2))
+        if i + 1 < 2 * n_a:
+            on(i - 1, next_slab(i + 1))
+            on(i, send_slab(i + 1))
+    on(2 * n_a, partial(rb.cores_sum, 0, 0))
+    on(2 * n_a, partial(rb.cores_sum, NB, 1))
+
+    def wslab(pair_rel):
+        return pair_rel + 1 if pair_rel < PT else NB + 1 + pair_rel - PT
+
+    late = []
+    wslot = lambda pair_rel: 2 + pair_rel % 2
+    for pr in range(TP * PT - 1):
+        on(pr * G + 2 * G - 1, partial(rb.cores_sum, wslab(pr), wslot(pr)))
+    on(5, partial(ra.rows_sum, 0))
+    on(8, partial(ra.rows_sum, 1))
+    on(11, partial(ra.rows_sum, 2))
+
+    def attend(it, carry):
+        pair_rel, g = it // G, it % G
+        t = jnp.where(pair_rel < PT, 1 - p.tp, p.tp)
+        pair = t * PT + pair_rel % PT
+        slot = it % 2
+
+        @pl.when(it + 1 < G * dm.PAIRS)
+        def _():
+            begin(load_kv(it + 1, 1 - slot))
+
         lanes = pl.ds(pl.multiple_of(pair * 128, 128), 128)
         rp = pl.ds(pl.multiple_of(g * PB, PB), PB)
         rc = pl.ds(pl.multiple_of(dm.NP + g * NCH, NCH), NCH)
@@ -613,13 +950,14 @@
             ],
             axis=1,
         )
-        stat = lse[i]
+        stat = lse[g * dm.PAIRS + pair]
+        ready(load_kv(it, slot))
 
         def grads(s, kt, vt, cols):
-            p = jnp.exp(s - stat[:, cols:])
+            pr = jnp.exp(s - stat[:, cols:])
             dp = dot(vt, gt[:, cols:])
-            ds = (p * (dp - delta[:, cols:])).astype(BF16)
-            gv = dot(p.astype(BF16), gs[cols:])
+            ds = (pr * (dp - delta[:, cols:])).astype(BF16)
+            gv = dot(pr.astype(BF16), gs[cols:])
             gk = dot(ds, qs[cols:])
             gq = dot(transpose(kt), ds)
             return gk, gv, gq
@@ -627,21 +965,23 @@
         acc = None
         for j in range(tiles):
             rows = slice(j * TILE, (j + 1) * TILE)
-            kt = k[g, rows, lanes]
+            kt = kbuf[slot, rows, :]
             s = dot(kt, qt)
             s = jnp.concatenate([s[:, : 2 * PB] + maskp[rows, :], s[:, 2 * PB :]], axis=1)
-            gk, gv, gq = grads(s, kt, v[g, rows, lanes], 0)
-            gk = rotate_back(gk, cos[rows, :], shi[rows, :], slo[rows, :])
-            out = pl.ds(pl.multiple_of(g * R + j * TILE, 128), TILE)
-            dk[out, lanes] = gk.astype(BF16)
-            dv[out, lanes] = gv.astype(BF16)
+            gk, gv, gq = grads(s, kt, vbuf[slot, rows, :], 0)
+            gk = rotate_back(gk, cos[rows, :], shi[rows, :], slo[rows, :]).astype(BF16)
+            gv = gv.astype(BF16)
+            for b in range(TILE // PB):
+                out = pl.ds(pl.multiple_of(((j * (TILE // PB) + b) * G + g) * PB, PB), PB)
+                dk[out, lanes] = gk[b * PB : (b + 1) * PB]
+                dv[out, lanes] = gv[b * PB : (b + 1) * PB]
             acc = gq if acc is None else acc + gq
-        kt = k[g, dm.P :, lanes]
+        kt = kbuf[slot, dm.P :, :]
         s = dot(kt, qt[:, 2 * PB :]) + maskx[...]
-        gk, gv, gq = grads(s, kt, v[g, dm.P :, lanes], 2 * PB)
+        gk, gv, gq = grads(s, kt, vbuf[slot, dm.P :, :], 2 * PB)
         for c in range(dm.NC):
             rows = slice(dm.P, dm.P + CL)
-            out = pl.ds(pl.multiple_of(g * R + dm.P + c * CL, 128), CL)
+            out = pl.ds(pl.multiple_of(G * dm.P + (g * dm.NC + c) * CL, CL), CL)
             part = rotate_back(gk[c * CL : (c + 1) * CL], cos[rows, :], shi[rows, :], slo[rows, :])
             dk[out, lanes] = part.astype(BF16)
             dv[out, lanes] = gv[c * CL : (c + 1) * CL].astype(BF16)
@@ -651,50 +991,167 @@
         outc = jnp.where(sublane_pick((128, NCH), True), accc[:, :NCH], accc[:, NCH:]).T
         tab = pl.ds(pl.multiple_of(block * PB, PB), PB)
         dq[rp, lanes] = rotate_back(outp, cos[tab, :], shi[tab, :], slo[tab, :]).astype(BF16)
-        tab = pl.ds(pl.multiple_of(dm.P + half_index() * dm.CH, dm.CH), dm.CH)
+        tab = pl.ds(pl.multiple_of(dm.P + p.core * dm.CH, dm.CH), dm.CH)
         for c in range(dm.NC):
             part = rotate_back(outc[c * dm.CH : (c + 1) * dm.CH], cos[tab, :], shi[tab, :], slo[tab, :])
             rows = pl.ds(pl.multiple_of(dm.NP + g * NCH + c * dm.CH, dm.CH), dm.CH)
             dq[rows, lanes] = part.astype(BF16)
+
+        @pl.when(g == G - 1)
+        def _():
+            put = 2 + pair_rel % 2
+            index = jnp.where(pair_rel < PT, pair_rel + 1, NB + 1 + pair_rel - PT)
+
+            @pl.when(pair_rel >= 2)
+            def _():
+                last = pair_rel - 2
+                rb.cores_sent(jnp.where(last < PT, last + 1, NB + 1 + last - PT), put)
+
+            size = D // (2 * chips)
+            shape = (chips, 2, size)
+            both = jnp.concatenate([dk[:, lanes], dv[:, lanes]], axis=1)
+            gkv = dot(nt[...], both).astype(BF16).reshape(shape + (256,))
+            rb.mine[put, :, :, :, 128:] = gkv
+            gqw = dot(own_nt[...], dq[:, lanes]).astype(BF16).reshape(shape + (128,))
+            rb.mine[put, :, :, :, :128] = gqw
+            rb.cores_send(index, put)
+
+        for when, steps in events.items():
+
+            @pl.when(it == when)
+            def _():
+                for step in steps:
+                    step()
+
         return carry
 
     lax.fori_loop(0, G * dm.PAIRS, attend, 0)
-
-    CHUNK = 256 if R % 256 == 0 else 128
-
-    def project(i, carry):
-        rows = pl.ds(pl.multiple_of(i * CHUNK, CHUNK), CHUNK)
+    last = G * dm.PAIRS
+    for when in sorted(events):
+        if when >= last:
+            for step in events[when]:
+                step()
+    tail = TP * PT - 1
+
+    def project(rows):
         total = None
         for t in range(TP):
             part = dot_nt(dk[rows, t * HC : (t + 1) * HC], w[t, :, HC : 2 * HC])
             total = part if total is None else total + part
             total += dot_nt(dv[rows, t * HC : (t + 1) * HC], w[t, :, 2 * HC : 3 * HC])
-        dx[rows, :] = total.astype(BF16)
-        nt[:, rows] = transpose(n_all[rows, :])
+        return total
+
+    def block_rows(b):
+        return pl.ds(pl.multiple_of(b * G * PB, G * PB), G * PB)
+
+    def to_mate(k):
+        b = p.ctx_after(k) * 2 + 1 - p.core
+        return ra.copy(dk.at[block_rows(b), :], dxm.at[k], m_send.at[k], m_recv.at[k], p.mate())
+
+    def to_plane(k):
+        b = p.ctx_after(k) * 2 + p.core
+        return ra.copy(
+            dk.at[block_rows(b), :],
+            dxz.at[k - 1],
+            z_send.at[k - 1],
+            z_recv.at[k - 1],
+            p.at(ctx=p.ctx_after(k)),
+        )
+
+    def planes(i, carry):
+        k = lax.rem(i + 1, p.ctxs)
+        rows = block_rows(p.ctx_after(k) * 2 + 1 - p.core)
+        dk[rows, :] = project(rows).astype(BF16)
+        to_mate(k).start()
+        rows = block_rows(p.ctx_after(k) * 2 + p.core)
+        part = project(rows)
+        to_mate(k).wait_recv()
+        dk[rows, :] = (part + dxm[k].astype(F32)).astype(BF16)
+
+        @pl.when(k > 0)
+        def _():
+            to_plane(k).start()
+
         return carry
 
-    lax.fori_loop(0, G * R // CHUNK, project, 0)
+    lax.fori_loop(0, p.ctxs, planes, 0)
+    rb.cores_sum(wslab(tail), wslot(tail))
+
+    def cont_rows(i, carry):
+        rows = pl.ds(pl.multiple_of(G * dm.P + i * CL, CL), CL)
+        total = project(rows).astype(BF16)
+        out = pl.ds(pl.multiple_of(i * dm.CH, dm.CH), dm.CH)
+        dxc[0, out, :] = total[: dm.CH]
+        dxc[1, out, :] = total[dm.CH :]
+        return carry
+
+    lax.fori_loop(0, G * dm.NC, cont_rows, 0)
+    cont_copy = ra.copy(dxc.at[1 - p.core], dxcm, c_send, c_recv, p.mate())
+    cont_copy.start()
     total = dot_nt(dq[:, :HC], w[0, :, :HC])
     for t in range(1, TP):
         total += dot_nt(dq[:, t * HC : (t + 1) * HC], w[t, :, :HC])
     dxq[...] = total
-    for t in range(TP):
-        gw[t, :, HC : 2 * HC] = dot(nt[...], dk[:, t * HC : (t + 1) * HC]).astype(BF16)
-        gw[t, :, 2 * HC :] = dot(nt[...], dv[:, t * HC : (t + 1) * HC]).astype(BF16)
-        acc = None
-        for g in range(G):
-            rows = pl.ds(pl.multiple_of(g * R + block * PB, PB), PB)
-            part = dot(transpose(n_all[rows, :]), dq[g * PB : (g + 1) * PB, t * HC : (t + 1) * HC])
-            acc = part if acc is None else acc + part
-            for c in range(dm.NC):
-                first = g * R + dm.P + c * CL + half_index() * dm.CH
-                rows = pl.ds(pl.multiple_of(first, dm.CH), dm.CH)
-                mine = dm.NP + g * NCH + c * dm.CH
-                acc += dot(
-                    transpose(n_all[rows, :]),
-                    dq[mine : mine + dm.CH, t * HC : (t + 1) * HC],
-                )
-        gw[t, :, :HC] = acc.astype(BF16)
+    for i in range(n_a, 2 * n_a):
+        ra.rows_sum(i)
+        ra.tp_sum(i - n_a)
+    for j in range(n_a):
+        ra.ctx_in(j)
+    gain = ln[0:1, :]
+    cont_copy.wait_recv()
+    gn = dxc[p.core].astype(F32) + dxcm[...].astype(F32) + dxq[dm.NP :, :]
+    hat, scale = norm_stats(own_c[...].reshape(dm.NT - dm.NP, D).astype(F32))
+    gin_c[...] = (resg[dm.NP :, :] + norm_back(gn, gain, hat, scale)).astype(BF16).reshape(gin_c.shape)
+    sums = [jnp.sum(gn * hat, axis=0, keepdims=True), jnp.sum(gn, axis=0, keepdims=True)]
+    for i in list(range(NB)) + [NB]:
+        rb.rows_sum(i)
+
+    def final_a(j):
+        total = ra.ctx_out(j)
+        gu_out[:, j * T : (j + 1) * T] = total[:, :T].astype(F32)
+        gd_out[j * T : (j + 1) * T, :] = total[:, T:].astype(F32).T
+
+    for j in range(n_a):
+        final_a(j)
+    gn = dk[block_rows(block), :].astype(F32) + dxq[: dm.NP, :]
+    for k in range(1, p.ctxs):
+        to_plane(k).wait_recv()
+        gn += dxz[k - 1].astype(F32)
+    hat, scale = norm_stats(own_p[...].reshape(dm.NP, D).astype(F32))
+    gin_p[...] = (resg[: dm.NP, :] + norm_back(gn, gain, hat, scale)).astype(BF16).reshape(gin_p.shape)
+    sm[...] = small[...]
+    sm[7:8, :] = sums[0] + jnp.sum(gn * hat, axis=0, keepdims=True)
+    sm[8:9, :] = sums[1] + jnp.sum(gn, axis=0, keepdims=True)
+    for i in range(NB + 1, 2 * NB):
+        rb.rows_sum(i)
+    for j in range(NB):
+        rb.tp_sum(j)
+    for j in range(NB):
+        rb.ctx_in(j)
+    small_out[...] = small_sum(
+        p, sm, sm_near, sm_rows, sm_across, sm_planes, sm_ss, sm_rc, sm_ry, sm_rx, sm_rz
+    )
+    for j in range(NB):
+        total = rb.ctx_out(j).astype(F32)
+        if j == 0:
+            go_out[...] = total.T
+        else:
+            for c in range(3):
+                first = c * HC + (j - 1) * 128
+                gq_out[:, first : first + 128] = total[:, c * 128 : (c + 1) * 128]
+    for i in range(max(0, 2 * n_a - 2), 2 * n_a):
+        ra.cores_sent(i, i % 2)
+    rb.cores_sent(0, 0)
+    rb.cores_sent(NB, 1)
+    for pr in (tail - 1, tail):
+        rb.cores_sent(wslab(pr), wslot(pr))
+    for k in range(p.ctxs):
+        to_mate(k).wait_send()
+    for k in range(1, p.ctxs):
+        to_plane(k).wait_send()
+    cont_copy.wait_send()
+    ra.drain()
+    rb.drain()
 
 
 def whole(shape):
@@ -760,10 +1217,11 @@
     any_ = pl.BlockSpec(memory_space=pl.ANY)
     vmem = pl.BlockSpec(memory_space=pltpu.VMEM)
     dma = pltpu.SemaphoreType.DMA
-    n_all, k, v, q, att, lse, wq, ln, wm = pl.pallas_call(
+    nt, own_nt, k, v, q, att, lse, wq, ln, wm = pl.pallas_call(
         partial(forward_kernel, dm),
         out_shape=(
-            sds((G, R, D), BF16),
+            sds((D, G * R), BF16),
+            sds((D, NT), BF16),
             sds((G, R, D), BF16),
             sds((G, R, D), BF16),
             sds((NT, D), BF16),
@@ -774,11 +1232,13 @@
             sds((TP, D, HC + 2 * FC), BF16),
         ),
         in_specs=[vmem] * 6 + [any_],
-        out_specs=(vmem,) * 6 + (any_, vmem, any_),
+        out_specs=(vmem,) * 7 + (any_, vmem, any_),
         scratch_shapes=[
             pltpu.VMEM((PROMPT, 2 * PB), F32),
             pltpu.VMEM((dm.NX, 2 * dm.NCH), F32),
             pltpu.VMEM((PROMPT, dm.COLS), F32),
+            pltpu.VMEM((G * R, D), BF16),
+            pltpu.VMEM((NT, D), BF16),
             pltpu.VMEM((2 * ctxs, G, PB, D), BF16),
             pltpu.VMEM((2, G, NC, CH, D), BF16),
             pltpu.VMEM((TP, D, 3 * HC + 128), BF16),
@@ -849,76 +1309,117 @@
         wd,
     )
 
-    dx, dxq, gwq = pl.pallas_call(
-        partial(backward_kernel, dm),
-        out_shape=(sds((G * R, D), BF16), sds((NT, D), F32), sds((TP, D, 3 * HC), BF16)),
-        in_specs=[vmem] * 11,
-        out_specs=(vmem,) * 3,
+    sums = []
+    for e, y, c in (
+        (prompt_embed, prompt_earlier, prompt_cot),
+        (cont_embed, cont_earlier, cont_cot),
+    ):
+        c = c.astype(F32)
+        terms = [e.astype(F32)] + [y[i].astype(F32) for i in range(3)]
+        sums.append(jnp.stack([jnp.sum((c * a).reshape(-1, D), axis=0) for a in terms]))
+    small = jnp.concatenate([small[:3], sums[0] + sums[1], jnp.zeros((9, D), F32)], axis=0)
+
+    blk = trade(blk).astype(F32)
+    n_a = FC // T
+    split = (TP, chips, 2, S)
+    far = max(chips - 1, 1)
+    gin_p, gin_c, gq, go, gu, gd, small = pl.pallas_call(
+        partial(backward_kernel, dm, T),
+        out_shape=(
+            sds(prompt_in.shape, BF16),
+            sds(cont_in.shape, BF16),
+            sds((S, 3 * HC), F32),
+            sds((HC, S), F32),
+            sds((S, FC), F32),
+            sds((FC, S), F32),
+            sds((16, D), F32),
+        ),
+        in_specs=[vmem] * 15 + [any_] * 5,
+        out_specs=(vmem,) * 7,
         scratch_shapes=[
             pltpu.VMEM((PROMPT, 2 * PB), F32),
             pltpu.VMEM((dm.NX, 2 * dm.NCH), F32),
+            pltpu.VMEM((2, R, 128), BF16),
+            pltpu.VMEM((2, R, 128), BF16),
             pltpu.VMEM((G * R, D), BF16),
             pltpu.VMEM((G * R, D), BF16),
             pltpu.VMEM((NT, D), BF16),
-            pltpu.VMEM((D, G * R), BF16),
-        ],
-        compiler_params=params(),
+            pltpu.VMEM((NT, D), F32),
+            pltpu.VMEM((ctxs, G * PB, D), BF16),
+            pltpu.VMEM((ctxs - 1, G * PB, D), BF16),
+            pltpu.VMEM((2, NT - NP, D), BF16),
+            pltpu.VMEM((NT - NP, D), BF16),
+            dma((2, 2)),
+            dma((2, 2)),
+            dma((2,)),
+            dma((ctxs,)),
+            dma((ctxs,)),
+            dma((ctxs - 1,)),
+            dma((ctxs - 1,)),
+            dma,
+            dma,
+            pltpu.VMEM((16, D), F32),
+            pltpu.VMEM((16, D), F32),
+            pltpu.VMEM((chips, 16, D), F32),
+            pltpu.VMEM((2, 16, D), F32),
+            pltpu.VMEM((ctxs, 16, D), F32),
+            dma((1 + chips + ctxs,)),
+            dma,
+            dma((far,)),
+            dma,
+            dma((ctxs - 1,)),
+        ]
+        + Reduce.scratch(n_a, chips, S, 2 * T)
+        + Reduce.scratch(1 + dm.PAIRS // TP, chips, S, HC, slots=4),
+        compiler_params=params(collective_id=1, has_side_effects=True),
         name="backward",
-    )(q, k, v, att, gatt, lse, n_all.reshape(G * R, D), cos, shi, slo, wq)
-
-    dx = dx.reshape(G, R, D)
-    ways = [[2 * i, 2 * i + 1] for i in range(chips)]
-
-    def halves(x, axis):
-        return lax.psum_scatter(x, "dp", scatter_dimension=axis, axis_index_groups=ways, tiled=True)
-
-    gp = halves(dx[:, :PROMPT].reshape(G, ctxs, 2, PB, D), 2)
-    gp = lax.psum_scatter(gp.reshape(G, ctxs * PB, D), "ctx", scatter_dimension=1, tiled=True)
-    gc = halves(dx[:, PROMPT:].reshape(G, NC, CL, D), 2)
-    gn = jnp.concatenate([gp.reshape(NP, D), gc.reshape(NT - NP, D)], axis=0).astype(F32) + dxq
-    x = jnp.concatenate([own_p.reshape(NP, D), own_c.reshape(NT - NP, D)], axis=0).astype(F32)
-    hat, scale = norm_stats(x)
-    gin = (resg + norm_back(gn, ln[0:1], hat, scale)).astype(BF16)
-    gin = trade(gin)
-    blk = trade(blk).astype(F32)
-    outs, sums = [], 0.0
-    for b, e, y, c in (
-        (blk[:NP].reshape(prompt_in.shape), prompt_embed, prompt_earlier, prompt_cot),
-        (blk[NP:].reshape(cont_in.shape), cont_embed, cont_earlier, cont_cot),
+    )(
+        q,
+        att,
+        gatt,
+        lse,
+        nt,
+        own_nt,
+        cos,
+        shi,
+        slo,
+        wq,
+        ln,
+        own_p,
+        own_c,
+        resg,
+        small,
+        k,
+        v,
+        gwo.reshape(split + (HC,)),
+        gwu.reshape(split + (FC,)),
+        gwd.reshape(split + (FC,)),
+    )
+    gin_p, gin_c = trade(gin_p), trade(gin_c)
+    outs = []
+    for b, e, y in (
+        (blk[:NP].reshape(prompt_in.shape), prompt_embed, prompt_earlier),
+        (blk[NP:].reshape(cont_in.shape), cont_embed, cont_earlier),
     ):
-        terms = [e.astype(F32)] + [y[i].astype(F32) for i in range(3)]
-        total = mix_weights[4] * b
-        for i in range(4):
-            total += mix_weights[i] * terms[i]
+        total = mix_weights[0] * e.astype(F32) + mix_weights[4] * b
+        for i in range(3):
+            total += mix_weights[1 + i] * y[i].astype(F32)
         outs.append(total.astype(BF16))
-        c = c.astype(F32)
-        sums += jnp.stack([jnp.sum((c * a).reshape(-1, D), axis=0) for a in terms])
-    small = jnp.concatenate(
-        [small[:3], sums, jnp.sum(gn * hat, axis=0)[None], jnp.sum(gn, axis=0)[None]], axis=0
-    )
-    small = lax.psum(small, ("dp", "ctx", "tp"))
-
-    def reduce(g):
-        g = lax.psum_scatter(g.reshape(TP * D, -1), ("tp", "dp"), scatter_dimension=0, tiled=True)
-        return lax.psum(g, "ctx").astype(F32)
-
-    gm = reduce(jnp.concatenate([gwo, gwu, gwd], axis=2))
-    gq = reduce(gwq)
     start = lax.axis_index("dp") * S
     mine = lax.dynamic_slice_in_dim(small, start, S, axis=1)
     return (
         outs[0],
         outs[1],
-        gin[:NP].reshape(prompt_in.shape),
-        gin[NP:].reshape(cont_in.shape),
+        gin_p,
+        gin_c,
         mine[7],
         mine[8],
         mine[0],
         mine[1],
         gq.reshape(S, 3, HC),
-        gm[:, :HC].T,
-        gm[:, HC : HC + FC],
-        gm[:, HC + FC :].T,
+        go,
+        gu,
+        gd,
         jnp.sum(jnp.concatenate([small[3:7], small[2:3]]), axis=1),
     )
 

time: 527 us -> 381 us (0.72)
  waiting for transfers between devices: 207 us -> 0.02 us
  Pallas kernels: 188 us -> 320 us
  blocking collectives: 42.2 us -> 0 us
  other arithmetic: 30.5 us -> 15.7 us
  between operations: 14.5 us -> 0.85 us
    reduce_scatter x5 -> x0, waiting for transfers between devices: 180 us -> none  [the longest x2 130 us: reduce(): lax.psum_scatter(g.reshape(TP * D, -1), ('tp', 'dp'), scatter_dimension=0...]
    pallas_call x2, Pallas kernels: 160 us -> 293 us  [the longest x1 185 us: per_device(): pl.pallas_call(partial(backward_kernel, dm, T), out_shape=(sds(prompt_in....]
    psum x1 -> x0, blocking collectives: 42.2 us -> none  [per_device(): small = lax.psum(small, ('dp', 'ctx', 'tp'))]
    psum x1 -> x0, waiting for transfers between devices: 25.5 us -> none  [reduce(): return lax.psum(g, 'ctx').astype(F32)]
    concatenate x2 -> x1, other arithmetic: 9.06 us -> 0.69 us  [per_device(): jnp.concatenate([small[:3], sums[0] + sums[1], jnp.zeros((9, D), F32)], a...]
    slice x6 -> x1, local copies, waits for them, and re-layouts: 7.62 us -> 0.59 us  [per_device(): total = mix_weights[0] * e.astype(F32) + mix_weights[4] * b]
    ppermute x6 -> x7, starting transfers between devices: 11.9 us -> 14.6 us  [trade(): return lax.ppermute(x, ('dp', 'tp'), swap)]
    reduce_sum x5 -> x2, other arithmetic: 10.6 us -> 7.9 us  [per_device(): jnp.sum((c * a).reshape(-1, D), axis=0)]
  transfers between devices with their start and end apart: 12 -> 7, of which waited for: 5 -> 0; matrix products, arithmetic and copies ran while one was open for 10% -> 8% of each run, Pallas kernels for 20% -> 28%
where the time goes in v3:
time: 381 us; the launch traced here: 379 us
  Pallas kernels  320 us (84%)
  local copies, waits for them, and re-layouts  28.1 us (7%)
  other arithmetic  15.7 us (4%)
  starting transfers between devices  14.6 us (4%)
    pallas_call x1, Pallas kernels, per_device(): pl.pallas_call(partial(backward_kernel, dm, T), out_shape=(sds(prompt_in....  185 us
    pallas_call x1, Pallas kernels, per_device(): pl.pallas_call(partial(forward_kernel, dm), out_shape=(sds((D, G * R), BF...  107 us
    pallas_call x1, Pallas kernels, per_device(): pl.pallas_call(partial(mlp_kernel, dm, steps), grid=(TP, steps), out_shap...  27.3 us
    ppermute x7, starting transfers between devices, trade(): return lax.ppermute(x, ('dp', 'tp'), swap)  14.6 us
    slice x2, local copies, waits for them, and re-layouts, per_device(): wo, wu, wd = (wm[:, :, :HC], wm[:, :, HC:HC + FC], wm[:, :, HC + FC:])  10.3 us
    unnamed x37, local copies, waits for them, and re-layouts  8.57 us
    reduce_sum x2, other arithmetic, per_device(): jnp.sum((c * a).reshape(-1, D), axis=0)  7.9 us
  transfers between devices with their start and end apart: 7, of which 0 were waited for; matrix products, arithmetic and copies ran while one was open for 8% of the time, Pallas kernels for 28%

profile of v3, /device:TPU:0, one launch (start us, length us, event | category | flops | bytes accessed | tf_op | source)
XLA Modules:
  0.0 379.4 jit_solution(1133650240032684531)
XLA Ops:
  0.6 1.7 collective-permute-start
  2.3 1.6 collective-permute-start.1
  3.9 1.6 collective-permute-start.2
  5.6 4.5 %collective-permute-start.3 = (bf16[2,2,64,768]{3,2,1,0:T(8,128)(2,1)}, bf16[2,2,64,768]{3,2,1,0:T(8,128)(2,1)}, u32[]{:S(2)}, u32[]{:S(2)}) collective-permute-start(bf16[2,2,64,768]{3,2,1,0:T(8,128)(2,1)} %param.33), channel_id=1, source_target_pairs={{0,0},{1,8},{8,1},{9,9},{16,16},{17,24},{24,17},{25,25},{2,2},{3,1... | collective-permute-start | bytes 1179656 | tf_op jit(solution)/shard_map/ppermute | solution.py:1199
  10.1 1.1 copy.48
  11.2 0.0 copy-start.6
  11.2 0.0 copy-start.14
  11.2 0.8 stack.45
  11.9 0.7 stack.46
  12.6 0.7 stack.47
  13.3 0.7 stack.48
  13.9 0.1 copy.43
  14.1 0.8 fusion.22.wq
  14.9 3.4 fusion.21
  18.4 1.2 pad_maximum_fusion.wm
  19.6 0.7 copy-done
  20.3 0.1 copy-done.1
  20.4 107.3 %forward.1 = (bf16[768,2560]{1,0:T(8,128)(2,1)}, bf16[768,512]{1,0:T(8,128)(2,1)}, bf16[2,1280,768]{2,1,0:T(8,128)(2,1)}, bf16[2,1280,768]{2,1,0:T(8,128)(2,1)},...) custom-call(bf16[2,128,768]{2,1,0:T(8,128)(2,1)} %copy-done, ...), custom_call_target="tpu_custom_call" | custom-call | tf_op jit(solution)/shard_map/forward/pallas_call | solution.py:1220
  127.7 7.9 %fusion.28 = (bf16[2,768,1536]{2,1,0:T(8,128)(2,1)}, bf16[2,768,1536]{2,1,0:T(8,128)(2,1)}) fusion(bf16[2,768,3456]{2,1,0:T(8,128)(2,1)} %get-tuple-element.39), kind=kLoop, calls=%fused_computation.59 | loop fusion | bytes 18874368 | tf_op jit(solution)/shard_map/slice | solution.py:1258
  135.6 2.4 slice.82.wo
  138.0 0.7 copy-done.8
  138.8 27.3 %feed.1 = (bf16[512,768]{1,0:T(8,128)(2,1)}, f32[512,768]{1,0:T(8,128)}, bf16[512,768]{1,0:T(8,128)(2,1)}, bf16[2,768,384]{2,1,0:T(8,128)(2,1)}, bf16[2,768,1536...) custom-call(f32[5]{0:T(128)} %mix.1, bf16[512,768]{1,0:T(8,128)(2,1)} %get-tuple-element.37.att, ...), custom_call_target="tpu_custom_call" | custom-call | tf_op jit(solution)/shard_map/feed/pallas_call | solution.py:1264
  166.1 1.8 collective-permute-start.4
  167.9 0.1 pad.9.clone
  168.0 0.6 fusion.30
  168.6 0.7 slice.96
  169.3 0.1 convert_element_type.104
  169.5 0.9 slice_multiply_fusion
  170.4 0.4 copy-done.3
  170.7 0.1 copy-done.10
  170.8 0.1 copy-done.11
  170.9 4.0 %fusion.18 = (f32[768]{0:T(1024)S(1)}, f32[768]{0:T(1024)S(1)}, f32[768]{0:T(1024)S(1)}, f32[768]{0:T(1024)S(1)}, bf16[2,2,64,768]{3,2,1,0:T(8,128)(2,1)}) fusion(bf16[2,2,64,768]{3,2,1,0:T(8,128)(2,1)S(1)} %copy-done.10, bf16[3,2,2,64,768]{4,3,2,1,0:T(8,128)(2,1)S(1)} %copy-done.3, bf16[2,2,64,768]{3,2,1,0:T(8,128)(2,1)S(1)} %copy-done.11, f32[]{:T(128)} %bitcast.9, ...), kind=kLoop, calls=%fused_computation.39 | loop fusion | flops 4322304 | bytes 3158032 | tf_op jit(solution)/shard_map/reduce_sum | solution.py:1319
  175.0 3.9 %fusion.14 = (f32[768]{0:T(1024)S(1)}, f32[768]{0:T(1024)S(1)}, f32[768]{0:T(1024)S(1)}, f32[768]{0:T(1024)S(1)}, bf16[2,128,768]{2,1,0:T(8,128)(2,1)}) fusion(bf16[2,128,768]{2,1,0:T(8,128)(2,1)S(1)} %copy-done.12, bf16[3,2,128,768]{3,2,1,0:T(8,128)(2,1)S(1)} %copy-done.4, bf16[2,128,768]{2,1,0:T(8,128)(2,1)S(1)} %copy-done.13, f32[]{:T(128)} %bitcast.9, ...), kind=kLoop, calls=%fused_computation.35 | loop fusion | flops 4322304 | bytes 3158032 | tf_op jit(solution)/shard_map/reduce_sum | solution.py:1319
  178.9 0.7 maximum_maximum_fusion.small
  179.6 185.4 %backward.1 = (bf16[2,128,768]{2,1,0:T(8,128)(2,1)}, bf16[2,2,64,768]{3,2,1,0:T(8,128)(2,1)}, f32[192,1152]{1,0:T(8,128)}, f32[384,192]{1,0:T(8,128)}, f32[192,1...) custom-call(bf16[512,768]{1,0:T(8,128)(2,1)} %get-tuple-element.41.q, bf16[512,768]{1,0:T(8,128)(2,1)} %get-tuple-element.37.att, ...), custom_call_target="tpu_custom_call" | custom-call | tf_op jit(solution)/shard_map/backward/pallas_call | solution.py:1326
  365.1 1.8 collective-permute-start.5
  366.9 1.6 collective-permute-start.6
  368.5 0.7 slice.101
  369.2 0.7 slice.102
  370.0 2.9 copy.46
  372.9 1.0 copy.50
  373.8 0.1 copy-done.9
  373.9 0.9 copy.45
  374.8 0.6 maximum_reduce_fusion
  375.4 1.5 fusion.29
  376.9 0.7 copy.54
  377.7 0.7 copy.55
  378.4 1.0 copy.56
  (44 shorter events, 0.2 us)
Async XLA Ops:
  0.6 18.9 %collective-permute-start = (bf16[2,128,768]{2,1,0:T(8,128)(2,1)}, bf16[2,128,768]{2,1,0:T(8,128)(2,1)S(1)}, u32[]{:S(2)}, u32[]{:S(2)}) collective-permute-start(bf16[2,128,768]{2,1,0:T(8,128)(2,1)} %param.17), channel_id=1, source_target_pairs={{0,0},{1,8},{8,1},{9,9},{16,16},{17,24},{24,17},{25,25},{2,2},{3,1... | collective-permute-start | bytes 1179656 | tf_op jit(solution)/shard_map/ppermute | solution.py:1199
  2.3 17.3 %collective-permute-start.1 = (bf16[2,2,64,768]{3,2,1,0:T(8,128)(2,1)}, bf16[2,2,64,768]{3,2,1,0:T(8,128)(2,1)S(1)}, u32[]{:S(2)}, u32[]{:S(2)}) collective-permute-start(bf16[2,2,64,768]{3,2,1,0:T(8,128)(2,1)} %param.18), channel_id=1, source_target_pairs={{0,0},{1,8},{8,1},{9,9},{16,16},{17,24},{24,17},{25,25},{2,2},{3,1... | collective-permute-start | bytes 1179656 | tf_op jit(solution)/shard_map/ppermute | solution.py:1199
  3.9 134.1 %collective-permute-start.2 = (bf16[2,128,768]{2,1,0:T(8,128)(2,1)}, bf16[2,128,768]{2,1,0:T(8,128)(2,1)S(1)}, u32[]{:S(2)}, u32[]{:S(2)}) collective-permute-start(bf16[2,128,768]{2,1,0:T(8,128)(2,1)} %param.32), channel_id=1, source_target_pairs={{0,0},{1,8},{8,1},{9,9},{16,16},{17,24},{24,17},{25,25},{2,2},{3,1... | collective-permute-start | bytes 1179656 | tf_op jit(solution)/shard_map/ppermute | solution.py:1199
  5.6 132.4 %collective-permute-start.3 = (bf16[2,2,64,768]{3,2,1,0:T(8,128)(2,1)}, bf16[2,2,64,768]{3,2,1,0:T(8,128)(2,1)}, u32[]{:S(2)}, u32[]{:S(2)}) collective-permute-start(bf16[2,2,64,768]{3,2,1,0:T(8,128)(2,1)} %param.33), channel_id=1, source_target_pairs={{0,0},{1,8},{8,1},{9,9},{16,16},{17,24},{24,17},{25,25},{2,2},{3,1... | collective-permute-start | bytes 1179656 | tf_op jit(solution)/shard_map/ppermute | solution.py:1199
  11.2 7.2 %copy-start.6 = (bf16[1536,192]{0,1:T(8,128)(2,1)S(1)}, bf16[1536,192]{0,1:T(8,128)(2,1)}, u32[]{:S(2)}) copy-start(bf16[1536,192]{0,1:T(8,128)(2,1)} %param.30) | copy-start | bytes 1769476
  11.2 7.2 %copy-start.7 = (bf16[192,1536]{1,0:T(8,128)(2,1)S(1)}, bf16[192,1536]{1,0:T(8,128)(2,1)}, u32[]{:S(2)}) copy-start(bf16[192,1536]{1,0:T(8,128)(2,1)} %param.29) | copy-start | bytes 1769476
  11.2 7.2 %copy-start.14 = (bf16[384,192]{0,1:T(8,128)(2,1)S(1)}, bf16[384,192]{0,1:T(8,128)(2,1)}, u32[]{:S(2)}) copy-start(bf16[384,192]{0,1:T(8,128)(2,1)} %param.28) | copy-start | bytes 442372
  19.5 0.7 copy-start
  19.6 0.9 copy-start.1
  138.0 0.7 copy-start.8
  138.8 29.2 %copy-start.15 = (f32[5]{0:T(128)S(1)}, f32[5]{0:T(128)}, u32[]{:S(2)}) copy-start(f32[5]{0:T(128)} %mix.1) | copy-start | bytes 64
  166.1 3.2 collective-permute-start.4
  169.4 1.3 copy-start.3
  169.4 1.4 copy-start.10
  169.5 1.5 copy-start.11
  170.9 4.1 %copy-start.4 = (bf16[3,2,128,768]{3,2,1,0:T(8,128)(2,1)S(1)}, bf16[3,2,128,768]{3,2,1,0:T(8,128)(2,1)}, u32[]{:S(2)}) copy-start(bf16[3,2,128,768]{3,2,1,0:T(8,128)(2,1)} %param.21) | copy-start | bytes 3538948
  170.9 4.1 %copy-start.12 = (bf16[2,128,768]{2,1,0:T(8,128)(2,1)S(1)}, bf16[2,128,768]{2,1,0:T(8,128)(2,1)}, u32[]{:S(2)}) copy-start(bf16[2,128,768]{2,1,0:T(8,128)(2,1)} %param.32) | copy-start | bytes 1179652
  170.9 4.1 %copy-start.13 = (bf16[2,128,768]{2,1,0:T(8,128)(2,1)S(1)}, bf16[2,128,768]{2,1,0:T(8,128)(2,1)}, u32[]{:S(2)}) copy-start(bf16[2,128,768]{2,1,0:T(8,128)(2,1)} %param.19) | copy-start | bytes 1179652
  365.1 7.8 %copy-start.5 = (f32[192,1152]{1,0:T(8,128)S(1)}, f32[192,1152]{1,0:T(8,128)}, u32[]{:S(2)}) copy-start(f32[192,1152]{1,0:T(8,128)} %get-tuple-element.57) | copy-start | bytes 2654212
  365.1 11.8 %collective-permute-start.5 = (bf16[2,128,768]{2,1,0:T(8,128)(2,1)}, bf16[2,128,768]{2,1,0:T(8,128)(2,1)S(1)}, u32[]{:S(2)}, u32[]{:S(2)}) collective-permute-start(bf16[2,128,768]{2,1,0:T(8,128)(2,1)} %get-tuple-element.54), channel_id=1, source_target_pairs={{0,0},{1,8},{8,1},{9,9},{16,16},{17,24},{24,17},{25,25},{2,2},{3,1... | collective-permute-start | bytes 1179656 | tf_op jit(solution)/shard_map/ppermute | solution.py:1199
  366.9 10.1 %collective-permute-start.6 = (bf16[2,2,64,768]{3,2,1,0:T(8,128)(2,1)}, bf16[2,2,64,768]{3,2,1,0:T(8,128)(2,1)S(1)}, u32[]{:S(2)}, u32[]{:S(2)}) collective-permute-start(bf16[2,2,64,768]{3,2,1,0:T(8,128)(2,1)} %get-tuple-element.55), channel_id=1, source_target_pairs={{0,0},{1,8},{8,1},{9,9},{16,16},{17,24},{24,17},{25,25},{2,2},{3,1... | collective-permute-start | bytes 1179656 | tf_op jit(solution)/shard_map/ppermute | solution.py:1199
  372.8 1.1 copy-start.9
  373.8 4.6 %copy-start.2 = (f32[192,1536]{1,0:T(8,128)S(1)}, f32[192,1536]{1,0:T(8,128)}, u32[]{:S(2)}) copy-start(f32[192,1536]{1,0:T(8,128)} %get-tuple-element.149) | copy-start | bytes 3538948

commit v4 on v3

--- a/solution.py
+++ b/solution.py
@@ -14,7 +14,7 @@
 NEG = -1e30
 F32 = jnp.float32
 BF16 = jnp.bfloat16
-VMEM_LIMIT = 62 * 1024 * 1024
+VMEM_LIMIT = 67043328
 
 
 def dot(a, b):
@@ -42,12 +42,17 @@
     )
 
 
-def rotate(x, cos, sin_hi, sin_lo):
-    return x * cos + pltpu.roll(x, 32, 1) * sin_hi + pltpu.roll(x, 96, 1) * sin_lo
-
-
-def rotate_back(x, cos, sin_hi, sin_lo):
-    return x * cos - pltpu.roll(x, 32, 1) * sin_hi - pltpu.roll(x, 96, 1) * sin_lo
+def swap_halves(x):
+    second = lax.broadcasted_iota(jnp.int32, x.shape, 1) % HD >= HD // 2
+    return jnp.where(second, pltpu.roll(x, 32, 1), pltpu.roll(x, 96, 1))
+
+
+def rotate(x, cos, sin):
+    return x * cos + swap_halves(x) * sin
+
+
+def rotate_back(x, cos, sin):
+    return x * cos - swap_halves(x) * sin
 
 
 def lane_pick(shape, low):
@@ -130,14 +135,28 @@
     def plane(self, k):
         return self.at(ctx=self.ctx_after(k))
 
-    def greet(self):
+    def partner(self):
+        return self.at(dp=self.chip * 2 + self.tp, tp=self.core)
+
+    def greet(self, trades=False):
         barrier = pltpu.get_barrier_semaphore()
         peers = [self.across(), self.mate()]
         peers += [self.row(k) for k in range(1, self.chips)]
         peers += [self.plane(k) for k in range(1, self.ctxs)]
         for peer in peers:
             pl.semaphore_signal(barrier, inc=1, device_id=peer, device_id_type=MESH)
-        pl.semaphore_wait(barrier, len(peers))
+        count = len(peers)
+        if trades:
+            away = self.core != self.tp
+
+            @pl.when(away)
+            def _():
+                pl.semaphore_signal(
+                    barrier, inc=1, device_id=self.partner(), device_id_type=MESH
+                )
+
+            count += jnp.where(away, 1, 0)
+        pl.semaphore_wait(barrier, count)
 
 
 def send(src, dst, send_sem, recv_sem, device):
@@ -270,8 +289,7 @@
     op,
     oc,
     cos,
-    shi,
-    slo,
+    sin,
     wq,
     wm,
     nt_out,
@@ -348,12 +366,11 @@
         n = normed(x)
         own_rows[pl.ds(row, rows), :] = n
         c = cos[pl.ds(table, rows), :]
-        hi = shi[pl.ds(table, rows), :]
-        lo = slo[pl.ds(table, rows), :]
+        sn = sin[pl.ds(table, rows), :]
         for t in range(TP):
             qq = dot(n, w[t, :, :HC])
             for j in range(HC // 128):
-                tile = rotate(qq[:, j * 128 : (j + 1) * 128], c, hi, lo).astype(BF16)
+                tile = rotate(qq[:, j * 128 : (j + 1) * 128], c, sn).astype(BF16)
                 q_out[pl.ds(row, rows), t * HC + j * 128 : t * HC + (j + 1) * 128] = (
                     tile.astype(F32) * 0.125
                 ).astype(BF16)
@@ -381,12 +398,11 @@
         n = normed(x)
         all_rows[pl.ds(place, rows), :] = n
         c = cos[pl.ds(table, rows), :]
-        hi = shi[pl.ds(table, rows), :]
-        lo = slo[pl.ds(table, rows), :]
+        sn = sin[pl.ds(table, rows), :]
         for t in range(TP):
             kk = dot(n, w[t, :, HC : 2 * HC])
             for j in range(HC // 128):
-                tile = rotate(kk[:, j * 128 : (j + 1) * 128], c, hi, lo)
+                tile = rotate(kk[:, j * 128 : (j + 1) * 128], c, sn)
                 k_out[g, pl.ds(row, rows), t * HC + j * 128 : t * HC + (j + 1) * 128] = tile.astype(BF16)
             v_out[g, pl.ds(row, rows), t * HC : (t + 1) * HC] = dot(n, w[t, :, 2 * HC : 3 * HC]).astype(BF16)
 
@@ -482,121 +498,31 @@
     put.wait()
 
 
-def mlp_kernel(
-    dm,
-    steps,
-    mix,
-    att,
-    op,
-    oc,
-    tp_,
-    tc,
-    ln,
-    wo,
-    wu,
-    wd,
-    blk_out,
-    resg,
-    gatt,
-    gwo,
-    gwu,
-    gwd,
-    small,
-    resid,
-    hat,
-    scale,
-    hn,
-    hnt,
-    gd,
-    gdt,
-    blk,
-    gh,
-):
-    D, NP, NT, G, PB = dm.D, dm.NP, dm.NT, dm.G, dm.PB
-    TP, HC = wo.shape[0], wo.shape[2]
-    t, j = pl.program_id(0), pl.program_id(1)
-    gain, bias = ln[2:3, :], ln[3:4, :]
-
-    def own(prompt, cont):
-        return jnp.concatenate([prompt.reshape(NP, D), cont.reshape(NT - NP, D)], axis=0)
-
-    @pl.when((t == 0) & (j == 0))
-    def _():
-        branch = dot_nt(att[:, :HC], wo[0])
-        for s in range(1, TP):
-            branch += dot_nt(att[:, s * HC : (s + 1) * HC], wo[s])
-        r = own(op[...], oc[...]).astype(F32) + branch
-        resid[...] = r
-        h, sc = norm_stats(r)
-        hat[...] = h
-        scale[...] = jnp.broadcast_to(sc, scale.shape)
-        n = (h * gain + bias).astype(BF16)
-        hn[...] = n
-        hnt[...] = transpose(n)
-        g = (mix[4] * own(tp_[...], tc[...]).astype(F32)).astype(BF16)
-        gd[...] = g
-        gdt[...] = transpose(g)
-        blk[...] = r
-        gh[...] = jnp.zeros_like(gh)
-
-    up, dn = wu[0], wd[0]
-    u = dot(hn[...], up)
-    c0 = 0.7978845608028654
-    u2 = u * u
-    th = jnp.tanh(c0 * u * (1.0 + 0.044715 * u2))
-    half = 0.5 * (1.0 + th)
-    act = (u * half).astype(BF16)
-    slope = half + 0.5 * u * (1.0 - th * th) * (c0 * (1.0 + 3 * 0.044715 * u2))
-    blk[...] += dot_nt(act, dn)
-    gwd[0] = dot(gdt[...], act).astype(BF16)
-    gu = (dot(gd[...], dn) * slope).astype(BF16)
-    gwu[0] = dot(hnt[...], gu).astype(BF16)
-    gh[...] += dot_nt(gu, up)
-
-    @pl.when((t == TP - 1) & (j == steps - 1))
-    def _():
-        cot = own(tp_[...], tc[...]).astype(F32)
-        block = blk[...]
-        blk_out[...] = block.astype(BF16)
-        small[2:3, :] = jnp.sum(cot * block, axis=0, keepdims=True)
-        small[3:, :] = jnp.zeros((5, D), F32)
-        g = gh[...]
-        h = hat[...]
-        small[0:1, :] = jnp.sum(g * h, axis=0, keepdims=True)
-        small[1:2, :] = jnp.sum(g, axis=0, keepdims=True)
-        gr = mix[4] * cot + norm_back(g, gain, h, scale[:, 0:1])
-        resg[...] = gr
-        gb = gr.astype(BF16)
-        gbt = transpose(gb)
-        for s in range(TP):
-            gatt[:, s * HC : (s + 1) * HC] = dot(gb, wo[s]).astype(BF16)
-            gwo[s] = dot(gbt, att[:, s * HC : (s + 1) * HC]).astype(BF16)
-
-
 class Reduce:
-    def __init__(self, p, n, refs):
-        self.p, self.n = p, n
+    REFS = 13
+
+    def __init__(self, p, cross_first, refs):
+        self.p, self.n, self.cross_first = p, len(cross_first), cross_first
         self.mine, self.got, self.row, self.acr, self.zin = refs[:5]
         self.sc, self.rc, self.sy, self.ry, self.sx, self.rx, self.sz, self.rz = refs[5:13]
-        self.mid = p.ctxs // 2
-        self.left = p.ctx < self.mid
-        self.centre = (p.ctx == self.mid - 1) | (p.ctx == self.mid)
+        mid = p.ctxs // 2
+        self.centre = (p.ctx == mid - 1) | (p.ctx == mid)
         self.outer = (p.ctx > 0) & (p.ctx < p.ctxs - 1)
-        step = jnp.where(self.left, 1, -1)
+        step = jnp.where(p.ctx < mid, 1, -1)
         self.inner_at = p.ctx + step
         self.outer_at = jnp.clip(p.ctx - step, 0, p.ctxs - 1)
 
-    REFS = 13
-
     @staticmethod
-    def scratch(n, chips, size, width, slots=2):
+    def scratch(cross_first, chips, size, width):
+        n = len(cross_first)
         dma = pltpu.SemaphoreType.DMA
         far = max(chips - 1, 1)
+        rows = n + sum(1 for c in cross_first if not c)
         return [
-            pltpu.VMEM((slots, chips, 2, size, width), BF16),
+            pltpu.VMEM((2, chips, 2, size, width), BF16),
             pltpu.VMEM((2 * n, chips, size, width), BF16),
-            pltpu.VMEM((2 * n, far, size, width), BF16),
-            pltpu.VMEM((n, size, width), BF16),
+            pltpu.VMEM((rows, far, size, width), BF16),
+            pltpu.VMEM((n, chips, size, width), BF16),
             pltpu.VMEM((n, 2, size, width), BF16),
             dma((2 * n,)),
             dma((2 * n,)),
@@ -618,17 +544,26 @@
             device_id_type=MESH,
         )
 
+    def crosses(self, i):
+        return self.cross_first[i % self.n]
+
+    def travels(self, i):
+        return i >= self.n or not self.crosses(i)
+
     def by_core(self, i, slot):
         p = self.p
         return self.copy(
             self.mine.at[slot, :, 1 - p.core], self.got.at[i], self.sc.at[i], self.rc.at[i], p.mate()
         )
 
+    def row_slot(self, i):
+        return sum(1 for e in range(i) if self.travels(e))
+
     def by_row(self, i, k):
         p = self.p
         return self.copy(
             self.got.at[i, p.chip_after(k)],
-            self.row.at[i, k - 1],
+            self.row.at[self.row_slot(i), k - 1],
             self.sy.at[i, k - 1],
             self.ry.at[i, k - 1],
             p.row(k),
@@ -636,8 +571,9 @@
 
     def by_tp(self, j):
         p = self.p
+        part = slice(None) if self.crosses(j) else p.chip
         return self.copy(
-            self.got.at[j, p.chip], self.acr.at[j], self.sx.at[j], self.rx.at[j], p.across()
+            self.got.at[j, part], self.acr.at[j, part], self.sx.at[j], self.rx.at[j], p.across()
         )
 
     def inward(self, j):
@@ -668,25 +604,38 @@
     def cores_sent(self, i, slot):
         self.by_core(i, slot).wait_send()
 
+    def rows_send(self, i):
+        for k in range(1, self.p.chips):
+            self.by_row(i, k).start()
+
     def cores_sum(self, i, slot):
         p = self.p
         self.by_core(i, slot).wait_recv()
         for y in range(p.chips):
             self.add(i, y, self.mine[slot, y, p.core])
-        for k in range(1, p.chips):
-            self.by_row(i, k).start()
+        if not self.crosses(i):
+            self.rows_send(i)
+        elif i < self.n:
+            self.by_tp(i).start()
+
+    def cross_sum(self, j):
+        self.by_tp(j).wait_recv()
+        for y in range(self.p.chips):
+            self.add(self.n + j, y, self.acr[j, y])
+        self.rows_send(self.n + j)
 
     def rows_sum(self, i):
         p = self.p
         for k in range(1, p.chips):
             self.by_row(i, k).wait_recv()
-            self.add(i, p.chip, self.row[i, k - 1])
+            self.add(i, p.chip, self.row[self.row_slot(i), k - 1])
         if i < self.n:
             self.by_tp(i).start()
-
-    def tp_sum(self, j):
-        self.by_tp(j).wait_recv()
-        self.add(self.n + j, self.p.chip, self.acr[j])
+            return
+        j = i - self.n
+        if not self.crosses(i):
+            self.by_tp(j).wait_recv()
+            self.add(i, p.chip, self.acr[j, p.chip])
 
         @pl.when(jnp.logical_not(self.outer))
         def _():
@@ -715,13 +664,16 @@
         @pl.when(self.outer)
         def _():
             self.outward(j).start()
-        return self.got[self.n + j, p.chip]
+
+    def result(self, j):
+        return self.got[self.n + j, self.p.chip].astype(F32)
 
     def drain(self):
         p = self.p
         for i in range(2 * self.n):
-            for k in range(1, p.chips):
-                self.by_row(i, k).wait_send()
+            if self.travels(i):
+                for k in range(1, p.chips):
+                    self.by_row(i, k).wait_send()
         for j in range(self.n):
             self.by_tp(j).wait_send()
 
@@ -762,29 +714,72 @@
     return total
 
 
+def schedule(ra, rb, on, n_a, NB, PT, TP, G):
+    def at_pair(pair_rel):
+        return pair_rel + 1 if pair_rel < PT else NB + 1 + pair_rel - PT
+
+    last = 2 * n_a - 1
+    late = ("a", 0)
+    plan = ra.cross_first
+    for j in range(n_a):
+        if not plan[j]:
+            on(("m", last) if j < n_a - 1 else ("a", 1), partial(ra.rows_sum, j))
+    for j in range(n_a):
+        if plan[j]:
+            on(("m", last), partial(ra.cross_sum, j))
+    own_at = {0: 6, 1: 3, 2: 8}
+    for j in range(n_a):
+        on(("a", own_at.get(j, 8)), partial(ra.rows_sum, n_a + j))
+        on(("a", min(own_at.get(j, 8) + 3, 11)), partial(ra.ctx_in, j))
+    on(late, partial(rb.cores_sum, 0, 0))
+    on(late, partial(rb.cores_sum, NB, 1))
+    on(("a", 2), partial(rb.cross_sum, 0))
+    on(("a", 5), partial(rb.rows_sum, NB))
+    on(("a", 8), partial(rb.ctx_in, 0))
+    for pr in range(TP * PT - 1):
+        on(("a", G * pr + G), partial(rb.cores_sum, at_pair(pr), pr % 2))
+        if pr >= PT:
+            on(("a", G * pr + G), partial(rb.cross_sum, pr - PT + 1))
+    for j in range(1, NB - 1):
+        on(("p", j), partial(rb.rows_sum, NB + j))
+    for j in range(n_a):
+        on(("p", j), partial(ra.ctx_out, j))
+    on(("t", 0), partial(rb.rows_sum, 2 * NB - 1))
+    for j in range(1, NB):
+        on(("t", 10 + j), partial(rb.ctx_in, j))
+
+
 def backward_kernel(
     dm,
     T,
-    q,
+    FC,
+    plan_a,
+    plan_b,
+    mix,
     att,
-    gatt,
-    lse,
-    nt,
-    own_nt,
-    cos,
-    shi,
-    slo,
-    w,
-    ln,
     own_p,
     own_c,
-    resg,
-    small,
+    cot_p,
+    cot_c,
+    ln,
+    q,
+    lse,
+    cos,
+    sin,
+    wm,
     k_hbm,
     v_hbm,
-    gwo,
-    gwu,
-    gwd,
+    nt_hbm,
+    own_nt_hbm,
+    wq_hbm,
+    home_arrays_p,
+    home_arrays_c,
+    early_p,
+    early_c,
+    home_cot_p,
+    home_cot_c,
+    out_p,
+    out_c,
     gin_p,
     gin_c,
     gq_out,
@@ -792,6 +787,14 @@
     gu_out,
     gd_out,
     small_out,
+    resid,
+    blk,
+    gh,
+    wo,
+    ring,
+    gatt,
+    nt,
+    own_nt,
     maskp,
     maskx,
     kbuf,
@@ -799,14 +802,22 @@
     dk,
     dv,
     dq,
-    dxq,
     dxm,
     dxz,
-    dxc,
-    dxcm,
+    blk_away,
+    blk_home,
+    gin_home,
+    put_sem,
+    ring_sem,
+    wo_sem,
     kv_sem,
-    load_a,
-    load_b,
+    nt_sem,
+    wq_sem,
+    home_sem,
+    b_send,
+    b_recv,
+    g_send,
+    g_recv,
     m_send,
     m_recv,
     z_send,
@@ -825,27 +836,18 @@
     sm_rz,
     *refs,
 ):
-    G, R, PB, NCH, D, NX = dm.G, dm.R, dm.PB, dm.NCH, dm.D, dm.NX
-    TP, HC = w.shape[0], (w.shape[2] - 128) // 3
+    G, R, PB, NCH, D, NX, NP, NT = dm.G, dm.R, dm.PB, dm.NCH, dm.D, dm.NX, dm.NP, dm.NT
+    TP, HC = wo.shape[0], wo.shape[2]
     PT = dm.PAIRS // TP
     p = Peers()
-    n_a = gwu.shape[-1] // T
-    ra = Reduce(p, n_a, refs[: Reduce.REFS])
-    rb = Reduce(p, 1 + PT, refs[Reduce.REFS :])
+    n_a, NB = len(plan_a), len(plan_b)
+    ra = Reduce(p, plan_a, refs[: Reduce.REFS])
+    rb = Reduce(p, plan_b, refs[Reduce.REFS :])
     block = block_index()
     TILE = 256
     tiles = dm.P // TILE
     chips = p.chips
-
-    def tp_of(i, n):
-        return 1 - p.tp if i < n else p.tp
-
-    def load_slab(i):
-        t, cols, slot = tp_of(i, n_a), slice((i % n_a) * T, (i % n_a + 1) * T), i % 2
-        return [
-            pltpu.make_async_copy(gwu.at[t, :, :, :, cols], ra.mine.at[slot, :, :, :, :T], load_a.at[0, slot]),
-            pltpu.make_async_copy(gwd.at[t, :, :, :, cols], ra.mine.at[slot, :, :, :, T:], load_a.at[1, slot]),
-        ]
+    S = D // (2 * chips)
 
     def begin(copies):
         for copy in copies:
@@ -854,6 +856,18 @@
     def ready(copies):
         for copy in copies:
             copy.wait()
+
+    def load_tile(i, slot):
+        t = jnp.where(i < n_a, 1 - p.tp, p.tp)
+        first = pl.multiple_of(HC + lax.rem(i, n_a) * T, 128)
+        return [
+            pltpu.make_async_copy(
+                wm.at[t, :, pl.ds(first, T)], ring.at[slot, :, pl.ds(0, T)], ring_sem.at[0, slot]
+            ),
+            pltpu.make_async_copy(
+                wm.at[t, :, pl.ds(first + FC, T)], ring.at[slot, :, pl.ds(T, T)], ring_sem.at[1, slot]
+            ),
+        ]
 
     def load_kv(it, slot):
         pair_rel, g = it // G, it % G
@@ -864,61 +878,159 @@
             pltpu.make_async_copy(v_hbm.at[g, :, lanes], vbuf.at[slot], kv_sem.at[1, slot]),
         ]
 
+    wo_load = pltpu.make_async_copy(wm.at[:, :, pl.ds(0, HC)], wo, wo_sem)
+    wo_load.start()
+    begin(load_tile(0, 0))
     begin(load_kv(0, 0))
-    begin(load_slab(0))
-    begin(load_slab(1))
-    wo_load = [
-        pltpu.make_async_copy(gwo.at[tp_of(i, 1)], rb.mine.at[i], load_b.at[i]) for i in range(2)
+    p.greet(trades=True)
+    fill_masks(dm, maskp, maskx)
+    gain_two, bias_two = ln[2:3, :], ln[3:4, :]
+
+    hn, gd = slice(0, NT), slice(NT, 2 * NT)
+    STEP = 128
+
+    def by_rows(step):
+        def prompt_part(i, carry):
+            rows = pl.ds(pl.multiple_of(i * STEP, STEP), STEP)
+            step(own_p[rows, :], cot_p[rows, :], i * STEP)
+            return carry
+
+        def cont_part(i, carry):
+            rows = pl.ds(pl.multiple_of(i * STEP, STEP), STEP)
+            step(own_c[rows, :], cot_c[rows, :], NP + i * STEP)
+            return carry
+
+        lax.fori_loop(0, NP // STEP, prompt_part, 0)
+        lax.fori_loop(0, (NT - NP) // STEP, cont_part, 0)
+
+    def shifted(first, row):
+        return pl.ds(pl.multiple_of(first + row, STEP), STEP)
+
+    wo_load.wait()
+
+    def enter(x, cot, row):
+        rows = shifted(0, row)
+        r = x.astype(F32)
+        for t in range(TP):
+            r += dot_nt(att[rows, t * HC : (t + 1) * HC], wo[t])
+        resid[rows, :] = r
+        blk[rows, :] = r
+        h, _ = norm_stats(r)
+        n = (h * gain_two + bias_two).astype(BF16)
+        dk[rows, :] = n
+        nt[:, rows] = transpose(n)
+        g = (mix[4] * cot.astype(F32)).astype(BF16)
+        dk[shifted(NT, row), :] = g
+        nt[:, shifted(NT, row)] = transpose(g)
+        gh[rows, :] = jnp.zeros((STEP, D), F32)
+
+    by_rows(enter)
+
+    during = {}
+
+    def on(stage, step):
+        during.setdefault(stage, []).append(step)
+
+    def run_when(index, name):
+        for (kind, when), steps in during.items():
+            if kind == name:
+
+                @pl.when(index == when)
+                def _():
+                    for step in steps:
+                        step()
+
+    for i in range(1, 2 * n_a):
+        on(("m", i), partial(ra.cores_sum, i - 1, (i - 1) % 2))
+    schedule(ra, rb, on, n_a, NB, PT, TP, G)
+
+    def feed(i, carry):
+        slot = lax.rem(i, 2)
+
+        @pl.when(i + 1 < 2 * n_a)
+        def _():
+            begin(load_tile(i + 1, 1 - slot))
+
+        ready(load_tile(i, slot))
+        up, dn = ring[slot, :, :T], ring[slot, :, T : 2 * T]
+        c0 = 0.7978845608028654
+        HALF = NT // 2
+        for e in range(2):
+            rows = slice(e * HALF, (e + 1) * HALF)
+            u = dot(dk[rows, :], up)
+            if e == 0:
+                run_when(i, "m")
+            u2 = u * u
+            th = jnp.tanh(c0 * u * (1.0 + 0.044715 * u2))
+            half = 0.5 * (1.0 + th)
+            act = (u * half).astype(BF16)
+            slope = half + 0.5 * u * (1.0 - th * th) * (c0 * (1.0 + 3 * 0.044715 * u2))
+            dv[rows, :T] = act
+            blk[rows, :] += dot_nt(act, dn)
+            gu = (dot(dk[NT + e * HALF : NT + (e + 1) * HALF, :], dn) * slope).astype(BF16)
+            dv[NT + e * HALF : NT + (e + 1) * HALF, :T] = gu
+            gh[rows, :] += dot_nt(gu, up)
+
+        @pl.when(i >= 2)
+        def _():
+            ra.cores_sent(i - 2, slot)
+
+        for y in range(chips):
+            mine = slice(y * 2 * S, (y + 1) * 2 * S)
+            ra.mine[slot, y, :, :, :T] = dot(nt[mine, hn], dv[gd, :T]).astype(BF16).reshape(2, S, T)
+            ra.mine[slot, y, :, :, T:] = dot(nt[mine, gd], dv[hn, :T]).astype(BF16).reshape(2, S, T)
+        ra.cores_send(i, slot)
+        return carry
+
+    lax.fori_loop(0, 2 * n_a, feed, 0)
+    blk_away[:NT, :] = blk[...].astype(BF16)
+    away = ra.copy(blk_away.at[pl.ds(0, NT), :], blk_home, b_send, b_recv, p.partner())
+
+    @pl.when(p.core != p.tp)
+    def _():
+        away.start()
+
+    @pl.when(p.core == p.tp)
+    def _():
+        blk_home[...] = blk_away[:NT, :]
+
+    sm[...] = jnp.zeros_like(sm)
+
+    def leave(x, cot, row):
+        rows = shifted(0, row)
+        cot = cot.astype(F32)
+        sm[2:3, :] += jnp.sum(cot * blk[rows, :], axis=0, keepdims=True)
+        h, scale = norm_stats(resid[rows, :])
+        g = gh[rows, :]
+        sm[0:1, :] += jnp.sum(g * h, axis=0, keepdims=True)
+        sm[1:2, :] += jnp.sum(g, axis=0, keepdims=True)
+        gr = mix[4] * cot + norm_back(g, gain_two, h, scale)
+        resid[rows, :] = gr
+        gb = gr.astype(BF16)
+        nt[:, shifted(NT, row)] = transpose(gb)
+        for t in range(TP):
+            gatt[rows, t * HC : (t + 1) * HC] = dot(gb, wo[t]).astype(BF16)
+
+    by_rows(leave)
+    for slot, i in enumerate((0, NB)):
+        t = p.tp if slot else 1 - p.tp
+        lanes = pl.ds(pl.multiple_of(t * HC, 128), HC)
+        for y in range(chips):
+            mine = slice(y * 2 * S, (y + 1) * 2 * S)
+            rb.mine[slot, y] = dot(nt[mine, gd], att[:, lanes]).astype(BF16).reshape(2, S, HC)
+        rb.cores_send(i, slot)
+    nt_load = [
+        pltpu.make_async_copy(nt_hbm, nt, nt_sem.at[0]),
+        pltpu.make_async_copy(own_nt_hbm, own_nt, nt_sem.at[1]),
     ]
-    begin(wo_load)
-    p.greet()
-    fill_masks(dm, maskp, maskx)
-    for i in range(2):
-        ready(load_slab(i))
-        ra.cores_send(i, i)
-    ready(wo_load)
-    NB = 1 + PT
-    rb.cores_send(0, 0)
-    rb.cores_send(NB, 1)
-    ra.cores_sum(0, 0)
-
-    def next_slab(i):
-        def run():
-            ra.cores_sent(i - 2, i % 2)
-            begin(load_slab(i))
-
-        return run
-
-    def send_slab(i):
-        def run():
-            ready(load_slab(i))
-            ra.cores_send(i, i % 2)
-
-        return run
-
-    events = {}
-
-    def on(it, step):
-        events.setdefault(it, []).append(step)
-
-    for i in range(1, 2 * n_a):
-        on(i, partial(ra.cores_sum, i, i % 2))
-        if i + 1 < 2 * n_a:
-            on(i - 1, next_slab(i + 1))
-            on(i, send_slab(i + 1))
-    on(2 * n_a, partial(rb.cores_sum, 0, 0))
-    on(2 * n_a, partial(rb.cores_sum, NB, 1))
+    begin(nt_load)
+    wq_load = pltpu.make_async_copy(wq_hbm.at[:, :, pl.ds(0, 3 * HC)], ring.at[:, :, pl.ds(0, 3 * HC)], wq_sem)
+    wq_load.start()
+    ra.cores_sum(2 * n_a - 1, 1)
+    during.setdefault(("a", 1), []).insert(0, partial(ready, nt_load))
 
     def wslab(pair_rel):
         return pair_rel + 1 if pair_rel < PT else NB + 1 + pair_rel - PT
-
-    late = []
-    wslot = lambda pair_rel: 2 + pair_rel % 2
-    for pr in range(TP * PT - 1):
-        on(pr * G + 2 * G - 1, partial(rb.cores_sum, wslab(pr), wslot(pr)))
-    on(5, partial(ra.rows_sum, 0))
-    on(8, partial(ra.rows_sum, 1))
-    on(11, partial(ra.rows_sum, 2))
 
     def attend(it, carry):
         pair_rel, g = it // G, it % G
@@ -930,6 +1042,7 @@
         def _():
             begin(load_kv(it + 1, 1 - slot))
 
+        run_when(it, "a")
         lanes = pl.ds(pl.multiple_of(pair * 128, 128), 128)
         rp = pl.ds(pl.multiple_of(g * PB, PB), PB)
         rc = pl.ds(pl.multiple_of(dm.NP + g * NCH, NCH), NCH)
@@ -969,7 +1082,7 @@
             s = dot(kt, qt)
             s = jnp.concatenate([s[:, : 2 * PB] + maskp[rows, :], s[:, 2 * PB :]], axis=1)
             gk, gv, gq = grads(s, kt, vbuf[slot, rows, :], 0)
-            gk = rotate_back(gk, cos[rows, :], shi[rows, :], slo[rows, :]).astype(BF16)
+            gk = rotate_back(gk, cos[rows, :], sin[rows, :]).astype(BF16)
             gv = gv.astype(BF16)
             for b in range(TILE // PB):
                 out = pl.ds(pl.multiple_of(((j * (TILE // PB) + b) * G + g) * PB, PB), PB)
@@ -982,7 +1095,7 @@
         for c in range(dm.NC):
             rows = slice(dm.P, dm.P + CL)
             out = pl.ds(pl.multiple_of(G * dm.P + (g * dm.NC + c) * CL, CL), CL)
-            part = rotate_back(gk[c * CL : (c + 1) * CL], cos[rows, :], shi[rows, :], slo[rows, :])
+            part = rotate_back(gk[c * CL : (c + 1) * CL], cos[rows, :], sin[rows, :])
             dk[out, lanes] = part.astype(BF16)
             dv[out, lanes] = gv[c * CL : (c + 1) * CL].astype(BF16)
         accp = acc[:, : 2 * PB] * 0.125
@@ -990,48 +1103,36 @@
         outp = jnp.where(sublane_pick((128, PB), True), accp[:, :PB], accp[:, PB:]).T
         outc = jnp.where(sublane_pick((128, NCH), True), accc[:, :NCH], accc[:, NCH:]).T
         tab = pl.ds(pl.multiple_of(block * PB, PB), PB)
-        dq[rp, lanes] = rotate_back(outp, cos[tab, :], shi[tab, :], slo[tab, :]).astype(BF16)
+        dq[rp, lanes] = rotate_back(outp, cos[tab, :], sin[tab, :]).astype(BF16)
         tab = pl.ds(pl.multiple_of(dm.P + p.core * dm.CH, dm.CH), dm.CH)
         for c in range(dm.NC):
-            part = rotate_back(outc[c * dm.CH : (c + 1) * dm.CH], cos[tab, :], shi[tab, :], slo[tab, :])
+            part = rotate_back(outc[c * dm.CH : (c + 1) * dm.CH], cos[tab, :], sin[tab, :])
             rows = pl.ds(pl.multiple_of(dm.NP + g * NCH + c * dm.CH, dm.CH), dm.CH)
             dq[rows, lanes] = part.astype(BF16)
 
         @pl.when(g == G - 1)
         def _():
-            put = 2 + pair_rel % 2
+            put = pair_rel % 2
             index = jnp.where(pair_rel < PT, pair_rel + 1, NB + 1 + pair_rel - PT)
-
-            @pl.when(pair_rel >= 2)
-            def _():
-                last = pair_rel - 2
-                rb.cores_sent(jnp.where(last < PT, last + 1, NB + 1 + last - PT), put)
-
-            size = D // (2 * chips)
-            shape = (chips, 2, size)
+            last = pair_rel - 2
+            before = jnp.where(last < PT, last + 1, NB + 1 + last - PT)
+            before = jnp.where(last < 0, jnp.where(put == 0, 0, NB), before)
+            rb.cores_sent(before, put)
             both = jnp.concatenate([dk[:, lanes], dv[:, lanes]], axis=1)
-            gkv = dot(nt[...], both).astype(BF16).reshape(shape + (256,))
-            rb.mine[put, :, :, :, 128:] = gkv
-            gqw = dot(own_nt[...], dq[:, lanes]).astype(BF16).reshape(shape + (128,))
-            rb.mine[put, :, :, :, :128] = gqw
+            for y in range(chips):
+                mine = slice(y * 2 * S, (y + 1) * 2 * S)
+                gkv = dot(nt[mine, :], both).astype(BF16)
+                rb.mine[put, y, :, :, 128:] = gkv.reshape(2, S, 256)
+                gqw = dot(own_nt[mine, :], dq[:, lanes]).astype(BF16)
+                rb.mine[put, y, :, :, :128] = gqw.reshape(2, S, 128)
             rb.cores_send(index, put)
 
-        for when, steps in events.items():
-
-            @pl.when(it == when)
-            def _():
-                for step in steps:
-                    step()
-
         return carry
 
     lax.fori_loop(0, G * dm.PAIRS, attend, 0)
-    last = G * dm.PAIRS
-    for when in sorted(events):
-        if when >= last:
-            for step in events[when]:
-                step()
-    tail = TP * PT - 1
+    last_pair = TP * PT - 1
+    wq_load.wait()
+    w = ring
 
     def project(rows):
         total = None
@@ -1072,79 +1173,173 @@
         def _():
             to_plane(k).start()
 
+        run_when(i, "p")
         return carry
 
     lax.fori_loop(0, p.ctxs, planes, 0)
-    rb.cores_sum(wslab(tail), wslot(tail))
+
+    NCONT = NT - NP
+
+    @pl.when(p.core != p.tp)
+    def _():
+        away.wait_send()
 
     def cont_rows(i, carry):
         rows = pl.ds(pl.multiple_of(G * dm.P + i * CL, CL), CL)
         total = project(rows).astype(BF16)
         out = pl.ds(pl.multiple_of(i * dm.CH, dm.CH), dm.CH)
-        dxc[0, out, :] = total[: dm.CH]
-        dxc[1, out, :] = total[dm.CH :]
+        blk_away[out, :] = total[: dm.CH]
+        blk_away[pl.ds(pl.multiple_of(NCONT + i * dm.CH, dm.CH), dm.CH), :] = total[dm.CH :]
         return carry
 
     lax.fori_loop(0, G * dm.NC, cont_rows, 0)
-    cont_copy = ra.copy(dxc.at[1 - p.core], dxcm, c_send, c_recv, p.mate())
+    halves = lambda core: pl.ds(pl.multiple_of(core * NCONT, 16), NCONT)
+    dxcm = nt.at[pl.ds(0, NCONT), pl.ds(0, D)]
+    cont_copy = ra.copy(blk_away.at[halves(1 - p.core), :], dxcm, c_send, c_recv, p.mate())
     cont_copy.start()
-    total = dot_nt(dq[:, :HC], w[0, :, :HC])
-    for t in range(1, TP):
-        total += dot_nt(dq[:, t * HC : (t + 1) * HC], w[t, :, :HC])
-    dxq[...] = total
-    for i in range(n_a, 2 * n_a):
-        ra.rows_sum(i)
-        ra.tp_sum(i - n_a)
-    for j in range(n_a):
-        ra.ctx_in(j)
-    gain = ln[0:1, :]
+    rb.cores_sum(wslab(last_pair), last_pair % 2)
+    rb.cross_sum(NB - 1)
+    homes = []
+    for i, (a, c) in enumerate(
+        [(home_arrays_p, home_arrays_c)]
+        + [(early_p.at[e], early_c.at[e]) for e in range(3)]
+        + [(home_cot_p, home_cot_c)]
+    ):
+        homes.append(pltpu.make_async_copy(a, dv.at[pl.ds(i * NT, NP), :], home_sem.at[0, i]))
+        homes.append(pltpu.make_async_copy(c, dv.at[pl.ds(i * NT + NP, NT - NP), :], home_sem.at[1, i]))
+    begin(homes)
+
+    def project_q(i, carry):
+        rows = shifted(0, i * STEP)
+        total = dot_nt(dq[rows, :HC], w[0, :, :HC])
+        for t in range(1, TP):
+            total += dot_nt(dq[rows, t * HC : (t + 1) * HC], w[t, :, :HC])
+        blk[rows, :] = total
+        return carry
+
+    lax.fori_loop(0, NT // STEP, project_q, 0)
+    gain_one = ln[0:1, :]
     cont_copy.wait_recv()
-    gn = dxc[p.core].astype(F32) + dxcm[...].astype(F32) + dxq[dm.NP :, :]
-    hat, scale = norm_stats(own_c[...].reshape(dm.NT - dm.NP, D).astype(F32))
-    gin_c[...] = (resg[dm.NP :, :] + norm_back(gn, gain, hat, scale)).astype(BF16).reshape(gin_c.shape)
-    sums = [jnp.sum(gn * hat, axis=0, keepdims=True), jnp.sum(gn, axis=0, keepdims=True)]
-    for i in list(range(NB)) + [NB]:
-        rb.rows_sum(i)
-
-    def final_a(j):
-        total = ra.ctx_out(j)
-        gu_out[:, j * T : (j + 1) * T] = total[:, :T].astype(F32)
-        gd_out[j * T : (j + 1) * T, :] = total[:, T:].astype(F32).T
-
-    for j in range(n_a):
-        final_a(j)
-    gn = dk[block_rows(block), :].astype(F32) + dxq[: dm.NP, :]
+    def enter_back(gn, x, row):
+        rows = shifted(0, row)
+        gn += blk[rows, :]
+        hat, scale = norm_stats(x.astype(F32))
+        gatt[rows, :] = (resid[rows, :] + norm_back(gn, gain_one, hat, scale)).astype(BF16)
+        sm[7:8, :] += jnp.sum(gn * hat, axis=0, keepdims=True)
+        sm[8:9, :] += jnp.sum(gn, axis=0, keepdims=True)
+
+    def cont_back(i, carry):
+        rows = shifted(0, i * STEP)
+        mine = blk_away[shifted(p.core * NCONT, i * STEP), :].astype(F32)
+        enter_back(mine + dxcm[rows, :].astype(F32), own_c[rows, :], NP + i * STEP)
+        return carry
+
+    lax.fori_loop(0, NCONT // STEP, cont_back, 0)
+
+    def gin_away(part):
+        rows = pl.ds(0, NP) if part == 0 else pl.ds(NP, NT - NP)
+        return ra.copy(gatt.at[rows, :], gin_home.at[rows, :], g_send.at[part], g_recv.at[part], p.partner())
+
+    def give(part):
+        rows = slice(0, NP) if part == 0 else slice(NP, NT)
+
+        @pl.when(p.core != p.tp)
+        def _():
+            gin_away(part).start()
+
+        @pl.when(p.core == p.tp)
+        def _():
+            gin_home[rows, :] = gatt[rows, :]
+
+    give(1)
+
+    ready(homes)
+
+    @pl.when(p.core != p.tp)
+    def _():
+        away.wait_recv()
+
+    def blend(i, carry):
+        rows = shifted(0, i * STEP)
+        res = mix[4] * blk_home[rows, :].astype(F32)
+        c = dv[shifted(4 * NT, i * STEP), :].astype(F32)
+        for e in range(4):
+            a = dv[shifted(e * NT, i * STEP), :].astype(F32)
+            res += mix[e] * a
+            sm[3 + e : 4 + e, :] += jnp.sum(c * a, axis=0, keepdims=True)
+        blk_home[rows, :] = res.astype(BF16)
+        return carry
+
+    lax.fori_loop(0, NT // STEP, blend, 0)
+    puts = [
+        pltpu.make_async_copy(blk_home.at[pl.ds(0, NP), :], out_p, put_sem.at[0]),
+        pltpu.make_async_copy(blk_home.at[pl.ds(NP, NT - NP), :], out_c, put_sem.at[1]),
+    ]
+    begin(puts)
+    for kind, when in sorted(key for key in during if key[0] == "t"):
+        if when < 10:
+            for step in during[kind, when]:
+                step()
     for k in range(1, p.ctxs):
         to_plane(k).wait_recv()
-        gn += dxz[k - 1].astype(F32)
-    hat, scale = norm_stats(own_p[...].reshape(dm.NP, D).astype(F32))
-    gin_p[...] = (resg[: dm.NP, :] + norm_back(gn, gain, hat, scale)).astype(BF16).reshape(gin_p.shape)
-    sm[...] = small[...]
-    sm[7:8, :] = sums[0] + jnp.sum(gn * hat, axis=0, keepdims=True)
-    sm[8:9, :] = sums[1] + jnp.sum(gn, axis=0, keepdims=True)
-    for i in range(NB + 1, 2 * NB):
-        rb.rows_sum(i)
-    for j in range(NB):
-        rb.tp_sum(j)
-    for j in range(NB):
-        rb.ctx_in(j)
+
+    def prompt_back(i, carry):
+        rows = shifted(0, i * STEP)
+        gn = dk[shifted(block * NP, i * STEP), :].astype(F32)
+        for k in range(1, p.ctxs):
+            gn += dxz[k - 1, rows, :].astype(F32)
+        enter_back(gn, own_p[rows, :], i * STEP)
+        return carry
+
+    lax.fori_loop(0, NP // STEP, prompt_back, 0)
+    give(0)
+    for kind, when in sorted(key for key in during if key[0] == "t"):
+        if when >= 10:
+            for step in during[kind, when]:
+                step()
     small_out[...] = small_sum(
         p, sm, sm_near, sm_rows, sm_across, sm_planes, sm_ss, sm_rc, sm_ry, sm_rx, sm_rz
     )
+    gu_puts = []
+    for j in range(n_a):
+        total = ra.result(j)
+        gd_out[j * T : (j + 1) * T, :] = total[:, T:].T
+        if len(gu_puts) > 0:
+            gu_puts[-1].wait()
+        gh[:S, :T] = total[:, :T]
+        gu_puts.append(
+            pltpu.make_async_copy(
+                gh.at[pl.ds(0, S), pl.ds(0, T)], gu_out.at[:, pl.ds(j * T, T)], put_sem.at[2]
+            )
+        )
+        gu_puts[-1].start()
+    gu_puts[-1].wait()
     for j in range(NB):
-        total = rb.ctx_out(j).astype(F32)
+        rb.ctx_out(j)
+        total = rb.result(j)
         if j == 0:
             go_out[...] = total.T
         else:
             for c in range(3):
                 first = c * HC + (j - 1) * 128
                 gq_out[:, first : first + 128] = total[:, c * 128 : (c + 1) * 128]
-    for i in range(max(0, 2 * n_a - 2), 2 * n_a):
+
+    @pl.when(p.core != p.tp)
+    def _():
+        for part in range(2):
+            gin_away(part).wait_recv()
+            gin_away(part).wait_send()
+
+    more = [
+        pltpu.make_async_copy(gin_home.at[pl.ds(0, NP), :], gin_p, put_sem.at[2]),
+        pltpu.make_async_copy(gin_home.at[pl.ds(NP, NT - NP), :], gin_c, put_sem.at[3]),
+    ]
+    begin(more)
+    ready(puts + more)
+    for i in range(2 * n_a - 2, 2 * n_a):
         ra.cores_sent(i, i % 2)
-    rb.cores_sent(0, 0)
-    rb.cores_sent(NB, 1)
-    for pr in (tail - 1, tail):
-        rb.cores_sent(wslab(pr), wslot(pr))
+    for pr in (last_pair - 1, last_pair):
+        rb.cores_sent(wslab(pr), pr % 2)
     for k in range(p.ctxs):
         to_mate(k).wait_send()
     for k in range(1, p.ctxs):
@@ -1152,11 +1347,6 @@
     cont_copy.wait_send()
     ra.drain()
     rb.drain()
-
-
-def whole(shape):
-    zeros = (0,) * len(shape)
-    return pl.BlockSpec(shape, lambda *_: zeros)
 
 
 def params(**more):
@@ -1211,8 +1401,7 @@
     angles = positions[:, None] * freq[None, :]
     cos, sin = jnp.cos(angles), jnp.sin(angles)
     second = (lane % 64) >= 32
-    shi = jnp.where(second[None, :], sin, 0.0)
-    slo = jnp.where(second[None, :], 0.0, -sin)
+    sin = jnp.where(second[None, :], sin, -sin)
 
     any_ = pl.BlockSpec(memory_space=pl.ANY)
     vmem = pl.BlockSpec(memory_space=pltpu.VMEM)
@@ -1231,7 +1420,7 @@
             sds((8, D), F32),
             sds((TP, D, HC + 2 * FC), BF16),
         ),
-        in_specs=[vmem] * 6 + [any_],
+        in_specs=[vmem] * 5 + [any_],
         out_specs=(vmem,) * 7 + (any_, vmem, any_),
         scratch_shapes=[
             pltpu.VMEM((PROMPT, 2 * PB), F32),
@@ -1254,89 +1443,36 @@
         + WeightGather.semaphores(chips),
         compiler_params=params(collective_id=0, has_side_effects=True),
         name="forward",
-    )(own_p, own_c, cos, shi, slo, wq_shard, wm_shard)
-    wo, wu, wd = wm[:, :, :HC], wm[:, :, HC : HC + FC], wm[:, :, HC + FC :]
-
+    )(own_p, own_c, cos, sin, wq_shard, wm_shard)
     T = 512 if FC % 512 == 0 else 256
-    steps = FC // T
-    row_specs = [whole(a.shape) for a in (att, own_p, own_c, cot_p, cot_c, ln, wo)]
-    tile = pl.BlockSpec((1, D, T), lambda t, j: (t, 0, j))
-    blk, resg, gatt, gwo, gwu, gwd, small = pl.pallas_call(
-        partial(mlp_kernel, dm, steps),
-        grid=(TP, steps),
+    plan_a = [j == 0 for j in range(FC // T)]
+    plan_b = [True] * (1 + dm.PAIRS // TP)
+    far = max(chips - 1, 1)
+    rows = lambda x: x.reshape(-1, D)
+    out_p, out_c, gin_p, gin_c, gq, go, gu, gd, small = pl.pallas_call(
+        partial(backward_kernel, dm, T, FC, plan_a, plan_b),
         out_shape=(
-            sds((NT, D), BF16),
-            sds((NT, D), F32),
-            sds((NT, D), BF16),
-            sds((TP, D, HC), BF16),
-            sds((TP, D, FC), BF16),
-            sds((TP, D, FC), BF16),
-            sds((8, D), F32),
-        ),
-        in_specs=[pl.BlockSpec(memory_space=pltpu.SMEM)] + row_specs + [tile, tile],
-        out_specs=(
-            whole((NT, D)),
-            whole((NT, D)),
-            whole((NT, D)),
-            whole((TP, D, HC)),
-            tile,
-            tile,
-            whole((8, D)),
-        ),
-        scratch_shapes=[
-            pltpu.VMEM((NT, D), F32),
-            pltpu.VMEM((NT, D), F32),
-            pltpu.VMEM((NT, 128), F32),
-            pltpu.VMEM((NT, D), BF16),
-            pltpu.VMEM((D, NT), BF16),
-            pltpu.VMEM((NT, D), BF16),
-            pltpu.VMEM((D, NT), BF16),
-            pltpu.VMEM((NT, D), F32),
-            pltpu.VMEM((NT, D), F32),
-        ],
-        compiler_params=params(),
-        name="feed",
-    )(
-        mix_weights,
-        att,
-        own_p,
-        own_c,
-        cot_p,
-        cot_c,
-        ln,
-        wo,
-        wu,
-        wd,
-    )
-
-    sums = []
-    for e, y, c in (
-        (prompt_embed, prompt_earlier, prompt_cot),
-        (cont_embed, cont_earlier, cont_cot),
-    ):
-        c = c.astype(F32)
-        terms = [e.astype(F32)] + [y[i].astype(F32) for i in range(3)]
-        sums.append(jnp.stack([jnp.sum((c * a).reshape(-1, D), axis=0) for a in terms]))
-    small = jnp.concatenate([small[:3], sums[0] + sums[1], jnp.zeros((9, D), F32)], axis=0)
-
-    blk = trade(blk).astype(F32)
-    n_a = FC // T
-    split = (TP, chips, 2, S)
-    far = max(chips - 1, 1)
-    gin_p, gin_c, gq, go, gu, gd, small = pl.pallas_call(
-        partial(backward_kernel, dm, T),
-        out_shape=(
-            sds(prompt_in.shape, BF16),
-            sds(cont_in.shape, BF16),
+            sds((NP, D), BF16),
+            sds((NT - NP, D), BF16),
+            sds((NP, D), BF16),
+            sds((NT - NP, D), BF16),
             sds((S, 3 * HC), F32),
             sds((HC, S), F32),
             sds((S, FC), F32),
             sds((FC, S), F32),
             sds((16, D), F32),
         ),
-        in_specs=[vmem] * 15 + [any_] * 5,
-        out_specs=(vmem,) * 7,
+        in_specs=[pl.BlockSpec(memory_space=pltpu.SMEM)] + [vmem] * 10 + [any_] * 12,
+        out_specs=(any_,) * 4 + (vmem, vmem, any_, vmem, vmem),
         scratch_shapes=[
+            pltpu.VMEM((NT, D), F32),
+            pltpu.VMEM((NT, D), F32),
+            pltpu.VMEM((NT, D), F32),
+            pltpu.VMEM((TP, D, HC), BF16),
+            pltpu.VMEM((2, D, max(2 * T, 3 * HC)), BF16),
+            pltpu.VMEM((NT, D), BF16),
+            pltpu.VMEM((D, G * R), BF16),
+            pltpu.VMEM((D, NT), BF16),
             pltpu.VMEM((PROMPT, 2 * PB), F32),
             pltpu.VMEM((dm.NX, 2 * dm.NCH), F32),
             pltpu.VMEM((2, R, 128), BF16),
@@ -1344,13 +1480,21 @@
             pltpu.VMEM((G * R, D), BF16),
             pltpu.VMEM((G * R, D), BF16),
             pltpu.VMEM((NT, D), BF16),
-            pltpu.VMEM((NT, D), F32),
             pltpu.VMEM((ctxs, G * PB, D), BF16),
             pltpu.VMEM((ctxs - 1, G * PB, D), BF16),
-            pltpu.VMEM((2, NT - NP, D), BF16),
-            pltpu.VMEM((NT - NP, D), BF16),
+            pltpu.VMEM((max(NT, 2 * (NT - NP)), D), BF16),
+            pltpu.VMEM((NT, D), BF16),
+            pltpu.VMEM((NT, D), BF16),
+            dma((4,)),
             dma((2, 2)),
+            dma,
             dma((2, 2)),
+            dma((2,)),
+            dma,
+            dma((2, 5)),
+            dma,
+            dma,
+            dma((2,)),
             dma((2,)),
             dma((ctxs,)),
             dma((ctxs,)),
@@ -1369,49 +1513,42 @@
             dma,
             dma((ctxs - 1,)),
         ]
-        + Reduce.scratch(n_a, chips, S, 2 * T)
-        + Reduce.scratch(1 + dm.PAIRS // TP, chips, S, HC, slots=4),
+        + Reduce.scratch(plan_a, chips, S, 2 * T)
+        + Reduce.scratch(plan_b, chips, S, HC),
         compiler_params=params(collective_id=1, has_side_effects=True),
         name="backward",
     )(
+        mix_weights,
+        att,
+        rows(own_p),
+        rows(own_c),
+        rows(cot_p),
+        rows(cot_c),
+        ln,
         q,
-        att,
-        gatt,
         lse,
+        cos,
+        sin,
+        wm,
+        k,
+        v,
         nt,
         own_nt,
-        cos,
-        shi,
-        slo,
         wq,
-        ln,
-        own_p,
-        own_c,
-        resg,
-        small,
-        k,
-        v,
-        gwo.reshape(split + (HC,)),
-        gwu.reshape(split + (FC,)),
-        gwd.reshape(split + (FC,)),
+        rows(prompt_embed),
+        rows(cont_embed),
+        prompt_earlier.reshape(3, NP, D),
+        cont_earlier.reshape(3, NT - NP, D),
+        rows(prompt_cot),
+        rows(cont_cot),
     )
-    gin_p, gin_c = trade(gin_p), trade(gin_c)
-    outs = []
-    for b, e, y in (
-        (blk[:NP].reshape(prompt_in.shape), prompt_embed, prompt_earlier),
-        (blk[NP:].reshape(cont_in.shape), cont_embed, cont_earlier),
-    ):
-        total = mix_weights[0] * e.astype(F32) + mix_weights[4] * b
-        for i in range(3):
-            total += mix_weights[1 + i] * y[i].astype(F32)
-        outs.append(total.astype(BF16))
     start = lax.axis_index("dp") * S
     mine = lax.dynamic_slice_in_dim(small, start, S, axis=1)
     return (
-        outs[0],
-        outs[1],
-        gin_p,
-        gin_c,
+        out_p.reshape(prompt_in.shape),
+        out_c.reshape(cont_in.shape),
+        gin_p.reshape(prompt_in.shape),
+        gin_c.reshape(cont_in.shape),
         mine[7],
         mine[8],
         mine[0],

time: 381 us -> 348 us (0.913)
  Pallas kernels: 320 us -> 306 us
  local copies, waits for them, and re-layouts: 28.1 us -> 15.8 us
  other arithmetic: 15.7 us -> 5.91 us
    pallas_call x2 -> x1, Pallas kernels: 213 us -> 201 us  [per_device(): pl.pallas_call(partial(backward_kernel, dm, T, FC, plan_a, plan_b), out_s...]
    slice x4 -> x0, local copies, waits for them, and re-layouts: 11.6 us -> none  [the longest x2 10.3 us: per_device(): wo, wu, wd = (wm[:, :, :HC], wm[:, :, HC:HC + FC], wm[:, :, HC + FC:])]
    reduce_sum x2 -> x0, other arithmetic: 7.9 us -> none  [per_device(): jnp.sum((c * a).reshape(-1, D), axis=0)]
    ppermute x7 -> x4, starting transfers between devices: 14.6 us -> 17.9 us  [trade(): return lax.ppermute(x, ('dp', 'tp'), swap)]
    unnamed x37 -> x27, local copies, waits for them, and re-layouts: 8.57 us -> 7.86 us
  transfers between devices with their start and end apart: 7 -> 4, of which waited for: 0 -> 0; matrix products, arithmetic and copies ran while one was open for 8% -> 3% of each run, Pallas kernels for 28% -> 30%
where the time goes in v4:
time: 348 us; the launch traced here: 346 us
  Pallas kernels  306 us (88%)
  starting transfers between devices  17.9 us (5%)
  local copies, waits for them, and re-layouts  15.8 us (5%)
  other arithmetic  5.91 us (2%)
    pallas_call x1, Pallas kernels, per_device(): pl.pallas_call(partial(backward_kernel, dm, T, FC, plan_a, plan_b), out_s...  201 us
    pallas_call x1, Pallas kernels, per_device(): pl.pallas_call(partial(forward_kernel, dm), out_shape=(sds((D, G * R), BF...  105 us
    ppermute x4, starting transfers between devices, trade(): return lax.ppermute(x, ('dp', 'tp'), swap)  17.9 us
    unnamed x27, local copies, waits for them, and re-layouts  7.86 us
  transfers between devices with their start and end apart: 4, of which 0 were waited for; matrix products, arithmetic and copies ran while one was open for 3% of the time, Pallas kernels for 30%

profile of v4, /device:TPU:0, one launch (start us, length us, event | category | flops | bytes accessed | tf_op | source)
XLA Modules:
  0.0 346.1 jit_solution(14557740324160383268)
XLA Ops:
  0.6 4.5 %collective-permute-start = (bf16[2,128,768]{2,1,0:T(8,128)(2,1)}, bf16[2,128,768]{2,1,0:T(8,128)(2,1)}, u32[]{:S(2)}, u32[]{:S(2)}) collective-permute-start(bf16[2,128,768]{2,1,0:T(8,128)(2,1)} %param.17), channel_id=1, source_target_pairs={{0,0},{1,8},{8,1},{9,9},{16,16},{17,24},{24,17},{25,25},{2,2},{3,1... | collective-permute-start | bytes 1179656 | tf_op jit(solution)/shard_map/ppermute | solution.py:1389
  5.1 4.5 %collective-permute-start.1 = (bf16[2,2,64,768]{3,2,1,0:T(8,128)(2,1)}, bf16[2,2,64,768]{3,2,1,0:T(8,128)(2,1)}, u32[]{:S(2)}, u32[]{:S(2)}) collective-permute-start(bf16[2,2,64,768]{3,2,1,0:T(8,128)(2,1)} %param.18), channel_id=1, source_target_pairs={{0,0},{1,8},{8,1},{9,9},{16,16},{17,24},{24,17},{25,25},{2,2},{3,1... | collective-permute-start | bytes 1179656 | tf_op jit(solution)/shard_map/ppermute | solution.py:1389
  9.6 4.5 %collective-permute-start.2 = (bf16[2,128,768]{2,1,0:T(8,128)(2,1)}, bf16[2,128,768]{2,1,0:T(8,128)(2,1)}, u32[]{:S(2)}, u32[]{:S(2)}) collective-permute-start(bf16[2,128,768]{2,1,0:T(8,128)(2,1)} %param.32), channel_id=1, source_target_pairs={{0,0},{1,8},{8,1},{9,9},{16,16},{17,24},{24,17},{25,25},{2,2},{3,1... | collective-permute-start | bytes 1179656 | tf_op jit(solution)/shard_map/ppermute | solution.py:1389
  14.1 4.5 %collective-permute-start.3 = (bf16[2,2,64,768]{3,2,1,0:T(8,128)(2,1)}, bf16[2,2,64,768]{3,2,1,0:T(8,128)(2,1)}, u32[]{:S(2)}, u32[]{:S(2)}) collective-permute-start(bf16[2,2,64,768]{3,2,1,0:T(8,128)(2,1)} %param.33), channel_id=1, source_target_pairs={{0,0},{1,8},{8,1},{9,9},{16,16},{17,24},{24,17},{25,25},{2,2},{3,1... | collective-permute-start | bytes 1179656 | tf_op jit(solution)/shard_map/ppermute | solution.py:1389
  18.6 0.0 copy-start.2
  18.6 0.0 copy-start.3
  18.6 0.0 copy-start.9
  18.6 1.2 copy.48
  19.8 0.7 stack.15
  20.4 0.7 stack.16
  21.1 0.7 stack.17
  21.7 0.7 stack.18
  22.4 0.1 copy.43
  22.6 0.8 fusion.1.wq
  23.4 3.3 negate_select_fusion
  26.7 0.0 copy-done.2
  26.7 0.0 copy-done.3
  26.7 0.0 copy-done.9
  26.7 1.2 pad_maximum_fusion.wm
  27.8 0.0 collective-permute-done.op
  27.8 0.0 collective-permute-done.1.oc
  27.8 104.7 %forward.1 = (bf16[768,2560]{1,0:T(8,128)(2,1)}, bf16[768,512]{1,0:T(8,128)(2,1)}, bf16[2,1280,768]{2,1,0:T(8,128)(2,1)}, bf16[2,1280,768]{2,1,0:T(8,128)(2,1)},...) custom-call(bf16[2,128,768]{2,1,0:T(8,128)(2,1)} %collective-permute, ...), custom_call_target="tpu_custom_call" | custom-call | tf_op jit(solution)/shard_map/forward/pallas_call | solution.py:1409
  132.5 0.0 collective-permute-done.2
  132.6 0.0 collective-permute-done.3
  132.6 201.0 %backward.1 = (bf16[256,768]{1,0:T(8,128)(2,1)}, bf16[256,768]{1,0:T(8,128)(2,1)}, bf16[256,768]{1,0:T(8,128)(2,1)}, bf16[256,768]{1,0:T(8,128)(2,1)}, f32[192,1...) custom-call(f32[5]{0:T(128)} %mix.1, ...), custom_call_target="tpu_custom_call" | custom-call | tf_op jit(solution)/shard_map/backward/pallas_call | solution.py:1452
  333.6 0.0 copy-start.1
  333.6 0.8 slice.22
  334.4 0.7 slice.23
  335.1 2.9 copy.46
  338.0 0.0 copy-start.8
  338.0 0.0 copy-start.7
  338.0 0.0 copy-done.1
  338.0 0.0 copy-start.6
  338.0 1.0 copy.50
  339.0 0.1 copy-done.8
  339.1 0.9 copy.45
  339.9 0.6 maximum_reduce_fusion
  340.6 1.5 fusion.7
  342.0 0.0 copy-done.7
  342.0 0.7 copy.56
  342.8 0.0 copy-done.6
  342.8 0.7 copy.57
  343.5 0.0 copy-done.5
  343.5 0.7 copy.58
  344.3 0.0 copy-done.4
  344.3 0.7 copy.59
  345.0 0.0 copy-done
  345.0 1.0 copy.60
  (7 shorter events, 0.0 us)
Async XLA Ops:
  0.6 27.2 %collective-permute-start = (bf16[2,128,768]{2,1,0:T(8,128)(2,1)}, bf16[2,128,768]{2,1,0:T(8,128)(2,1)}, u32[]{:S(2)}, u32[]{:S(2)}) collective-permute-start(bf16[2,128,768]{2,1,0:T(8,128)(2,1)} %param.17), channel_id=1, source_target_pairs={{0,0},{1,8},{8,1},{9,9},{16,16},{17,24},{24,17},{25,25},{2,2},{3,1... | collective-permute-start | bytes 1179656 | tf_op jit(solution)/shard_map/ppermute | solution.py:1389
  5.1 22.7 %collective-permute-start.1 = (bf16[2,2,64,768]{3,2,1,0:T(8,128)(2,1)}, bf16[2,2,64,768]{3,2,1,0:T(8,128)(2,1)}, u32[]{:S(2)}, u32[]{:S(2)}) collective-permute-start(bf16[2,2,64,768]{3,2,1,0:T(8,128)(2,1)} %param.18), channel_id=1, source_target_pairs={{0,0},{1,8},{8,1},{9,9},{16,16},{17,24},{24,17},{25,25},{2,2},{3,1... | collective-permute-start | bytes 1179656 | tf_op jit(solution)/shard_map/ppermute | solution.py:1389
  9.6 122.9 %collective-permute-start.2 = (bf16[2,128,768]{2,1,0:T(8,128)(2,1)}, bf16[2,128,768]{2,1,0:T(8,128)(2,1)}, u32[]{:S(2)}, u32[]{:S(2)}) collective-permute-start(bf16[2,128,768]{2,1,0:T(8,128)(2,1)} %param.32), channel_id=1, source_target_pairs={{0,0},{1,8},{8,1},{9,9},{16,16},{17,24},{24,17},{25,25},{2,2},{3,1... | collective-permute-start | bytes 1179656 | tf_op jit(solution)/shard_map/ppermute | solution.py:1389
  14.1 118.5 %collective-permute-start.3 = (bf16[2,2,64,768]{3,2,1,0:T(8,128)(2,1)}, bf16[2,2,64,768]{3,2,1,0:T(8,128)(2,1)}, u32[]{:S(2)}, u32[]{:S(2)}) collective-permute-start(bf16[2,2,64,768]{3,2,1,0:T(8,128)(2,1)} %param.33), channel_id=1, source_target_pairs={{0,0},{1,8},{8,1},{9,9},{16,16},{17,24},{24,17},{25,25},{2,2},{3,1... | collective-permute-start | bytes 1179656 | tf_op jit(solution)/shard_map/ppermute | solution.py:1389
  18.6 8.1 %copy-start.2 = (bf16[1536,192]{0,1:T(8,128)(2,1)S(1)}, bf16[1536,192]{0,1:T(8,128)(2,1)}, u32[]{:S(2)}) copy-start(bf16[1536,192]{0,1:T(8,128)(2,1)} %param.30) | copy-start | bytes 1769476
  18.6 8.1 %copy-start.3 = (bf16[192,1536]{1,0:T(8,128)(2,1)S(1)}, bf16[192,1536]{1,0:T(8,128)(2,1)}, u32[]{:S(2)}) copy-start(bf16[192,1536]{1,0:T(8,128)(2,1)} %param.29) | copy-start | bytes 1769476
  18.6 8.1 %copy-start.9 = (bf16[384,192]{0,1:T(8,128)(2,1)S(1)}, bf16[384,192]{0,1:T(8,128)(2,1)}, u32[]{:S(2)}) copy-start(bf16[384,192]{0,1:T(8,128)(2,1)} %param.28) | copy-start | bytes 442372
  333.6 4.5 %copy-start.1 = (f32[192,1152]{1,0:T(8,128)S(1)}, f32[192,1152]{1,0:T(8,128)}, u32[]{:S(2)}) copy-start(f32[192,1152]{1,0:T(8,128)} %get-tuple-element.47) | copy-start | bytes 2654212
  338.0 1.1 copy-start.8
  338.0 4.0 %copy-start.7 = (bf16[256,768]{1,0:T(8,128)(2,1)S(1)}, bf16[256,768]{1,0:T(8,128)(2,1)}, u32[]{:S(2)}) copy-start(bf16[256,768]{1,0:T(8,128)(2,1)} %get-tuple-element.42) | copy-start | bytes 1179652
  338.0 4.8 %copy-start.6 = (bf16[256,768]{1,0:T(8,128)(2,1)S(1)}, bf16[256,768]{1,0:T(8,128)(2,1)}, u32[]{:S(2)}) copy-start(bf16[256,768]{1,0:T(8,128)(2,1)} %get-tuple-element.43) | copy-start | bytes 1179652
  339.0 4.6 %copy-start.5 = (bf16[256,768]{1,0:T(8,128)(2,1)S(1)}, bf16[256,768]{1,0:T(8,128)(2,1)}, u32[]{:S(2)}) copy-start(bf16[256,768]{1,0:T(8,128)(2,1)} %get-tuple-element.44) | copy-start | bytes 1179652
  339.0 5.3 %copy-start.4 = (bf16[256,768]{1,0:T(8,128)(2,1)S(1)}, bf16[256,768]{1,0:T(8,128)(2,1)}, u32[]{:S(2)}) copy-start(bf16[256,768]{1,0:T(8,128)(2,1)} %get-tuple-element.45) | copy-start | bytes 1179652
  342.0 3.0 copy-start

commit v5 on v4

--- a/solution.py
+++ b/solution.py
@@ -241,6 +241,10 @@
     def drain(self):
         for copy in self.copies:
             copy.wait_send()
+
+
+def twice(x):
+    return jnp.concatenate([x, x], axis=1)
 
 
 def fill_masks(dm, maskp, maskx):
@@ -408,7 +412,7 @@
 
     def block_chunk(g, b):
         row = pl.multiple_of(b * PB, PB)
-        keys_values(g, xp[b, g], row, row, pl.multiple_of((b * G + g) * PB, PB))
+        keys_values(g, xp[b, g], row, row, pl.multiple_of(g * R + row, PB))
 
     arrived(xc.at[1 - p.core], c_mate, p)
 
@@ -416,7 +420,7 @@
         g, c = i // dm.NC, i % dm.NC
         row = pl.multiple_of(dm.P + c * CL, CL)
         x = jnp.concatenate([xc[0, g, c], xc[1, g, c]], axis=0)
-        keys_values(g, x, row, dm.P, pl.multiple_of(G * dm.P + i * CL, CL))
+        keys_values(g, x, row, dm.P, pl.multiple_of(g * R + row, CL))
         return carry
 
     lax.fori_loop(0, G * dm.NC, cont_chunk, 0)
@@ -458,7 +462,7 @@
         for j in range(tiles):
             s = dot(k_out[g, j * TILE : (j + 1) * TILE, lanes], qt)
             sbuf[j * TILE : (j + 1) * TILE, : 2 * PB] = (
-                s[:, : 2 * PB] + maskp[j * TILE : (j + 1) * TILE, :]
+                s[:, : 2 * PB] + twice(maskp[j * TILE : (j + 1) * TILE, :])
             )
             sbuf[j * TILE : (j + 1) * TILE, 2 * PB :] = s[:, 2 * PB :]
             here = jnp.max(sbuf[j * TILE : (j + 1) * TILE, :], axis=0, keepdims=True)
@@ -519,13 +523,13 @@
         far = max(chips - 1, 1)
         rows = n + sum(1 for c in cross_first if not c)
         return [
-            pltpu.VMEM((2, chips, 2, size, width), BF16),
+            pltpu.VMEM((2, chips * 2 * size, width), BF16),
             pltpu.VMEM((2 * n, chips, size, width), BF16),
             pltpu.VMEM((rows, far, size, width), BF16),
             pltpu.VMEM((n, chips, size, width), BF16),
             pltpu.VMEM((n, 2, size, width), BF16),
-            dma((2 * n,)),
-            dma((2 * n,)),
+            dma((2 * n, chips)),
+            dma((2 * n, chips)),
             dma((2 * n, far)),
             dma((2 * n, far)),
             dma((n,)),
@@ -550,10 +554,18 @@
     def travels(self, i):
         return i >= self.n or not self.crosses(i)
 
-    def by_core(self, i, slot):
+    def mine_of(self, y, core):
+        size = self.got.shape[2]
+        return pl.ds(pl.multiple_of((2 * y + core) * size, 16), size)
+
+    def by_core(self, i, slot, y):
         p = self.p
         return self.copy(
-            self.mine.at[slot, :, 1 - p.core], self.got.at[i], self.sc.at[i], self.rc.at[i], p.mate()
+            self.mine.at[slot, self.mine_of(y, 1 - p.core), :],
+            self.got.at[i, y],
+            self.sc.at[i, y],
+            self.rc.at[i, y],
+            p.mate(),
         )
 
     def row_slot(self, i):
@@ -599,10 +611,12 @@
         self.got[i, y] = (self.got[i, y].astype(F32) + other.astype(F32)).astype(BF16)
 
     def cores_send(self, i, slot):
-        self.by_core(i, slot).start()
+        for y in range(self.p.chips):
+            self.by_core(i, slot, y).start()
 
     def cores_sent(self, i, slot):
-        self.by_core(i, slot).wait_send()
+        for y in range(self.p.chips):
+            self.by_core(i, slot, y).wait_send()
 
     def rows_send(self, i):
         for k in range(1, self.p.chips):
@@ -610,9 +624,9 @@
 
     def cores_sum(self, i, slot):
         p = self.p
-        self.by_core(i, slot).wait_recv()
         for y in range(p.chips):
-            self.add(i, y, self.mine[slot, y, p.core])
+            self.by_core(i, slot, y).wait_recv()
+            self.add(i, y, self.mine[slot, self.mine_of(y, p.core), :])
         if not self.crosses(i):
             self.rows_send(i)
         elif i < self.n:
@@ -648,22 +662,29 @@
             self.add(self.n + j, self.p.chip, self.zin[j, 0])
             self.inward(j).start()
 
-    def ctx_out(self, j):
-        p = self.p
+    def ctx_mid(self, j):
+        @pl.when(self.centre)
+        def _():
+            self.from_inner(j)
+            self.add(self.n + j, self.p.chip, self.zin[j, 1])
+
+            @pl.when(self.outer)
+            def _():
+                self.outward(j).start()
+
+    def ctx_end(self, j):
+        @pl.when(jnp.logical_not(self.centre))
+        def _():
+            self.from_inner(j)
+            self.got[self.n + j, self.p.chip] = self.zin[j, 1]
+
+            @pl.when(self.outer)
+            def _():
+                self.outward(j).start()
+
+    def from_inner(self, j):
         pltpu.make_async_copy(self.zin.at[j, 1], self.zin.at[j, 1], self.rz.at[j, 1]).wait()
         self.inward(j).wait_send()
-
-        @pl.when(self.centre)
-        def _():
-            self.add(self.n + j, p.chip, self.zin[j, 1])
-
-        @pl.when(jnp.logical_not(self.centre))
-        def _():
-            self.got[self.n + j, p.chip] = self.zin[j, 1]
-
-        @pl.when(self.outer)
-        def _():
-            self.outward(j).start()
 
     def result(self, j):
         return self.got[self.n + j, self.p.chip].astype(F32)
@@ -714,39 +735,46 @@
     return total
 
 
-def schedule(ra, rb, on, n_a, NB, PT, TP, G):
-    def at_pair(pair_rel):
-        return pair_rel + 1 if pair_rel < PT else NB + 1 + pair_rel - PT
-
-    last = 2 * n_a - 1
-    late = ("a", 0)
-    plan = ra.cross_first
-    for j in range(n_a):
-        if not plan[j]:
-            on(("m", last) if j < n_a - 1 else ("a", 1), partial(ra.rows_sum, j))
-    for j in range(n_a):
-        if plan[j]:
-            on(("m", last), partial(ra.cross_sum, j))
-    own_at = {0: 6, 1: 3, 2: 8}
-    for j in range(n_a):
-        on(("a", own_at.get(j, 8)), partial(ra.rows_sum, n_a + j))
-        on(("a", min(own_at.get(j, 8) + 3, 11)), partial(ra.ctx_in, j))
-    on(late, partial(rb.cores_sum, 0, 0))
-    on(late, partial(rb.cores_sum, NB, 1))
-    on(("a", 2), partial(rb.cross_sum, 0))
-    on(("a", 5), partial(rb.rows_sum, NB))
-    on(("a", 8), partial(rb.ctx_in, 0))
-    for pr in range(TP * PT - 1):
-        on(("a", G * pr + G), partial(rb.cores_sum, at_pair(pr), pr % 2))
-        if pr >= PT:
-            on(("a", G * pr + G), partial(rb.cross_sum, pr - PT + 1))
-    for j in range(1, NB - 1):
-        on(("p", j), partial(rb.rows_sum, NB + j))
-    for j in range(n_a):
-        on(("p", j), partial(ra.ctx_out, j))
-    on(("t", 0), partial(rb.rows_sum, 2 * NB - 1))
-    for j in range(1, NB):
-        on(("t", 10 + j), partial(rb.ctx_in, j))
+def schedule(ra, rb, on, pairs, planes):
+    n, nb = ra.n, rb.n
+    for i in range(2 * n - 1):
+        if i == 2:
+            on(("m", 3), partial(ra.rows_sum, 0))
+        on(("m", i + 1), partial(ra.cores_sum, (i % 2) * n + i // 2, i % 2))
+    on(("e", 0), partial(ra.rows_sum, n))
+    on(("e", 0), partial(ra.cores_sum, 2 * n - 1, 1))
+    on(("a", 0), partial(rb.cores_sum, 0, 0))
+    on(("a", 0), partial(rb.cores_sum, nb, 1))
+    on(("a", 2), partial(ra.rows_sum, 2))
+    on(("a", 3), partial(rb.cross_sum, 0))
+    on(("a", 4), partial(ra.ctx_in, 0))
+    on(("a", 5), partial(ra.cross_sum, 1))
+    last = pairs
+    on(("a", last - 1), partial(rb.rows_sum, nb))
+    on(("a", last), partial(ra.ctx_mid, 0))
+    on(("a", last + 1), partial(ra.rows_sum, n + 1))
+    on(("a", last + 1), partial(ra.rows_sum, n + 2))
+    on(("a", last + 1), partial(rb.ctx_in, 0))
+    on(("a", last + 3), partial(rb.ctx_mid, 0))
+    on(("a", last + 5), partial(ra.ctx_in, 1))
+    for i in range(pairs - 1):
+        on(("a", last + 1 + i), partial(rb.cores_sum, (i % 2) * nb + 1 + i // 2, i % 2))
+    on(("a", last + 3), partial(rb.cross_sum, 1))
+    on(("a", last + 5), partial(rb.cross_sum, 2))
+    on(("a", last + 5), partial(rb.rows_sum, nb + 1))
+    on(("p", planes), partial(rb.cores_sum, 2 * nb - 1, 1))
+    on(("p", planes), partial(rb.rows_sum, nb - 1))
+    on(("p", planes + 1), partial(rb.rows_sum, nb + 2))
+    on(("p", planes + 1), partial(rb.ctx_in, 1))
+    on(("p", planes + 2), partial(ra.ctx_in, 2))
+    on(("p", planes + 2), partial(ra.ctx_mid, 1))
+    on(("t", 0), partial(rb.rows_sum, 2 * nb - 1))
+    on(("t", 1), partial(rb.ctx_in, 2))
+    on(("t", 2), partial(rb.ctx_mid, 1))
+    on(("t", 3), partial(ra.ctx_mid, 2))
+    on(("t", 4), partial(rb.ctx_in, 3))
+    on(("t", 5), partial(rb.ctx_mid, 2))
+    on(("t", 11), partial(rb.ctx_mid, 3))
 
 
 def backward_kernel(
@@ -804,6 +832,7 @@
     dq,
     dxm,
     dxz,
+    dxcm,
     blk_away,
     blk_home,
     gin_home,
@@ -858,8 +887,8 @@
             copy.wait()
 
     def load_tile(i, slot):
-        t = jnp.where(i < n_a, 1 - p.tp, p.tp)
-        first = pl.multiple_of(HC + lax.rem(i, n_a) * T, 128)
+        t = jnp.where(lax.rem(i, 2) == 0, 1 - p.tp, p.tp)
+        first = pl.multiple_of(HC + i // 2 * T, 128)
         return [
             pltpu.make_async_copy(
                 wm.at[t, :, pl.ds(first, T)], ring.at[slot, :, pl.ds(0, T)], ring_sem.at[0, slot]
@@ -869,10 +898,13 @@
             ),
         ]
 
+    def pair_at(it):
+        turn = it % dm.PAIRS
+        return jnp.where(turn % 2 == 0, 1 - p.tp, p.tp) * PT + turn // 2
+
     def load_kv(it, slot):
-        pair_rel, g = it // G, it % G
-        t = jnp.where(pair_rel < PT, 1 - p.tp, p.tp)
-        lanes = pl.ds(pl.multiple_of((t * PT + pair_rel % PT) * 128, 128), 128)
+        pair, g = pair_at(it), it // dm.PAIRS
+        lanes = pl.ds(pl.multiple_of(pair * 128, 128), 128)
         return [
             pltpu.make_async_copy(k_hbm.at[g, :, lanes], kbuf.at[slot], kv_sem.at[0, slot]),
             pltpu.make_async_copy(v_hbm.at[g, :, lanes], vbuf.at[slot], kv_sem.at[1, slot]),
@@ -940,9 +972,12 @@
                     for step in steps:
                         step()
 
-    for i in range(1, 2 * n_a):
-        on(("m", i), partial(ra.cores_sum, i - 1, (i - 1) % 2))
-    schedule(ra, rb, on, n_a, NB, PT, TP, G)
+    schedule(ra, rb, on, dm.PAIRS, p.ctxs)
+
+    def run(name):
+        for kind, when in sorted(key for key in during if key[0] == name):
+            for step in during[kind, when]:
+                step()
 
     def feed(i, carry):
         slot = lax.rem(i, 2)
@@ -958,7 +993,7 @@
         for e in range(2):
             rows = slice(e * HALF, (e + 1) * HALF)
             u = dot(dk[rows, :], up)
-            if e == 0:
+            if e == 1:
                 run_when(i, "m")
             u2 = u * u
             th = jnp.tanh(c0 * u * (1.0 + 0.044715 * u2))
@@ -973,16 +1008,17 @@
 
         @pl.when(i >= 2)
         def _():
-            ra.cores_sent(i - 2, slot)
+            ra.cores_sent(slot * n_a + i // 2 - 1, slot)
 
         for y in range(chips):
             mine = slice(y * 2 * S, (y + 1) * 2 * S)
-            ra.mine[slot, y, :, :, :T] = dot(nt[mine, hn], dv[gd, :T]).astype(BF16).reshape(2, S, T)
-            ra.mine[slot, y, :, :, T:] = dot(nt[mine, gd], dv[hn, :T]).astype(BF16).reshape(2, S, T)
-        ra.cores_send(i, slot)
+            ra.mine[slot, mine, :T] = dot(nt[mine, hn], dv[gd, :T]).astype(BF16)
+            ra.mine[slot, mine, T:] = dot(nt[mine, gd], dv[hn, :T]).astype(BF16)
+        ra.cores_send(slot * n_a + i // 2, slot)
         return carry
 
     lax.fori_loop(0, 2 * n_a, feed, 0)
+    run("e")
     blk_away[:NT, :] = blk[...].astype(BF16)
     away = ra.copy(blk_away.at[pl.ds(0, NT), :], blk_home, b_send, b_recv, p.partner())
 
@@ -1017,7 +1053,7 @@
         lanes = pl.ds(pl.multiple_of(t * HC, 128), HC)
         for y in range(chips):
             mine = slice(y * 2 * S, (y + 1) * 2 * S)
-            rb.mine[slot, y] = dot(nt[mine, gd], att[:, lanes]).astype(BF16).reshape(2, S, HC)
+            rb.mine[slot, mine, :] = dot(nt[mine, gd], att[:, lanes]).astype(BF16)
         rb.cores_send(i, slot)
     nt_load = [
         pltpu.make_async_copy(nt_hbm, nt, nt_sem.at[0]),
@@ -1026,23 +1062,17 @@
     begin(nt_load)
     wq_load = pltpu.make_async_copy(wq_hbm.at[:, :, pl.ds(0, 3 * HC)], ring.at[:, :, pl.ds(0, 3 * HC)], wq_sem)
     wq_load.start()
-    ra.cores_sum(2 * n_a - 1, 1)
-    during.setdefault(("a", 1), []).insert(0, partial(ready, nt_load))
-
-    def wslab(pair_rel):
-        return pair_rel + 1 if pair_rel < PT else NB + 1 + pair_rel - PT
-
-    def attend(it, carry):
-        pair_rel, g = it // G, it % G
-        t = jnp.where(pair_rel < PT, 1 - p.tp, p.tp)
-        pair = t * PT + pair_rel % PT
+    during.setdefault(("a", dm.PAIRS), []).insert(0, partial(ready, nt_load))
+
+    def attend(turn, g):
+        it = g * dm.PAIRS + turn
+        pair = pair_at(it)
         slot = it % 2
 
         @pl.when(it + 1 < G * dm.PAIRS)
         def _():
             begin(load_kv(it + 1, 1 - slot))
 
-        run_when(it, "a")
         lanes = pl.ds(pl.multiple_of(pair * 128, 128), 128)
         rp = pl.ds(pl.multiple_of(g * PB, PB), PB)
         rc = pl.ds(pl.multiple_of(dm.NP + g * NCH, NCH), NCH)
@@ -1080,21 +1110,22 @@
             rows = slice(j * TILE, (j + 1) * TILE)
             kt = kbuf[slot, rows, :]
             s = dot(kt, qt)
-            s = jnp.concatenate([s[:, : 2 * PB] + maskp[rows, :], s[:, 2 * PB :]], axis=1)
+            s = jnp.concatenate([s[:, : 2 * PB] + twice(maskp[rows, :]), s[:, 2 * PB :]], axis=1)
             gk, gv, gq = grads(s, kt, vbuf[slot, rows, :], 0)
             gk = rotate_back(gk, cos[rows, :], sin[rows, :]).astype(BF16)
             gv = gv.astype(BF16)
-            for b in range(TILE // PB):
-                out = pl.ds(pl.multiple_of(((j * (TILE // PB) + b) * G + g) * PB, PB), PB)
-                dk[out, lanes] = gk[b * PB : (b + 1) * PB]
-                dv[out, lanes] = gv[b * PB : (b + 1) * PB]
+            out = pl.ds(pl.multiple_of(g * R + j * TILE, 128), TILE)
+            dk[out, lanes] = gk
+            dv[out, lanes] = gv
+            if j == tiles // 2:
+                run_when(it, "a")
             acc = gq if acc is None else acc + gq
         kt = kbuf[slot, dm.P :, :]
         s = dot(kt, qt[:, 2 * PB :]) + maskx[...]
         gk, gv, gq = grads(s, kt, vbuf[slot, dm.P :, :], 2 * PB)
         for c in range(dm.NC):
             rows = slice(dm.P, dm.P + CL)
-            out = pl.ds(pl.multiple_of(G * dm.P + (g * dm.NC + c) * CL, CL), CL)
+            out = pl.ds(pl.multiple_of(g * R + dm.P + c * CL, CL), CL)
             part = rotate_back(gk[c * CL : (c + 1) * CL], cos[rows, :], sin[rows, :])
             dk[out, lanes] = part.astype(BF16)
             dv[out, lanes] = gv[c * CL : (c + 1) * CL].astype(BF16)
@@ -1112,26 +1143,18 @@
 
         @pl.when(g == G - 1)
         def _():
-            put = pair_rel % 2
-            index = jnp.where(pair_rel < PT, pair_rel + 1, NB + 1 + pair_rel - PT)
-            last = pair_rel - 2
-            before = jnp.where(last < PT, last + 1, NB + 1 + last - PT)
-            before = jnp.where(last < 0, jnp.where(put == 0, 0, NB), before)
-            rb.cores_sent(before, put)
+            put = turn % 2
+            index = put * NB + 1 + turn // 2
+            rb.cores_sent(index - 1, put)
             both = jnp.concatenate([dk[:, lanes], dv[:, lanes]], axis=1)
             for y in range(chips):
                 mine = slice(y * 2 * S, (y + 1) * 2 * S)
-                gkv = dot(nt[mine, :], both).astype(BF16)
-                rb.mine[put, y, :, :, 128:] = gkv.reshape(2, S, 256)
-                gqw = dot(own_nt[mine, :], dq[:, lanes]).astype(BF16)
-                rb.mine[put, y, :, :, :128] = gqw.reshape(2, S, 128)
+                rb.mine[put, mine, 128:] = dot(nt[mine, :], both).astype(BF16)
+                rb.mine[put, mine, :128] = dot(own_nt[mine, :], dq[:, lanes]).astype(BF16)
             rb.cores_send(index, put)
 
-        return carry
-
-    lax.fori_loop(0, G * dm.PAIRS, attend, 0)
-    last_pair = TP * PT - 1
-    wq_load.wait()
+        return g
+
     w = ring
 
     def project(rows):
@@ -1142,63 +1165,123 @@
             total += dot_nt(dv[rows, t * HC : (t + 1) * HC], w[t, :, 2 * HC : 3 * HC])
         return total
 
-    def block_rows(b):
-        return pl.ds(pl.multiple_of(b * G * PB, G * PB), G * PB)
-
-    def to_mate(k):
-        b = p.ctx_after(k) * 2 + 1 - p.core
-        return ra.copy(dk.at[block_rows(b), :], dxm.at[k], m_send.at[k], m_recv.at[k], p.mate())
-
-    def to_plane(k):
-        b = p.ctx_after(k) * 2 + p.core
+    NCONT = NT - NP
+    gain_one = ln[0:1, :]
+    halves = lambda core, g: pl.ds(pl.multiple_of(core * NCONT + g * NCH, 16), NCH)
+
+    def dx_at(g, k, first, count):
+        c = p.ctx_after(k)
+        if g == G - 1:
+            return dk.at[pl.ds(pl.multiple_of(g * R + c * 2 * PB + first, PB), count), :]
+        fit = D // (2 * PB)
+        row = pl.multiple_of(c % fit * 2 * PB + first, PB)
+        return ra.mine.at[c // fit, pl.ds(row, count), pl.ds(0, D)]
+
+    def dx_rows(g, k, core):
+        return dx_at(g, k, core * PB, PB)
+
+    def to_mate(g, k):
+        i = g * p.ctxs + k
+        return ra.copy(dx_rows(g, k, 1 - p.core), dxm.at[i], m_send.at[i], m_recv.at[i], p.mate())
+
+    def to_plane(g, k):
+        i = g * (p.ctxs - 1) + k - 1
         return ra.copy(
-            dk.at[block_rows(b), :],
-            dxz.at[k - 1],
-            z_send.at[k - 1],
-            z_recv.at[k - 1],
-            p.at(ctx=p.ctx_after(k)),
+            dx_rows(g, k, p.core), dxz.at[i], z_send.at[i], z_recv.at[i], p.at(ctx=p.ctx_after(k))
         )
 
-    def planes(i, carry):
-        k = lax.rem(i + 1, p.ctxs)
-        rows = block_rows(p.ctx_after(k) * 2 + 1 - p.core)
-        dk[rows, :] = project(rows).astype(BF16)
-        to_mate(k).start()
-        rows = block_rows(p.ctx_after(k) * 2 + p.core)
-        part = project(rows)
-        to_mate(k).wait_recv()
-        dk[rows, :] = (part + dxm[k].astype(F32)).astype(BF16)
-
-        @pl.when(k > 0)
+    def each_group(g, step):
+        for e in range(G):
+
+            @pl.when(g == e)
+            def _():
+                step(e)
+
+    def cont_copy(g):
+        return ra.copy(
+            blk_away.at[halves(1 - p.core, g), :],
+            dxcm.at[pl.ds(pl.multiple_of(g * NCH, 16), NCH), :],
+            c_send.at[g],
+            c_recv.at[g],
+            p.mate(),
+        )
+
+    def group(g, carry):
+        lax.fori_loop(0, dm.PAIRS, attend, g)
+
+        @pl.when(g == 0)
         def _():
-            to_plane(k).start()
-
-        run_when(i, "p")
+            wq_load.wait()
+            ra.cores_sent(n_a - 1, 0)
+            ra.cores_sent(2 * n_a - 1, 1)
+
+            @pl.when(p.core != p.tp)
+            def _():
+                away.wait_send()
+
+        def planes(i, carry):
+            k = lax.rem(i + 1, p.ctxs)
+            both = pl.ds(pl.multiple_of(g * R + p.ctx_after(k) * 2 * PB, 2 * PB), 2 * PB)
+            total = project(both).astype(BF16)
+
+            def out(e):
+                dx_at(e, k, 0, 2 * PB)[...] = total
+                to_mate(e, k).start()
+
+            each_group(g, out)
+            run_when(g * p.ctxs + i, "p")
+
+            def back(e):
+                to_mate(e, k).wait_recv()
+                mine = dx_rows(e, k, p.core)
+                mine[...] = (mine[...].astype(F32) + dxm[e * p.ctxs + k].astype(F32)).astype(BF16)
+
+                @pl.when(k > 0)
+                def _():
+                    to_plane(e, k).start()
+
+            each_group(g, back)
+            return carry
+
+        lax.fori_loop(0, p.ctxs, planes, 0)
+        rows = pl.ds(pl.multiple_of(g * R + dm.P, CL), NX)
+        total = project(rows).astype(BF16)
+        for c in range(dm.NC):
+            for e in range(2):
+                out = pl.ds(pl.multiple_of(e * NCONT + g * NCH + c * dm.CH, dm.CH), dm.CH)
+                blk_away[out, :] = total[c * CL + e * dm.CH : c * CL + (e + 1) * dm.CH]
+        cont_copy(g).start()
+        for first, count in ((g * PB, PB), (NP + g * NCH, NCH)):
+            rows = pl.ds(pl.multiple_of(first, 16), count)
+            total = dot_nt(dq[rows, :HC], w[0, :, :HC])
+            for t in range(1, TP):
+                total += dot_nt(dq[rows, t * HC : (t + 1) * HC], w[t, :, :HC])
+            blk[rows, :] = total
         return carry
 
-    lax.fori_loop(0, p.ctxs, planes, 0)
-
-    NCONT = NT - NP
-
-    @pl.when(p.core != p.tp)
-    def _():
-        away.wait_send()
-
-    def cont_rows(i, carry):
-        rows = pl.ds(pl.multiple_of(G * dm.P + i * CL, CL), CL)
-        total = project(rows).astype(BF16)
-        out = pl.ds(pl.multiple_of(i * dm.CH, dm.CH), dm.CH)
-        blk_away[out, :] = total[: dm.CH]
-        blk_away[pl.ds(pl.multiple_of(NCONT + i * dm.CH, dm.CH), dm.CH), :] = total[dm.CH :]
-        return carry
-
-    lax.fori_loop(0, G * dm.NC, cont_rows, 0)
-    halves = lambda core: pl.ds(pl.multiple_of(core * NCONT, 16), NCONT)
-    dxcm = nt.at[pl.ds(0, NCONT), pl.ds(0, D)]
-    cont_copy = ra.copy(blk_away.at[halves(1 - p.core), :], dxcm, c_send, c_recv, p.mate())
-    cont_copy.start()
-    rb.cores_sum(wslab(last_pair), last_pair % 2)
-    rb.cross_sum(NB - 1)
+    def enter_back(gn, x, rows):
+        gn += blk[rows, :]
+        hat, scale = norm_stats(x.astype(F32))
+        gatt[rows, :] = (resid[rows, :] + norm_back(gn, gain_one, hat, scale)).astype(BF16)
+        sm[7:8, :] += jnp.sum(gn * hat, axis=0, keepdims=True)
+        sm[8:9, :] += jnp.sum(gn, axis=0, keepdims=True)
+
+    def gin_away(part):
+        rows = pl.ds(0, NP) if part == 0 else pl.ds(NP, NT - NP)
+        return ra.copy(gatt.at[rows, :], gin_home.at[rows, :], g_send.at[part], g_recv.at[part], p.partner())
+
+    def give(part):
+        rows = slice(0, NP) if part == 0 else slice(NP, NT)
+
+        @pl.when(p.core != p.tp)
+        def _():
+            gin_away(part).start()
+
+        @pl.when(p.core == p.tp)
+        def _():
+            gin_home[rows, :] = gatt[rows, :]
+
+    lax.fori_loop(0, G, group, 0)
     homes = []
     for i, (a, c) in enumerate(
         [(home_arrays_p, home_arrays_c)]
@@ -1209,48 +1292,14 @@
         homes.append(pltpu.make_async_copy(c, dv.at[pl.ds(i * NT + NP, NT - NP), :], home_sem.at[1, i]))
     begin(homes)
 
-    def project_q(i, carry):
-        rows = shifted(0, i * STEP)
-        total = dot_nt(dq[rows, :HC], w[0, :, :HC])
-        for t in range(1, TP):
-            total += dot_nt(dq[rows, t * HC : (t + 1) * HC], w[t, :, :HC])
-        blk[rows, :] = total
+    def cont_back(g, carry):
+        cont_copy(g).wait_recv()
+        here = pl.ds(pl.multiple_of(g * NCH, 16), NCH)
+        gn = blk_away[halves(p.core, g), :].astype(F32) + dxcm[here, :].astype(F32)
+        enter_back(gn, own_c[here, :], pl.ds(pl.multiple_of(NP + g * NCH, 16), NCH))
         return carry
 
-    lax.fori_loop(0, NT // STEP, project_q, 0)
-    gain_one = ln[0:1, :]
-    cont_copy.wait_recv()
-    def enter_back(gn, x, row):
-        rows = shifted(0, row)
-        gn += blk[rows, :]
-        hat, scale = norm_stats(x.astype(F32))
-        gatt[rows, :] = (resid[rows, :] + norm_back(gn, gain_one, hat, scale)).astype(BF16)
-        sm[7:8, :] += jnp.sum(gn * hat, axis=0, keepdims=True)
-        sm[8:9, :] += jnp.sum(gn, axis=0, keepdims=True)
-
-    def cont_back(i, carry):
-        rows = shifted(0, i * STEP)
-        mine = blk_away[shifted(p.core * NCONT, i * STEP), :].astype(F32)
-        enter_back(mine + dxcm[rows, :].astype(F32), own_c[rows, :], NP + i * STEP)
-        return carry
-
-    lax.fori_loop(0, NCONT // STEP, cont_back, 0)
-
-    def gin_away(part):
-        rows = pl.ds(0, NP) if part == 0 else pl.ds(NP, NT - NP)
-        return ra.copy(gatt.at[rows, :], gin_home.at[rows, :], g_send.at[part], g_recv.at[part], p.partner())
-
-    def give(part):
-        rows = slice(0, NP) if part == 0 else slice(NP, NT)
-
-        @pl.when(p.core != p.tp)
-        def _():
-            gin_away(part).start()
-
-        @pl.when(p.core == p.tp)
-        def _():
-            gin_home[rows, :] = gatt[rows, :]
-
+    lax.fori_loop(0, G, cont_back, 0)
     give(1)
 
     ready(homes)
@@ -1276,32 +1325,27 @@
         pltpu.make_async_copy(blk_home.at[pl.ds(NP, NT - NP), :], out_c, put_sem.at[1]),
     ]
     begin(puts)
-    for kind, when in sorted(key for key in during if key[0] == "t"):
-        if when < 10:
-            for step in during[kind, when]:
-                step()
-    for k in range(1, p.ctxs):
-        to_plane(k).wait_recv()
-
-    def prompt_back(i, carry):
-        rows = shifted(0, i * STEP)
-        gn = dk[shifted(block * NP, i * STEP), :].astype(F32)
+    for when in range(10):
+        for step in during.get(("t", when), []):
+            step()
+
+    for g in range(G):
+        gn = dx_rows(g, 0, p.core)[...].astype(F32)
         for k in range(1, p.ctxs):
-            gn += dxz[k - 1, rows, :].astype(F32)
-        enter_back(gn, own_p[rows, :], i * STEP)
-        return carry
-
-    lax.fori_loop(0, NP // STEP, prompt_back, 0)
+            to_plane(g, k).wait_recv()
+            gn += dxz[g * (p.ctxs - 1) + k - 1].astype(F32)
+        here = slice(g * PB, (g + 1) * PB)
+        enter_back(gn, own_p[here, :], here)
     give(0)
-    for kind, when in sorted(key for key in during if key[0] == "t"):
-        if when >= 10:
-            for step in during[kind, when]:
-                step()
+    for when in range(10, 20):
+        for step in during.get(("t", when), []):
+            step()
     small_out[...] = small_sum(
         p, sm, sm_near, sm_rows, sm_across, sm_planes, sm_ss, sm_rc, sm_ry, sm_rx, sm_rz
     )
     gu_puts = []
     for j in range(n_a):
+        ra.ctx_end(j)
         total = ra.result(j)
         gd_out[j * T : (j + 1) * T, :] = total[:, T:].T
         if len(gu_puts) > 0:
@@ -1315,7 +1359,7 @@
         gu_puts[-1].start()
     gu_puts[-1].wait()
     for j in range(NB):
-        rb.ctx_out(j)
+        rb.ctx_end(j)
         total = rb.result(j)
         if j == 0:
             go_out[...] = total.T
@@ -1336,15 +1380,14 @@
     ]
     begin(more)
     ready(puts + more)
-    for i in range(2 * n_a - 2, 2 * n_a):
-        ra.cores_sent(i, i % 2)
-    for pr in (last_pair - 1, last_pair):
-        rb.cores_sent(wslab(pr), pr % 2)
-    for k in range(p.ctxs):
-        to_mate(k).wait_send()
-    for k in range(1, p.ctxs):
-        to_plane(k).wait_send()
-    cont_copy.wait_send()
+    rb.cores_sent(NB - 1, 0)
+    rb.cores_sent(2 * NB - 1, 1)
+    for g in range(G):
+        for k in range(p.ctxs):
+            to_mate(g, k).wait_send()
+        for k in range(1, p.ctxs):
+            to_plane(g, k).wait_send()
+        cont_copy(g).wait_send()
     ra.drain()
     rb.drain()
 
@@ -1423,7 +1466,7 @@
         in_specs=[vmem] * 5 + [any_],
         out_specs=(vmem,) * 7 + (any_, vmem, any_),
         scratch_shapes=[
-            pltpu.VMEM((PROMPT, 2 * PB), F32),
+            pltpu.VMEM((PROMPT, PB), F32),
             pltpu.VMEM((dm.NX, 2 * dm.NCH), F32),
             pltpu.VMEM((PROMPT, dm.COLS), F32),
             pltpu.VMEM((G * R, D), BF16),
@@ -1445,8 +1488,8 @@
         name="forward",
     )(own_p, own_c, cos, sin, wq_shard, wm_shard)
     T = 512 if FC % 512 == 0 else 256
-    plan_a = [j == 0 for j in range(FC // T)]
-    plan_b = [True] * (1 + dm.PAIRS // TP)
+    plan_a = [j == 1 for j in range(FC // T)]
+    plan_b = [j < dm.PAIRS // TP for j in range(1 + dm.PAIRS // TP)]
     far = max(chips - 1, 1)
     rows = lambda x: x.reshape(-1, D)
     out_p, out_c, gin_p, gin_c, gq, go, gu, gd, small = pl.pallas_call(
@@ -1473,15 +1516,16 @@
             pltpu.VMEM((NT, D), BF16),
             pltpu.VMEM((D, G * R), BF16),
             pltpu.VMEM((D, NT), BF16),
-            pltpu.VMEM((PROMPT, 2 * PB), F32),
+            pltpu.VMEM((PROMPT, PB), F32),
             pltpu.VMEM((dm.NX, 2 * dm.NCH), F32),
             pltpu.VMEM((2, R, 128), BF16),
             pltpu.VMEM((2, R, 128), BF16),
             pltpu.VMEM((G * R, D), BF16),
             pltpu.VMEM((G * R, D), BF16),
             pltpu.VMEM((NT, D), BF16),
-            pltpu.VMEM((ctxs, G * PB, D), BF16),
-            pltpu.VMEM((ctxs - 1, G * PB, D), BF16),
+            pltpu.VMEM((G * ctxs, PB, D), BF16),
+            pltpu.VMEM((G * (ctxs - 1), PB, D), BF16),
+            pltpu.VMEM((NT - NP, D), BF16),
             pltpu.VMEM((max(NT, 2 * (NT - NP)), D), BF16),
             pltpu.VMEM((NT, D), BF16),
             pltpu.VMEM((NT, D), BF16),
@@ -1496,12 +1540,12 @@
             dma,
             dma((2,)),
             dma((2,)),
-            dma((ctxs,)),
-            dma((ctxs,)),
-            dma((ctxs - 1,)),
-            dma((ctxs - 1,)),
-            dma,
-            dma,
+            dma((G * ctxs,)),
+            dma((G * ctxs,)),
+            dma((G * (ctxs - 1),)),
+            dma((G * (ctxs - 1),)),
+            dma((G,)),
+            dma((G,)),
             pltpu.VMEM((16, D), F32),
             pltpu.VMEM((16, D), F32),
             pltpu.VMEM((chips, 16, D), F32),

time: 348 us -> 321 us (0.922)
  Pallas kernels: 306 us -> 279 us
    pallas_call x1, Pallas kernels: 201 us -> 174 us  [per_device(): pl.pallas_call(partial(backward_kernel, dm, T, FC, plan_a, plan_b), out_s...]
  transfers between devices with their start and end apart: 4 -> 4, of which waited for: 0 -> 0; matrix products, arithmetic and copies ran while one was open for 3% -> 3% of each run, Pallas kernels for 30% -> 33%
where the time goes in v5:
time: 321 us; the launch traced here: 319 us
  Pallas kernels  279 us (87%)
  starting transfers between devices  17.9 us (6%)
  local copies, waits for them, and re-layouts  15.8 us (5%)
  other arithmetic  5.91 us (2%)
    pallas_call x1, Pallas kernels, per_device(): pl.pallas_call(partial(backward_kernel, dm, T, FC, plan_a, plan_b), out_s...  174 us
    pallas_call x1, Pallas kernels, per_device(): pl.pallas_call(partial(forward_kernel, dm), out_shape=(sds((D, G * R), BF...  105 us
    ppermute x4, starting transfers between devices, trade(): return lax.ppermute(x, ('dp', 'tp'), swap)  17.9 us
    unnamed x27, local copies, waits for them, and re-layouts  7.86 us
  transfers between devices with their start and end apart: 4, of which 0 were waited for; matrix products, arithmetic and copies ran while one was open for 3% of the time, Pallas kernels for 33%

profile of v5, /device:TPU:0, one launch (start us, length us, event | category | flops | bytes accessed | tf_op | source)
XLA Modules:
  0.0 319.5 jit_solution(4095811623925862950)
XLA Ops:
  0.6 4.5 %collective-permute-start = (bf16[2,128,768]{2,1,0:T(8,128)(2,1)}, bf16[2,128,768]{2,1,0:T(8,128)(2,1)}, u32[]{:S(2)}, u32[]{:S(2)}) collective-permute-start(bf16[2,128,768]{2,1,0:T(8,128)(2,1)} %param.17), channel_id=1, source_target_pairs={{0,0},{1,8},{8,1},{9,9},{16,16},{17,24},{24,17},{25,25},{2,2},{3,1... | collective-permute-start | bytes 1179656 | tf_op jit(solution)/shard_map/ppermute | solution.py:1432
  5.1 4.5 %collective-permute-start.1 = (bf16[2,2,64,768]{3,2,1,0:T(8,128)(2,1)}, bf16[2,2,64,768]{3,2,1,0:T(8,128)(2,1)}, u32[]{:S(2)}, u32[]{:S(2)}) collective-permute-start(bf16[2,2,64,768]{3,2,1,0:T(8,128)(2,1)} %param.18), channel_id=1, source_target_pairs={{0,0},{1,8},{8,1},{9,9},{16,16},{17,24},{24,17},{25,25},{2,2},{3,1... | collective-permute-start | bytes 1179656 | tf_op jit(solution)/shard_map/ppermute | solution.py:1432
  9.6 4.5 %collective-permute-start.2 = (bf16[2,128,768]{2,1,0:T(8,128)(2,1)}, bf16[2,128,768]{2,1,0:T(8,128)(2,1)}, u32[]{:S(2)}, u32[]{:S(2)}) collective-permute-start(bf16[2,128,768]{2,1,0:T(8,128)(2,1)} %param.32), channel_id=1, source_target_pairs={{0,0},{1,8},{8,1},{9,9},{16,16},{17,24},{24,17},{25,25},{2,2},{3,1... | collective-permute-start | bytes 1179656 | tf_op jit(solution)/shard_map/ppermute | solution.py:1432
  14.1 4.5 %collective-permute-start.3 = (bf16[2,2,64,768]{3,2,1,0:T(8,128)(2,1)}, bf16[2,2,64,768]{3,2,1,0:T(8,128)(2,1)}, u32[]{:S(2)}, u32[]{:S(2)}) collective-permute-start(bf16[2,2,64,768]{3,2,1,0:T(8,128)(2,1)} %param.33), channel_id=1, source_target_pairs={{0,0},{1,8},{8,1},{9,9},{16,16},{17,24},{24,17},{25,25},{2,2},{3,1... | collective-permute-start | bytes 1179656 | tf_op jit(solution)/shard_map/ppermute | solution.py:1432
  18.6 0.0 copy-start.2
  18.6 0.0 copy-start.3
  18.6 0.0 copy-start.9
  18.6 1.2 copy.48
  19.8 0.7 stack.15
  20.4 0.7 stack.16
  21.1 0.7 stack.17
  21.7 0.7 stack.18
  22.4 0.1 copy.43
  22.6 0.8 fusion.1.wq
  23.4 3.3 %negate_select_fusion = (f32[1152,128]{1,0:T(8,128)}, f32[1152,128]{1,0:T(8,128)}) fusion(f32[128]{0:T(128)S(1)} %fusion.5, f32[1152]{0:T(1024)S(1)} %iota_convert_fusion, pred[128]{0:T(512)(128)(4,1)S(1)} %fusion.6), kind=kLoop, calls=%fused_computation.4 | loop fusion | flops 442368 | bytes 1184896 | tf_op jit(solution)/shard_map/jit(_where)/select_n | solution.py:1447
  26.7 0.0 copy-done.2
  26.7 0.0 copy-done.3
  26.7 0.0 copy-done.9
  26.7 1.2 pad_maximum_fusion.wm
  27.8 0.0 collective-permute-done.op
  27.8 0.0 collective-permute-done.1.oc
  27.8 104.7 %forward.1 = (bf16[768,2560]{1,0:T(8,128)(2,1)}, bf16[768,512]{1,0:T(8,128)(2,1)}, bf16[2,1280,768]{2,1,0:T(8,128)(2,1)}, bf16[2,1280,768]{2,1,0:T(8,128)(2,1)},...) custom-call(bf16[2,128,768]{2,1,0:T(8,128)(2,1)} %collective-permute, ...), custom_call_target="tpu_custom_call" | custom-call | tf_op jit(solution)/shard_map/forward/pallas_call | solution.py:1452
  132.5 0.0 collective-permute-done.2
  132.5 0.0 collective-permute-done.3
  132.5 174.4 %backward.1 = (bf16[256,768]{1,0:T(8,128)(2,1)}, bf16[256,768]{1,0:T(8,128)(2,1)}, bf16[256,768]{1,0:T(8,128)(2,1)}, bf16[256,768]{1,0:T(8,128)(2,1)}, f32[192,1...) custom-call(f32[5]{0:T(128)} %mix.1, ...), custom_call_target="tpu_custom_call" | custom-call | tf_op jit(solution)/shard_map/backward/pallas_call | solution.py:1495
  307.0 0.0 copy-start.1
  307.0 0.8 slice.22
  307.8 0.7 slice.23
  308.5 2.9 copy.46
  311.4 0.0 copy-start.7
  311.4 0.0 copy-done.1
  311.4 0.0 copy-start.6
  311.4 1.0 copy.50
  312.4 0.0 copy-start.5
  312.4 0.1 copy-done.8
  312.5 0.9 copy.45
  313.3 0.6 maximum_reduce_fusion
  314.0 1.5 fusion.7
  315.4 0.0 copy-done.7
  315.4 0.7 copy.56
  316.2 0.0 copy-done.6
  316.2 0.7 copy.57
  316.9 0.0 copy-done.5
  316.9 0.7 copy.58
  317.7 0.0 copy-done.4
  317.7 0.7 copy.59
  318.4 0.0 copy-done
  318.4 1.0 copy.60
  (7 shorter events, 0.0 us)
Async XLA Ops:
  0.6 27.2 %collective-permute-start = (bf16[2,128,768]{2,1,0:T(8,128)(2,1)}, bf16[2,128,768]{2,1,0:T(8,128)(2,1)}, u32[]{:S(2)}, u32[]{:S(2)}) collective-permute-start(bf16[2,128,768]{2,1,0:T(8,128)(2,1)} %param.17), channel_id=1, source_target_pairs={{0,0},{1,8},{8,1},{9,9},{16,16},{17,24},{24,17},{25,25},{2,2},{3,1... | collective-permute-start | bytes 1179656 | tf_op jit(solution)/shard_map/ppermute | solution.py:1432
  5.1 22.7 %collective-permute-start.1 = (bf16[2,2,64,768]{3,2,1,0:T(8,128)(2,1)}, bf16[2,2,64,768]{3,2,1,0:T(8,128)(2,1)}, u32[]{:S(2)}, u32[]{:S(2)}) collective-permute-start(bf16[2,2,64,768]{3,2,1,0:T(8,128)(2,1)} %param.18), channel_id=1, source_target_pairs={{0,0},{1,8},{8,1},{9,9},{16,16},{17,24},{24,17},{25,25},{2,2},{3,1... | collective-permute-start | bytes 1179656 | tf_op jit(solution)/shard_map/ppermute | solution.py:1432
  9.6 122.9 %collective-permute-start.2 = (bf16[2,128,768]{2,1,0:T(8,128)(2,1)}, bf16[2,128,768]{2,1,0:T(8,128)(2,1)}, u32[]{:S(2)}, u32[]{:S(2)}) collective-permute-start(bf16[2,128,768]{2,1,0:T(8,128)(2,1)} %param.32), channel_id=1, source_target_pairs={{0,0},{1,8},{8,1},{9,9},{16,16},{17,24},{24,17},{25,25},{2,2},{3,1... | collective-permute-start | bytes 1179656 | tf_op jit(solution)/shard_map/ppermute | solution.py:1432
  14.1 118.5 %collective-permute-start.3 = (bf16[2,2,64,768]{3,2,1,0:T(8,128)(2,1)}, bf16[2,2,64,768]{3,2,1,0:T(8,128)(2,1)}, u32[]{:S(2)}, u32[]{:S(2)}) collective-permute-start(bf16[2,2,64,768]{3,2,1,0:T(8,128)(2,1)} %param.33), channel_id=1, source_target_pairs={{0,0},{1,8},{8,1},{9,9},{16,16},{17,24},{24,17},{25,25},{2,2},{3,1... | collective-permute-start | bytes 1179656 | tf_op jit(solution)/shard_map/ppermute | solution.py:1432
  18.6 8.1 %copy-start.2 = (bf16[1536,192]{0,1:T(8,128)(2,1)S(1)}, bf16[1536,192]{0,1:T(8,128)(2,1)}, u32[]{:S(2)}) copy-start(bf16[1536,192]{0,1:T(8,128)(2,1)} %param.30) | copy-start | bytes 1769476
  18.6 8.1 %copy-start.3 = (bf16[192,1536]{1,0:T(8,128)(2,1)S(1)}, bf16[192,1536]{1,0:T(8,128)(2,1)}, u32[]{:S(2)}) copy-start(bf16[192,1536]{1,0:T(8,128)(2,1)} %param.29) | copy-start | bytes 1769476
  18.6 8.1 %copy-start.9 = (bf16[384,192]{0,1:T(8,128)(2,1)S(1)}, bf16[384,192]{0,1:T(8,128)(2,1)}, u32[]{:S(2)}) copy-start(bf16[384,192]{0,1:T(8,128)(2,1)} %param.28) | copy-start | bytes 442372
  307.0 4.5 %copy-start.1 = (f32[192,1152]{1,0:T(8,128)S(1)}, f32[192,1152]{1,0:T(8,128)}, u32[]{:S(2)}) copy-start(f32[192,1152]{1,0:T(8,128)} %get-tuple-element.47) | copy-start | bytes 2654212
  311.4 1.1 copy-start.8
  311.4 4.0 %copy-start.7 = (bf16[256,768]{1,0:T(8,128)(2,1)S(1)}, bf16[256,768]{1,0:T(8,128)(2,1)}, u32[]{:S(2)}) copy-start(bf16[256,768]{1,0:T(8,128)(2,1)} %get-tuple-element.42) | copy-start | bytes 1179652
  311.4 4.8 %copy-start.6 = (bf16[256,768]{1,0:T(8,128)(2,1)S(1)}, bf16[256,768]{1,0:T(8,128)(2,1)}, u32[]{:S(2)}) copy-start(bf16[256,768]{1,0:T(8,128)(2,1)} %get-tuple-element.43) | copy-start | bytes 1179652
  312.4 4.6 %copy-start.5 = (bf16[256,768]{1,0:T(8,128)(2,1)S(1)}, bf16[256,768]{1,0:T(8,128)(2,1)}, u32[]{:S(2)}) copy-start(bf16[256,768]{1,0:T(8,128)(2,1)} %get-tuple-element.44) | copy-start | bytes 1179652
  312.4 5.3 %copy-start.4 = (bf16[256,768]{1,0:T(8,128)(2,1)S(1)}, bf16[256,768]{1,0:T(8,128)(2,1)}, u32[]{:S(2)}) copy-start(bf16[256,768]{1,0:T(8,128)(2,1)} %get-tuple-element.45) | copy-start | bytes 1179652
  315.4 3.0 copy-start

commit v6 on v5

--- a/solution.py
+++ b/solution.py
@@ -184,28 +184,30 @@
 
 
 class WeightGather:
-    def __init__(self, peers, shard, full, sends, across, rows, mate):
-        self.p, self.shard, self.full = peers, shard, full
+    def __init__(self, peers, shard, full, left, sends, across, rows, mate):
+        self.p, self.shard, self.full, self.left = peers, shard, full, left
         self.sends, self.across, self.rows, self.from_mate = sends, across, rows, mate
         self.copies = []
-        self.count = 0
-        self.size = shard.shape[0]
+        self.size, self.cols = shard.shape
 
     @staticmethod
     def semaphores(chips):
+        far = chips - 1
         return [
-            pltpu.SemaphoreType.DMA((1 + 2 * (chips - 1) + 2 * chips,)),
-            pltpu.SemaphoreType.DMA((1,)),
-            pltpu.SemaphoreType.DMA((2, max(chips - 1, 1))),
+            pltpu.SemaphoreType.DMA((3 + 6 * far,)),
+            pltpu.SemaphoreType.DMA((chips,)),
+            pltpu.SemaphoreType.DMA((2, max(far, 1))),
             pltpu.SemaphoreType.DMA((2, chips)),
         ]
 
-    def piece(self, tp, dp):
-        return self.full.at[tp, pl.ds(pl.multiple_of(dp * self.size, 16), self.size), :]
+    def piece(self, tp, dp, cols=slice(None)):
+        rows = pl.ds(pl.multiple_of(dp * self.size, 16), self.size)
+        if cols == slice(None):
+            return self.full.at[tp, rows, :]
+        return self.full.at[tp, rows, pl.ds(cols.start, cols.stop - cols.start)]
 
     def go(self, src, dst, recv_sem, device):
-        self.copies.append(send(src, dst, self.sends.at[self.count], recv_sem, device))
-        self.count += 1
+        self.copies.append(send(src, dst, self.sends.at[len(self.copies)], recv_sem, device))
 
     def start(self):
         p = self.p
@@ -218,17 +220,32 @@
         p = self.p
         got = self.piece(1 - p.tp, p.dp)
         arrived(got, self.across.at[0], p)
+        part = self.piece(1 - p.tp, p.dp, slice(0, self.left))
         for k in range(1, p.chips):
-            self.go(got, got, self.rows.at[1, k - 1], p.row(k))
+            self.go(part, part, self.rows.at[1, k - 1], p.row(k))
         self.go(got, got, self.from_mate.at[1, 0], p.mate())
 
-    def relay_rows(self, part):
+    def relay_rows(self):
         p = self.p
-        tp = p.tp if part == 0 else 1 - p.tp
         for k in range(1, p.chips):
-            got = self.piece(tp, p.chip_before(k) * 2 + p.core)
-            arrived(got, self.rows.at[part, k - 1], p)
-            self.go(got, got, self.from_mate.at[part, k], p.mate())
+            dp = p.chip_before(k) * 2 + p.core
+            got = self.piece(p.tp, dp)
+            arrived(got, self.rows.at[0, k - 1], p)
+            if self.left < self.cols:
+                part = self.piece(p.tp, dp, slice(self.left, self.cols))
+                self.go(part, part, self.across.at[k], p.across())
+            self.go(got, got, self.from_mate.at[0, k], p.mate())
+
+    def relay_last(self):
+        p = self.p
+        for k in range(1, p.chips):
+            dp = p.chip_before(k) * 2 + p.core
+            arrived(self.piece(1 - p.tp, dp, slice(0, self.left)), self.rows.at[1, k - 1], p)
+            if self.left < self.cols:
+                part = self.piece(1 - p.tp, dp, slice(self.left, self.cols))
+                arrived(part, self.across.at[k], p)
+            got = self.piece(1 - p.tp, dp)
+            self.go(got, got, self.from_mate.at[1, k], p.mate())
 
     def finish(self):
         p = self.p
@@ -290,22 +307,33 @@
 
 def forward_kernel(
     dm,
-    op,
-    oc,
+    left,
+    prompt,
+    cont,
     cos,
     sin,
     wq,
     wm,
+    cot_p,
+    cot_c,
+    q_out,
+    att_out,
+    lse_out,
+    ln_out,
+    nt_hbm,
+    own_nt_hbm,
+    k_hbm,
+    v_hbm,
+    w_hbm,
+    wm_out,
+    own_p_hbm,
+    own_c_hbm,
+    cot_p_out,
+    cot_c_out,
     nt_out,
     own_out,
     k_out,
     v_out,
-    q_out,
-    att_out,
-    lse_out,
-    w_out,
-    ln_out,
-    wm_out,
     maskp,
     maskx,
     sbuf,
@@ -315,6 +343,8 @@
     xc,
     w,
     put_sem,
+    trade_send,
+    trade_recv,
     x_send,
     x_plane,
     x_mate,
@@ -323,40 +353,87 @@
     own_sem,
     *sems,
 ):
-    G, R, PB, NCH, D = dm.G, dm.R, dm.PB, dm.NCH, dm.D
+    G, R, PB, NCH, D, NP, NT = dm.G, dm.R, dm.PB, dm.NCH, dm.D, dm.NP, dm.NT
+    NC, CH = dm.NC, dm.CH
     HC = (w.shape[2] - 128) // 3
     TP = w.shape[0]
     p = Peers()
     block = block_index()
-    gq = WeightGather(p, wq, w, *sems[:4])
-    gm = WeightGather(p, wm, wm_out, *sems[4:])
+    gq = WeightGather(p, wq, w, wq.shape[1], *sems[:4])
+    gm = WeightGather(p, wm, wm_out, left, *sems[4:])
     size = wq.shape[0]
     mine = pl.ds(pl.multiple_of(p.dp * size, 16), size)
+
+    landing = [xp.at[p.ctx * 2 + p.tp], xc.at[p.tp], cot_p_out, cot_c_out]
+
+    def moved(i):
+        src = [prompt, cont, cot_p, cot_c][i]
+        return pltpu.make_async_remote_copy(
+            src_ref=src,
+            dst_ref=landing[i],
+            send_sem=trade_send.at[i],
+            recv_sem=trade_recv.at[i],
+            device_id=p.partner(),
+            device_id_type=MESH,
+        )
+
+    def kept(i):
+        return pltpu.make_async_copy([prompt, cont, cot_p, cot_c][i], landing[i], trade_send.at[i])
+
+    moves = p.core != p.tp
+
+    def trade(i):
+        @pl.when(moves)
+        def _():
+            moved(i).start()
+
+        @pl.when(jnp.logical_not(moves))
+        def _():
+            kept(i).start()
+
+    def traded(i):
+        @pl.when(moves)
+        def _():
+            moved(i).wait_recv()
+
+        @pl.when(jnp.logical_not(moves))
+        def _():
+            kept(i).wait()
+
     local = [
         pltpu.make_async_copy(wq, w.at[p.tp, mine, :], own_sem.at[0]),
         pltpu.make_async_copy(wm, wm_out.at[p.tp, mine, :], own_sem.at[1]),
-        pltpu.make_async_copy(op, xp.at[block], own_sem.at[2]),
-        pltpu.make_async_copy(oc, xc.at[p.core], own_sem.at[3]),
     ]
     for copy in local:
         copy.start()
-    p.greet()
+    p.greet(trades=True)
+    trade(0)
     gq.start()
+    trade(1)
+    fill_masks(dm, maskp, maskx)
+    traded(0)
+    own = xp.at[block]
     sent = []
     for k in range(1, p.ctxs):
-        sent.append(send(op, xp.at[block], x_send.at[k - 1], x_plane.at[k - 1], p.plane(k)))
-    sent.append(send(op, xp.at[block], x_send.at[p.ctxs - 1], x_mate.at[0], p.mate()))
-    sent.append(send(oc, xc.at[p.core], c_send, c_mate, p.mate()))
-    fill_masks(dm, maskp, maskx)
+        sent.append(send(own, own, x_send.at[k - 1], x_plane.at[k - 1], p.plane(k)))
+    sent.append(send(own, own, x_send.at[p.ctxs - 1], x_mate.at[0], p.mate()))
     gq.relay_across()
-    gq.relay_rows(0)
-    gq.relay_rows(1)
+    gq.relay_rows()
+    traded(1)
+    sent.append(send(xc.at[p.core], xc.at[p.core], c_send, c_mate, p.mate()))
+    gq.relay_last()
     gm.start()
+    trade(2)
+    trade(3)
     gq.finish()
-    for copy in local:
-        copy.wait()
-    put = pltpu.make_async_copy(w, w_out, put_sem)
-    put.start()
+    local[0].wait()
+    puts = [
+        pltpu.make_async_copy(w, w_hbm, put_sem.at[0]),
+        pltpu.make_async_copy(xp.at[block], own_p_hbm, put_sem.at[1]),
+        pltpu.make_async_copy(xc.at[p.core], own_c_hbm, put_sem.at[2]),
+    ]
+    for put in puts:
+        put.start()
     ln = w[0, :, 3 * HC :].astype(F32).T[:8, :]
     ln_out[...] = ln
     gain, bias = ln[0:1, :], ln[1:2, :]
@@ -365,82 +442,83 @@
         hat, _ = norm_stats(x.astype(F32))
         return (hat * gain + bias).astype(BF16)
 
-    def queries(x, row, table):
+    def turned(x, table):
         rows = x.shape[0]
-        n = normed(x)
-        own_rows[pl.ds(row, rows), :] = n
-        c = cos[pl.ds(table, rows), :]
-        sn = sin[pl.ds(table, rows), :]
-        for t in range(TP):
-            qq = dot(n, w[t, :, :HC])
+        return rotate(x, cos[pl.ds(table, rows), :], sin[pl.ds(table, rows), :])
+
+    x = jnp.concatenate([xp[block].reshape(NP, D), xc[p.core].reshape(NT - NP, D)], axis=0)
+    n = normed(x)
+    own_rows[...] = n
+    places = [(g * PB, PB, pl.multiple_of(block * PB, PB)) for g in range(G)]
+    places += [
+        (NP + i * CH, CH, pl.multiple_of(dm.P + p.core * CH, CH)) for i in range(G * NC)
+    ]
+    for t in range(TP):
+        qq = dot(n, w[t, :, :HC])
+        for first, count, table in places:
             for j in range(HC // 128):
-                tile = rotate(qq[:, j * 128 : (j + 1) * 128], c, sn).astype(BF16)
-                q_out[pl.ds(row, rows), t * HC + j * 128 : t * HC + (j + 1) * 128] = (
+                tile = turned(qq[first : first + count, j * 128 : (j + 1) * 128], table).astype(BF16)
+                q_out[first : first + count, t * HC + j * 128 : t * HC + (j + 1) * 128] = (
                     tile.astype(F32) * 0.125
                 ).astype(BF16)
-
-    def own_prompt(g, carry):
-        queries(op[g], pl.multiple_of(g * PB, PB), pl.multiple_of(block * PB, PB))
-        return carry
-
-    lax.fori_loop(0, G, own_prompt, 0)
-
-    def own_cont(i, carry):
-        g, c = i // dm.NC, i % dm.NC
-        queries(
-            oc[g, c],
-            pl.multiple_of(dm.NP + i * dm.CH, dm.CH),
-            pl.multiple_of(dm.P + p.core * dm.CH, dm.CH),
-        )
-        return carry
-
-    lax.fori_loop(0, G * dm.NC, own_cont, 0)
     own_out[...] = transpose(own_rows[...])
 
-    def keys_values(g, x, row, table, place):
-        rows = x.shape[0]
+    def keys_values(x, places):
         n = normed(x)
-        all_rows[pl.ds(place, rows), :] = n
-        c = cos[pl.ds(table, rows), :]
-        sn = sin[pl.ds(table, rows), :]
+        for first, count, g, row, table in places:
+            all_rows[pl.ds(pl.multiple_of(g * R + row, 16), count), :] = n[first : first + count]
         for t in range(TP):
             kk = dot(n, w[t, :, HC : 2 * HC])
-            for j in range(HC // 128):
-                tile = rotate(kk[:, j * 128 : (j + 1) * 128], c, sn)
-                k_out[g, pl.ds(row, rows), t * HC + j * 128 : t * HC + (j + 1) * 128] = tile.astype(BF16)
-            v_out[g, pl.ds(row, rows), t * HC : (t + 1) * HC] = dot(n, w[t, :, 2 * HC : 3 * HC]).astype(BF16)
-
-    def block_chunk(g, b):
-        row = pl.multiple_of(b * PB, PB)
-        keys_values(g, xp[b, g], row, row, pl.multiple_of(g * R + row, PB))
+            for first, count, g, row, table in places:
+                for j in range(HC // 128):
+                    tile = turned(kk[first : first + count, j * 128 : (j + 1) * 128], table)
+                    k_out[g, pl.ds(row, count), t * HC + j * 128 : t * HC + (j + 1) * 128] = tile.astype(BF16)
+            vv = dot(n, w[t, :, 2 * HC : 3 * HC]).astype(BF16)
+            for first, count, g, row, table in places:
+                v_out[g, pl.ds(row, count), t * HC : (t + 1) * HC] = vv[first : first + count]
 
     arrived(xc.at[1 - p.core], c_mate, p)
-
-    def cont_chunk(i, carry):
-        g, c = i // dm.NC, i % dm.NC
-        row = pl.multiple_of(dm.P + c * CL, CL)
-        x = jnp.concatenate([xc[0, g, c], xc[1, g, c]], axis=0)
-        keys_values(g, x, row, dm.P, pl.multiple_of(g * R + row, CL))
-        return carry
-
-    lax.fori_loop(0, G * dm.NC, cont_chunk, 0)
+    x = [xc[e, g, c] for g in range(G) for c in range(NC) for e in range(2)]
+    keys_values(
+        jnp.concatenate(x, axis=0),
+        [((g * NC + c) * CL, CL, g, dm.P + c * CL, dm.P) for g in range(G) for c in range(NC)],
+    )
 
     def relay(k):
         b = p.ctx_before(k) * 2 + p.core
-        arrived(xp.at[b], x_plane.at[k - 1], p)
-        return send(xp.at[b], xp.at[b], x_send.at[p.ctxs + k - 1], x_mate.at[k], p.mate())
-
-    for k in range(1, p.ctxs):
-        sent.append(relay(k))
-    for k in range(p.ctxs):
-        arrived(xp.at[p.ctx_before(k) * 2 + 1 - p.core], x_mate.at[k], p)
-
-    def prompt_chunk(i, carry):
-        block_chunk(i // (2 * p.ctxs), i % (2 * p.ctxs))
+        return pltpu.make_async_remote_copy(
+            src_ref=xp.at[b],
+            dst_ref=xp.at[b],
+            send_sem=x_send.at[p.ctxs + k - 1],
+            recv_sem=x_mate.at[k],
+            device_id=p.mate(),
+            device_id_type=MESH,
+        )
+
+    def plane(k, carry):
+        c = p.ctx_before(k)
+
+        @pl.when(k > 0)
+        def _():
+            arrived(xp.at[c * 2 + p.core], x_plane.at[k - 1], p)
+            relay(k).start()
+
+        arrived(xp.at[c * 2 + 1 - p.core], x_mate.at[k], p)
+        x = xp[pl.ds(c * 2, 2)].reshape(2 * NP, D)
+        places = []
+        for e in range(2):
+            row = pl.multiple_of((c * 2 + e) * PB, PB)
+            places += [((e * G + g) * PB, PB, g, row, row) for g in range(G)]
+        keys_values(x, places)
         return carry
 
-    lax.fori_loop(0, G * 2 * p.ctxs, prompt_chunk, 0)
-    gm.relay_across()
+    lax.fori_loop(0, p.ctxs, plane, 0)
+    puts += [
+        pltpu.make_async_copy(k_out, k_hbm, put_sem.at[3]),
+        pltpu.make_async_copy(v_out, v_hbm, put_sem.at[4]),
+    ]
+    for put in puts[3:]:
+        put.start()
 
     def turn(i, carry):
         rows = pl.ds(pl.multiple_of(i * 256, 256), 256)
@@ -448,6 +526,14 @@
         return carry
 
     lax.fori_loop(0, G * R // 256, turn, 0)
+    puts += [
+        pltpu.make_async_copy(nt_out, nt_hbm, put_sem.at[5]),
+        pltpu.make_async_copy(own_out, own_nt_hbm, put_sem.at[6]),
+    ]
+    for put in puts[5:]:
+        put.start()
+    gm.relay_across()
+    gm.relay_rows()
 
     TILE = 256
     tiles = dm.P // TILE
@@ -492,14 +578,25 @@
         return carry
 
     lax.fori_loop(0, G * dm.PAIRS, attend, 0)
-    gm.relay_rows(0)
-    gm.relay_rows(1)
+    gm.relay_last()
     gm.finish()
     gq.drain()
     gm.drain()
     for copy in sent:
         copy.wait_send()
-    put.wait()
+    for k in range(1, p.ctxs):
+        relay(k).wait_send()
+    local[1].wait()
+    for i in (2, 3):
+        traded(i)
+
+    @pl.when(moves)
+    def _():
+        for i in range(4):
+            moved(i).wait_send()
+
+    for put in puts:
+        put.wait()
 
 
 class Reduce:
@@ -1426,13 +1523,6 @@
 
     sds = jax.ShapeDtypeStruct
     chips, ctxs = lax.axis_size("dp") // 2, lax.axis_size("ctx")
-    swap = [(4 * y + 2 * c + t, 4 * y + 2 * t + c) for y in range(chips) for c in (0, 1) for t in (0, 1)]
-
-    def trade(x):
-        return lax.ppermute(x, ("dp", "tp"), swap)
-
-    own_p, own_c = trade(prompt_in), trade(cont_in)
-    cot_p, cot_c = trade(prompt_cot), trade(cont_cot)
     norms = jnp.stack([ln1_gain, ln1_bias, ln2_gain, ln2_bias], axis=1)
     norms = jnp.pad(norms, ((0, 0), (0, 124)))
     wq_shard = jnp.concatenate([w_qkv.reshape(S, 3 * HC), norms], axis=1)
@@ -1449,23 +1539,32 @@
     any_ = pl.BlockSpec(memory_space=pl.ANY)
     vmem = pl.BlockSpec(memory_space=pltpu.VMEM)
     dma = pltpu.SemaphoreType.DMA
-    nt, own_nt, k, v, q, att, lse, wq, ln, wm = pl.pallas_call(
-        partial(forward_kernel, dm),
+    left = (HC + 2 * FC) // 128 * 2 // 3 * 128
+    q, att, lse, ln, nt, own_nt, k, v, wq, wm, own_p, own_c, cot_p, cot_c = pl.pallas_call(
+        partial(forward_kernel, dm, left),
         out_shape=(
+            sds((NT, D), BF16),
+            sds((NT, D), BF16),
+            sds((G * dm.PAIRS, 1, dm.COLS), F32),
+            sds((8, D), F32),
             sds((D, G * R), BF16),
             sds((D, NT), BF16),
             sds((G, R, D), BF16),
             sds((G, R, D), BF16),
-            sds((NT, D), BF16),
-            sds((NT, D), BF16),
-            sds((G * dm.PAIRS, 1, dm.COLS), F32),
             sds((TP, D, 3 * HC + 128), BF16),
-            sds((8, D), F32),
             sds((TP, D, HC + 2 * FC), BF16),
+            sds(prompt_in.shape, BF16),
+            sds(cont_in.shape, BF16),
+            sds(prompt_in.shape, BF16),
+            sds(cont_in.shape, BF16),
         ),
-        in_specs=[vmem] * 5 + [any_],
-        out_specs=(vmem,) * 7 + (any_, vmem, any_),
+        in_specs=[vmem] * 5 + [any_] * 3,
+        out_specs=(vmem,) * 4 + (any_,) * 10,
         scratch_shapes=[
+            pltpu.VMEM((D, G * R), BF16),
+            pltpu.VMEM((D, NT), BF16),
+            pltpu.VMEM((G, R, D), BF16),
+            pltpu.VMEM((G, R, D), BF16),
             pltpu.VMEM((PROMPT, PB), F32),
             pltpu.VMEM((dm.NX, 2 * dm.NCH), F32),
             pltpu.VMEM((PROMPT, dm.COLS), F32),
@@ -1474,19 +1573,21 @@
             pltpu.VMEM((2 * ctxs, G, PB, D), BF16),
             pltpu.VMEM((2, G, NC, CH, D), BF16),
             pltpu.VMEM((TP, D, 3 * HC + 128), BF16),
-            dma,
+            dma((7,)),
+            dma((4,)),
+            dma((4,)),
             dma((2 * ctxs - 1,)),
             dma((ctxs - 1,)),
             dma((ctxs,)),
             dma,
             dma,
-            dma((4,)),
+            dma((2,)),
         ]
         + WeightGather.semaphores(chips)
         + WeightGather.semaphores(chips),
         compiler_params=params(collective_id=0, has_side_effects=True),
         name="forward",
-    )(own_p, own_c, cos, sin, wq_shard, wm_shard)
+    )(prompt_in, cont_in, cos, sin, wq_shard, wm_shard, prompt_cot, cont_cot)
     T = 512 if FC % 512 == 0 else 256
     plan_a = [j == 1 for j in range(FC // T)]
     plan_b = [j < dm.PAIRS // TP for j in range(1 + dm.PAIRS // TP)]

time: 321 us -> 280 us (0.87)
  Pallas kernels: 279 us -> 260 us
  starting transfers between devices: 17.9 us -> 0 us
  local copies, waits for them, and re-layouts: 15.8 us -> 12.1 us
    ppermute x4 -> x0, starting transfers between devices: 17.9 us -> none  [trade(): return lax.ppermute(x, ('dp', 'tp'), swap)]
    pallas_call x1, Pallas kernels: 105 us -> 87.8 us  [per_device(): pl.pallas_call(partial(forward_kernel, dm, left), out_shape=(sds((NT, D),...]
    unnamed x27 -> x35, local copies, waits for them, and re-layouts: 7.86 us -> 7.88 us
  transfers between devices with their start and end apart: 4 -> 0, of which waited for: 0 -> 0; matrix products, arithmetic and copies ran while one was open for 3% -> 0% of each run, Pallas kernels for 33% -> 0%
where the time goes in v6:
time: 280 us
  Pallas kernels  260 us (93%)
  local copies, waits for them, and re-layouts  12.1 us (4%)
  other arithmetic  6.9 us (2%)
    pallas_call x1, Pallas kernels, per_device(): pl.pallas_call(partial(backward_kernel, dm, T, FC, plan_a, plan_b), out_s...  173 us
    pallas_call x1, Pallas kernels, per_device(): pl.pallas_call(partial(forward_kernel, dm, left), out_shape=(sds((NT, D),...  87.8 us
    unnamed x35, local copies, waits for them, and re-layouts  7.88 us

profile of v6, /device:TPU:0, one launch (start us, length us, event | category | flops | bytes accessed | tf_op | source)
XLA Modules:
  0.0 280.2 jit_solution(16330625536530207970)
XLA Ops:
  0.6 0.0 copy-start.2
  0.7 0.0 copy-start.3
  0.7 3.3 %negate_select_fusion = (f32[1152,128]{1,0:T(8,128)}, f32[1152,128]{1,0:T(8,128)}) fusion(f32[128]{0:T(128)S(1)} %fusion.5, f32[1152]{0:T(1024)S(1)} %iota_convert_fusion, pred[128]{0:T(512)(128)(4,1)S(1)} %fusion.6), kind=kLoop, calls=%fused_computation.4 | loop fusion | flops 442368 | bytes 1184896 | tf_op jit(solution)/shard_map/jit(_where)/select_n | solution.py:1537
  4.0 0.0 copy-start.4
  4.0 0.0 copy-done.2
  4.0 0.0 copy-done.3
  4.0 0.0 copy-start.10
  4.0 0.0 copy-start.11
  4.0 0.0 copy-start.12
  4.0 0.0 copy-start.13
  4.0 2.1 pad_maximum_fusion.wm
  6.2 0.0 copy-done.4
  6.2 0.0 copy-done.10
  6.2 0.0 copy-done.11
  6.3 0.0 copy-done.12
  6.3 0.0 copy-done.13
  6.3 0.1 copy.43
  6.5 0.8 fusion.1.wq
  7.3 87.8 %forward.1 = (bf16[512,768]{1,0:T(8,128)(2,1)}, bf16[512,768]{1,0:T(8,128)(2,1)}, f32[12,1,512]{2,1,0:T(1,128)}, f32[8,768]{1,0:T(8,128)}, bf16[768,2560]{1,0:T(...) custom-call(bf16[2,128,768]{2,1,0:T(8,128)(2,1)} %prompt.1, ...), custom_call_target="tpu_custom_call" | custom-call | tf_op jit(solution)/shard_map/forward/pallas_call | solution.py:1543
  95.1 172.5 %backward.1 = (bf16[256,768]{1,0:T(8,128)(2,1)}, bf16[256,768]{1,0:T(8,128)(2,1)}, bf16[256,768]{1,0:T(8,128)(2,1)}, bf16[256,768]{1,0:T(8,128)(2,1)}, f32[192,1...) custom-call(f32[5]{0:T(128)} %mix.1, ...), custom_call_target="tpu_custom_call" | custom-call | tf_op jit(solution)/shard_map/backward/pallas_call | solution.py:1596
  267.7 0.0 copy-start.1
  267.7 0.8 slice.22
  268.5 0.7 slice.23
  269.2 0.6 maximum_reduce_fusion
  269.9 2.9 %copy.46 = f32[1536,192]{0,1:T(8,128)} copy(f32[1536,192]{1,0:T(8,128)} %get-tuple-element.96) | data formatting | bytes 2359296
  272.7 0.0 copy-start.9
  272.7 0.0 copy-start.8
  272.7 0.0 copy-done.1
  272.8 0.0 copy-start.7
  272.8 1.0 copy.50
  273.7 0.0 copy-start.6
  273.7 0.0 copy-start.5
  273.7 0.1 copy-done.9
  273.8 0.9 copy.45
  274.7 1.5 fusion.7
  276.1 0.0 copy-done.8
  276.1 0.0 copy-start
  276.1 0.7 copy.56
  276.9 0.0 copy-done.7
  276.9 0.7 copy.57
  277.6 0.0 copy-done.6
  277.6 0.7 copy.58
  278.4 0.0 copy-done.5
  278.4 0.7 copy.59
  279.1 0.0 copy-done
  279.1 1.0 copy.60
  (9 shorter events, 0.1 us)
Async XLA Ops:
  0.6 3.3 %copy-start.2 = (bf16[1536,192]{0,1:T(8,128)(2,1)S(1)}, bf16[1536,192]{0,1:T(8,128)(2,1)}, u32[]{:S(2)}) copy-start(bf16[1536,192]{0,1:T(8,128)(2,1)} %param.30) | copy-start | bytes 1769476
  0.7 3.3 %copy-start.3 = (bf16[192,1536]{1,0:T(8,128)(2,1)S(1)}, bf16[192,1536]{1,0:T(8,128)(2,1)}, u32[]{:S(2)}) copy-start(bf16[192,1536]{1,0:T(8,128)(2,1)} %param.29) | copy-start | bytes 1769476
  4.0 2.2 copy-start.4
  4.0 2.2 copy-start.10
  4.0 2.2 copy-start.11
  4.0 2.2 copy-start.12
  4.0 2.3 copy-start.13
  267.7 5.1 %copy-start.1 = (f32[192,1152]{1,0:T(8,128)S(1)}, f32[192,1152]{1,0:T(8,128)}, u32[]{:S(2)}) copy-start(f32[192,1152]{1,0:T(8,128)} %get-tuple-element.55) | copy-start | bytes 2654212
  272.7 1.1 copy-start.9
  272.7 3.4 %copy-start.8 = (bf16[256,768]{1,0:T(8,128)(2,1)S(1)}, bf16[256,768]{1,0:T(8,128)(2,1)}, u32[]{:S(2)}) copy-start(bf16[256,768]{1,0:T(8,128)(2,1)} %get-tuple-element.50) | copy-start | bytes 1179652
  272.8 4.1 %copy-start.7 = (bf16[256,768]{1,0:T(8,128)(2,1)S(1)}, bf16[256,768]{1,0:T(8,128)(2,1)}, u32[]{:S(2)}) copy-start(bf16[256,768]{1,0:T(8,128)(2,1)} %get-tuple-element.51) | copy-start | bytes 1179652
  273.7 3.9 %copy-start.6 = (bf16[256,768]{1,0:T(8,128)(2,1)S(1)}, bf16[256,768]{1,0:T(8,128)(2,1)}, u32[]{:S(2)}) copy-start(bf16[256,768]{1,0:T(8,128)(2,1)} %get-tuple-element.52) | copy-start | bytes 1179652
  273.7 4.7 %copy-start.5 = (bf16[256,768]{1,0:T(8,128)(2,1)S(1)}, bf16[256,768]{1,0:T(8,128)(2,1)}, u32[]{:S(2)}) copy-start(bf16[256,768]{1,0:T(8,128)(2,1)} %get-tuple-element.53) | copy-start | bytes 1179652
  276.1 3.0 %copy-start = (f32[192,1536]{1,0:T(8,128)S(1)}, f32[192,1536]{1,0:T(8,128)}, u32[]{:S(2)}) copy-start(f32[192,1536]{1,0:T(8,128)} %get-tuple-element.127) | copy-start | bytes 3538948

commit v7 on v6

--- a/solution.py
+++ b/solution.py
@@ -645,6 +645,9 @@
             device_id_type=MESH,
         )
 
+    def slot(self, whose, j):
+        return 0 if whose == "other" else 1
+
     def crosses(self, i):
         return self.cross_first[i % self.n]
 
@@ -832,46 +835,55 @@
     return total
 
 
-def schedule(ra, rb, on, pairs, planes):
-    n, nb = ra.n, rb.n
-    for i in range(2 * n - 1):
-        if i == 2:
-            on(("m", 3), partial(ra.rows_sum, 0))
-        on(("m", i + 1), partial(ra.cores_sum, (i % 2) * n + i // 2, i % 2))
-    on(("e", 0), partial(ra.rows_sum, n))
-    on(("e", 0), partial(ra.cores_sum, 2 * n - 1, 1))
-    on(("a", 0), partial(rb.cores_sum, 0, 0))
-    on(("a", 0), partial(rb.cores_sum, nb, 1))
-    on(("a", 2), partial(ra.rows_sum, 2))
-    on(("a", 3), partial(rb.cross_sum, 0))
-    on(("a", 4), partial(ra.ctx_in, 0))
-    on(("a", 5), partial(ra.cross_sum, 1))
-    last = pairs
-    on(("a", last - 1), partial(rb.rows_sum, nb))
-    on(("a", last), partial(ra.ctx_mid, 0))
-    on(("a", last + 1), partial(ra.rows_sum, n + 1))
-    on(("a", last + 1), partial(ra.rows_sum, n + 2))
-    on(("a", last + 1), partial(rb.ctx_in, 0))
-    on(("a", last + 3), partial(rb.ctx_mid, 0))
-    on(("a", last + 5), partial(ra.ctx_in, 1))
-    for i in range(pairs - 1):
-        on(("a", last + 1 + i), partial(rb.cores_sum, (i % 2) * nb + 1 + i // 2, i % 2))
-    on(("a", last + 3), partial(rb.cross_sum, 1))
-    on(("a", last + 5), partial(rb.cross_sum, 2))
-    on(("a", last + 5), partial(rb.rows_sum, nb + 1))
-    on(("p", planes), partial(rb.cores_sum, 2 * nb - 1, 1))
-    on(("p", planes), partial(rb.rows_sum, nb - 1))
-    on(("p", planes + 1), partial(rb.rows_sum, nb + 2))
-    on(("p", planes + 1), partial(rb.ctx_in, 1))
-    on(("p", planes + 2), partial(ra.ctx_in, 2))
-    on(("p", planes + 2), partial(ra.ctx_mid, 1))
-    on(("t", 0), partial(rb.rows_sum, 2 * nb - 1))
-    on(("t", 1), partial(rb.ctx_in, 2))
-    on(("t", 2), partial(rb.ctx_mid, 1))
-    on(("t", 3), partial(ra.ctx_mid, 2))
-    on(("t", 4), partial(rb.ctx_in, 3))
-    on(("t", 5), partial(rb.ctx_mid, 2))
-    on(("t", 11), partial(rb.ctx_mid, 3))
+PLAN = {
+    ("m", 2): [("a", "cores_sum", "other", 0)],
+    ("m", 3): [("a", "cores_sum", "own", 0)],
+    ("m", 4): [("a", "cores_sum", "other", 1)],
+    ("m", 5): [("a", "cores_sum", "own", 1)],
+    ("e", 0): [("a", "rows_sum", "other", 0)],
+    ("a", 1): [("a", "cores_sum", "own", 2), ("a", "cores_sum", "other", 2)],
+    ("a", 3): [("a", "rows_sum", "own", 0)],
+    ("p", 0, 1): [("a", "rows_sum", "other", 1)],
+    ("a", 6): [("a", "ctx_in", "own", 0), ("b", "cores_sum", "other", 0)],
+    ("a", 7): [("a", "rows_sum", "own", 1), ("b", "cores_sum", "own", 0)],
+    ("a", 8): [("b", "cores_sum", "other", 1)],
+    ("a", 9): [("b", "cores_sum", "own", 1)],
+    ("a", 10): [("b", "cores_sum", "other", 2)],
+    ("a", 11): [("b", "cross_sum", "own", 0), ("b", "cores_sum", "own", 2)],
+    ("p", 1, 0): [("b", "cross_sum", "own", 1)],
+    ("p", 1, 2): [("a", "rows_sum", "other", 2)],
+    ("p", 1, 3): [("a", "ctx_in", "own", 1), ("b", "rows_sum", "own", 0), ("b", "cores_sum", "other", 3)],
+    ("t", 0): [("b", "ctx_in", "own", 0)],
+    ("t", 1): [("b", "cross_sum", "own", 2)],
+    ("t", 2): [("a", "rows_sum", "own", 2), ("a", "ctx_mid", "own", 0), ("a", "ctx_mid", "own", 1)],
+    ("t", 10): [("b", "rows_sum", "own", 2)],
+    ("t", 11): [("b", "rows_sum", "own", 1)],
+    ("t", 12): [("a", "ctx_in", "own", 2)],
+    ("t", 13): [("b", "rows_sum", "other", 3)],
+    ("t", 14): [("b", "ctx_mid", "own", 0)],
+    ("t", 16): [("small",)],
+    ("t", 17): [("a", "ctx_mid", "own", 2), ("b", "ctx_in", "own", 1)],
+    ("t", 18): [("b", "cores_sum", "own", 3), ("b", "rows_sum", "own", 3)],
+    ("t", 19): [("b", "ctx_in", "own", 2), ("b", "ctx_mid", "own", 1), ("b", "ctx_in", "own", 3), ("b", "ctx_mid", "own", 2), ("b", "ctx_mid", "own", 3)],
+}
+
+
+def schedule(ra, rb, on, planes, small):
+    for stage, steps in PLAN.items():
+        if stage[0] == "p":
+            stage = ("p", stage[1] * planes + stage[2])
+        for step in steps:
+            if step[0] == "small":
+                on(stage, small)
+                continue
+            name, what, whose, j = step
+            r = ra if name == "a" else rb
+            if what == "cores_sum":
+                on(stage, partial(r.cores_sum, j if whose == "other" else r.n + j, r.slot(whose, j)))
+            elif what == "rows_sum":
+                on(stage, partial(r.rows_sum, j if whose == "other" else r.n + j))
+            else:
+                on(stage, partial(getattr(r, what), j))
 
 
 def backward_kernel(
@@ -1069,7 +1081,13 @@
                     for step in steps:
                         step()
 
-    schedule(ra, rb, on, dm.PAIRS, p.ctxs)
+
+    def small():
+        small_out[...] = small_sum(
+            p, sm, sm_near, sm_rows, sm_across, sm_planes, sm_ss, sm_rc, sm_ry, sm_rx, sm_rz
+        )
+
+    schedule(ra, rb, on, p.ctxs, small)
 
     def run(name):
         for kind, when in sorted(key for key in during if key[0] == name):
@@ -1317,30 +1335,37 @@
                 away.wait_send()
 
         def planes(i, carry):
-            k = lax.rem(i + 1, p.ctxs)
-            both = pl.ds(pl.multiple_of(g * R + p.ctx_after(k) * 2 * PB, 2 * PB), 2 * PB)
-            total = project(both).astype(BF16)
-
-            def out(e):
-                dx_at(e, k, 0, 2 * PB)[...] = total
-                to_mate(e, k).start()
-
-            each_group(g, out)
-            run_when(g * p.ctxs + i, "p")
-
-            def back(e):
-                to_mate(e, k).wait_recv()
-                mine = dx_rows(e, k, p.core)
-                mine[...] = (mine[...].astype(F32) + dxm[e * p.ctxs + k].astype(F32)).astype(BF16)
-
-                @pl.when(k > 0)
-                def _():
-                    to_plane(e, k).start()
-
-            each_group(g, back)
+            @pl.when(i < p.ctxs)
+            def _():
+                k = lax.rem(i + 1, p.ctxs)
+                both = pl.ds(pl.multiple_of(g * R + p.ctx_after(k) * 2 * PB, 2 * PB), 2 * PB)
+                total = project(both).astype(BF16)
+
+                def out(e):
+                    dx_at(e, k, 0, 2 * PB)[...] = total
+                    to_mate(e, k).start()
+
+                each_group(g, out)
+                run_when(g * p.ctxs + i, "p")
+
+            @pl.when(i > 0)
+            def _():
+                k = lax.rem(i, p.ctxs)
+
+                def back(e):
+                    to_mate(e, k).wait_recv()
+                    mine = dx_rows(e, k, p.core)
+                    mine[...] = (mine[...].astype(F32) + dxm[e * p.ctxs + k].astype(F32)).astype(BF16)
+
+                    @pl.when(k > 0)
+                    def _():
+                        to_plane(e, k).start()
+
+                each_group(g, back)
+
             return carry
 
-        lax.fori_loop(0, p.ctxs, planes, 0)
+        lax.fori_loop(0, p.ctxs + 1, planes, 0)
         rows = pl.ds(pl.multiple_of(g * R + dm.P, CL), NX)
         total = project(rows).astype(BF16)
         for c in range(dm.NC):
@@ -1437,9 +1462,6 @@
     for when in range(10, 20):
         for step in during.get(("t", when), []):
             step()
-    small_out[...] = small_sum(
-        p, sm, sm_near, sm_rows, sm_across, sm_planes, sm_ss, sm_rc, sm_ry, sm_rx, sm_rz
-    )
     gu_puts = []
     for j in range(n_a):
         ra.ctx_end(j)
@@ -1589,8 +1611,7 @@
         name="forward",
     )(prompt_in, cont_in, cos, sin, wq_shard, wm_shard, prompt_cot, cont_cot)
     T = 512 if FC % 512 == 0 else 256
-    plan_a = [j == 1 for j in range(FC // T)]
-    plan_b = [j < dm.PAIRS // TP for j in range(1 + dm.PAIRS // TP)]
+    plan_a, plan_b = [False, False, False], [True, True, True, False]
     far = max(chips - 1, 1)
     rows = lambda x: x.reshape(-1, D)
     out_p, out_c, gin_p, gin_c, gq, go, gu, gd, small = pl.pallas_call(

time: 280 us -> 258 us (0.921)
  Pallas kernels: 260 us -> 238 us
    pallas_call x1, Pallas kernels: 173 us -> 150 us  [per_device(): pl.pallas_call(partial(backward_kernel, dm, T, FC, plan_a, plan_b), out_s...]
where the time goes in v7:
time: 258 us; the launch traced here: 257 us
  Pallas kernels  238 us (92%)
  local copies, waits for them, and re-layouts  12.1 us (5%)
  other arithmetic  6.9 us (3%)
    pallas_call x1, Pallas kernels, per_device(): pl.pallas_call(partial(backward_kernel, dm, T, FC, plan_a, plan_b), out_s...  150 us
    pallas_call x1, Pallas kernels, per_device(): pl.pallas_call(partial(forward_kernel, dm, left), out_shape=(sds((NT, D),...  87.8 us
    unnamed x35, local copies, waits for them, and re-layouts  7.88 us

profile of v7, /device:TPU:0, one launch (start us, length us, event | category | flops | bytes accessed | tf_op | source)
XLA Modules:
  0.0 257.4 jit_solution(16627869229508712621)
XLA Ops:
  0.6 0.0 copy-start.2
  0.7 0.0 copy-start.3
  0.7 3.3 %negate_select_fusion = (f32[1152,128]{1,0:T(8,128)}, f32[1152,128]{1,0:T(8,128)}) fusion(f32[128]{0:T(128)S(1)} %fusion.5, f32[1152]{0:T(1024)S(1)} %iota_convert_fusion, pred[128]{0:T(512)(128)(4,1)S(1)} %fusion.6), kind=kLoop, calls=%fused_computation.4 | loop fusion | flops 442368 | bytes 1184896 | tf_op jit(solution)/shard_map/jit(_where)/select_n | solution.py:1559
  4.0 0.0 copy-start.4
  4.0 0.0 copy-done.2
  4.0 0.0 copy-done.3
  4.0 0.0 copy-start.10
  4.0 0.0 copy-start.11
  4.0 0.0 copy-start.12
  4.0 0.0 copy-start.13
  4.0 2.1 pad_maximum_fusion.wm
  6.2 0.0 copy-done.4
  6.2 0.0 copy-done.10
  6.2 0.0 copy-done.11
  6.3 0.0 copy-done.12
  6.3 0.0 copy-done.13
  6.3 0.1 copy.43
  6.5 0.8 fusion.1.wq
  7.3 87.8 %forward.1 = (bf16[512,768]{1,0:T(8,128)(2,1)}, bf16[512,768]{1,0:T(8,128)(2,1)}, f32[12,1,512]{2,1,0:T(1,128)}, f32[8,768]{1,0:T(8,128)}, bf16[768,2560]{1,0:T(...) custom-call(bf16[2,128,768]{2,1,0:T(8,128)(2,1)} %prompt.1, ...), custom_call_target="tpu_custom_call" | custom-call | tf_op jit(solution)/shard_map/forward/pallas_call | solution.py:1565
  95.1 149.7 %backward.1 = (bf16[256,768]{1,0:T(8,128)(2,1)}, bf16[256,768]{1,0:T(8,128)(2,1)}, bf16[256,768]{1,0:T(8,128)(2,1)}, bf16[256,768]{1,0:T(8,128)(2,1)}, f32[192,1...) custom-call(f32[5]{0:T(128)} %mix.1, ...), custom_call_target="tpu_custom_call" | custom-call | tf_op jit(solution)/shard_map/backward/pallas_call | solution.py:1617
  244.9 0.0 copy-start.1
  244.9 0.8 slice.22
  245.7 0.7 slice.23
  246.4 0.6 maximum_reduce_fusion
  247.1 2.9 %copy.46 = f32[1536,192]{0,1:T(8,128)} copy(f32[1536,192]{1,0:T(8,128)} %get-tuple-element.96) | data formatting | bytes 2359296
  249.9 0.0 copy-start.9
  249.9 0.0 copy-start.8
  249.9 0.0 copy-done.1
  249.9 0.0 copy-start.7
  249.9 1.0 copy.50
  250.9 0.0 copy-start.6
  250.9 0.0 copy-start.5
  250.9 0.1 copy-done.9
  251.0 0.9 copy.45
  251.9 1.5 fusion.7
  253.3 0.0 copy-done.8
  253.3 0.0 copy-start
  253.3 0.7 copy.56
  254.1 0.0 copy-done.7
  254.1 0.7 copy.57
  254.8 0.0 copy-done.6
  254.8 0.7 copy.58
  255.6 0.0 copy-done.5
  255.6 0.7 copy.59
  256.3 0.0 copy-done
  256.3 1.0 copy.60
  (9 shorter events, 0.1 us)
Async XLA Ops:
  0.6 3.3 %copy-start.2 = (bf16[1536,192]{0,1:T(8,128)(2,1)S(1)}, bf16[1536,192]{0,1:T(8,128)(2,1)}, u32[]{:S(2)}) copy-start(bf16[1536,192]{0,1:T(8,128)(2,1)} %param.30) | copy-start | bytes 1769476
  0.7 3.3 %copy-start.3 = (bf16[192,1536]{1,0:T(8,128)(2,1)S(1)}, bf16[192,1536]{1,0:T(8,128)(2,1)}, u32[]{:S(2)}) copy-start(bf16[192,1536]{1,0:T(8,128)(2,1)} %param.29) | copy-start | bytes 1769476
  4.0 2.2 copy-start.4
  4.0 2.2 copy-start.10
  4.0 2.2 copy-start.11
  4.0 2.2 copy-start.12
  4.0 2.3 copy-start.13
  244.9 5.1 %copy-start.1 = (f32[192,1152]{1,0:T(8,128)S(1)}, f32[192,1152]{1,0:T(8,128)}, u32[]{:S(2)}) copy-start(f32[192,1152]{1,0:T(8,128)} %get-tuple-element.55) | copy-start | bytes 2654212
  249.9 1.1 copy-start.9
  249.9 3.4 %copy-start.8 = (bf16[256,768]{1,0:T(8,128)(2,1)S(1)}, bf16[256,768]{1,0:T(8,128)(2,1)}, u32[]{:S(2)}) copy-start(bf16[256,768]{1,0:T(8,128)(2,1)} %get-tuple-element.50) | copy-start | bytes 1179652
  249.9 4.1 %copy-start.7 = (bf16[256,768]{1,0:T(8,128)(2,1)S(1)}, bf16[256,768]{1,0:T(8,128)(2,1)}, u32[]{:S(2)}) copy-start(bf16[256,768]{1,0:T(8,128)(2,1)} %get-tuple-element.51) | copy-start | bytes 1179652
  250.9 3.9 %copy-start.6 = (bf16[256,768]{1,0:T(8,128)(2,1)S(1)}, bf16[256,768]{1,0:T(8,128)(2,1)}, u32[]{:S(2)}) copy-start(bf16[256,768]{1,0:T(8,128)(2,1)} %get-tuple-element.52) | copy-start | bytes 1179652
  250.9 4.7 %copy-start.5 = (bf16[256,768]{1,0:T(8,128)(2,1)S(1)}, bf16[256,768]{1,0:T(8,128)(2,1)}, u32[]{:S(2)}) copy-start(bf16[256,768]{1,0:T(8,128)(2,1)} %get-tuple-element.53) | copy-start | bytes 1179652
  253.3 3.0 %copy-start = (f32[192,1536]{1,0:T(8,128)S(1)}, f32[192,1536]{1,0:T(8,128)}, u32[]{:S(2)}) copy-start(f32[192,1536]{1,0:T(8,128)} %get-tuple-element.127) | copy-start | bytes 3538948

commit v8 on v7

--- a/solution.py
+++ b/solution.py
@@ -619,11 +619,12 @@
         dma = pltpu.SemaphoreType.DMA
         far = max(chips - 1, 1)
         rows = n + sum(1 for c in cross_first if not c)
+        parts = sum(chips if c else 1 for c in cross_first)
         return [
             pltpu.VMEM((2, chips * 2 * size, width), BF16),
             pltpu.VMEM((2 * n, chips, size, width), BF16),
             pltpu.VMEM((rows, far, size, width), BF16),
-            pltpu.VMEM((n, chips, size, width), BF16),
+            pltpu.VMEM((parts, size, width), BF16),
             pltpu.VMEM((n, 2, size, width), BF16),
             dma((2 * n, chips)),
             dma((2 * n, chips)),
@@ -683,10 +684,15 @@
 
     def by_tp(self, j):
         p = self.p
-        part = slice(None) if self.crosses(j) else p.chip
-        return self.copy(
-            self.got.at[j, part], self.acr.at[j, part], self.sx.at[j], self.rx.at[j], p.across()
-        )
+        slot = self.acr_slot(j)
+        if self.crosses(j):
+            src, dst = self.got.at[j], self.acr.at[pl.ds(slot, p.chips)]
+        else:
+            src, dst = self.got.at[j, p.chip], self.acr.at[slot]
+        return self.copy(src, dst, self.sx.at[j], self.rx.at[j], p.across())
+
+    def acr_slot(self, j):
+        return sum(self.p.chips if c else 1 for c in self.cross_first[:j])
 
     def inward(self, j):
         slot = jnp.where(self.centre, 1, 0)
@@ -735,7 +741,7 @@
     def cross_sum(self, j):
         self.by_tp(j).wait_recv()
         for y in range(self.p.chips):
-            self.add(self.n + j, y, self.acr[j, y])
+            self.add(self.n + j, y, self.acr[self.acr_slot(j) + y])
         self.rows_send(self.n + j)
 
     def rows_sum(self, i):
@@ -749,7 +755,7 @@
         j = i - self.n
         if not self.crosses(i):
             self.by_tp(j).wait_recv()
-            self.add(i, p.chip, self.acr[j, p.chip])
+            self.add(i, p.chip, self.acr[self.acr_slot(j)])
 
         @pl.when(jnp.logical_not(self.outer))
         def _():
@@ -803,78 +809,115 @@
                 self.outward(j).wait_send()
 
 
-def small_sum(p, sm, near, rows, across, planes, ss, rc, ry, rx, rz):
-    copies = []
-
-    def go(src, dst, recv_sem, device):
-        copies.append(send(src, dst, ss.at[len(copies)], recv_sem, device))
-
-    go(sm, near, rc, p.mate())
-    copies[-1].wait_recv()
-    rows[p.chip] = sm[...] + near[...]
-    for k in range(1, p.chips):
-        go(rows.at[p.chip], rows.at[p.chip], ry.at[k - 1], p.row(k))
-    for k in range(1, p.chips):
-        arrived(rows.at[p.chip_before(k)], ry.at[k - 1], p)
-    total = rows[0]
-    for y in range(1, p.chips):
-        total += rows[y]
-    across[0] = total
-    go(across.at[0], across.at[1], rx, p.across())
-    copies[-1].wait_recv()
-    planes[p.ctx] = across[0] + across[1]
-    for k in range(1, p.ctxs):
-        go(planes.at[p.ctx], planes.at[p.ctx], rz.at[k - 1], p.plane(k))
-    for k in range(1, p.ctxs):
-        arrived(planes.at[p.ctx_before(k)], rz.at[k - 1], p)
-    total = planes[0]
-    for z in range(1, p.ctxs):
-        total += planes[z]
-    for copy in copies:
-        copy.wait_send()
-    return total
-
-
+class SmallSum:
+    def __init__(self, p, sm, near, rows, across, planes, ss, rc, ry, rx, rz):
+        self.p, self.sm, self.near, self.rows, self.across, self.planes = p, sm, near, rows, across, planes
+        self.ss, self.rc, self.ry, self.rx, self.rz = ss, rc, ry, rx, rz
+
+    def copy(self, index, src, dst, recv_sem, device):
+        return pltpu.make_async_remote_copy(
+            src_ref=src,
+            dst_ref=dst,
+            send_sem=self.ss.at[index],
+            recv_sem=recv_sem,
+            device_id=device,
+            device_id_type=MESH,
+        )
+
+    def to_mate(self):
+        return self.copy(0, self.sm, self.near, self.rc, self.p.mate())
+
+    def to_row(self, k):
+        mine = self.rows.at[self.p.chip]
+        return self.copy(1 + k, mine, mine, self.ry.at[k - 1], self.p.row(k))
+
+    def to_across(self):
+        return self.copy(1, self.across.at[0], self.across.at[1], self.rx, self.p.across())
+
+    def to_plane(self, k):
+        mine = self.planes.at[self.p.ctx]
+        return self.copy(self.p.chips + k, mine, mine, self.rz.at[k - 1], self.p.plane(k))
+
+    def step(self, which):
+        p = self.p
+        if which == 0:
+            self.to_mate().start()
+        elif which == 1:
+            self.to_mate().wait_recv()
+            self.rows[p.chip] = self.sm[...] + self.near[...]
+            for k in range(1, p.chips):
+                self.to_row(k).start()
+        elif which == 2:
+            for k in range(1, p.chips):
+                arrived(self.rows.at[p.chip_before(k)], self.ry.at[k - 1], p)
+            total = self.rows[0]
+            for y in range(1, p.chips):
+                total += self.rows[y]
+            self.across[0] = total
+            self.to_across().start()
+        elif which == 3:
+            self.to_across().wait_recv()
+            self.planes[p.ctx] = self.across[0] + self.across[1]
+            for k in range(1, p.ctxs):
+                self.to_plane(k).start()
+
+    def result(self):
+        p = self.p
+        for k in range(1, p.ctxs):
+            arrived(self.planes.at[p.ctx_before(k)], self.rz.at[k - 1], p)
+        total = self.planes[0]
+        for z in range(1, p.ctxs):
+            total += self.planes[z]
+        self.to_mate().wait_send()
+        self.to_across().wait_send()
+        for k in range(1, p.chips):
+            self.to_row(k).wait_send()
+        for k in range(1, p.ctxs):
+            self.to_plane(k).wait_send()
+        return total
+
+
+SMALL_AT = {2: 1, 5: 2, 8: 3}
 PLAN = {
-    ("m", 2): [("a", "cores_sum", "other", 0)],
+    ("m", 1): [("a", "cores_sum", "other", 0)],
     ("m", 3): [("a", "cores_sum", "own", 0)],
-    ("m", 4): [("a", "cores_sum", "other", 1)],
+    ("m", 4): [("a", "cores_sum", "other", 1), ("a", "rows_sum", "other", 0)],
     ("m", 5): [("a", "cores_sum", "own", 1)],
-    ("e", 0): [("a", "rows_sum", "other", 0)],
-    ("a", 1): [("a", "cores_sum", "own", 2), ("a", "cores_sum", "other", 2)],
-    ("a", 3): [("a", "rows_sum", "own", 0)],
-    ("p", 0, 1): [("a", "rows_sum", "other", 1)],
-    ("a", 6): [("a", "ctx_in", "own", 0), ("b", "cores_sum", "other", 0)],
-    ("a", 7): [("a", "rows_sum", "own", 1), ("b", "cores_sum", "own", 0)],
-    ("a", 8): [("b", "cores_sum", "other", 1)],
-    ("a", 9): [("b", "cores_sum", "own", 1)],
-    ("a", 10): [("b", "cores_sum", "other", 2)],
-    ("a", 11): [("b", "cross_sum", "own", 0), ("b", "cores_sum", "own", 2)],
-    ("p", 1, 0): [("b", "cross_sum", "own", 1)],
-    ("p", 1, 2): [("a", "rows_sum", "other", 2)],
-    ("p", 1, 3): [("a", "ctx_in", "own", 1), ("b", "rows_sum", "own", 0), ("b", "cores_sum", "other", 3)],
-    ("t", 0): [("b", "ctx_in", "own", 0)],
-    ("t", 1): [("b", "cross_sum", "own", 2)],
-    ("t", 2): [("a", "rows_sum", "own", 2), ("a", "ctx_mid", "own", 0), ("a", "ctx_mid", "own", 1)],
-    ("t", 10): [("b", "rows_sum", "own", 2)],
-    ("t", 11): [("b", "rows_sum", "own", 1)],
-    ("t", 12): [("a", "ctx_in", "own", 2)],
-    ("t", 13): [("b", "rows_sum", "other", 3)],
-    ("t", 14): [("b", "ctx_mid", "own", 0)],
-    ("t", 16): [("small",)],
-    ("t", 17): [("a", "ctx_mid", "own", 2), ("b", "ctx_in", "own", 1)],
-    ("t", 18): [("b", "cores_sum", "own", 3), ("b", "rows_sum", "own", 3)],
-    ("t", 19): [("b", "ctx_in", "own", 2), ("b", "ctx_mid", "own", 1), ("b", "ctx_in", "own", 3), ("b", "ctx_mid", "own", 2), ("b", "ctx_mid", "own", 3)],
+    ("e", 0): [("a", "cores_sum", "other", 2)],
+    ("a", 0): [("a", "rows_sum", "own", 0)],
+    ("a", 1): [("a", "cores_sum", "own", 2)],
+    ("p", 0, 0): [("a", "ctx_in", "own", 0)],
+    ("p", 0, 1): [("b", "cores_sum", "own", 0), ("b", "cores_sum", "other", 0)],
+    ("p", 0, 3): [("a", "cross_sum", "own", 2), ("a", "rows_sum", "other", 1)],
+    ("a", 7): [("a", "ctx_mid", "own", 0)],
+    ("a", 8): [("a", "rows_sum", "own", 2), ("hop", 0, 0), ("b", "cores_sum", "other", 1)],
+    ("a", 9): [("a", "rows_sum", "own", 1), ("b", "cores_sum", "own", 1), ("b", "cores_sum", "other", 2), ("hop", 0, 1)],
+    ("a", 10): [("a", "ctx_in", "own", 2), ("b", "cross_sum", "own", 0)],
+    ("a", 11): [("b", "cores_sum", "own", 2), ("hop", 0, 2)],
+    ("p", 1, 1): [("b", "cores_sum", "other", 3), ("a", "ctx_in", "own", 1), ("b", "cross_sum", "own", 1)],
+    ("p", 1, 3): [("a", "ctx_mid", "own", 2)],
+    ("t", 0): [("hop", 1, 0)],
+    ("t", 2): [("b", "rows_sum", "other", 3), ("a", "ctx_mid", "own", 1)],
+    ("t", 3): [("b", "cross_sum", "own", 2), ("b", "rows_sum", "own", 0), ("b", "cores_sum", "own", 3)],
+    ("t", 4): [("b", "rows_sum", "own", 1)],
+    ("t", 5): [("hop", 1, 1)],
+    ("t", 6): [("b", "ctx_in", "own", 0), ("b", "rows_sum", "own", 3)],
+    ("t", 8): [("b", "ctx_in", "own", 1)],
+    ("t", 9): [("hop", 1, 2), ("b", "ctx_in", "own", 3), ("b", "rows_sum", "own", 2)],
+    ("t", 10): [("b", "ctx_mid", "own", 0)],
+    ("t", 11): [("b", "ctx_in", "own", 2)],
+    ("t", 14): [("b", "ctx_mid", "own", 1), ("b", "ctx_mid", "own", 3)],
+    ("t", 18): [("b", "ctx_mid", "own", 2)],
 }
 
 
-def schedule(ra, rb, on, planes, small):
+def schedule(ra, rb, on, planes, hop):
     for stage, steps in PLAN.items():
         if stage[0] == "p":
             stage = ("p", stage[1] * planes + stage[2])
         for step in steps:
-            if step[0] == "small":
-                on(stage, small)
+            if step[0] == "hop":
+                on(stage, partial(hop, step[1], step[2]))
                 continue
             name, what, whose, j = step
             r = ra if name == "a" else rb
@@ -1082,12 +1125,32 @@
                         step()
 
 
-    def small():
-        small_out[...] = small_sum(
-            p, sm, sm_near, sm_rows, sm_across, sm_planes, sm_ss, sm_rc, sm_ry, sm_rx, sm_rz
-        )
-
-    schedule(ra, rb, on, p.ctxs, small)
+    sums = SmallSum(p, sm, sm_near, sm_rows, sm_across, sm_planes, sm_ss, sm_rc, sm_ry, sm_rx, sm_rz)
+    hops = [(c, b) for c in range(1, p.ctxs - 1) for b in range(c + 1, p.ctxs)]
+
+    def hop(g, part):
+        third = pl.cdiv(len(hops), 3)
+        for c, b in hops[part * third : (part + 1) * third]:
+
+            @pl.when(p.ctx == c)
+            def _():
+                at = b - c
+                landed(g, at)
+                mine = dx_rows(g, b, p.core)[...].astype(F32)
+                dxz[g, at] = (dxz[g, at].astype(F32) + mine).astype(BF16)
+                rightward(g, dxz.at[g, at], c, b).start()
+
+            far, to = p.ctxs - 1 - c, p.ctxs - 1 - b
+
+            @pl.when(p.ctx == far)
+            def _():
+                at = p.ctxs - far + to
+                landed(g, at)
+                mine = dx_rows(g, to, p.core)[...].astype(F32)
+                dxz[g, at] = (dxz[g, at].astype(F32) + mine).astype(BF16)
+                leftward(g, dxz.at[g, at], far, to).start()
+
+    schedule(ra, rb, on, p.ctxs, hop)
 
     def run(name):
         for kind, when in sorted(key for key in during if key[0] == name):
@@ -1177,7 +1240,7 @@
     begin(nt_load)
     wq_load = pltpu.make_async_copy(wq_hbm.at[:, :, pl.ds(0, 3 * HC)], ring.at[:, :, pl.ds(0, 3 * HC)], wq_sem)
     wq_load.start()
-    during.setdefault(("a", dm.PAIRS), []).insert(0, partial(ready, nt_load))
+    during.setdefault(("a", dm.PAIRS - 1), []).insert(0, partial(ready, nt_load))
 
     def attend(turn, g):
         it = g * dm.PAIRS + turn
@@ -1284,26 +1347,31 @@
     gain_one = ln[0:1, :]
     halves = lambda core, g: pl.ds(pl.multiple_of(core * NCONT + g * NCH, 16), NCH)
 
-    def dx_at(g, k, first, count):
-        c = p.ctx_after(k)
+    def dx_at(g, c, first, count):
         if g == G - 1:
             return dk.at[pl.ds(pl.multiple_of(g * R + c * 2 * PB + first, PB), count), :]
         fit = D // (2 * PB)
         row = pl.multiple_of(c % fit * 2 * PB + first, PB)
         return ra.mine.at[c // fit, pl.ds(row, count), pl.ds(0, D)]
 
-    def dx_rows(g, k, core):
-        return dx_at(g, k, core * PB, PB)
+    def dx_rows(g, c, core):
+        return dx_at(g, c, core * PB, PB)
 
     def to_mate(g, k):
         i = g * p.ctxs + k
-        return ra.copy(dx_rows(g, k, 1 - p.core), dxm.at[i], m_send.at[i], m_recv.at[i], p.mate())
-
-    def to_plane(g, k):
-        i = g * (p.ctxs - 1) + k - 1
-        return ra.copy(
-            dx_rows(g, k, p.core), dxz.at[i], z_send.at[i], z_recv.at[i], p.at(ctx=p.ctx_after(k))
-        )
+        rows = dx_rows(g, p.ctx_after(k), 1 - p.core)
+        return ra.copy(rows, dxm.at[i], m_send.at[i], m_recv.at[i], p.mate())
+
+    def rightward(g, src, c, b):
+        i = b - c - 1
+        return ra.copy(src, dxz.at[g, i], z_send.at[g, b], z_recv.at[g, i], p.at(ctx=c + 1))
+
+    def leftward(g, src, c, b):
+        i = p.ctxs - c + 1 + b
+        return ra.copy(src, dxz.at[g, i], z_send.at[g, b], z_recv.at[g, i], p.at(ctx=c - 1))
+
+    def landed(g, i):
+        pltpu.make_async_copy(dxz.at[g, i], dxz.at[g, i], z_recv.at[g, i]).wait()
 
     def each_group(g, step):
         for e in range(G):
@@ -1321,6 +1389,25 @@
             p.mate(),
         )
 
+    def norm_sums(x, turned, rows):
+        sm[8:9, :] += jnp.sum(x.astype(F32), axis=0, keepdims=True)
+        for d in range(0, D, 128):
+            gh[:128, d : d + 128] += dot(turned[d : d + 128, rows], x[:, d : d + 128])
+
+    def norm_grads():
+        same = lax.broadcasted_iota(jnp.int32, (128, 128), 0) == lax.broadcasted_iota(
+            jnp.int32, (128, 128), 1
+        )
+        for d in range(0, D, 128):
+            cols = slice(d, d + 128)
+            x = blk[:, cols].astype(BF16)
+            sm[8:9, cols] += jnp.sum(x.astype(F32), axis=0, keepdims=True)
+            gh[:128, cols] += dot(own_nt[cols, :], x)
+            total = jnp.sum(jnp.where(same, gh[:128, cols], 0.0), axis=0, keepdims=True)
+            sm[7:8, cols] = (total - ln[1:2, cols] * sm[8:9, cols]) / ln[0:1, cols]
+
+    gh[:128, :] = jnp.zeros((128, D), F32)
+
     def group(g, carry):
         lax.fori_loop(0, dm.PAIRS, attend, g)
 
@@ -1340,9 +1427,10 @@
                 k = lax.rem(i + 1, p.ctxs)
                 both = pl.ds(pl.multiple_of(g * R + p.ctx_after(k) * 2 * PB, 2 * PB), 2 * PB)
                 total = project(both).astype(BF16)
+                norm_sums(total, nt, both)
 
                 def out(e):
-                    dx_at(e, k, 0, 2 * PB)[...] = total
+                    dx_at(e, p.ctx_after(k), 0, 2 * PB)[...] = total
                     to_mate(e, k).start()
 
                 each_group(g, out)
@@ -1354,12 +1442,17 @@
 
                 def back(e):
                     to_mate(e, k).wait_recv()
-                    mine = dx_rows(e, k, p.core)
+                    b = p.ctx_after(k)
+                    mine = dx_rows(e, b, p.core)
                     mine[...] = (mine[...].astype(F32) + dxm[e * p.ctxs + k].astype(F32)).astype(BF16)
 
-                    @pl.when(k > 0)
+                    @pl.when((k > 0) & (p.ctx == 0))
                     def _():
-                        to_plane(e, k).start()
+                        rightward(e, mine, 0, b).start()
+
+                    @pl.when((k > 0) & (p.ctx == p.ctxs - 1))
+                    def _():
+                        leftward(e, mine, p.ctxs - 1, b).start()
 
                 each_group(g, back)
 
@@ -1368,6 +1461,7 @@
         lax.fori_loop(0, p.ctxs + 1, planes, 0)
         rows = pl.ds(pl.multiple_of(g * R + dm.P, CL), NX)
         total = project(rows).astype(BF16)
+        norm_sums(total, nt, rows)
         for c in range(dm.NC):
             for e in range(2):
                 out = pl.ds(pl.multiple_of(e * NCONT + g * NCH + c * dm.CH, dm.CH), dm.CH)
@@ -1385,8 +1479,6 @@
         gn += blk[rows, :]
         hat, scale = norm_stats(x.astype(F32))
         gatt[rows, :] = (resid[rows, :] + norm_back(gn, gain_one, hat, scale)).astype(BF16)
-        sm[7:8, :] += jnp.sum(gn * hat, axis=0, keepdims=True)
-        sm[8:9, :] += jnp.sum(gn, axis=0, keepdims=True)
 
     def gin_away(part):
         rows = pl.ds(0, NP) if part == 0 else pl.ds(NP, NT - NP)
@@ -1447,26 +1539,38 @@
         pltpu.make_async_copy(blk_home.at[pl.ds(NP, NT - NP), :], out_c, put_sem.at[1]),
     ]
     begin(puts)
+    norm_grads()
+    sums.step(0)
     for when in range(10):
         for step in during.get(("t", when), []):
             step()
+        if SMALL_AT.get(when):
+            sums.step(SMALL_AT[when])
 
     for g in range(G):
-        gn = dx_rows(g, 0, p.core)[...].astype(F32)
-        for k in range(1, p.ctxs):
-            to_plane(g, k).wait_recv()
-            gn += dxz[g * (p.ctxs - 1) + k - 1].astype(F32)
         here = slice(g * PB, (g + 1) * PB)
-        enter_back(gn, own_p[here, :], here)
+
+        @pl.when(p.ctx > 0)
+        def _():
+            landed(g, 0)
+            blk[here, :] += dxz[g, 0].astype(F32)
+
+        @pl.when(p.ctx < p.ctxs - 1)
+        def _():
+            landed(g, p.ctxs)
+            blk[here, :] += dxz[g, p.ctxs].astype(F32)
+
+        enter_back(dx_rows(g, p.ctx, p.core)[...].astype(F32), own_p[here, :], here)
     give(0)
     for when in range(10, 20):
         for step in during.get(("t", when), []):
             step()
+    small_out[...] = sums.result()
     gu_puts = []
     for j in range(n_a):
         ra.ctx_end(j)
         total = ra.result(j)
-        gd_out[j * T : (j + 1) * T, :] = total[:, T:].T
+        gd_out[:, j * T : (j + 1) * T] = total[:, T:]
         if len(gu_puts) > 0:
             gu_puts[-1].wait()
         gh[:S, :T] = total[:, :T]
@@ -1481,11 +1585,10 @@
         rb.ctx_end(j)
         total = rb.result(j)
         if j == 0:
-            go_out[...] = total.T
+            go_out[...] = total
         else:
             for c in range(3):
-                first = c * HC + (j - 1) * 128
-                gq_out[:, first : first + 128] = total[:, c * 128 : (c + 1) * 128]
+                gq_out[c, :, (j - 1) * 128 : j * 128] = total[:, c * 128 : (c + 1) * 128]
 
     @pl.when(p.core != p.tp)
     def _():
@@ -1505,10 +1608,41 @@
         for k in range(p.ctxs):
             to_mate(g, k).wait_send()
         for k in range(1, p.ctxs):
-            to_plane(g, k).wait_send()
+            b = p.ctx_after(k)
+            ra.copy(dxz.at[g, 0], dxz.at[g, 0], z_send.at[g, b], z_send.at[g, b], p.mate()).wait_send()
         cont_copy(g).wait_send()
     ra.drain()
     rb.drain()
+
+
+def deliver_kernel(count, *refs):
+    sources, small, targets = refs[:count], refs[count], refs[count + 1 : 2 * count + 1]
+    outs = refs[2 * count + 1 : 2 * count + 6]
+    kept = refs[2 * count + 6 : 3 * count + 6]
+    in_sem, out_sem, parts = refs[3 * count + 6 :]
+    loads = [pltpu.make_async_copy(sources[i], kept[i], in_sem.at[i]) for i in range(count)]
+    puts = [pltpu.make_async_copy(kept[i], targets[i], out_sem.at[i]) for i in range(count)]
+    for load in loads:
+        load.start()
+    S = parts.shape[2]
+    norms = jnp.concatenate([small[7:9, :], small[0:2, :], jnp.zeros((4, small.shape[1]), F32)], axis=0)
+    for d in range(parts.shape[0]):
+        parts[d] = norms[:, d * S : (d + 1) * S]
+    mine = parts[lax.axis_index("dp")]
+    for i in range(4):
+        outs[i][...] = mine[i : i + 1, :]
+    sums = jnp.sum(small[...], axis=1, keepdims=True)
+    order = (3, 4, 5, 6, 2)
+    lanes = lax.broadcasted_iota(jnp.int32, (1, 8), 1)
+    mix = jnp.zeros((1, 8), F32)
+    for i, row in enumerate(order):
+        mix = jnp.where(lanes == i, sums[row : row + 1, :], mix)
+    outs[4][...] = mix
+    for i in range(count):
+        loads[i].wait()
+        puts[i].start()
+    for put in puts:
+        put.wait()
 
 
 def params(**more):
@@ -1611,7 +1745,7 @@
         name="forward",
     )(prompt_in, cont_in, cos, sin, wq_shard, wm_shard, prompt_cot, cont_cot)
     T = 512 if FC % 512 == 0 else 256
-    plan_a, plan_b = [False, False, False], [True, True, True, False]
+    plan_a, plan_b = [False, False, True], [True, True, True, False]
     far = max(chips - 1, 1)
     rows = lambda x: x.reshape(-1, D)
     out_p, out_c, gin_p, gin_c, gq, go, gu, gd, small = pl.pallas_call(
@@ -1621,10 +1755,10 @@
             sds((NT - NP, D), BF16),
             sds((NP, D), BF16),
             sds((NT - NP, D), BF16),
-            sds((S, 3 * HC), F32),
-            sds((HC, S), F32),
+            sds((3, S, HC), F32),
+            sds((S, HC), F32),
             sds((S, FC), F32),
-            sds((FC, S), F32),
+            sds((S, FC), F32),
             sds((16, D), F32),
         ),
         in_specs=[pl.BlockSpec(memory_space=pltpu.SMEM)] + [vmem] * 10 + [any_] * 12,
@@ -1646,7 +1780,7 @@
             pltpu.VMEM((G * R, D), BF16),
             pltpu.VMEM((NT, D), BF16),
             pltpu.VMEM((G * ctxs, PB, D), BF16),
-            pltpu.VMEM((G * (ctxs - 1), PB, D), BF16),
+            pltpu.VMEM((G, ctxs + 1, PB, D), BF16),
             pltpu.VMEM((NT - NP, D), BF16),
             pltpu.VMEM((max(NT, 2 * (NT - NP)), D), BF16),
             pltpu.VMEM((NT, D), BF16),
@@ -1664,8 +1798,8 @@
             dma((2,)),
             dma((G * ctxs,)),
             dma((G * ctxs,)),
-            dma((G * (ctxs - 1),)),
-            dma((G * (ctxs - 1),)),
+            dma((G, ctxs)),
+            dma((G, ctxs + 1)),
             dma((G,)),
             dma((G,)),
             pltpu.VMEM((16, D), F32),
@@ -1708,22 +1842,31 @@
         rows(prompt_cot),
         rows(cont_cot),
     )
-    start = lax.axis_index("dp") * S
-    mine = lax.dynamic_slice_in_dim(small, start, S, axis=1)
+    results = (out_p, out_c, gin_p, gin_c, gq, go, gu, gd)
+    shapes = tuple(sds(x.shape, x.dtype) for x in results)
+    out = pl.pallas_call(
+        partial(deliver_kernel, len(results)),
+        out_shape=shapes + (sds((1, S), F32),) * 4 + (sds((1, 8), F32),),
+        in_specs=[any_] * len(results) + [vmem],
+        out_specs=(any_,) * len(results) + (vmem,) * 5,
+        scratch_shapes=[pltpu.VMEM(x.shape, x.dtype) for x in results]
+        + [dma((len(results),)), dma((len(results),)), pltpu.VMEM((2 * chips, 8, S), F32)],
+        compiler_params=params(),
+        name="deliver",
+    )(*results, small)
+    out_p, out_c, gin_p, gin_c, gq, go, gu, gd = out[:8]
+    gains = [x.reshape(S) for x in out[8:12]]
     return (
         out_p.reshape(prompt_in.shape),
         out_c.reshape(cont_in.shape),
         gin_p.reshape(prompt_in.shape),
         gin_c.reshape(cont_in.shape),
-        mine[7],
-        mine[8],
-        mine[0],
-        mine[1],
-        gq.reshape(S, 3, HC),
-        go,
+        *gains,
+        jnp.transpose(gq, (1, 0, 2)),
+        go.T,
         gu,
-        gd,
-        jnp.sum(jnp.concatenate([small[3:7], small[2:3]]), axis=1),
+        gd.T,
+        out[12][0, :5],
     )
 
 

time: 258 us -> 251 us (0.973)
  local copies, waits for them, and re-layouts: 12.1 us -> 5.15 us
    unnamed x35 -> x6, local copies, waits for them, and re-layouts: 7.88 us -> 0.02 us
    pallas_call x0 -> x1, Pallas kernels: none -> 6.03 us  [per_device(): pl.pallas_call(partial(deliver_kernel, len(results)), out_shape=shapes +...]
    pallas_call x1, Pallas kernels: 150 us -> 146 us  [per_device(): pl.pallas_call(partial(backward_kernel, dm, T, FC, plan_a, plan_b), out_s...]
    slice x3 -> x0, local copies, waits for them, and re-layouts: 3.03 us -> none  [the longest x1 1.47 us: per_device(): mine[1]]
    another operation x5, local copies, waits for them, and re-layouts: 0.16 us -> 2.78 us  [per_device(): norms = jnp.stack([ln1_gain, ln1_bias, ln2_gain, ln2_bias], axis=1)]
where the time goes in v8:
time: 251 us
  Pallas kernels  240 us (96%)
  other arithmetic  5.3 us (2%)
  local copies, waits for them, and re-layouts  5.15 us (2%)
    pallas_call x1, Pallas kernels, per_device(): pl.pallas_call(partial(backward_kernel, dm, T, FC, plan_a, plan_b), out_s...  146 us
    pallas_call x1, Pallas kernels, per_device(): pl.pallas_call(partial(forward_kernel, dm, left), out_shape=(sds((NT, D),...  87.8 us
    pallas_call x1, Pallas kernels, per_device(): pl.pallas_call(partial(deliver_kernel, len(results)), out_shape=shapes +...  6.03 us

profile of v8, /device:TPU:0, one launch (start us, length us, event | category | flops | bytes accessed | tf_op | source)
XLA Modules:
  0.0 250.9 jit_solution(10950682245152715768)
XLA Ops:
  0.7 0.7 stack.15
  1.3 0.7 stack.16
  2.0 0.7 stack.17
  2.6 0.7 stack.18
  3.3 0.1 copy.37
  3.5 0.0 copy-start
  3.5 0.0 copy-start.1
  3.5 0.0 copy-start.2
  3.5 1.2 copy.38
  4.7 0.8 fusion.1.wq
  5.5 3.3 %negate_select_fusion = (f32[1152,128]{1,0:T(8,128)}, f32[1152,128]{1,0:T(8,128)}) fusion(f32[128]{0:T(128)S(1)} %fusion.5, f32[1152]{0:T(1024)S(1)} %iota_convert_fusion, pred[128]{0:T(512)(128)(4,1)S(1)} %fusion.6), kind=kLoop, calls=%fused_computation.3 | loop fusion | flops 442368 | bytes 1184896 | tf_op jit(solution)/shard_map/jit(_where)/select_n | solution.py:1693
  8.8 0.0 copy-done
  8.8 0.0 copy-done.1
  8.8 0.0 copy-done.2
  8.8 1.2 pad_maximum_fusion.wm
  10.0 87.8 %forward.1 = (bf16[512,768]{1,0:T(8,128)(2,1)}, bf16[512,768]{1,0:T(8,128)(2,1)}, f32[12,1,512]{2,1,0:T(1,128)}, f32[8,768]{1,0:T(8,128)}, bf16[768,2560]{1,0:T(...) custom-call(bf16[2,128,768]{2,1,0:T(8,128)(2,1)} %prompt.1, ...), custom_call_target="tpu_custom_call" | custom-call | tf_op jit(solution)/shard_map/forward/pallas_call | solution.py:1699
  97.8 145.9 %backward.1 = (bf16[256,768]{1,0:T(8,128)(2,1)}, bf16[256,768]{1,0:T(8,128)(2,1)}, bf16[256,768]{1,0:T(8,128)(2,1)}, bf16[256,768]{1,0:T(8,128)(2,1)}, f32[3,192...) custom-call(f32[5]{0:T(128)} %mix.1, ...), custom_call_target="tpu_custom_call" | custom-call | tf_op jit(solution)/shard_map/backward/pallas_call | solution.py:1751
  243.7 6.0 %deliver.1 = (bf16[256,768]{1,0:T(8,128)(2,1)}, bf16[256,768]{1,0:T(8,128)(2,1)}, bf16[256,768]{1,0:T(8,128)(2,1)}, bf16[256,768]{1,0:T(8,128)(2,1)}, f32[3,192,...) custom-call(bf16[256,768]{1,0:T(8,128)(2,1)} %get-tuple-element.63.r, ...), custom_call_target="tpu_custom_call" | custom-call | tf_op jit(solution)/shard_map/deliver/pallas_call | solution.py:1847
  249.7 1.2 slice_bitcast_fusion
  (4 shorter events, 0.0 us)
Async XLA Ops:
  3.5 5.3 %copy-start = (bf16[1536,192]{0,1:T(8,128)(2,1)S(1)}, bf16[1536,192]{0,1:T(8,128)(2,1)}, u32[]{:S(2)}) copy-start(bf16[1536,192]{0,1:T(8,128)(2,1)} %param.30) | copy-start | bytes 1769476
  3.5 5.3 %copy-start.1 = (bf16[192,1536]{1,0:T(8,128)(2,1)S(1)}, bf16[192,1536]{1,0:T(8,128)(2,1)}, u32[]{:S(2)}) copy-start(bf16[192,1536]{1,0:T(8,128)(2,1)} %param.29) | copy-start | bytes 1769476
  3.5 5.3 %copy-start.2 = (bf16[384,192]{0,1:T(8,128)(2,1)S(1)}, bf16[384,192]{0,1:T(8,128)(2,1)}, u32[]{:S(2)}) copy-start(bf16[384,192]{0,1:T(8,128)(2,1)} %param.28) | copy-start | bytes 442372

commit v9 on v8

--- a/solution.py
+++ b/solution.py
@@ -310,8 +310,8 @@
     left,
     prompt,
     cont,
-    cos,
-    sin,
+    cos_few,
+    sin_few,
     wq,
     wm,
     cot_p,
@@ -320,6 +320,8 @@
     att_out,
     lse_out,
     ln_out,
+    cos,
+    sin,
     nt_hbm,
     own_nt_hbm,
     k_hbm,
@@ -359,7 +361,7 @@
     TP = w.shape[0]
     p = Peers()
     block = block_index()
-    gq = WeightGather(p, wq, w, wq.shape[1], *sems[:4])
+    gq = WeightGather(p, wq, w, wq.shape[1] // 256 * 128, *sems[:4])
     gm = WeightGather(p, wm, wm_out, left, *sems[4:])
     size = wq.shape[0]
     mine = pl.ds(pl.multiple_of(p.dp * size, 16), size)
@@ -409,20 +411,27 @@
     p.greet(trades=True)
     trade(0)
     gq.start()
-    trade(1)
-    fill_masks(dm, maskp, maskx)
     traded(0)
     own = xp.at[block]
     sent = []
     for k in range(1, p.ctxs):
         sent.append(send(own, own, x_send.at[k - 1], x_plane.at[k - 1], p.plane(k)))
     sent.append(send(own, own, x_send.at[p.ctxs - 1], x_mate.at[0], p.mate()))
+    fill_masks(dm, maskp, maskx)
+    second = lax.broadcasted_iota(jnp.int32, (128, 128), 1) % HD >= HD // 2
+    for i in range(0, dm.P + CL, 128):
+        part = cos_few[:, i : i + 128]
+        cos[i : i + 128, :] = jnp.concatenate([part] * 4, axis=0).T
+        part = sin_few[:, i : i + 128]
+        part = jnp.concatenate([part] * 4, axis=0).T
+        sin[i : i + 128, :] = jnp.where(second, part, -part)
+    gq.relay_rows()
     gq.relay_across()
-    gq.relay_rows()
+    trade(1)
+    gm.start()
+    gq.relay_last()
     traded(1)
     sent.append(send(xc.at[p.core], xc.at[p.core], c_send, c_mate, p.mate()))
-    gq.relay_last()
-    gm.start()
     trade(2)
     trade(3)
     gq.finish()
@@ -1633,8 +1642,8 @@
         outs[i][...] = mine[i : i + 1, :]
     sums = jnp.sum(small[...], axis=1, keepdims=True)
     order = (3, 4, 5, 6, 2)
-    lanes = lax.broadcasted_iota(jnp.int32, (1, 8), 1)
-    mix = jnp.zeros((1, 8), F32)
+    lanes = lax.broadcasted_iota(jnp.int32, (1, 5), 1)
+    mix = jnp.zeros((1, 5), F32)
     for i, row in enumerate(order):
         mix = jnp.where(lanes == i, sums[row : row + 1, :], mix)
     outs[4][...] = mix
@@ -1685,24 +1694,23 @@
     wm_shard = jnp.concatenate([w_out.T, w_up, w_down.T], axis=1)
 
     positions = jnp.arange(PROMPT + CL, dtype=jnp.int32).astype(F32)
-    lane = jnp.arange(128, dtype=jnp.int32)
-    freq = 10000.0 ** (-((lane % 32).astype(F32) / 32))
-    angles = positions[:, None] * freq[None, :]
-    cos, sin = jnp.cos(angles), jnp.sin(angles)
-    second = (lane % 64) >= 32
-    sin = jnp.where(second[None, :], sin, -sin)
+    freq = 10000.0 ** (-(jnp.arange(HD // 2, dtype=jnp.int32).astype(F32) / (HD // 2)))
+    angles = freq[:, None] * positions[None, :]
+    cos_few, sin_few = jnp.cos(angles), jnp.sin(angles)
 
     any_ = pl.BlockSpec(memory_space=pl.ANY)
     vmem = pl.BlockSpec(memory_space=pltpu.VMEM)
     dma = pltpu.SemaphoreType.DMA
     left = (HC + 2 * FC) // 128 * 2 // 3 * 128
-    q, att, lse, ln, nt, own_nt, k, v, wq, wm, own_p, own_c, cot_p, cot_c = pl.pallas_call(
+    q, att, lse, ln, cos, sin, nt, own_nt, k, v, wq, wm, own_p, own_c, cot_p, cot_c = pl.pallas_call(
         partial(forward_kernel, dm, left),
         out_shape=(
             sds((NT, D), BF16),
             sds((NT, D), BF16),
             sds((G * dm.PAIRS, 1, dm.COLS), F32),
             sds((8, D), F32),
+            sds((PROMPT + CL, 128), F32),
+            sds((PROMPT + CL, 128), F32),
             sds((D, G * R), BF16),
             sds((D, NT), BF16),
             sds((G, R, D), BF16),
@@ -1715,7 +1723,7 @@
             sds(cont_in.shape, BF16),
         ),
         in_specs=[vmem] * 5 + [any_] * 3,
-        out_specs=(vmem,) * 4 + (any_,) * 10,
+        out_specs=(vmem,) * 6 + (any_,) * 10,
         scratch_shapes=[
             pltpu.VMEM((D, G * R), BF16),
             pltpu.VMEM((D, NT), BF16),
@@ -1743,7 +1751,7 @@
         + WeightGather.semaphores(chips),
         compiler_params=params(collective_id=0, has_side_effects=True),
         name="forward",
-    )(prompt_in, cont_in, cos, sin, wq_shard, wm_shard, prompt_cot, cont_cot)
+    )(prompt_in, cont_in, cos_few, sin_few, wq_shard, wm_shard, prompt_cot, cont_cot)
     T = 512 if FC % 512 == 0 else 256
     plan_a, plan_b = [False, False, True], [True, True, True, False]
     far = max(chips - 1, 1)
@@ -1846,7 +1854,7 @@
     shapes = tuple(sds(x.shape, x.dtype) for x in results)
     out = pl.pallas_call(
         partial(deliver_kernel, len(results)),
-        out_shape=shapes + (sds((1, S), F32),) * 4 + (sds((1, 8), F32),),
+        out_shape=shapes + (sds((1, S), F32),) * 4 + (sds((1, 5), F32),),
         in_specs=[any_] * len(results) + [vmem],
         out_specs=(any_,) * len(results) + (vmem,) * 5,
         scratch_shapes=[pltpu.VMEM(x.shape, x.dtype) for x in results]
@@ -1866,7 +1874,7 @@
         go.T,
         gu,
         gd.T,
-        out[12][0, :5],
+        out[12].reshape(5),
     )
 
 

time: 251 us -> 246 us (0.980)
  Pallas kernels: 240 us -> 237 us
    select_n x1 -> x0, other arithmetic: 3.25 us -> none  [per_device(): sin = jnp.where(second[None, :], sin, -sin)]
    pallas_call x1, Pallas kernels: 87.8 us -> 85.2 us  [per_device(): pl.pallas_call(partial(forward_kernel, dm, left), out_shape=(sds((NT, D),...]
where the time goes in v9:
time: 246 us; the launch traced here: 245 us
  Pallas kernels  237 us (96%)
  local copies, waits for them, and re-layouts  3.95 us (2%)
  other arithmetic  3.35 us (1%)
    pallas_call x1, Pallas kernels, per_device(): pl.pallas_call(partial(backward_kernel, dm, T, FC, plan_a, plan_b), out_s...  146 us
    pallas_call x1, Pallas kernels, per_device(): pl.pallas_call(partial(forward_kernel, dm, left), out_shape=(sds((NT, D),...  85.2 us
    pallas_call x1, Pallas kernels, per_device(): pl.pallas_call(partial(deliver_kernel, len(results)), out_shape=shapes +...  6 us

profile of v9, /device:TPU:0, one launch (start us, length us, event | category | flops | bytes accessed | tf_op | source)
XLA Modules:
  0.0 245.2 jit_solution(9700653368654621092)
XLA Ops:
  0.6 0.0 copy-start
  0.7 0.0 copy-start.1
  0.7 0.0 copy-start.2
  0.7 0.8 stack.15
  1.4 0.7 stack.16
  2.1 0.7 stack.17
  2.8 0.7 stack.18
  3.4 0.1 copy.37
  3.6 1.3 multiply_sine_fusion
  4.9 1.1 copy.38
  6.0 0.8 fusion.1.wq
  6.8 0.0 copy-done
  6.8 0.0 copy-done.1
  6.8 0.0 copy-done.2
  6.8 1.2 pad_maximum_fusion.wm
  8.0 85.2 %forward.1 = (bf16[512,768]{1,0:T(8,128)(2,1)}, bf16[512,768]{1,0:T(8,128)(2,1)}, f32[12,1,512]{2,1,0:T(1,128)}, f32[8,768]{1,0:T(8,128)}, f32[1152,128]{1,0:T(8...) custom-call(bf16[2,128,768]{2,1,0:T(8,128)(2,1)} %prompt.1, ...), custom_call_target="tpu_custom_call" | custom-call | tf_op jit(solution)/shard_map/forward/pallas_call | solution.py:1705
  93.2 145.9 %backward.1 = (bf16[256,768]{1,0:T(8,128)(2,1)}, bf16[256,768]{1,0:T(8,128)(2,1)}, bf16[256,768]{1,0:T(8,128)(2,1)}, bf16[256,768]{1,0:T(8,128)(2,1)}, f32[3,192...) custom-call(f32[5]{0:T(128)} %mix.1, ...), custom_call_target="tpu_custom_call" | custom-call | tf_op jit(solution)/shard_map/backward/pallas_call | solution.py:1759
  239.0 6.0 %deliver.1 = (bf16[256,768]{1,0:T(8,128)(2,1)}, bf16[256,768]{1,0:T(8,128)(2,1)}, bf16[256,768]{1,0:T(8,128)(2,1)}, bf16[256,768]{1,0:T(8,128)(2,1)}, f32[3,192,...) custom-call(bf16[256,768]{1,0:T(8,128)(2,1)} %get-tuple-element.67.r, ...), custom_call_target="tpu_custom_call" | custom-call | tf_op jit(solution)/shard_map/deliver/pallas_call | solution.py:1855
  (3 shorter events, 0.0 us)
Async XLA Ops:
  0.6 6.1 %copy-start = (bf16[1536,192]{0,1:T(8,128)(2,1)S(1)}, bf16[1536,192]{0,1:T(8,128)(2,1)}, u32[]{:S(2)}) copy-start(bf16[1536,192]{0,1:T(8,128)(2,1)} %param.30) | copy-start | bytes 1769476
  0.7 6.1 %copy-start.1 = (bf16[192,1536]{1,0:T(8,128)(2,1)S(1)}, bf16[192,1536]{1,0:T(8,128)(2,1)}, u32[]{:S(2)}) copy-start(bf16[192,1536]{1,0:T(8,128)(2,1)} %param.29) | copy-start | bytes 1769476
  0.7 6.1 %copy-start.2 = (bf16[384,192]{0,1:T(8,128)(2,1)S(1)}, bf16[384,192]{0,1:T(8,128)(2,1)}, u32[]{:S(2)}) copy-start(bf16[384,192]{0,1:T(8,128)(2,1)} %param.28) | copy-start | bytes 442372

commit v10 on v9

--- a/solution.py
+++ b/solution.py
@@ -1688,8 +1688,8 @@
 
     sds = jax.ShapeDtypeStruct
     chips, ctxs = lax.axis_size("dp") // 2, lax.axis_size("ctx")
-    norms = jnp.stack([ln1_gain, ln1_bias, ln2_gain, ln2_bias], axis=1)
-    norms = jnp.pad(norms, ((0, 0), (0, 124)))
+    norms = jnp.concatenate([ln1_gain, ln1_bias, ln2_gain, ln2_bias]).reshape(4, S)
+    norms = jnp.pad(norms, ((0, 124), (0, 0))).T
     wq_shard = jnp.concatenate([w_qkv.reshape(S, 3 * HC), norms], axis=1)
     wm_shard = jnp.concatenate([w_out.T, w_up, w_down.T], axis=1)
 

time: 246 us -> 244 us (level)
  local copies, waits for them, and re-layouts: 3.95 us -> 1.32 us
    another operation x5 -> x0, local copies, waits for them, and re-layouts: 2.88 us -> none  [per_device(): norms = jnp.stack([ln1_gain, ln1_bias, ln2_gain, ln2_bias], axis=1)]
where the time goes in v10:
time: 244 us; the launch traced here: 243 us
  Pallas kernels  237 us (97%)
  other arithmetic  4.21 us (2%)
    pallas_call x1, Pallas kernels, per_device(): pl.pallas_call(partial(backward_kernel, dm, T, FC, plan_a, plan_b), out_s...  146 us
    pallas_call x1, Pallas kernels, per_device(): pl.pallas_call(partial(forward_kernel, dm, left), out_shape=(sds((NT, D),...  85.2 us
    pallas_call x1, Pallas kernels, per_device(): pl.pallas_call(partial(deliver_kernel, len(results)), out_shape=shapes +...  6 us

profile of v10, /device:TPU:0, one launch (start us, length us, event | category | flops | bytes accessed | tf_op | source)
XLA Modules:
  0.0 243.4 jit_solution(1415063210146929638)
XLA Ops:
  0.6 0.0 copy-start
  0.7 0.0 copy-start.1
  0.7 0.0 copy-start.2
  0.7 0.9 pad_maximum_fusion.2
  1.6 0.1 reshape.101
  1.7 0.1 copy.32
  1.8 1.3 multiply_sine_fusion
  3.1 1.1 copy.33
  4.2 0.8 pad_maximum_fusion.1.wq
  5.0 0.0 copy-done
  5.0 0.0 copy-done.1
  5.0 0.0 copy-done.2
  5.0 1.2 pad_maximum_fusion.wm
  6.2 85.2 %forward.1 = (bf16[512,768]{1,0:T(8,128)(2,1)}, bf16[512,768]{1,0:T(8,128)(2,1)}, f32[12,1,512]{2,1,0:T(1,128)}, f32[8,768]{1,0:T(8,128)}, f32[1152,128]{1,0:T(8...) custom-call(bf16[2,128,768]{2,1,0:T(8,128)(2,1)} %prompt.1, ...), custom_call_target="tpu_custom_call" | custom-call | tf_op jit(solution)/shard_map/forward/pallas_call | solution.py:1705
  91.4 145.9 %backward.1 = (bf16[256,768]{1,0:T(8,128)(2,1)}, bf16[256,768]{1,0:T(8,128)(2,1)}, bf16[256,768]{1,0:T(8,128)(2,1)}, bf16[256,768]{1,0:T(8,128)(2,1)}, f32[3,192...) custom-call(f32[5]{0:T(128)} %mix.1, ...), custom_call_target="tpu_custom_call" | custom-call | tf_op jit(solution)/shard_map/backward/pallas_call | solution.py:1759
  237.3 6.0 %deliver.1 = (bf16[256,768]{1,0:T(8,128)(2,1)}, bf16[256,768]{1,0:T(8,128)(2,1)}, bf16[256,768]{1,0:T(8,128)(2,1)}, bf16[256,768]{1,0:T(8,128)(2,1)}, f32[3,192,...) custom-call(bf16[256,768]{1,0:T(8,128)(2,1)} %get-tuple-element.67.r, ...), custom_call_target="tpu_custom_call" | custom-call | tf_op jit(solution)/shard_map/deliver/pallas_call | solution.py:1855
  (3 shorter events, 0.0 us)
Async XLA Ops:
  0.6 4.4 %copy-start = (bf16[1536,192]{0,1:T(8,128)(2,1)S(1)}, bf16[1536,192]{0,1:T(8,128)(2,1)}, u32[]{:S(2)}) copy-start(bf16[1536,192]{0,1:T(8,128)(2,1)} %param.30) | copy-start | bytes 1769476
  0.7 4.4 %copy-start.1 = (bf16[192,1536]{1,0:T(8,128)(2,1)S(1)}, bf16[192,1536]{1,0:T(8,128)(2,1)}, u32[]{:S(2)}) copy-start(bf16[192,1536]{1,0:T(8,128)(2,1)} %param.29) | copy-start | bytes 1769476
  0.7 4.4 %copy-start.2 = (bf16[384,192]{0,1:T(8,128)(2,1)S(1)}, bf16[384,192]{0,1:T(8,128)(2,1)}, u32[]{:S(2)}) copy-start(bf16[384,192]{0,1:T(8,128)(2,1)} %param.28) | copy-start | bytes 442372

commit v11 on v10

--- a/solution.py
+++ b/solution.py
@@ -432,8 +432,6 @@
     gq.relay_last()
     traded(1)
     sent.append(send(xc.at[p.core], xc.at[p.core], c_send, c_mate, p.mate()))
-    trade(2)
-    trade(3)
     gq.finish()
     local[0].wait()
     puts = [
@@ -543,6 +541,8 @@
         put.start()
     gm.relay_across()
     gm.relay_rows()
+    trade(2)
+    trade(3)
 
     TILE = 256
     tiles = dm.P // TILE

time: 244 us -> 248 us (1.016)
  Pallas kernels: 237 us -> 241 us
    pallas_call x1, Pallas kernels: 85.2 us -> 88.8 us  [per_device(): pl.pallas_call(partial(forward_kernel, dm, left), out_shape=(sds((NT, D),...]
where the time goes in v11:
time: 248 us; the launch traced here: 247 us
  Pallas kernels  241 us (97%)
  other arithmetic  4.21 us (2%)
    pallas_call x1, Pallas kernels, per_device(): pl.pallas_call(partial(backward_kernel, dm, T, FC, plan_a, plan_b), out_s...  146 us
    pallas_call x1, Pallas kernels, per_device(): pl.pallas_call(partial(forward_kernel, dm, left), out_shape=(sds((NT, D),...  88.8 us
    pallas_call x1, Pallas kernels, per_device(): pl.pallas_call(partial(deliver_kernel, len(results)), out_shape=shapes +...  6 us

profile of v11, /device:TPU:0, one launch (start us, length us, event | category | flops | bytes accessed | tf_op | source)
XLA Modules:
  0.0 247.2 jit_solution(16345036836590110386)
XLA Ops:
  0.6 0.0 copy-start
  0.7 0.0 copy-start.1
  0.7 0.0 copy-start.2
  0.7 0.9 pad_maximum_fusion.2
  1.6 0.1 reshape.101
  1.7 0.1 copy.32
  1.8 1.3 multiply_sine_fusion
  3.1 1.1 copy.33
  4.2 0.8 pad_maximum_fusion.1.wq
  5.0 0.0 copy-done
  5.0 0.0 copy-done.1
  5.0 0.0 copy-done.2
  5.0 1.2 pad_maximum_fusion.wm
  6.2 88.8 %forward.1 = (bf16[512,768]{1,0:T(8,128)(2,1)}, bf16[512,768]{1,0:T(8,128)(2,1)}, f32[12,1,512]{2,1,0:T(1,128)}, f32[8,768]{1,0:T(8,128)}, f32[1152,128]{1,0:T(8...) custom-call(bf16[2,128,768]{2,1,0:T(8,128)(2,1)} %prompt.1, ...), custom_call_target="tpu_custom_call" | custom-call | tf_op jit(solution)/shard_map/forward/pallas_call | solution.py:1705
  95.0 146.1 %backward.1 = (bf16[256,768]{1,0:T(8,128)(2,1)}, bf16[256,768]{1,0:T(8,128)(2,1)}, bf16[256,768]{1,0:T(8,128)(2,1)}, bf16[256,768]{1,0:T(8,128)(2,1)}, f32[3,192...) custom-call(f32[5]{0:T(128)} %mix.1, ...), custom_call_target="tpu_custom_call" | custom-call | tf_op jit(solution)/shard_map/backward/pallas_call | solution.py:1759
  241.1 6.0 %deliver.1 = (bf16[256,768]{1,0:T(8,128)(2,1)}, bf16[256,768]{1,0:T(8,128)(2,1)}, bf16[256,768]{1,0:T(8,128)(2,1)}, bf16[256,768]{1,0:T(8,128)(2,1)}, f32[3,192,...) custom-call(bf16[256,768]{1,0:T(8,128)(2,1)} %get-tuple-element.67.r, ...), custom_call_target="tpu_custom_call" | custom-call | tf_op jit(solution)/shard_map/deliver/pallas_call | solution.py:1855
  (3 shorter events, 0.0 us)
Async XLA Ops:
  0.6 4.4 %copy-start = (bf16[1536,192]{0,1:T(8,128)(2,1)S(1)}, bf16[1536,192]{0,1:T(8,128)(2,1)}, u32[]{:S(2)}) copy-start(bf16[1536,192]{0,1:T(8,128)(2,1)} %param.30) | copy-start | bytes 1769476
  0.7 4.4 %copy-start.1 = (bf16[192,1536]{1,0:T(8,128)(2,1)S(1)}, bf16[192,1536]{1,0:T(8,128)(2,1)}, u32[]{:S(2)}) copy-start(bf16[192,1536]{1,0:T(8,128)(2,1)} %param.29) | copy-start | bytes 1769476
  0.7 4.4 %copy-start.2 = (bf16[384,192]{0,1:T(8,128)(2,1)S(1)}, bf16[384,192]{0,1:T(8,128)(2,1)}, u32[]{:S(2)}) copy-start(bf16[384,192]{0,1:T(8,128)(2,1)} %param.28) | copy-start | bytes 442372
